TPU v7x, 32 devices: a whole 2x2x4 slice. The times are simulated.
32 devices in a mesh: dp: 8 (over z, x), tensor: 4 (over y, core).
Axes of the slice: x: 2, y: 2, z: 4, core: 2. Of those that a mesh axis runs over, the one named last changes fastest.
Arguments:
- tokens: bfloat16 [8192, 768], P(('dp', 'tensor')), may hold values from -6 to 6
- cotangent: bfloat16 [8192, 768], P(('dp', 'tensor')), may hold values from -6 to 6
- seq_lengths: int32 [8], P('dp'), may hold values from 513 to 1024, as said below
- gain_mixer: bfloat16 [768], P('dp'), may hold values from 0.5 to 1.5
- mixer_query: bfloat16 [768, 768], P('dp', 'tensor'), may hold values from -0.21875 to 0.21875
- mixer_key: bfloat16 [768, 768], P('dp', 'tensor'), may hold values from -0.21875 to 0.21875
- mixer_value: bfloat16 [768, 768], P('dp', 'tensor'), may hold values from -0.21875 to 0.21875
- shift_taps: bfloat16 [64, 768], P('dp', 'tensor'), may hold values from -0.75 to 0.75
- ssm_decay: bfloat16 [768, 64], P('tensor', 'dp'), may hold values from 0.0019989014 to 0.5
- ssm_coef: bfloat16 [768, 64], P('tensor', 'dp'), may hold values from -0.75 to 0.75
- mixer_out: bfloat16 [768, 768], P('tensor', 'dp'), may hold values from -0.21875 to 0.21875
- gain_ffn1: bfloat16 [768], P('dp'), may hold values from 0.5 to 1.5
- ffn1_up: bfloat16 [768, 3072], P('dp', 'tensor'), may hold values from -0.21875 to 0.21875
- ffn1_down: bfloat16 [3072, 768], P('tensor', 'dp'), may hold values from -0.109375 to 0.109375
- gain_attn: bfloat16 [768], P('dp'), may hold values from 0.5 to 1.5
- attn_query: bfloat16 [768, 768], P('dp', 'tensor'), may hold values from -0.21875 to 0.21875
- attn_key: bfloat16 [768, 768], P('dp', 'tensor'), may hold values from -0.21875 to 0.21875
- attn_value: bfloat16 [768, 768], P('dp', 'tensor'), may hold values from -0.21875 to 0.21875
- attn_out: bfloat16 [768, 768], P('tensor', 'dp'), may hold values from -3.5 to 3.5
- gain_ffn2: bfloat16 [768], P('dp'), may hold values from 0.5 to 1.5
- ffn2_up: bfloat16 [768, 3072], P('dp', 'tensor'), may hold values from -0.21875 to 0.21875
- ffn2_down: bfloat16 [3072, 768], P('tensor', 'dp'), may hold values from -0.109375 to 0.109375
Outputs:
- output: bfloat16 [8192, 768], P(('dp', 'tensor'))
- input_grad: bfloat16 [8192, 768], P(('dp', 'tensor'))
- grad_gain_mixer: float32 [768], P('dp')
- grad_mixer_query: float32 [768, 768], P('dp', 'tensor')
- grad_mixer_key: float32 [768, 768], P('dp', 'tensor')
- grad_mixer_value: float32 [768, 768], P('dp', 'tensor')
- grad_shift_taps: float32 [64, 768], P('dp', 'tensor')
- grad_ssm_decay: float32 [768, 64], P('tensor', 'dp')
- grad_ssm_coef: float32 [768, 64], P('tensor', 'dp')
- grad_mixer_out: float32 [768, 768], P('tensor', 'dp')
- grad_gain_ffn1: float32 [768], P('dp')
- grad_ffn1_up: float32 [768, 3072], P('dp', 'tensor')
- grad_ffn1_down: float32 [3072, 768], P('tensor', 'dp')
- grad_gain_attn: float32 [768], P('dp')
- grad_attn_query: float32 [768, 768], P('dp', 'tensor')
- grad_attn_key: float32 [768, 768], P('dp', 'tensor')
- grad_attn_value: float32 [768, 768], P('dp', 'tensor')
- grad_attn_out: float32 [768, 768], P('tensor', 'dp')
- grad_gain_ffn2: float32 [768], P('dp')
- grad_ffn2_up: float32 [768, 3072], P('dp', 'tensor')
- grad_ffn2_down: float32 [3072, 768], P('tensor', 'dp')
Inputs may be any that keep to these rules, and one draw needn't show every extreme that they name: Row r holds one sequence in its first seq_lengths[r] positions, the rest of the row is padding; some row is full and some row holds 513 live tokens.
All inputs are finite; a program needn't handle non-finite values.
Results may differ from a plain program's by a relative error of at most 0.035.
Values may be sent and summed in bfloat16 or wider, within the bound.
No kernel may reach another device: no remote copies, remote signals or barrier semaphores. Data moves between devices by JAX's collectives and lax.ppermute only.
A program may use at most 320 MiB of HBM per device.

v0:
```python
import math

import jax
import jax.numpy as jnp
from jax import lax
from jax.sharding import PartitionSpec as P

HEAD = 64
SPAN = 128
BLOCK = 512


EPSILON = 1e-05
PRECISE = lax.Precision.HIGHEST


def norm_rows(hidden, gain):
    average = jnp.mean(hidden, axis=1, keepdims=True)
    centred = hidden - average
    inverse = lax.rsqrt(jnp.mean(centred * centred, axis=1, keepdims=True) + EPSILON)
    unit = centred * inverse
    return ((unit * gain[None, :]).astype(jnp.bfloat16), unit, inverse)


def norm_back(grad_norm, unit, inverse, gain):
    scaled = grad_norm * gain[None, :]
    first_mean = jnp.mean(scaled, axis=1, keepdims=True)
    second_mean = jnp.mean(scaled * unit, axis=1, keepdims=True)
    return (inverse * (scaled - first_mean - unit * second_mean), jnp.sum(grad_norm * unit, axis=0))


def rows_dot(left, right):
    return lax.dot_general(
        left, right, (((0,), (0,)), ((), ())), preferred_element_type=jnp.float32
    )


def cols_dot(left, right):
    return lax.dot_general(
        left, right, (((1,), (1,)), ((), ())), preferred_element_type=jnp.float32
    )


def spread(normed):
    return lax.all_gather(normed, "tensor", axis=0, tiled=True)


def merge_out(branch, weight):
    return lax.psum_scatter(
        jnp.dot(branch, weight, preferred_element_type=jnp.float32).astype(jnp.bfloat16),
        "tensor",
        scatter_dimension=0,
        tiled=True,
    ).astype(jnp.float32)


def pull_grad(grad_local):
    return lax.all_gather(grad_local.astype(jnp.bfloat16), "tensor", axis=0, tiled=True)


def push_grad(grad_rows, weight):
    return lax.psum_scatter(
        cols_dot(grad_rows, weight).astype(jnp.bfloat16), "tensor", scatter_dimension=0, tiled=True
    ).astype(jnp.float32)


def gelu_tanh(values):
    return jax.nn.gelu(values, approximate=True)


def mixer_head(operands):
    queries, key_rows, value_rows, taps_head, decay_head, coef_head = operands
    length = queries.shape[0]
    blocks = length // SPAN
    offsets = jnp.arange(SPAN)
    lag_grid = offsets[:, None] - offsets[None, :]
    taps_ext = jnp.concatenate(
        [taps_head, jnp.zeros((2 * SPAN - taps_head.shape[0], taps_head.shape[1]), jnp.float32)],
        axis=0,
    )
    near_tile = taps_ext[jnp.where(lag_grid >= 0, lag_grid, 2 * SPAN - 1)]
    far_tile = taps_ext[lag_grid + SPAN]
    key_blocks = key_rows.reshape(blocks, SPAN, -1)
    earlier = jnp.concatenate([jnp.zeros_like(key_blocks[:1]), key_blocks[:-1]], axis=0)
    shifted = jnp.einsum("ijc,mjc->mic", near_tile, key_blocks, precision=PRECISE) + jnp.einsum(
        "ijc,mjc->mic", far_tile, earlier, precision=PRECISE
    )
    inputs_ssm = shifted * value_rows.reshape(blocks, SPAN, -1)
    mixing = jnp.sqrt(2.0 * decay_head) * coef_head
    steps_f = offsets.astype(jnp.float32)
    kernel_near = jnp.einsum(
        "tcn,cn->tc", jnp.exp(-decay_head[None] * steps_f[:, None, None]), mixing, precision=PRECISE
    )
    inner_tile = jnp.where((lag_grid >= 0)[:, :, None], kernel_near[jnp.maximum(lag_grid, 0)], 0.0)
    local_part = jnp.einsum("ijc,mjc->mic", inner_tile, inputs_ssm, precision=PRECISE)
    leaving = jnp.exp(-decay_head[None] * (SPAN - 1.0 - steps_f)[:, None, None])
    block_sums = jnp.einsum("mjc,jcn->mcn", inputs_ssm, leaving, precision=PRECISE)
    block_decay = jnp.exp(-decay_head * SPAN)

    def advance(running, addend):
        return (block_decay * running + addend, running)

    _, prior_states = lax.scan(advance, jnp.zeros_like(block_sums[0]), block_sums)
    entering = jnp.exp(-decay_head[None] * (steps_f + 1.0)[:, None, None])
    carried = jnp.einsum("icn,mcn->mic", entering, prior_states * mixing[None], precision=PRECISE)
    return (queries.reshape(blocks, SPAN, -1) * (local_part + carried)).reshape(length, -1)


def mixer_core(projected, taps_all, decay_all, coef_all):
    columns = projected.shape[1] // 3
    length = projected.shape[0]
    head_count = columns // HEAD

    def to_heads(array):
        return array.reshape(array.shape[0], head_count, HEAD).transpose(1, 0, 2)

    outputs = lax.map(
        mixer_head,
        (
            to_heads(projected[:, :columns]),
            to_heads(projected[:, columns : 2 * columns]),
            to_heads(projected[:, 2 * columns :]),
            to_heads(taps_all),
            decay_all.reshape(head_count, HEAD, -1),
            coef_all.reshape(head_count, HEAD, -1),
        ),
    )
    return outputs.transpose(1, 0, 2).reshape(length, columns)


def joined_of(weights):
    return jnp.concatenate([weights[1], weights[2], weights[3]], axis=1)


def block_inputs(hidden, weights):
    normed, unit, inverse = norm_rows(hidden, weights[0].astype(jnp.float32))
    gathered = spread(normed)
    joined = joined_of(weights)
    projected = jnp.dot(gathered, joined, preferred_element_type=jnp.float32)
    return (gathered, unit, inverse, joined, projected)


def split_grads(grad_joined, gain_grad):
    columns = grad_joined.shape[1] // 3
    return (
        gain_grad,
        grad_joined[:, :columns],
        grad_joined[:, columns : 2 * columns],
        grad_joined[:, 2 * columns :],
    )


def mixer_forward(hidden, weights):
    gathered, unit, inverse, joined, projected = block_inputs(hidden, weights)
    mixed, pull_back = jax.vjp(
        mixer_core,
        projected,
        weights[4].astype(jnp.float32),
        weights[5].astype(jnp.float32),
        weights[6].astype(jnp.float32),
    )
    mixed_low = mixed.astype(jnp.bfloat16)
    out = merge_out(mixed_low, weights[7])
    return (out, (gathered, unit, inverse, mixed_low, pull_back))


def mixer_backward(saved, weights, grad_state):
    gathered, unit, inverse, mixed_low, pull_back = saved
    joined = joined_of(weights)
    grad_branch = pull_grad(grad_state)
    grad_outw = rows_dot(mixed_low, grad_branch)
    grad_proj, grad_taps, grad_decay, grad_coef = pull_back(cols_dot(grad_branch, weights[7]))
    grad_proj = grad_proj.astype(jnp.bfloat16)
    grad_joined = rows_dot(gathered, grad_proj)
    grad_norm = push_grad(grad_proj, joined)
    grad_hidden, grad_gain = norm_back(grad_norm, unit, inverse, weights[0].astype(jnp.float32))
    return (
        grad_state + grad_hidden,
        split_grads(grad_joined, grad_gain) + (grad_taps, grad_decay, grad_coef, grad_outw),
    )


def ffn_forward(hidden, gain, up_weight, down_weight):
    normed, unit, inverse = norm_rows(hidden, gain.astype(jnp.float32))
    gathered = spread(normed)
    hidden_up = jnp.dot(gathered, up_weight, preferred_element_type=jnp.float32)
    out = merge_out(gelu_tanh(hidden_up).astype(jnp.bfloat16), down_weight)
    return (out, (gathered, unit, inverse, hidden_up))


def ffn_backward(saved, gain, up_weight, down_weight, grad_state):
    rows_in, unit, inverse, hidden_up = saved
    active, gelu_pull = jax.vjp(gelu_tanh, hidden_up)
    grad_branch = pull_grad(grad_state)
    grad_down = rows_dot(active.astype(jnp.bfloat16), grad_branch)
    grad_up_rows = gelu_pull(cols_dot(grad_branch, down_weight))[0].astype(jnp.bfloat16)
    grad_upw = rows_dot(rows_in, grad_up_rows)
    grad_norm = push_grad(grad_up_rows, up_weight)
    grad_hidden, grad_gain = norm_back(grad_norm, unit, inverse, gain.astype(jnp.float32))
    return (grad_state + grad_hidden, (grad_gain, grad_upw, grad_down))


def masked_scores(query_blk, key_rows, first_row, length):
    scores = cols_dot(query_blk, key_rows) * (1.0 / math.sqrt(query_blk.shape[1]))
    query_pos = first_row + jnp.arange(query_blk.shape[0])
    key_pos = jnp.arange(key_rows.shape[0])
    allowed = (key_pos[None, :] <= query_pos[:, None]) & (key_pos[None, :] < length)
    return jnp.where(allowed, scores, -jnp.inf)


def head_forward(operands, length):
    queries, key_rows, value_rows = operands
    blocks = queries.shape[0] // BLOCK

    def one_block(block_idx):
        first_row = block_idx * BLOCK
        query_blk = lax.dynamic_slice_in_dim(queries, first_row, BLOCK, 0)
        scores = masked_scores(query_blk, key_rows, first_row, length)
        row_max = jnp.max(scores, axis=1, keepdims=True)
        powers = jnp.exp(scores - row_max)
        row_sum = jnp.sum(powers, axis=1, keepdims=True)
        probs_low = (powers / row_sum).astype(jnp.bfloat16)
        attended = jnp.dot(probs_low, value_rows, preferred_element_type=jnp.float32).astype(
            jnp.bfloat16
        )
        return (attended, (row_max + jnp.log(row_sum))[:, 0])

    attended, log_total = lax.map(one_block, jnp.arange(blocks))
    return (attended.reshape(queries.shape[0], -1), log_total.reshape(queries.shape[0]))


def head_back(operands, length):
    queries, key_rows, value_rows, log_total, grad_out = operands
    blocks = queries.shape[0] // BLOCK
    scale = 1.0 / math.sqrt(queries.shape[1])

    def one_block(totals, block_idx):
        grad_keys, grad_values = totals
        first_row = block_idx * BLOCK
        query_blk = lax.dynamic_slice_in_dim(queries, first_row, BLOCK, 0)
        total_blk = lax.dynamic_slice_in_dim(log_total, first_row, BLOCK, 0)
        grad_blk = lax.dynamic_slice_in_dim(grad_out, first_row, BLOCK, 0)
        probs = jnp.exp(masked_scores(query_blk, key_rows, first_row, length) - total_blk[:, None])
        grad_probs = cols_dot(grad_blk, value_rows)
        inner = jnp.sum(probs * grad_probs, axis=1, keepdims=True)
        grad_scores = (probs * (grad_probs - inner)).astype(jnp.bfloat16)
        grad_query = jnp.dot(grad_scores, key_rows, preferred_element_type=jnp.float32) * scale
        grad_keys = grad_keys + rows_dot(grad_scores, query_blk) * scale
        grad_values = grad_values + rows_dot(probs.astype(jnp.bfloat16), grad_blk)
        return ((grad_keys, grad_values), grad_query)

    empty = jnp.zeros(key_rows.shape, jnp.float32)
    (grad_keys, grad_values), grad_queries = lax.scan(one_block, (empty, empty), jnp.arange(blocks))
    return (grad_queries.reshape(queries.shape[0], -1), grad_keys, grad_values)


def to_heads(array):
    return array.reshape(array.shape[0], -1, HEAD).transpose(1, 0, 2)


def from_heads(array):
    return array.transpose(1, 0, 2).reshape(array.shape[1], -1)


def attn_forward(hidden, weights, length):
    gathered, unit, inverse, joined, projected = block_inputs(hidden, weights)
    columns = projected.shape[1] // 3
    queries = to_heads(projected[:, :columns].astype(jnp.bfloat16))
    key_rows = to_heads(projected[:, columns : 2 * columns].astype(jnp.bfloat16))
    value_rows = to_heads(projected[:, 2 * columns :].astype(jnp.bfloat16))

    def per_head(operands):
        return head_forward(operands, length)

    attended, log_total = lax.map(per_head, (queries, key_rows, value_rows))
    attended = from_heads(attended)
    out = merge_out(attended, weights[4])
    return (out, (gathered, unit, inverse, queries, key_rows, value_rows, attended, log_total))


def attn_backward(saved, weights, length, grad_state):
    gathered, unit, inverse, queries, key_rows, value_rows, attended, log_total = saved
    joined = joined_of(weights)
    grad_branch = pull_grad(grad_state)
    grad_outw = rows_dot(attended, grad_branch)
    grad_att = to_heads(cols_dot(grad_branch, weights[4]).astype(jnp.bfloat16))

    def per_head(operands):
        return head_back(operands, length)

    grad_q, grad_k, grad_v = lax.map(per_head, (queries, key_rows, value_rows, log_total, grad_att))
    grad_proj = jnp.concatenate(
        [from_heads(grad_q), from_heads(grad_k), from_heads(grad_v)], axis=1
    ).astype(jnp.bfloat16)
    grad_joined = rows_dot(gathered, grad_proj)
    grad_norm = push_grad(grad_proj, joined)
    grad_hidden, grad_gain = norm_back(grad_norm, unit, inverse, weights[0].astype(jnp.float32))
    return (grad_state + grad_hidden, split_grads(grad_joined, grad_gain) + (grad_outw,))


def on_device(
    tokens,
    cotangent,
    seq_lengths,
    gain_mixer,
    mixer_query,
    mixer_key,
    mixer_value,
    shift_taps,
    ssm_decay,
    ssm_coef,
    mixer_out,
    gain_ffn1,
    ffn1_up,
    ffn1_down,
    gain_attn,
    attn_query,
    attn_key,
    attn_value,
    attn_out,
    gain_ffn2,
    ffn2_up,
    ffn2_down,
):
    local_rows = tokens.shape[0]
    length = seq_lengths[0]
    positions = lax.axis_index("tensor") * local_rows + jnp.arange(local_rows)
    live = (positions < length).astype(jnp.float32)[:, None]
    mixer_set = (
        lax.all_gather(gain_mixer, "dp", axis=0, tiled=True),
        lax.all_gather(mixer_query, "dp", axis=0, tiled=True),
        lax.all_gather(mixer_key, "dp", axis=0, tiled=True),
        lax.all_gather(mixer_value, "dp", axis=0, tiled=True),
        lax.all_gather(shift_taps, "dp", axis=0, tiled=True),
        lax.all_gather(ssm_decay, "dp", axis=1, tiled=True),
        lax.all_gather(ssm_coef, "dp", axis=1, tiled=True),
        lax.all_gather(mixer_out, "dp", axis=1, tiled=True),
        lax.all_gather(gain_ffn1, "dp", axis=0, tiled=True),
        lax.all_gather(ffn1_up, "dp", axis=0, tiled=True),
        lax.all_gather(ffn1_down, "dp", axis=1, tiled=True),
    )
    start_state = tokens.astype(jnp.float32)
    mixer_branch, mixer_saved = mixer_forward(start_state, mixer_set)
    after_mixer = start_state + mixer_branch
    ffn1_branch, ffn1_saved = ffn_forward(after_mixer, mixer_set[8], mixer_set[9], mixer_set[10])
    after_ffn1 = after_mixer + ffn1_branch
    attn_set = (
        lax.all_gather(gain_attn, "dp", axis=0, tiled=True),
        lax.all_gather(attn_query, "dp", axis=0, tiled=True),
        lax.all_gather(attn_key, "dp", axis=0, tiled=True),
        lax.all_gather(attn_value, "dp", axis=0, tiled=True),
        lax.all_gather(attn_out, "dp", axis=1, tiled=True),
        lax.all_gather(gain_ffn2, "dp", axis=0, tiled=True),
        lax.all_gather(ffn2_up, "dp", axis=0, tiled=True),
        lax.all_gather(ffn2_down, "dp", axis=1, tiled=True),
    )
    attn_branch, attn_saved = attn_forward(after_ffn1, attn_set, length)
    after_attn = after_ffn1 + attn_branch
    ffn2_branch, ffn2_saved = ffn_forward(after_attn, attn_set[5], attn_set[6], attn_set[7])
    final_state = after_attn + ffn2_branch
    output = final_state.astype(jnp.bfloat16)
    grad_state = cotangent.astype(jnp.float32) * live
    attn_back_set = (
        lax.all_gather(gain_attn, "dp", axis=0, tiled=True),
        lax.all_gather(attn_query, "dp", axis=0, tiled=True),
        lax.all_gather(attn_key, "dp", axis=0, tiled=True),
        lax.all_gather(attn_value, "dp", axis=0, tiled=True),
        lax.all_gather(attn_out, "dp", axis=1, tiled=True),
        lax.all_gather(gain_ffn2, "dp", axis=0, tiled=True),
        lax.all_gather(ffn2_up, "dp", axis=0, tiled=True),
        lax.all_gather(ffn2_down, "dp", axis=1, tiled=True),
    )
    grad_state, ffn2_grads = ffn_backward(
        ffn2_saved, attn_back_set[5], attn_back_set[6], attn_back_set[7], grad_state
    )
    grad_state, attn_grads = attn_backward(attn_saved, attn_back_set, length, grad_state)
    attn_done = (
        lax.psum_scatter(
            attn_grads[0].astype(jnp.bfloat16), "dp", scatter_dimension=0, tiled=True
        ).astype(jnp.float32),
        lax.psum_scatter(
            attn_grads[1].astype(jnp.bfloat16), "dp", scatter_dimension=0, tiled=True
        ).astype(jnp.float32),
        lax.psum_scatter(
            attn_grads[2].astype(jnp.bfloat16), "dp", scatter_dimension=0, tiled=True
        ).astype(jnp.float32),
        lax.psum_scatter(
            attn_grads[3].astype(jnp.bfloat16), "dp", scatter_dimension=0, tiled=True
        ).astype(jnp.float32),
        lax.psum_scatter(
            attn_grads[4].astype(jnp.bfloat16), "dp", scatter_dimension=1, tiled=True
        ).astype(jnp.float32),
        lax.psum_scatter(
            ffn2_grads[0].astype(jnp.bfloat16), "dp", scatter_dimension=0, tiled=True
        ).astype(jnp.float32),
        lax.psum_scatter(
            ffn2_grads[1].astype(jnp.bfloat16), "dp", scatter_dimension=0, tiled=True
        ).astype(jnp.float32),
        lax.psum_scatter(
            ffn2_grads[2].astype(jnp.bfloat16), "dp", scatter_dimension=1, tiled=True
        ).astype(jnp.float32),
    )
    mixer_back_set = (
        lax.all_gather(gain_mixer, "dp", axis=0, tiled=True),
        lax.all_gather(mixer_query, "dp", axis=0, tiled=True),
        lax.all_gather(mixer_key, "dp", axis=0, tiled=True),
        lax.all_gather(mixer_value, "dp", axis=0, tiled=True),
        lax.all_gather(shift_taps, "dp", axis=0, tiled=True),
        lax.all_gather(ssm_decay, "dp", axis=1, tiled=True),
        lax.all_gather(ssm_coef, "dp", axis=1, tiled=True),
        lax.all_gather(mixer_out, "dp", axis=1, tiled=True),
        lax.all_gather(gain_ffn1, "dp", axis=0, tiled=True),
        lax.all_gather(ffn1_up, "dp", axis=0, tiled=True),
        lax.all_gather(ffn1_down, "dp", axis=1, tiled=True),
    )
    grad_state, ffn1_grads = ffn_backward(
        ffn1_saved, mixer_back_set[8], mixer_back_set[9], mixer_back_set[10], grad_state
    )
    grad_state, mixer_grads = mixer_backward(mixer_saved, mixer_back_set, grad_state)
    mixer_done = (
        lax.psum_scatter(
            mixer_grads[0].astype(jnp.bfloat16), "dp", scatter_dimension=0, tiled=True
        ).astype(jnp.float32),
        lax.psum_scatter(
            mixer_grads[1].astype(jnp.bfloat16), "dp", scatter_dimension=0, tiled=True
        ).astype(jnp.float32),
        lax.psum_scatter(
            mixer_grads[2].astype(jnp.bfloat16), "dp", scatter_dimension=0, tiled=True
        ).astype(jnp.float32),
        lax.psum_scatter(
            mixer_grads[3].astype(jnp.bfloat16), "dp", scatter_dimension=0, tiled=True
        ).astype(jnp.float32),
        lax.psum_scatter(
            mixer_grads[4].astype(jnp.bfloat16), "dp", scatter_dimension=0, tiled=True
        ).astype(jnp.float32),
        lax.psum_scatter(
            mixer_grads[5].astype(jnp.bfloat16), "dp", scatter_dimension=1, tiled=True
        ).astype(jnp.float32),
        lax.psum_scatter(
            mixer_grads[6].astype(jnp.bfloat16), "dp", scatter_dimension=1, tiled=True
        ).astype(jnp.float32),
        lax.psum_scatter(
            mixer_grads[7].astype(jnp.bfloat16), "dp", scatter_dimension=1, tiled=True
        ).astype(jnp.float32),
        lax.psum_scatter(
            ffn1_grads[0].astype(jnp.bfloat16), "dp", scatter_dimension=0, tiled=True
        ).astype(jnp.float32),
        lax.psum_scatter(
            ffn1_grads[1].astype(jnp.bfloat16), "dp", scatter_dimension=0, tiled=True
        ).astype(jnp.float32),
        lax.psum_scatter(
            ffn1_grads[2].astype(jnp.bfloat16), "dp", scatter_dimension=1, tiled=True
        ).astype(jnp.float32),
    )
    gain_grads = lax.psum((mixer_done[0], mixer_done[8], attn_done[0], attn_done[5]), "tensor")
    return (
        output,
        grad_state.astype(jnp.bfloat16),
        gain_grads[0],
        mixer_done[1],
        mixer_done[2],
        mixer_done[3],
        mixer_done[4],
        mixer_done[5],
        mixer_done[6],
        mixer_done[7],
        gain_grads[1],
        mixer_done[9],
        mixer_done[10],
        gain_grads[2],
        attn_done[1],
        attn_done[2],
        attn_done[3],
        attn_done[4],
        gain_grads[3],
        attn_done[6],
        attn_done[7],
    )


def solution(mesh):
    placed = (
        P(("dp", "tensor"), None),
        P(("dp", "tensor"), None),
        P("dp"),
        P("dp"),
        P("dp", "tensor"),
        P("dp", "tensor"),
        P("dp", "tensor"),
        P("dp", "tensor"),
        P("tensor", "dp"),
        P("tensor", "dp"),
        P("tensor", "dp"),
        P("dp"),
        P("dp", "tensor"),
        P("tensor", "dp"),
        P("dp"),
        P("dp", "tensor"),
        P("dp", "tensor"),
        P("dp", "tensor"),
        P("tensor", "dp"),
        P("dp"),
        P("dp", "tensor"),
        P("tensor", "dp"),
    )
    return jax.shard_map(
        on_device,
        mesh=mesh,
        in_specs=placed,
        out_specs=(
            P(("dp", "tensor"), None),
            P(("dp", "tensor"), None),
            P("dp"),
            P("dp", "tensor"),
            P("dp", "tensor"),
            P("dp", "tensor"),
            P("dp", "tensor"),
            P("tensor", "dp"),
            P("tensor", "dp"),
            P("tensor", "dp"),
            P("dp"),
            P("dp", "tensor"),
            P("tensor", "dp"),
            P("dp"),
            P("dp", "tensor"),
            P("dp", "tensor"),
            P("dp", "tensor"),
            P("tensor", "dp"),
            P("dp"),
            P("dp", "tensor"),
            P("tensor", "dp"),
        ),
        check_vma=False,
    )
```

profile of v0, /device:TPU:0, one launch (start us, length us, event | category | flops | bytes accessed | tf_op | source)
XLA Modules:
  0.0 3536.5 jit_solution(15452049427732482334)
XLA Ops:
  265.8 822.6 %while.212 = (s32[]{:T(128)}, bf16[3,1024,64]{1,2,0:T(8,128)(2,1)S(1)}, f32[3,128,128,64]{2,1,3,0:T(8,128)}, f32[3,8,128,64]{2,1,3,0:T(8,128)}, f32[3,128,128,64...) while((s32[]{:T(128)}, ...), condition=%wide.region_5.6_spmd.clone.clone.clone, body=%wide.region_2.5_spmd.clone.clone.sunk.clone | while | flops 414851712 | bytes 165325712 | solution.py:117
  337.0 54.8 %gather_fusion.1 = f32[16384,64]{1,0:T(8,128)} fusion(f32[256,64]{1,0:T(8,128)S(1)} %concatenate.40, s32[16384]{0:T(1024)S(1)} %fusion.450), kind=kCustom, calls=%fused_computation.1.clone.clone.1.clone | custom fusion | bytes 8454144 | tf_op jit(solution)/shard_map/jvp()/while/body/eval_jaxpr/gather | solution.py:82
  412.1 54.8 %gather_fusion.2 = f32[16384,64]{1,0:T(8,128)} fusion(f32[128,64]{1,0:T(8,128)S(1)} %bitcast.792, s32[16384]{0:T(1024)S(1)} %bitcast_clamp_fusion.3), kind=kCustom, calls=%fused_computation.2.clone.clone.1.clone | custom fusion | bytes 8454144 | tf_op jit(solution)/shard_map/jvp()/while/body/eval_jaxpr/gather | solution.py:94
  611.2 54.8 %gather_fusion.1 = f32[16384,64]{1,0:T(8,128)} fusion(f32[256,64]{1,0:T(8,128)S(1)} %concatenate.40, s32[16384]{0:T(1024)S(1)} %fusion.450), kind=kCustom, calls=%fused_computation.1.clone.clone.1.clone | custom fusion | bytes 8454144 | tf_op jit(solution)/shard_map/jvp()/while/body/eval_jaxpr/gather | solution.py:82
  686.2 54.8 %gather_fusion.2 = f32[16384,64]{1,0:T(8,128)} fusion(f32[128,64]{1,0:T(8,128)S(1)} %bitcast.792, s32[16384]{0:T(1024)S(1)} %bitcast_clamp_fusion.3), kind=kCustom, calls=%fused_computation.2.clone.clone.1.clone | custom fusion | bytes 8454144 | tf_op jit(solution)/shard_map/jvp()/while/body/eval_jaxpr/gather | solution.py:94
  885.1 54.8 %gather_fusion.1 = f32[16384,64]{1,0:T(8,128)} fusion(f32[256,64]{1,0:T(8,128)S(1)} %concatenate.40, s32[16384]{0:T(1024)S(1)} %fusion.450), kind=kCustom, calls=%fused_computation.1.clone.clone.1.clone | custom fusion | bytes 8454144 | tf_op jit(solution)/shard_map/jvp()/while/body/eval_jaxpr/gather | solution.py:82
  960.1 54.8 %gather_fusion.2 = f32[16384,64]{1,0:T(8,128)} fusion(f32[128,64]{1,0:T(8,128)S(1)} %bitcast.792, s32[16384]{0:T(1024)S(1)} %bitcast_clamp_fusion.3), kind=kCustom, calls=%fused_computation.2.clone.clone.1.clone | custom fusion | bytes 8454144 | tf_op jit(solution)/shard_map/jvp()/while/body/eval_jaxpr/gather | solution.py:94
  1636.9 93.5 %while.208 = (s32[]{:T(128)}, bf16[3,1024,64]{1,2,0:T(8,128)(2,1)}, bf16[3,1024,64]{1,2,0:T(8,128)(2,1)}, bf16[3,1024,64]{1,2,0:T(8,128)(2,1)}, bf16[3,1024,64]{...) while((s32[]{:T(128)}, bf16[3,1024,64]{1,2,0:T(8,128)(2,1)}, ...), condition=%wide.region_29.30_spmd.clone, body=%wide.region_25.29_spmd.sunk.clone | while | flops 341672960 | bytes 20997648 | solution.py:291
  1860.8 1180.8 %while.210 = (s32[]{:T(128)}, f32[3,1024,64]{1,2,0:T(8,128)}, f32[3,1024,64]{1,2,0:T(8,128)}, f32[3,1024,64]{1,2,0:T(8,128)}, bf16[3,64,64]{2,1,0:T(8,128)(2,1)}...) while((s32[]{:T(128)}, f32[3,1024,64]{1,2,0:T(8,128)}, ...), condition=%wide.region_46.47_spmd.clone.clone, body=%wide.region_36.46_spmd.clone.sunk.clone | while | flops 816571008 | bytes 78044440 | solution.py:117
  1918.4 98.1 %scatter_custom_fusion.25 = f32[256,64]{1,0:T(8,128)S(1)} fusion(s32[16384]{0:T(1024)S(1)} %fusion.437, f32[16384,64]{1,0:T(8,128)} %bitcast.799, f32[]{:T(128)} %constant.339.clone.1..sunk.2), kind=kCustom, calls=%fused_computation.219.clone.1.clone | custom fusion | flops 1048576 | bytes 66048 | tf_op jit(solution)/shard_map/transpose(jvp())/while/body/eval_jaxpr/scatter-add | solution.py:81
  2032.7 87.7 %scatter_custom_fusion.26 = f32[256,64]{1,0:T(8,128)S(1)} fusion(s32[16384]{0:T(1024)S(1)} %fusion.438, f32[16384,64]{1,0:T(8,128)} %bitcast.800, f32[]{:T(128)} %constant.339.clone.1..sunk.2), kind=kCustom, calls=%fused_computation.221.clone.1.clone | custom fusion | flops 1048576 | bytes 66048 | tf_op jit(solution)/shard_map/transpose(jvp())/while/body/eval_jaxpr/scatter-add | solution.py:82
  2135.7 98.3 %scatter_custom_fusion.24 = f32[128,64]{1,0:T(8,128)S(1)} fusion(s32[16384]{0:T(1024)S(1)} %maximum_bitcast_fusion.3, f32[16384,64]{1,0:T(8,128)} %bitcast.798, f32[]{:T(128)} %constant.339.clone.1..sunk.2), kind=kCustom, calls=%fused_computation.234.clone.1.clone | custom fusion | flops 1048576 | bytes 33280 | tf_op jit(solution)/shard_map/transpose(jvp())/while/body/eval_jaxpr/scatter-add | solution.py:94
  2303.4 98.1 %scatter_custom_fusion.25 = f32[256,64]{1,0:T(8,128)S(1)} fusion(s32[16384]{0:T(1024)S(1)} %fusion.437, f32[16384,64]{1,0:T(8,128)} %bitcast.799, f32[]{:T(128)} %constant.339.clone.1..sunk.2), kind=kCustom, calls=%fused_computation.219.clone.1.clone | custom fusion | flops 1048576 | bytes 66048 | tf_op jit(solution)/shard_map/transpose(jvp())/while/body/eval_jaxpr/scatter-add | solution.py:81
  2417.7 87.7 %scatter_custom_fusion.26 = f32[256,64]{1,0:T(8,128)S(1)} fusion(s32[16384]{0:T(1024)S(1)} %fusion.438, f32[16384,64]{1,0:T(8,128)} %bitcast.800, f32[]{:T(128)} %constant.339.clone.1..sunk.2), kind=kCustom, calls=%fused_computation.221.clone.1.clone | custom fusion | flops 1048576 | bytes 66048 | tf_op jit(solution)/shard_map/transpose(jvp())/while/body/eval_jaxpr/scatter-add | solution.py:82
  2520.6 98.3 %scatter_custom_fusion.24 = f32[128,64]{1,0:T(8,128)S(1)} fusion(s32[16384]{0:T(1024)S(1)} %maximum_bitcast_fusion.3, f32[16384,64]{1,0:T(8,128)} %bitcast.798, f32[]{:T(128)} %constant.339.clone.1..sunk.2), kind=kCustom, calls=%fused_computation.234.clone.1.clone | custom fusion | flops 1048576 | bytes 33280 | tf_op jit(solution)/shard_map/transpose(jvp())/while/body/eval_jaxpr/scatter-add | solution.py:94
  2688.3 98.1 %scatter_custom_fusion.25 = f32[256,64]{1,0:T(8,128)S(1)} fusion(s32[16384]{0:T(1024)S(1)} %fusion.437, f32[16384,64]{1,0:T(8,128)} %bitcast.799, f32[]{:T(128)} %constant.339.clone.1..sunk.2), kind=kCustom, calls=%fused_computation.219.clone.1.clone | custom fusion | flops 1048576 | bytes 66048 | tf_op jit(solution)/shard_map/transpose(jvp())/while/body/eval_jaxpr/scatter-add | solution.py:81
  2802.6 87.7 %scatter_custom_fusion.26 = f32[256,64]{1,0:T(8,128)S(1)} fusion(s32[16384]{0:T(1024)S(1)} %fusion.438, f32[16384,64]{1,0:T(8,128)} %bitcast.800, f32[]{:T(128)} %constant.339.clone.1..sunk.2), kind=kCustom, calls=%fused_computation.221.clone.1.clone | custom fusion | flops 1048576 | bytes 66048 | tf_op jit(solution)/shard_map/transpose(jvp())/while/body/eval_jaxpr/scatter-add | solution.py:82
  2905.5 98.3 %scatter_custom_fusion.24 = f32[128,64]{1,0:T(8,128)S(1)} fusion(s32[16384]{0:T(1024)S(1)} %maximum_bitcast_fusion.3, f32[16384,64]{1,0:T(8,128)} %bitcast.798, f32[]{:T(128)} %constant.339.clone.1..sunk.2), kind=kCustom, calls=%fused_computation.234.clone.1.clone | custom fusion | flops 1048576 | bytes 33280 | tf_op jit(solution)/shard_map/transpose(jvp())/while/body/eval_jaxpr/scatter-add | solution.py:94
  3098.6 55.1 %reduce-scatter.78.cloned.1.call-done = bf16[8,192]{1,0:T(8,128)(2,1)} async-done(((bf16[64,192]{1,0:T(8,128)(2,1)}), bf16[8,192]{1,0:T(8,128)(2,1)}) %reduce-scatter.78.cloned.1.call-update) | async-done | bytes 3088
  3155.2 55.1 %reduce-scatter.80.cloned.1.call-done = bf16[8,192]{1,0:T(8,128)(2,1)} async-done(((bf16[64,192]{1,0:T(8,128)(2,1)}), bf16[8,192]{1,0:T(8,128)(2,1)}) %reduce-scatter.80.cloned.1.call-update) | async-done | bytes 3088
  3211.7 62.5 %reduce-scatter.82.cloned.1.call-done = bf16[96,192]{1,0:T(8,128)(2,1)} async-done(((bf16[768,192]{1,0:T(8,128)(2,1)}), bf16[96,192]{1,0:T(8,128)(2,1)}) %reduce-scatter.82.cloned.1.call-update) | async-done | bytes 36880
  3275.8 63.2 %reduce-scatter.70.cloned.1.call-done = bf16[96,192]{1,0:T(8,128)(2,1)} async-done(((bf16[768,192]{1,0:T(8,128)(2,1)}), bf16[96,192]{1,0:T(8,128)(2,1)}) %reduce-scatter.70.cloned.1.call-update) | async-done | bytes 36880
  3340.7 62.3 %reduce-scatter.72.cloned.1.call-done = bf16[96,192]{1,0:T(8,128)(2,1)} async-done(((bf16[768,192]{1,0:T(8,128)(2,1)}), bf16[96,192]{1,0:T(8,128)(2,1)}) %reduce-scatter.72.cloned.1.call-update) | async-done | bytes 36880
  3404.7 62.5 %reduce-scatter.74.cloned.1.call-done = bf16[96,192]{1,0:T(8,128)(2,1)} async-done(((bf16[768,192]{1,0:T(8,128)(2,1)}), bf16[96,192]{1,0:T(8,128)(2,1)}) %reduce-scatter.74.cloned.1.call-update) | async-done | bytes 36880
  (1172 shorter events, 2078.5 us)
Async XLA Ops:
  8.1 254.0 %all-gather.13.cloned.1.call-start = ((), (), s32[]{:S(2)}) async-start(), calls=%async_computation.23 | async-start | bytes 1966080 | tf_op jit(solution)/shard_map/all_gather | solution.py:45
  41.8 1075.4 %reduce-scatter.46.cloned.1.call-start = ((), (), s32[]{:S(2)}) async-start(), calls=%async_computation.24 | async-start | bytes 1966080 | tf_op jit(solution)/shard_map/reduce_scatter | solution.py:49
  1122.3 107.2 %reduce-scatter.48.cloned.1.call-start = ((), (), s32[]{:S(2)}) async-start(), calls=%async_computation.28 | async-start | bytes 1966080 | tf_op jit(solution)/shard_map/reduce_scatter | solution.py:49
  1202.7 156.1 %all-gather.21.cloned.1.call-start = ((), (), s32[]{:S(2)}) async-start(), calls=%async_computation.29 | async-start | bytes 1966080 | tf_op jit(solution)/shard_map/all_gather | solution.py:45
  1231.9 208.9 %reduce-scatter.50.cloned.1.call-start = ((), (), s32[]{:S(2)}) async-start(), calls=%async_computation.30 | async-start | bytes 1966080 | tf_op jit(solution)/shard_map/reduce_scatter | solution.py:49
  1415.4 126.0 %all-gather.23.cloned.1.call-start = ((), (), s32[]{:S(2)}) async-start(), calls=%async_computation.31 | async-start | bytes 1966080 | tf_op jit(solution)/shard_map/all_gather | solution.py:45
  1443.1 137.5 %reduce-scatter.54.cloned.1.call-start = ((), (), s32[]{:S(2)}) async-start(), calls=%async_computation.36 | async-start | bytes 1966080 | tf_op jit(solution)/shard_map/reduce_scatter | solution.py:62
  1614.0 149.2 %reduce-scatter.56.cloned.1.call-start = ((), (), s32[]{:S(2)}) async-start(), calls=%async_computation.38 | async-start | bytes 1966080 | tf_op jit(solution)/shard_map/reduce_scatter | solution.py:62
  1829.0 1230.4 %reduce-scatter.66.cloned.1.call-start = ((), (), s32[]{:S(2)}) async-start(), calls=%async_computation.45 | async-start | bytes 1327104 | tf_op jit(solution)/shard_map/reduce_scatter | solution.py:396
  1833.8 1227.3 %reduce-scatter.68.cloned.1.call-start = ((), (), s32[]{:S(2)}) async-start(), calls=%async_computation.46 | async-start | bytes 1327104 | tf_op jit(solution)/shard_map/reduce_scatter | solution.py:399
  1838.8 1224.0 %reduce-scatter.90.cloned.1.call-start = ((), (), s32[]{:S(2)}) async-start(), calls=%async_computation.57 | async-start | bytes 442368
  1840.3 1224.0 %reduce-scatter.84.cloned.1.call-start = ((), (), s32[]{:S(2)}) async-start(), calls=%async_computation.54 | async-start | bytes 442368
  1844.0 1222.0 %reduce-scatter.86.cloned.1.call-start = ((), (), s32[]{:S(2)}) async-start(), calls=%async_computation.55 | async-start | bytes 442368
  1845.0 1222.6 %reduce-scatter.88.cloned.1.call-start = ((), (), s32[]{:S(2)}) async-start(), calls=%async_computation.56 | async-start | bytes 442368
  1846.0 1223.2 %reduce-scatter.64.cloned.1.call-start = ((), (), s32[]{:S(2)}) async-start(), calls=%async_computation.44 | async-start | bytes 1327104 | tf_op jit(solution)/shard_map/reduce_scatter | solution.py:451
  1850.9 1220.0 %reduce-scatter.62.cloned.1.call-start = ((), (), s32[]{:S(2)}) async-start(), calls=%async_computation.43 | async-start | bytes 1327104 | tf_op jit(solution)/shard_map/reduce_scatter | solution.py:448
  1855.6 1241.5 %reduce-scatter.76.cloned.1.call-start = ((), (), s32[]{:S(2)}) async-start(), calls=%async_computation.50 | async-start | bytes 36864
  3043.3 110.3 %reduce-scatter.78.cloned.1.call-start = ((), (), s32[]{:S(2)}) async-start(), calls=%async_computation.51 | async-start | bytes 36864
  3044.1 166.1 %reduce-scatter.80.cloned.1.call-start = ((), (), s32[]{:S(2)}) async-start(), calls=%async_computation.52 | async-start | bytes 36864
  3045.7 228.6 %reduce-scatter.82.cloned.1.call-start = ((), (), s32[]{:S(2)}) async-start(), calls=%async_computation.53 | async-start | bytes 442368
  3048.6 290.4 %reduce-scatter.70.cloned.1.call-start = ((), (), s32[]{:S(2)}) async-start(), calls=%async_computation.47 | async-start | bytes 442368
  3052.5 350.5 %reduce-scatter.72.cloned.1.call-start = ((), (), s32[]{:S(2)}) async-start(), calls=%async_computation.48 | async-start | bytes 442368
  3053.5 413.6 %reduce-scatter.74.cloned.1.call-start = ((), (), s32[]{:S(2)}) async-start(), calls=%async_computation.49 | async-start | bytes 442368
  3054.5 442.5 %reduce-scatter.60.cloned.1.call-start = ((), (), s32[]{:S(2)}) async-start(), calls=%async_computation.42 | async-start | bytes 1966080 | tf_op jit(solution)/shard_map/reduce_scatter | solution.py:62
  (162 other events, 10514.6 us)
Sparse Core Ops, SparseCore 0:
  41.9 16.9 all-gather.12
  1091.7 25.4 reduce-scatter.45
  1202.8 26.6 reduce-scatter.47
  1412.6 28.1 reduce-scatter.49
  1552.5 28.1 reduce-scatter.53
  1583.1 28.1 reduce-scatter.51
  1734.9 28.1 reduce-scatter.55
  1796.3 28.1 reduce-scatter.57
Sparse Core Ops, SparseCore 1:
  1094.5 38.8 all-gather.16
  1155.7 41.5 all-gather.18
  1232.0 19.5 all-gather.20
  1415.7 41.5 all-gather.26
  1479.7 41.5 all-gather.24
  1614.1 19.5 all-gather.30
  1767.4 19.5 all-gather.32
  1829.0 19.5 all-gather.34
  1852.3 64.1 reduce-scatter.65
  1920.1 63.3 reduce-scatter.67
  1987.1 60.5 reduce-scatter.89
  2051.3 60.5 reduce-scatter.83
  2115.5 60.5 reduce-scatter.85
  2179.8 60.5 reduce-scatter.87
  2244.1 63.2 reduce-scatter.63
  2311.0 63.2 reduce-scatter.61
  3043.4 53.6 reduce-scatter.75
  3101.0 52.6 reduce-scatter.77
  3157.5 52.6 reduce-scatter.79
  3213.7 60.5 reduce-scatter.81
  3278.5 60.5 reduce-scatter.69
  3342.5 60.5 reduce-scatter.71
  3406.6 60.4 reduce-scatter.73
  3469.8 27.1 reduce-scatter.59
  (3 shorter events, 53.9 us)
where the time goes:
time: 3550 us; the launch traced here: 3540 us
  other arithmetic  985 us (28%)
  local copies, waits for them, and re-layouts  860 us (24%)
  waiting for transfers between devices  800 us (23%)
  matrix products  436 us (12%)
  blocking collectives  396 us (11%)
  loops' own time  38.6 us (1%)
    unnamed x46, waiting for transfers between devices  388 us
    scatter-add x3, other arithmetic, mixer_head(): kernel_near[jnp.maximum(lag_grid, 0)]  295 us
    scatter-add x3, other arithmetic, mixer_head(): near_tile = taps_ext[jnp.where(lag_grid >= 0, lag_grid, 2 * SPAN - 1)]  294 us
    scatter-add x3, other arithmetic, mixer_head(): far_tile = taps_ext[lag_grid + SPAN]  263 us
    gather x6, local copies, waits for them, and re-layouts, mixer_head(): far_tile = taps_ext[lag_grid + SPAN]  187 us
    gather x6, local copies, waits for them, and re-layouts, mixer_head(): kernel_near[jnp.maximum(lag_grid, 0)]  186 us
    gather x6, local copies, waits for them, and re-layouts, mixer_head(): near_tile = taps_ext[jnp.where(lag_grid >= 0, lag_grid, 2 * SPAN - 1)]  186 us
    dynamic_update_slice x45, local copies, waits for them, and re-layouts, mixer_core(): lax.map(mixer_head, (to_heads(projected[:, :columns]), to_heads(projected...  117 us
  transfers between devices with their start and end apart: 35, of which 24 were waited for; matrix products, arithmetic and copies ran while one was open for 35% of the time, Pallas kernels for 0%

commit v1 on v0

v1 whole, which is shorter than its diff:
```python
import math
import numpy as np
import jax
import jax.numpy as jnp
from jax import lax
from jax.experimental import pallas as pl
from jax.experimental.pallas import tpu as pltpu
from jax.sharding import PartitionSpec as P

F32 = jnp.float32
BF16 = jnp.bfloat16
BLK = 128
VMEM_LIMIT = 56 * 1024 * 1024


def dot(a, b):
    return jnp.dot(a, b, preferred_element_type=F32)


def dot_nt(a, b):
    return lax.dot_general(a, b, (((1,), (1,)), ((), ())), preferred_element_type=F32)


def split(x):
    high = x.astype(BF16)
    return high, (x - high.astype(F32)).astype(BF16)


def spectral_tables():
    j = np.arange(BLK)
    f = np.arange(BLK)
    angle = 2.0 * np.pi * np.outer(f, j) / (2 * BLK)
    alternating = (-1.0) ** j
    real = np.cos(angle)
    imag = -np.sin(angle)
    imag[0] = alternating
    forward = np.concatenate([real, imag], axis=0)
    weight = np.full((BLK, 1), 2.0)
    weight[0] = 1.0
    back_real = weight * real / (2 * BLK)
    back_imag = 2.0 * imag / (2 * BLK)
    back_imag[0] = alternating / (2 * BLK)
    inverse = np.concatenate([back_real, back_imag], axis=0).T

    def halves(table):
        high = table.astype(jnp.bfloat16)
        low = (table - high.astype(np.float64)).astype(jnp.bfloat16)
        return high, low

    fh, fl = halves(forward)
    ih, il = halves(inverse)
    fwd = np.concatenate([fh, fh, fl], axis=1)
    inv = np.concatenate([ih, il], axis=0)
    return jnp.asarray(fwd), jnp.asarray(inv)


def to_spectrum(fwd_ref, x):
    high, low = split(x)
    return dot(fwd_ref[:, : 2 * BLK], jnp.concatenate([high, low], axis=0)) + dot(
        fwd_ref[:, 2 * BLK :], high
    )


def from_spectrum(inv_ref, z):
    high, low = split(z)
    both = dot(inv_ref[...], high)
    return both[:BLK] + both[BLK:] + dot(inv_ref[:BLK, :], low)


def sign_rows(shape):
    row = lax.broadcasted_iota(jnp.int32, shape, 0)
    return jnp.where(row % 2 == 0, 1.0, -1.0).astype(F32)


def lane_tiles(width):
    return [(s, min(128, width - s)) for s in range(0, width, 128)]


def fix_first(tile, re, im):
    row = lax.broadcasted_iota(jnp.int32, re.shape, 0)
    special = (row == 0) & (tile == 0)
    return jnp.where(special, im, re), jnp.where(special, 0.0, im)


def kgen_body(decay_ref, coef_ref, taps_ref, fwd_ref, kre_ref, kim_ref, tre_ref, tim_ref, mixp, kern):
    states, width = decay_ref.shape
    blocks = kre_ref.shape[0]
    decay = decay_ref[...]
    mixing = jnp.sqrt(2.0 * decay) * coef_ref[...]
    for m in range(blocks):
        mixp[m] = mixing * jnp.exp(decay * (-float(BLK * m)))
    for start, size in lane_tiles(width):
        lanes = slice(start, start + size)

        def per_tile(jt, _, lanes=lanes, size=size):
            steps = (lax.broadcasted_iota(jnp.int32, (8, size), 0) + jt * 8).astype(F32)

            def per_states(ng, acc):
                rows = pl.ds(pl.multiple_of(ng * 8, 8), 8)
                rates = -decay_ref[rows, lanes]
                scales = [mixp[m, rows, lanes] for m in range(blocks)]
                for i in range(8):
                    e = jnp.exp(rates[i : i + 1] * steps)
                    acc = tuple(a + e * s[i : i + 1] for a, s in zip(acc, scales))
                return acc

            acc = lax.fori_loop(
                0, states // 8, per_states, tuple(jnp.zeros((8, size), F32) for _ in range(blocks))
            )
            for m in range(blocks):
                kern[m, pl.ds(pl.multiple_of(jt * 8, 8), 8), lanes] = acc[m]
            return 0

        lax.fori_loop(0, BLK // 8, per_tile, 0)
    for m in range(blocks):
        spec = to_spectrum(fwd_ref, kern[m])
        kre_ref[m] = spec[:BLK]
        kim_ref[m] = spec[BLK:]
    taps = jnp.concatenate(
        [taps_ref[...], jnp.zeros((BLK - taps_ref.shape[0], width), F32)], axis=0
    )
    spec = to_spectrum(fwd_ref, taps)
    tre_ref[...] = spec[:BLK]
    tim_ref[...] = spec[BLK:]


def kernel_spectra(decay_t, coef_t, taps, fwd, length):
    states, width = decay_t.shape
    blocks = length // BLK
    return pl.pallas_call(
        kgen_body,
        out_shape=(
            jax.ShapeDtypeStruct((blocks, BLK, width), F32),
            jax.ShapeDtypeStruct((blocks, BLK, width), F32),
            jax.ShapeDtypeStruct((BLK, width), F32),
            jax.ShapeDtypeStruct((BLK, width), F32),
        ),
        scratch_shapes=[
            pltpu.VMEM((blocks, states, width), F32),
            pltpu.VMEM((blocks, BLK, width), F32),
        ],
        compiler_params=pltpu.CompilerParams(vmem_limit_bytes=VMEM_LIMIT),
        name="kernel_spectra",
    )(decay_t, coef_t, taps, fwd)


def conv_tiles(width, body):
    for start, size in lane_tiles(width):
        lanes = slice(start, start + size)

        def step(ft, _, lanes=lanes):
            body(ft, pl.ds(pl.multiple_of(ft * 8, 8), 8), lanes)
            return 0

        lax.fori_loop(0, BLK // 8, step, 0)


def mixer_fwd_body(
    x_ref, wq_ref, wk_ref, wv_ref, wo_ref, kre_ref, kim_ref, tre_ref, tim_ref, fwd_ref, inv_ref,
    out_ref, mixed_ref, q_ref, v_ref, sh_ref, st_ref, sre_ref, sim_ref, ure_ref, uim_ref,
    zre, zim,
):
    length, width = q_ref.shape
    blocks = length // BLK
    sign = sign_rows((BLK, width))
    row0 = lax.broadcasted_iota(jnp.int32, (BLK, width), 0) == 0
    x = x_ref[...]
    q_ref[...] = dot(x, wq_ref[...])
    v_ref[...] = dot(x, wv_ref[...])
    keys = dot(x, wk_ref[...])
    tre = tre_ref[...]
    tim = tim_ref[...]
    tre2 = jnp.where(row0, tim, tre)
    tim0 = jnp.where(row0, 0.0, tim)
    last = None
    for p in range(blocks):
        rows = slice(p * BLK, (p + 1) * BLK)
        spec = to_spectrum(fwd_ref, keys[rows])
        re, im = spec[:BLK], spec[BLK:]
        sre_ref[p] = re
        sim_ref[p] = im
        pr = re * tre - im * tim0
        pi = re * tim0 + im * tre2
        if last is None:
            z = jnp.concatenate([pr, pi], axis=0)
        else:
            z = jnp.concatenate([pr + sign * last[0], pi + sign * last[1]], axis=0)
        last = (pr, pi)
        shifted = from_spectrum(inv_ref, z)
        sh_ref[rows] = shifted
        spec = to_spectrum(fwd_ref, shifted * v_ref[rows])
        ure_ref[p] = spec[:BLK]
        uim_ref[p] = spec[BLK:]

    def products(ft, fr, lanes):
        sgn = sign[:8, lanes]
        k = [(kre_ref[m, fr, lanes], kim_ref[m, fr, lanes]) for m in range(blocks)]
        k = [(a,) + fix_first(ft, a, b) for a, b in k]
        u = [(ure_ref[m, fr, lanes], uim_ref[m, fr, lanes]) for m in range(blocks)]
        prev = None
        for p in range(blocks):
            yr = yi = None
            for m in range(p + 1):
                ur, ui = u[m]
                kr, kr2, ki0 = k[p - m]
                a = ur * kr - ui * ki0
                b = ur * ki0 + ui * kr2
                yr = a if yr is None else yr + a
                yi = b if yi is None else yi + b
            if prev is None:
                zre[p, fr, lanes] = yr
                zim[p, fr, lanes] = yi
            else:
                zre[p, fr, lanes] = yr + sgn * prev[0]
                zim[p, fr, lanes] = yi + sgn * prev[1]
            prev = (yr, yi)

    conv_tiles(width, products)
    for p in range(blocks):
        rows = slice(p * BLK, (p + 1) * BLK)
        state = from_spectrum(inv_ref, jnp.concatenate([zre[p], zim[p]], axis=0))
        st_ref[rows] = state
        mixed_ref[rows] = (q_ref[rows] * state).astype(BF16)
    out_ref[...] = dot(mixed_ref[...], wo_ref[...]).astype(BF16)


def mixer_forward_kernel(x, wq, wk, wv, wo, kre, kim, tre, tim, fwd, inv):
    length, model = x.shape
    width = wq.shape[1]
    blocks = length // BLK
    row_f = jax.ShapeDtypeStruct((length, width), F32)
    spec_f = jax.ShapeDtypeStruct((blocks, BLK, width), F32)
    return pl.pallas_call(
        mixer_fwd_body,
        out_shape=(
            jax.ShapeDtypeStruct((length, model), BF16),
            jax.ShapeDtypeStruct((length, width), BF16),
            row_f, row_f, row_f, row_f, spec_f, spec_f, spec_f, spec_f,
        ),
        scratch_shapes=[pltpu.VMEM((blocks, BLK, width), F32)] * 2,
        compiler_params=pltpu.CompilerParams(vmem_limit_bytes=VMEM_LIMIT),
        name="mixer_forward",
    )(x, wq, wk, wv, wo, kre, kim, tre, tim, fwd, inv)


def mixer_bwd_body(
    g_ref, wo_ref, q_ref, v_ref, sh_ref, st_ref, sre_ref, sim_ref, ure_ref, uim_ref,
    kre_ref, kim_ref, tre_ref, tim_ref, fwd_ref, inv_ref,
    gq_ref, gk_ref, gv_ref, taps_ref, dk_ref,
    gre, gim, wre, wim, vre, vim,
):
    length, width = q_ref.shape
    blocks = length // BLK
    sign = sign_rows((BLK, width))
    row0 = lax.broadcasted_iota(jnp.int32, (BLK, width), 0) == 0
    grad_mixed = dot_nt(g_ref[...], wo_ref[...])
    for p in range(blocks):
        rows = slice(p * BLK, (p + 1) * BLK)
        gm = grad_mixed[rows]
        gq_ref[rows] = (gm * st_ref[rows]).astype(BF16)
        spec = to_spectrum(fwd_ref, gm * q_ref[rows])
        gre[p] = spec[:BLK]
        gim[p] = spec[BLK:]

    def products(ft, fr, lanes, other_re, other_im, to_re, to_im):
        sgn = sign[:8, lanes]
        k = [(other_re[m, fr, lanes], other_im[m, fr, lanes]) for m in range(blocks)]
        k = [(a,) + fix_first(ft, a, b) for a, b in k]
        g = [(gre[m, fr, lanes], gim[m, fr, lanes]) for m in range(blocks)]
        after = None
        for p in reversed(range(blocks)):
            wr = wi = None
            for m in range(p, blocks):
                gr, gi = g[m]
                kr, kr2, ki0 = k[m - p]
                a = gr * kr + gi * ki0
                b = gi * kr2 - gr * ki0
                wr = a if wr is None else wr + a
                wi = b if wi is None else wi + b
            if after is None:
                to_re[p, fr, lanes] = wr
                to_im[p, fr, lanes] = wi
            else:
                to_re[p, fr, lanes] = wr + sgn * after[0]
                to_im[p, fr, lanes] = wi + sgn * after[1]
            after = (wr, wi)

    conv_tiles(width, lambda ft, fr, lanes: products(ft, fr, lanes, kre_ref, kim_ref, wre, wim))
    tre = tre_ref[...]
    tim = tim_ref[...]
    tre2 = jnp.where(row0, tim, tre)
    tim0 = jnp.where(row0, 0.0, tim)
    after = None
    next_gs = None
    zero = jnp.zeros((BLK, width), F32)
    corr = [zero, zero, zero, zero]
    for p in reversed(range(blocks)):
        rows = slice(p * BLK, (p + 1) * BLK)
        grad_u = from_spectrum(inv_ref, jnp.concatenate([wre[p], wim[p]], axis=0))
        gv_ref[rows] = (grad_u * sh_ref[rows]).astype(BF16)
        spec = to_spectrum(fwd_ref, grad_u * v_ref[rows])
        re, im = spec[:BLK], spec[BLK:]
        pr = re * tre + im * tim0
        pi = im * tre2 - re * tim0
        if after is None:
            z = jnp.concatenate([pr, pi], axis=0)
        else:
            z = jnp.concatenate([pr + sign * after[0], pi + sign * after[1]], axis=0)
        after = (pr, pi)
        gk_ref[rows] = from_spectrum(inv_ref, z).astype(BF16)
        sr, si = sre_ref[p], sim_ref[p]
        sr2 = jnp.where(row0, si, sr)
        si0 = jnp.where(row0, 0.0, si)
        corr[0] = corr[0] + (re * sr + im * si0)
        corr[1] = corr[1] + (im * sr2 - re * si0)
        if next_gs is not None:
            nr, ni = next_gs
            corr[2] = corr[2] + (nr * sr + ni * si0)
            corr[3] = corr[3] + (ni * sr2 - nr * si0)
        next_gs = (re, im)
    z = jnp.concatenate([corr[0] + sign * corr[2], corr[1] + sign * corr[3]], axis=0)
    taps_ref[...] = from_spectrum(inv_ref, z)[: taps_ref.shape[0]]
    conv_tiles(width, lambda ft, fr, lanes: products(ft, fr, lanes, ure_ref, uim_ref, vre, vim))
    for p in range(blocks):
        rows = slice(p * BLK, (p + 1) * BLK)
        dk_ref[rows] = from_spectrum(inv_ref, jnp.concatenate([vre[p], vim[p]], axis=0))


def mixer_backward_kernel(g, wo, saved, kre, kim, tre, tim, fwd, inv, taps):
    q, v, sh, st, sre, sim, ure, uim = saved
    length, width = q.shape
    blocks = length // BLK
    row_b = jax.ShapeDtypeStruct((length, width), BF16)
    return pl.pallas_call(
        mixer_bwd_body,
        out_shape=(
            row_b, row_b, row_b,
            jax.ShapeDtypeStruct((taps, width), F32),
            jax.ShapeDtypeStruct((length, width), F32),
        ),
        scratch_shapes=[pltpu.VMEM((blocks, BLK, width), F32)] * 6,
        compiler_params=pltpu.CompilerParams(vmem_limit_bytes=VMEM_LIMIT),
        name="mixer_backward",
    )(g, wo, q, v, sh, st, sre, sim, ure, uim, kre, kim, tre, tim, fwd, inv)


def ssm_grad_body(dk_ref, decay_ref, coef_ref, gd_ref, gc_ref):
    states, width = decay_ref.shape
    length = dk_ref.shape[0]
    blocks = length // BLK
    group = 4
    for start, size in lane_tiles(width):
        lanes = slice(start, start + size)
        base = lax.broadcasted_iota(jnp.int32, (8, size), 0).astype(F32)

        def per_group(ng, _, lanes=lanes, size=size, base=base):
            rows = pl.ds(pl.multiple_of(ng * 8, 8), 8)
            rates = decay_ref[rows, lanes]
            row_ids = lax.broadcasted_iota(jnp.int32, (8, size), 0)
            sums_a = jnp.zeros((8, size), F32)
            sums_b = jnp.zeros((8, size), F32)
            for half in range(8 // group):
                d = [rates[half * group + i : half * group + i + 1] for i in range(group)]
                p = [jnp.broadcast_to(jnp.exp(-float(BLK) * x), (8, size)) for x in d]
                step8 = [jnp.broadcast_to(jnp.exp(-8.0 * x), (8, size)) for x in d]
                e0 = tuple(jnp.exp(-x * base) for x in d)
                zero = jnp.zeros((8, size), F32)

                def per_tile(jt, carry, p=p, step8=step8):
                    e, a, b = carry
                    steps = base + (jt * 8).astype(F32)
                    dk = [
                        dk_ref[pl.ds(pl.multiple_of(m * BLK + jt * 8, 8), 8), lanes]
                        for m in range(blocks)
                    ]
                    ne, na, nb = [], [], []
                    for i in range(group):
                        h = dk[blocks - 1]
                        s = None
                        for m in reversed(range(blocks - 1)):
                            s = h if s is None else s * p[i] + h
                            h = h * p[i] + dk[m]
                        eh = e[i] * h
                        na.append(a[i] + eh)
                        nb.append(b[i] + steps * eh + (float(BLK) * e[i]) * (s * p[i]))
                        ne.append(e[i] * step8[i])
                    return tuple(ne), tuple(na), tuple(nb)

                _, a, b = lax.fori_loop(
                    0, BLK // 8, per_tile, (e0, (zero,) * group, (zero,) * group)
                )
                for i in range(group):
                    here = row_ids == half * group + i
                    sums_a = jnp.where(here, jnp.sum(a[i], axis=0, keepdims=True), sums_a)
                    sums_b = jnp.where(here, jnp.sum(b[i], axis=0, keepdims=True), sums_b)
            root = jnp.sqrt(2.0 * rates)
            gc_ref[rows, lanes] = root * sums_a
            gd_ref[rows, lanes] = coef_ref[rows, lanes] * (sums_a / root - root * sums_b)
            return 0

        lax.fori_loop(0, states // 8, per_group, 0)


def ssm_grad_kernel(dk, decay_t, coef_t):
    states, width = decay_t.shape
    out = jax.ShapeDtypeStruct((states, width), F32)
    return pl.pallas_call(
        ssm_grad_body,
        out_shape=(out, out),
        compiler_params=pltpu.CompilerParams(vmem_limit_bytes=VMEM_LIMIT),
        name="ssm_grad",
    )(dk, decay_t, coef_t)


HEAD = 64
QROWS = 256


def dot_tn(a, b):
    return lax.dot_general(a, b, (((0,), (0,)), ((), ())), preferred_element_type=F32)


def allowed_keys(keys, first_query, queries, length):
    key = lax.broadcasted_iota(jnp.int32, (keys, queries), 0)
    query = lax.broadcasted_iota(jnp.int32, (keys, queries), 1) + first_query
    return (key <= query) & (key < length)


def attn_fwd_body(len_ref, x_ref, w_ref, out_ref, q_ref, k_ref, v_ref, att_ref, lse_ref):
    rows, width = q_ref.shape
    x = x_ref[...]
    q_ref[...] = dot(x, w_ref[:, :width]).astype(BF16)
    k_ref[...] = dot(x, w_ref[:, width : 2 * width]).astype(BF16)
    v_ref[...] = dot(x, w_ref[:, 2 * width : 3 * width]).astype(BF16)
    length = len_ref[0]
    lse_ref[...] = jnp.zeros(lse_ref.shape, F32)
    scale = HEAD**-0.5
    for h in range(width // HEAD):
        lanes = slice(h * HEAD, (h + 1) * HEAD)
        q = q_ref[:, lanes] * jnp.asarray(scale, BF16)
        k = k_ref[:, lanes]
        vt = v_ref[:, lanes].T
        for first in range(0, rows, QROWS):
            n = first + QROWS
            s = dot_nt(k[:n], q[first:n])
            s = jnp.where(allowed_keys(n, first, QROWS, length), s, -jnp.inf)
            top = jnp.max(s, axis=0, keepdims=True)
            e = jnp.exp(s - top)
            total = jnp.sum(e, axis=0, keepdims=True)
            probs = (e * (1.0 / total)).astype(BF16)
            att_ref[lanes, first:n] = dot(vt[:, :n], probs).astype(BF16)
            lse_ref[h : h + 1, first:n] = top + jnp.log(total)
    out_ref[...] = lax.dot_general(
        att_ref[...], w_ref[:, 3 * width :], (((0,), (1,)), ((), ())), preferred_element_type=F32
    ).astype(BF16)


def attn_forward_kernel(length, x, w):
    rows, model = x.shape
    width = w.shape[1] // 4
    row_b = jax.ShapeDtypeStruct((rows, width), BF16)
    vmem = pl.BlockSpec(memory_space=pltpu.VMEM)
    return pl.pallas_call(
        attn_fwd_body,
        in_specs=[pl.BlockSpec(memory_space=pltpu.SMEM), vmem, vmem],
        out_shape=(
            jax.ShapeDtypeStruct((rows, model), BF16),
            row_b, row_b, row_b,
            jax.ShapeDtypeStruct((width, rows), BF16),
            jax.ShapeDtypeStruct((8, rows), F32),
        ),
        compiler_params=pltpu.CompilerParams(vmem_limit_bytes=VMEM_LIMIT),
        name="attn_forward",
    )(length, x, w)


def attn_bwd_body(
    len_ref, g_ref, w_ref, q_ref, k_ref, v_ref, lse_ref, out_ref, gq_ref, gk_ref, gv_ref, ga, gqt, acck, accv
):
    rows, width = q_ref.shape
    ga[...] = dot(g_ref[...], w_ref[:, 3 * width :]).astype(BF16)
    length = len_ref[0]
    scale = HEAD**-0.5
    acck[...] = jnp.zeros(acck.shape, F32)
    accv[...] = jnp.zeros(accv.shape, F32)
    for h in range(width // HEAD):
        lanes = slice(h * HEAD, (h + 1) * HEAD)
        q = q_ref[:, lanes] * jnp.asarray(scale, BF16)
        k = k_ref[:, lanes]
        kt = k.T
        v = v_ref[:, lanes]
        g = ga[:, lanes]
        for first in range(0, rows, QROWS):
            n = first + QROWS
            s = dot_nt(k[:n], q[first:n])
            probs = jnp.where(
                allowed_keys(n, first, QROWS, length), jnp.exp(s - lse_ref[h : h + 1, first:n]), 0.0
            )
            gp = dot_nt(v[:n], g[first:n])
            inner = jnp.sum(probs * gp, axis=0, keepdims=True)
            gs = (probs * (gp - inner)).astype(BF16)
            gqt[lanes, first:n] = dot(kt[:, :n], gs) * scale
            acck[h, :n] += dot(gs, q[first:n])
            accv[h, :n] += dot(probs.astype(BF16), g[first:n])
        gk_ref[:, lanes] = acck[h].astype(BF16)
        gv_ref[:, lanes] = accv[h].astype(BF16)
    gq_ref[...] = gqt[...].T.astype(BF16)
    out_ref[...] = (
        dot_nt(gq_ref[...], w_ref[:, :width])
        + dot_nt(gk_ref[...], w_ref[:, width : 2 * width])
        + dot_nt(gv_ref[...], w_ref[:, 2 * width : 3 * width])
    ).astype(BF16)


def attn_backward_kernel(length, g, w, q, k, v, lse):
    rows, width = q.shape
    row_b = jax.ShapeDtypeStruct((rows, width), BF16)
    vmem = pl.BlockSpec(memory_space=pltpu.VMEM)
    heads = width // HEAD
    return pl.pallas_call(
        attn_bwd_body,
        in_specs=[pl.BlockSpec(memory_space=pltpu.SMEM)] + [vmem] * 6,
        out_shape=(jax.ShapeDtypeStruct(g.shape, BF16), row_b, row_b, row_b),
        scratch_shapes=[
            pltpu.VMEM((rows, width), BF16),
            pltpu.VMEM((width, rows), F32),
            pltpu.VMEM((heads, rows, HEAD), F32),
            pltpu.VMEM((heads, rows, HEAD), F32),
        ],
        compiler_params=pltpu.CompilerParams(vmem_limit_bytes=VMEM_LIMIT),
        name="attn_backward",
    )(length, g, w, q, k, v, lse)


EPSILON = 1e-05
TENSOR = "tensor"
DATA = "dp"


def swap(x, bit):
    return lax.ppermute(x, TENSOR, [(i, i ^ bit) for i in range(4)])


def norm_rows(hidden, gain):
    average = jnp.mean(hidden, axis=-1, keepdims=True)
    centred = hidden - average
    inverse = lax.rsqrt(jnp.mean(centred * centred, axis=-1, keepdims=True) + EPSILON)
    unit = centred * inverse
    return (unit * gain).astype(BF16), unit, inverse


def norm_back(grad_norm, unit, inverse, gain):
    scaled = grad_norm * gain
    first_mean = jnp.mean(scaled, axis=-1, keepdims=True)
    second_mean = jnp.mean(scaled * unit, axis=-1, keepdims=True)
    return inverse * (scaled - first_mean - unit * second_mean)


def rows_dot(left, right):
    return lax.dot_general(left, right, (((0,), (0,)), ((), ())), preferred_element_type=F32)


def gelu_tanh(values):
    return jax.nn.gelu(values, approximate=True)


class Group:
    def __init__(self):
        index = lax.axis_index(TENSOR)
        self.core = index & 1
        self.chip = index >> 1

    def all_rows(self, mine):
        other = swap(mine, 1)
        first = jnp.where(self.core == 0, mine, other)
        second = jnp.where(self.core == 0, other, mine)
        return jnp.stack([first, second], axis=1).reshape(-1, mine.shape[-1])

    def both_halves(self, mine):
        other = swap(mine, 2)
        first = jnp.where(self.chip == 0, mine, other)
        second = jnp.where(self.chip == 0, other, mine)
        return jnp.stack([first, second], axis=0)

    def total(self, partial):
        quarters = partial.reshape(2, 2, -1, partial.shape[-1])
        keep = lax.dynamic_index_in_dim(quarters, self.core, 1, keepdims=False)
        send = lax.dynamic_index_in_dim(quarters, 1 - self.core, 1, keepdims=False)
        pair = (keep.astype(F32) + swap(send, 1).astype(F32)).astype(BF16)
        return pair.astype(F32) + swap(pair, 2).astype(F32)


def ffn_forward(x, up, down_t):
    hidden = jnp.dot(x, up, preferred_element_type=F32)
    active = gelu_tanh(hidden).astype(BF16)
    out = lax.dot_general(
        active, down_t, (((1,), (1,)), ((), ())), preferred_element_type=F32
    ).astype(BF16)
    return out, hidden


def ffn_backward(x, hidden, grad, up, down_t):
    active, pull = jax.vjp(gelu_tanh, hidden)
    active = active.astype(BF16)
    grad_hidden = pull(jnp.dot(grad, down_t, preferred_element_type=F32))[0].astype(BF16)
    out = lax.dot_general(
        grad_hidden, up, (((1,), (1,)), ((), ())), preferred_element_type=F32
    ).astype(BF16)
    grads = jnp.concatenate([rows_dot(x, grad_hidden), rows_dot(grad, active)], axis=1)
    return out, grads.astype(BF16)


def gather_rows(x):
    return lax.all_gather(x, DATA, axis=0, tiled=True)


def scatter_rows(x):
    return lax.psum_scatter(x, DATA, scatter_dimension=0, tiled=True).astype(F32)


def on_device(
    tokens, cotangent, seq_lengths,
    gain_mixer, mixer_query, mixer_key, mixer_value, shift_taps, ssm_decay, ssm_coef, mixer_out,
    gain_ffn1, ffn1_up, ffn1_down,
    gain_attn, attn_query, attn_key, attn_value, attn_out,
    gain_ffn2, ffn2_up, ffn2_down,
):
    group = Group()
    fwd, inv = spectral_tables()
    quarter, model = tokens.shape
    length = 4 * quarter
    width = mixer_query.shape[1]
    states = ssm_decay.shape[1] * lax.axis_size(DATA)
    taps = shift_taps.shape[0] * lax.axis_size(DATA)

    own_gains = jnp.stack([gain_mixer, gain_ffn1, gain_attn, gain_ffn2], axis=0)
    small = gather_rows(
        jnp.concatenate([shift_taps, ssm_decay.T, ssm_coef.T], axis=1)
    ).astype(F32)
    gains = lax.all_gather(own_gains, DATA, axis=1, tiled=True).astype(F32)
    mixer_w = gather_rows(
        jnp.concatenate([mixer_query, mixer_key, mixer_value, mixer_out.T], axis=1)
    )
    ffn1_w = gather_rows(jnp.concatenate([ffn1_up, ffn1_down.T], axis=1))
    attn_w = gather_rows(jnp.concatenate([attn_query, attn_key, attn_value, attn_out.T], axis=1))
    ffn2_w = gather_rows(jnp.concatenate([ffn2_up, ffn2_down.T], axis=1))
    hidden_units = ffn1_up.shape[1]

    start = group.both_halves(tokens).astype(F32)
    taps_w, decay_t, coef_t = (small[:, i * width : (i + 1) * width] for i in range(3))
    spectra = kernel_spectra(decay_t, coef_t, taps_w, fwd, length)

    normed1, unit1, inverse1 = norm_rows(start, gains[0])
    x1 = group.all_rows(normed1)
    saved = mixer_forward_kernel(
        x1, mixer_w[:, :width], mixer_w[:, width : 2 * width], mixer_w[:, 2 * width : 3 * width],
        mixer_w[:, 3 * width :].T, *spectra, fwd, inv,
    )
    mixed = saved[1]
    after_mixer = start + group.total(saved[0])

    normed2, unit2, inverse2 = norm_rows(after_mixer, gains[1])
    x2 = group.all_rows(normed2)
    out, hidden1 = ffn_forward(x2, ffn1_w[:, :hidden_units], ffn1_w[:, hidden_units:])
    after_ffn1 = after_mixer + group.total(out)

    normed3, unit3, inverse3 = norm_rows(after_ffn1, gains[2])
    x3 = group.all_rows(normed3)
    out, q2, k2, v2, attended_t, log_total = attn_forward_kernel(seq_lengths, x3, attn_w)
    after_attn = after_ffn1 + group.total(out)

    normed4, unit4, inverse4 = norm_rows(after_attn, gains[3])
    x4 = group.all_rows(normed4)
    out, hidden2 = ffn_forward(x4, ffn2_w[:, :hidden_units], ffn2_w[:, hidden_units:])
    final = after_attn + group.total(out)
    output = lax.dynamic_index_in_dim(final, group.chip, 0, keepdims=False).astype(BF16)

    positions = lax.axis_index(TENSOR) * quarter + jnp.arange(quarter)
    live = (positions < seq_lengths[0])[:, None]
    masked = jnp.where(live, cotangent, jnp.zeros_like(cotangent))
    grad_low = group.both_halves(masked)
    grad = grad_low.astype(F32)

    g4 = group.all_rows(grad_low)
    out, ffn2_g = ffn_backward(x4, hidden2, g4, ffn2_w[:, :hidden_units], ffn2_w[:, hidden_units:])
    grad = grad + norm_back(group.total(out), unit4, inverse4, gains[3])
    ffn2_g = scatter_rows(ffn2_g)

    g3 = group.all_rows(grad.astype(BF16))
    out, gq, gk, gv = attn_backward_kernel(seq_lengths, g3, attn_w, q2, k2, v2, log_total)
    attn_g = jnp.concatenate(
        [rows_dot(x3, gq), rows_dot(x3, gk), rows_dot(x3, gv), rows_dot(g3, attended_t.T)], axis=1
    )
    grad = grad + norm_back(group.total(out), unit3, inverse3, gains[2])
    attn_g = scatter_rows(attn_g.astype(BF16))

    g2 = group.all_rows(grad.astype(BF16))
    out, ffn1_g = ffn_backward(x2, hidden1, g2, ffn1_w[:, :hidden_units], ffn1_w[:, hidden_units:])
    grad = grad + norm_back(group.total(out), unit2, inverse2, gains[1])
    ffn1_g = scatter_rows(ffn1_g)

    g1 = group.all_rows(grad.astype(BF16))
    gq, gk, gv, grad_taps, grad_kernel = mixer_backward_kernel(
        g1, mixer_w[:, 3 * width :].T, saved[2:], *spectra, fwd, inv, taps
    )
    grad_joined = jnp.concatenate([gq, gk, gv], axis=1)
    out = lax.dot_general(
        grad_joined, mixer_w[:, : 3 * width], (((1,), (1,)), ((), ())), preferred_element_type=F32
    ).astype(BF16)
    grad = grad + norm_back(group.total(out), unit1, inverse1, gains[0])
    input_grad = lax.dynamic_index_in_dim(grad, group.chip, 0, keepdims=False).astype(BF16)
    mixer_g = scatter_rows(
        jnp.concatenate([rows_dot(x1, grad_joined), rows_dot(g1, mixed)], axis=1).astype(BF16)
    )
    grad_decay, grad_coef = ssm_grad_kernel(grad_kernel, decay_t, coef_t)
    small_g = scatter_rows(
        jnp.concatenate([grad_taps, grad_decay, grad_coef], axis=1).astype(BF16)
    )

    def gain_sum(grads, weights, gain):
        products = sum(g * w.astype(F32) for g, w in zip(grads, weights))
        return jnp.sum(products, axis=1) / gain.astype(F32)

    def cut(grads, size):
        return [grads[:, i : i + size] for i in range(0, grads.shape[1], size)]

    mq, mk, mv, mo = cut(mixer_g, width)
    aq, ak, av, ao = cut(attn_g, width)
    u1, d1 = cut(ffn1_g, hidden_units)
    u2, d2 = cut(ffn2_g, hidden_units)
    gt, gd, gc = cut(small_g, width)
    gain_grads = lax.psum(
        jnp.stack(
            [
                gain_sum((mq, mk, mv), (mixer_query, mixer_key, mixer_value), gain_mixer),
                gain_sum((u1,), (ffn1_up,), gain_ffn1),
                gain_sum((aq, ak, av), (attn_query, attn_key, attn_value), gain_attn),
                gain_sum((u2,), (ffn2_up,), gain_ffn2),
            ]
        ),
        TENSOR,
    )
    return (
        output, input_grad,
        gain_grads[0], mq, mk, mv, gt, gd.T, gc.T, mo.T,
        gain_grads[1], u1, d1.T,
        gain_grads[2], aq, ak, av, ao.T,
        gain_grads[3], u2, d2.T,
    )


def solution(mesh):
    rows = P(("dp", "tensor"), None)
    up = P("dp", "tensor")
    down = P("tensor", "dp")
    vector = P("dp")
    mixer = (vector, up, up, up, up, down, down, down)
    ffn = (vector, up, down)
    attn = (vector, up, up, up, down)
    weights = mixer + ffn + attn + ffn
    return jax.shard_map(
        on_device,
        mesh=mesh,
        in_specs=(rows, rows, vector) + weights,
        out_specs=(rows, rows) + weights,
        check_vma=False,
    )
```

time: 3550 us -> 704 us (0.20)
  other arithmetic: 985 us -> 50 us
  local copies, waits for them, and re-layouts: 860 us -> 70 us
  waiting for transfers between devices: 800 us -> 363 us
  matrix products: 436 us -> 38.4 us
  blocking collectives: 396 us -> 57.1 us
  Pallas kernels: 0 us -> 82 us
  loops' own time: 38.6 us -> 0 us
    scatter-add x9 -> x0, other arithmetic: 852 us -> none  [the longest x3 295 us: mixer_head(): kernel_near[jnp.maximum(lag_grid, 0)]]
    gather x18 -> x0, local copies, waits for them, and re-layouts: 559 us -> none  [the longest x6 187 us: mixer_head(): far_tile = taps_ext[lag_grid + SPAN]]
    dot_general x94 -> x9, matrix products: 390 us -> 25.3 us  [the longest x2 7.43 us: ffn_backward(): jnp.dot(grad, down_t, preferred_element_type=F32)]
    all_gather x11 -> x2, blocking collectives: 344 us -> 51.4 us  [the longest x1 30.6 us: gather_rows(): return lax.all_gather(x, DATA, axis=0, tiled=True)]
    reduce_scatter x12 -> x0, waiting for transfers between devices: 214 us -> none  [the longest x4 108 us: push_grad(): lax.psum_scatter(cols_dot(grad_rows, weight).astype(jnp.bfloat16), 'tenso...]
    unnamed x46 -> x14, waiting for transfers between devices: 388 us -> 184 us
    all_gather x12 -> x4, waiting for transfers between devices: 198 us -> 58 us  [gather_rows(): return lax.all_gather(x, DATA, axis=0, tiled=True)]
    dynamic_update_slice x60 -> x0, local copies, waits for them, and re-layouts: 123 us -> none  [the longest x45 117 us: mixer_core(): lax.map(mixer_head, (to_heads(projected[:, :columns]), to_heads(projected...]
  transfers between devices with their start and end apart: 35 -> 35, of which waited for: 24 -> 24; matrix products, arithmetic and copies ran while one was open for 35% -> 16% of each run, Pallas kernels for 0% -> 6%
where the time goes in v1:
time: 704 us; the launch traced here: 696 us
  waiting for transfers between devices  363 us (52%)
  Pallas kernels  82 us (12%)
  local copies, waits for them, and re-layouts  70 us (10%)
  blocking collectives  57.1 us (8%)
  other arithmetic  50 us (7%)
  matrix products  38.4 us (5%)
  starting transfers between devices  17.8 us (3%)
  between operations  17.2 us (2%)
    unnamed x14, waiting for transfers between devices  184 us
    ppermute x26, waiting for transfers between devices, swap(): return lax.ppermute(x, TENSOR, [(i, i ^ bit) for i in range(4)])  121 us
    all_gather x4, waiting for transfers between devices, gather_rows(): return lax.all_gather(x, DATA, axis=0, tiled=True)  58 us
    unnamed x216, local copies, waits for them, and re-layouts  50.5 us
    all_gather x1, blocking collectives, gather_rows(): return lax.all_gather(x, DATA, axis=0, tiled=True)  30.6 us
    all_gather x1, blocking collectives, on_device(): gains = lax.all_gather(own_gains, DATA, axis=1, tiled=True).astype(F32)  20.8 us
    ppermute x26, starting transfers between devices, swap(): return lax.ppermute(x, TENSOR, [(i, i ^ bit) for i in range(4)])  16 us
    pallas_call x1, Pallas kernels, ssm_grad_kernel(): pl.pallas_call(ssm_grad_body, out_shape=(out, out), compiler_params=pltpu...  15.8 us
  transfers between devices with their start and end apart: 35, of which 24 were waited for; matrix products, arithmetic and copies ran while one was open for 16% of the time, Pallas kernels for 6%

profile of v1, /device:TPU:0, one launch (start us, length us, event | category | flops | bytes accessed | tf_op | source)
XLA Modules:
  0.0 695.8 jit_solution(2559874280979096727)
XLA Ops:
  13.6 20.8 %all-gather = bf16[8,96,4]{1,2,0:T(4,128)(2,1)S(1)} all-gather(bf16[1,96,4]{1,2,0:T(4,128)(2,1)S(1)} %maximum_bitcast_fusion), channel_id=1, replica_groups=mesh['dp'=8,'tensor'=4] {'dp'}, dimensions={0}, use_global_device_ids=true | all-gather | bytes 6912 | tf_op jit(solution)/shard_map/all_gather | solution.py:640
  36.7 30.6 %all_gather.20 = bf16[64,576]{1,0:T(8,128)(2,1)S(1)} all-gather(bf16[8,576]{1,0:T(8,128)(2,1)S(1)} %pad_maximum_fusion.22), channel_id=1, replica_groups=mesh['dp'=8,'tensor'=4] {'dp'}, dimensions={0}, use_global_device_ids=true | all-gather | bytes 82944 | tf_op jit(solution)/shard_map/all_gather | solution.py:614
  68.0 11.5 %kernel_spectra.1 = (f32[8,128,192]{2,1,0:T(8,128)}, f32[8,128,192]{2,1,0:T(8,128)}, f32[128,192]{1,0:T(8,128)}, f32[128,192]{1,0:T(8,128)}) custom-call(f32[64,192]{1,0:T(8,128)} %get-tuple-element.231.decay_ref, f32[64,192]{1,0:T(8,128)} %get-tuple-element.230.coef_ref, f32[64,192]{1,0:T(8,128)} %get-tuple-element.229.taps_ref, ...), custom_call_target="tpu_custom_call" | custom-call | tf_op jit(solution)/shard_map/kernel_spectra/pallas_call | solution.py:130
  85.1 13.8 %mixer_forward.1 = (bf16[1024,768]{1,0:T(8,128)(2,1)}, bf16[1024,192]{1,0:T(8,128)(2,1)}, f32[1024,192]{1,0:T(8,128)}, f32[1024,192]{1,0:T(8,128)}, f32[1024,192...) custom-call(bf16[1024,768]{1,0:T(8,128)(2,1)} %bitcast.202, ...), custom_call_target="tpu_custom_call" | custom-call | tf_op jit(solution)/shard_map/mixer_forward/pallas_call | solution.py:233
  104.4 19.0 %collective-permute-done.3 = bf16[2,256,768]{2,1,0:T(8,128)(2,1)S(1)} collective-permute-done((bf16[2,256,768]{2,1,0:T(8,128)(2,1)S(1)}, bf16[2,256,768]{2,1,0:T(8,128)(2,1)S(1)}, u32[]{:S(2)}, u32[]{:S(2)}) %collective-permute-start.3) | collective-permute-done | bytes 786464 | tf_op jit(solution)/shard_map/ppermute | solution.py:541
  127.4 23.2 %all-gather.8.cloned.1.call-done = bf16[768,1536]{1,0:T(8,128)(2,1)} async-done(((bf16[96,1536]{1,0:T(8,128)(2,1)}), bf16[768,1536]{1,0:T(8,128)(2,1)}) %all-gather.8.cloned.1.call-update) | async-done | bytes 2359312 | tf_op jit(solution)/shard_map/all_gather | solution.py:614
  163.1 14.7 %collective-permute-done.6 = bf16[2,256,768]{2,1,0:T(8,128)(2,1)S(1)} collective-permute-done((bf16[2,256,768]{2,1,0:T(8,128)(2,1)S(1)}, bf16[2,256,768]{2,1,0:T(8,128)(2,1)S(1)}, u32[]{:S(2)}, u32[]{:S(2)}) %collective-permute-start.6) | collective-permute-done | bytes 786464 | tf_op jit(solution)/shard_map/ppermute | solution.py:541
  183.0 18.7 %all-gather.10.cloned.1.call-done.w_ref = bf16[768,768]{1,0:T(8,128)(2,1)} async-done(((bf16[96,768]{1,0:T(8,128)(2,1)}), bf16[768,768]{1,0:T(8,128)(2,1)}) %all-gather.10.cloned.1.call-update) | async-done | bytes 1179664 | tf_op jit(solution)/shard_map/all_gather | solution.py:614
  201.7 10.7 %attn_forward.1 = (bf16[1024,768]{1,0:T(8,128)(2,1)}, bf16[1024,192]{1,0:T(8,128)(2,1)}, bf16[1024,192]{1,0:T(8,128)(2,1)}, bf16[1024,192]{1,0:T(8,128)(2,1)}, b...) custom-call(s32[1]{0:T(128)} %copy.219.len_ref, bf16[1024,768]{1,0:T(8,128)(2,1)} %bitcast.196, ...), custom_call_target="tpu_custom_call" | custom-call | tf_op jit(solution)/shard_map/attn_forward/pallas_call | solution.py:463
  220.4 8.5 %collective-permute-done.13 = bf16[256,768]{1,0:T(8,128)(2,1)S(1)} collective-permute-done((bf16[256,768]{1,0:T(8,128)(2,1)S(1)}, bf16[256,768]{1,0:T(8,128)(2,1)S(1)}, u32[]{:S(2)}, u32[]{:S(2)}) %collective-permute-start.13) | collective-permute-done | bytes 393248 | tf_op jit(solution)/shard_map/ppermute | solution.py:541
  229.2 16.2 %collective-permute-done.9 = bf16[2,256,768]{2,1,0:T(8,128)(2,1)S(1)} collective-permute-done((bf16[2,256,768]{2,1,0:T(8,128)(2,1)S(1)}, bf16[2,256,768]{2,1,0:T(8,128)(2,1)S(1)}, u32[]{:S(2)}, u32[]{:S(2)}) %collective-permute-start.9) | collective-permute-done | bytes 786464 | tf_op jit(solution)/shard_map/ppermute | solution.py:541
  250.5 16.1 %all-gather.12.cloned.1.call-done = bf16[768,1536]{1,0:T(8,128)(2,1)} async-done(((bf16[96,1536]{1,0:T(8,128)(2,1)}), bf16[768,1536]{1,0:T(8,128)(2,1)}) %all-gather.12.cloned.1.call-update) | async-done | bytes 2359312 | tf_op jit(solution)/shard_map/all_gather | solution.py:614
  279.5 18.1 %collective-permute-done.16 = bf16[2,256,768]{2,1,0:T(8,128)(2,1)S(1)} collective-permute-done((bf16[2,256,768]{2,1,0:T(8,128)(2,1)S(1)}, bf16[2,256,768]{2,1,0:T(8,128)(2,1)S(1)}, u32[]{:S(2)}, u32[]{:S(2)}) %collective-permute-start.16) | collective-permute-done | bytes 786464 | tf_op jit(solution)/shard_map/ppermute | solution.py:541
  303.2 14.7 %attn_backward.1 = (bf16[1024,768]{1,0:T(8,128)(2,1)}, bf16[1024,192]{1,0:T(8,128)(2,1)}, bf16[1024,192]{1,0:T(8,128)(2,1)}, bf16[1024,192]{1,0:T(8,128)(2,1)}) custom-call(s32[1]{0:T(128)} %copy.219.len_ref, bf16[1024,768]{1,0:T(8,128)(2,1)} %bitcast.194, bf16[768,768]{1,0:T(8,128)(2,1)} %all-gather.10.cloned.1.call-done.w_ref, ...), custom_call_target="tpu_custom_call" | custom-call | tf_op jit(solution)/shard_map/attn_backward/pallas_call | solution.py:520
  333.2 10.7 %collective-permute-done.19 = bf16[2,256,768]{2,1,0:T(8,128)(2,1)} collective-permute-done((bf16[2,256,768]{2,1,0:T(8,128)(2,1)}, bf16[2,256,768]{2,1,0:T(8,128)(2,1)}, u32[]{:S(2)}, u32[]{:S(2)}) %collective-permute-start.19) | collective-permute-done | bytes 786464 | tf_op jit(solution)/shard_map/ppermute | solution.py:541
  371.6 12.5 %collective-permute-done.22 = bf16[2,256,768]{2,1,0:T(8,128)(2,1)} collective-permute-done((bf16[2,256,768]{2,1,0:T(8,128)(2,1)}, bf16[2,256,768]{2,1,0:T(8,128)(2,1)}, u32[]{:S(2)}, u32[]{:S(2)}) %collective-permute-start.22) | collective-permute-done | bytes 786464 | tf_op jit(solution)/shard_map/ppermute | solution.py:541
  396.7 15.5 %mixer_backward.1 = (bf16[1024,192]{1,0:T(8,128)(2,1)}, bf16[1024,192]{1,0:T(8,128)(2,1)}, bf16[1024,192]{1,0:T(8,128)(2,1)}, f32[64,192]{1,0:T(8,128)}, f32[1024,192]{1,0:T(8,128)}) custom-call(bf16[1024,768]{1,0:T(8,128)(2,1)} %bitcast.200, bf16[192,768]{1,0:T(8,128)(2,1)} %bitcast.205, f32[1024,192]{1,0:T(8,128)} %get-tuple-element.63.q_ref, ...), custom_call_target="tpu_custom_call" | custom-call | tf_op jit(solution)/shard_map/mixer_backward/pallas_call | solution.py:334
  413.0 15.8 %ssm_grad.1 = (f32[64,192]{1,0:T(8,128)}, f32[64,192]{1,0:T(8,128)}) custom-call(f32[1024,192]{1,0:T(8,128)} %get-tuple-element.80.dk_ref, f32[64,192]{1,0:T(8,128)} %get-tuple-element.231.decay_ref, f32[64,192]{1,0:T(8,128)} %get-tuple-element.230.coef_ref), custom_call_target="tpu_custom_call" | custom-call | tf_op jit(solution)/shard_map/ssm_grad/pallas_call | solution.py:407
  434.3 4.3 copy.202
  461.1 4.3 collective-permute-done.12
  487.9 50.0 %all-reduce.3.cloned.1.call-done = bf16[64,576]{1,0:T(8,128)(2,1)} async-done(((bf16[64,576]{1,0:T(8,128)(2,1)}), bf16[64,576]{1,0:T(8,128)(2,1)}) %all-reduce.3.cloned.1.call-update) | async-done | bytes 73744
  541.7 68.4 %reduce-scatter.15.cloned.1.call-done = bf16[96,1536]{1,0:T(8,128)(2,1)} async-done(((bf16[768,1536]{1,0:T(8,128)(2,1)}), bf16[96,1536]{1,0:T(8,128)(2,1)}) %reduce-scatter.15.cloned.1.call-update) | async-done | bytes 294928
  611.4 65.2 %reduce-scatter.13.cloned.1.call-done = bf16[96,768]{1,0:T(8,128)(2,1)} async-done(((bf16[768,768]{1,0:T(8,128)(2,1)}), bf16[96,768]{1,0:T(8,128)(2,1)}) %reduce-scatter.13.cloned.1.call-update) | async-done | bytes 147472
  682.6 5.7 psum.7
  (419 shorter events, 189.7 us)
Async XLA Ops:
  7.2 74.2 %all-gather.6.cloned.1.call-start = ((), (), s32[]{:S(2)}) async-start(), calls=%async_computation.4 | async-start | bytes 1327104 | tf_op jit(solution)/shard_map/all_gather | solution.py:614
  9.8 140.9 %all-gather.8.cloned.1.call-start = ((), (), s32[]{:S(2)}) async-start(), calls=%async_computation.5 | async-start | bytes 2654208 | tf_op jit(solution)/shard_map/all_gather | solution.py:614
  9.8 24.7 %collective-permute-start = (bf16[256,768]{1,0:T(8,128)(2,1)}, bf16[256,768]{1,0:T(8,128)(2,1)S(1)}, u32[]{:S(2)}, u32[]{:S(2)}) collective-permute-start(bf16[256,768]{1,0:T(8,128)(2,1)} %param.24), channel_id=1, source_target_pairs={{0,2},{1,3},{2,0},{3,1},{4,6},{5,7},{6,4},{7,5},{8,10},{9,11},{10,... | collective-permute-start | bytes 1179656 | tf_op jit(solution)/shard_map/ppermute | solution.py:541
  36.5 43.0 %collective-permute-start.1 = (bf16[2,256,768]{2,1,0:T(8,128)(2,1)S(1)}, bf16[2,256,768]{2,1,0:T(8,128)(2,1)S(1)}, u32[]{:S(2)}, u32[]{:S(2)}) collective-permute-start(bf16[2,256,768]{2,1,0:T(8,128)(2,1)S(1)} %multiply_convert_fusion.5), channel_id=1, source_target_pairs={{0,1},{1,0},{2,3},{3,2},{4,5},{5,4},{6,7},{7,6},{8,9},{9,8},{10,11... | collective-permute-start | bytes 2359304 | tf_op jit(solution)/shard_map/ppermute | solution.py:541
  101.8 99.9 %all-gather.10.cloned.1.call-start = ((), (), s32[]{:S(2)}) async-start(), calls=%async_computation.6 | async-start | bytes 1327104 | tf_op jit(solution)/shard_map/all_gather | solution.py:614
  103.8 19.6 %collective-permute-start.3 = (bf16[2,256,768]{2,1,0:T(8,128)(2,1)S(1)}, bf16[2,256,768]{2,1,0:T(8,128)(2,1)S(1)}, u32[]{:S(2)}, u32[]{:S(2)}) collective-permute-start(bf16[2,256,768]{2,1,0:T(8,128)(2,1)S(1)} %fusion.24), channel_id=1, source_target_pairs={{0,2},{1,3},{2,0},{3,1},{4,6},{5,7},{6,4},{7,5},{8,10},{9,11},{10,... | collective-permute-start | bytes 2359304 | tf_op jit(solution)/shard_map/ppermute | solution.py:541
  158.1 19.6 %collective-permute-start.6 = (bf16[2,256,768]{2,1,0:T(8,128)(2,1)S(1)}, bf16[2,256,768]{2,1,0:T(8,128)(2,1)S(1)}, u32[]{:S(2)}, u32[]{:S(2)}) collective-permute-start(bf16[2,256,768]{2,1,0:T(8,128)(2,1)S(1)} %fusion.23), channel_id=1, source_target_pairs={{0,2},{1,3},{2,0},{3,1},{4,6},{5,7},{6,4},{7,5},{8,10},{9,11},{10,... | collective-permute-start | bytes 2359304 | tf_op jit(solution)/shard_map/ppermute | solution.py:541
  162.8 103.7 %all-gather.12.cloned.1.call-start = ((), (), s32[]{:S(2)}) async-start(), calls=%async_computation.7 | async-start | bytes 2654208 | tf_op jit(solution)/shard_map/all_gather | solution.py:614
  214.7 3.8 collective-permute-start.8
  215.4 250.9 %reduce-scatter.19.cloned.1.call-start = ((), (), s32[]{:S(2)}) async-start(), calls=%async_computation.11 | async-start | bytes 2654208
  216.9 12.0 %collective-permute-start.13 = (bf16[256,768]{1,0:T(8,128)(2,1)S(1)}, bf16[256,768]{1,0:T(8,128)(2,1)S(1)}, u32[]{:S(2)}, u32[]{:S(2)}) collective-permute-start(bf16[256,768]{1,0:T(8,128)(2,1)S(1)} %broadcast_select_fusion), channel_id=1, source_target_pairs={{0,2},{1,3},{2,0},{3,1},{4,6},{5,7},{6,4},{7,5},{8,10},{9,11},{10,... | collective-permute-start | bytes 1179656 | tf_op jit(solution)/shard_map/ppermute | solution.py:541
  219.8 25.6 %collective-permute-start.9 = (bf16[2,256,768]{2,1,0:T(8,128)(2,1)S(1)}, bf16[2,256,768]{2,1,0:T(8,128)(2,1)S(1)}, u32[]{:S(2)}, u32[]{:S(2)}) collective-permute-start(bf16[2,256,768]{2,1,0:T(8,128)(2,1)S(1)} %fusion.22), channel_id=1, source_target_pairs={{0,2},{1,3},{2,0},{3,1},{4,6},{5,7},{6,4},{7,5},{8,10},{9,11},{10,... | collective-permute-start | bytes 2359304 | tf_op jit(solution)/shard_map/ppermute | solution.py:541
  229.1 17.3 %collective-permute-start.14 = (bf16[2,256,768]{2,1,0:T(8,128)(2,1)S(1)}, bf16[2,256,768]{2,1,0:T(8,128)(2,1)S(1)}, u32[]{:S(2)}, u32[]{:S(2)}) collective-permute-start(bf16[2,256,768]{2,1,0:T(8,128)(2,1)S(1)} %pad_maximum_fusion.14), channel_id=1, source_target_pairs={{0,1},{1,0},{2,3},{3,2},{4,5},{5,4},{6,7},{7,6},{8,9},{9,8},{10,11... | collective-permute-start | bytes 2359304 | tf_op jit(solution)/shard_map/ppermute | solution.py:541
  278.0 19.6 %collective-permute-start.16 = (bf16[2,256,768]{2,1,0:T(8,128)(2,1)S(1)}, bf16[2,256,768]{2,1,0:T(8,128)(2,1)S(1)}, u32[]{:S(2)}, u32[]{:S(2)}) collective-permute-start(bf16[2,256,768]{2,1,0:T(8,128)(2,1)S(1)} %fusion.20), channel_id=1, source_target_pairs={{0,2},{1,3},{2,0},{3,1},{4,6},{5,7},{6,4},{7,5},{8,10},{9,11},{10,... | collective-permute-start | bytes 2359304 | tf_op jit(solution)/shard_map/ppermute | solution.py:541
  323.8 20.0 %collective-permute-start.19 = (bf16[2,256,768]{2,1,0:T(8,128)(2,1)}, bf16[2,256,768]{2,1,0:T(8,128)(2,1)}, u32[]{:S(2)}, u32[]{:S(2)}) collective-permute-start(bf16[2,256,768]{2,1,0:T(8,128)(2,1)} %fusion.19), channel_id=1, source_target_pairs={{0,2},{1,3},{2,0},{3,1},{4,6},{5,7},{6,4},{7,5},{8,10},{9,11},{10,... | collective-permute-start | bytes 2359304 | tf_op jit(solution)/shard_map/ppermute | solution.py:541
  333.0 136.5 %reduce-scatter.17.cloned.1.call-start = ((), (), s32[]{:S(2)}) async-start(), calls=%async_computation.10 | async-start | bytes 1327104
  364.2 19.9 %collective-permute-start.22 = (bf16[2,256,768]{2,1,0:T(8,128)(2,1)}, bf16[2,256,768]{2,1,0:T(8,128)(2,1)}, u32[]{:S(2)}, u32[]{:S(2)}) collective-permute-start(bf16[2,256,768]{2,1,0:T(8,128)(2,1)} %fusion.18), channel_id=1, source_target_pairs={{0,2},{1,3},{2,0},{3,1},{4,6},{5,7},{6,4},{7,5},{8,10},{9,11},{10,... | collective-permute-start | bytes 2359304 | tf_op jit(solution)/shard_map/ppermute | solution.py:541
  371.4 166.6 %all-reduce.3.cloned.1.call-start = ((), (), s32[]{:S(2)}) async-start(), calls=%async_computation.12 | async-start | bytes 163840
  389.8 5.3 collective-permute-start.23
  431.3 178.8 %reduce-scatter.15.cloned.1.call-start = ((), (), s32[]{:S(2)}) async-start(), calls=%async_computation.9 | async-start | bytes 2654208
  438.6 238.1 %reduce-scatter.13.cloned.1.call-start = ((), (), s32[]{:S(2)}) async-start(), calls=%async_computation.8 | async-start | bytes 1327104
  445.8 19.6 %collective-permute-start.12 = (bf16[2,256,768]{2,1,0:T(8,128)(2,1)S(1)}, bf16[2,256,768]{2,1,0:T(8,128)(2,1)S(1)}, u32[]{:S(2)}, u32[]{:S(2)}) collective-permute-start(bf16[2,256,768]{2,1,0:T(8,128)(2,1)S(1)} %fusion.21), channel_id=1, source_target_pairs={{0,2},{1,3},{2,0},{3,1},{4,6},{5,7},{6,4},{7,5},{8,10},{9,11},{10,... | collective-permute-start | bytes 2359304 | tf_op jit(solution)/shard_map/ppermute | solution.py:541
  475.0 8.2 %collective-permute-start.24 = (bf16[2,256,768]{2,1,0:T(8,128)(2,1)}, bf16[2,256,768]{2,1,0:T(8,128)(2,1)}, u32[]{:S(2)}, u32[]{:S(2)}) collective-permute-start(bf16[2,256,768]{2,1,0:T(8,128)(2,1)} %dynamic-slice_bitcast_fusion), channel_id=1, source_target_pairs={{0,1},{1,0},{2,3},{3,2},{4,5},{5,4},{6,7},{7,6},{8,9},{9,8},{10,11... | collective-permute-start | bytes 2359304 | tf_op jit(solution)/shard_map/ppermute | solution.py:541
  484.6 54.7 %collective-permute-start.25 = (bf16[2,256,768]{2,1,0:T(8,128)(2,1)S(1)}, bf16[2,256,768]{2,1,0:T(8,128)(2,1)S(1)}, u32[]{:S(2)}, u32[]{:S(2)}) collective-permute-start(bf16[2,256,768]{2,1,0:T(8,128)(2,1)S(1)} %fusion.17), channel_id=1, source_target_pairs={{0,2},{1,3},{2,0},{3,1},{4,6},{5,7},{6,4},{7,5},{8,10},{9,11},{10,... | collective-permute-start | bytes 2359304 | tf_op jit(solution)/shard_map/ppermute | solution.py:541
  (104 other events, 1092.9 us)
Sparse Core Ops, SparseCore 0:
  10.8 44.0 all-gather.5
  102.0 48.6 all-gather.7
  163.0 38.7 all-gather.9
  215.5 50.9 all-gather.11
  333.1 66.6 reduce-scatter.18
  403.1 63.1 reduce-scatter.16
  470.2 67.7 all-reduce.2
  541.5 68.6 reduce-scatter.14
  613.5 63.0 reduce-scatter.12

commit v2 on v1

--- a/solution.py
+++ b/solution.py
@@ -606,16 +606,37 @@
     out = lax.dot_general(
         grad_hidden, up, (((1,), (1,)), ((), ())), preferred_element_type=F32
     ).astype(BF16)
-    grads = jnp.concatenate([rows_dot(x, grad_hidden), rows_dot(grad, active)], axis=1)
-    return out, grads.astype(BF16)
-
-
-def gather_rows(x):
-    return lax.all_gather(x, DATA, axis=0, tiled=True)
-
-
-def scatter_rows(x):
-    return lax.psum_scatter(x, DATA, scatter_dimension=0, tiled=True).astype(F32)
+    return out, rows_dot(x, grad_hidden), rows_dot(grad, active)
+
+
+class Rows:
+    def __init__(self):
+        self.count = lax.axis_size(DATA)
+        self.index = lax.axis_index(DATA)
+        self.bits = [1 << i for i in reversed(range(self.count.bit_length() - 1))]
+
+    def swap(self, x, bit):
+        return lax.ppermute(x, DATA, [(i, i ^ bit) for i in range(self.count)])
+
+    def gather(self, x):
+        for bit in self.bits:
+            x = jnp.concatenate([x, self.swap(x, bit)], axis=0)
+        return x
+
+    def scatter(self, x):
+        for bit in reversed(self.bits):
+            half = x.shape[0] // 2
+            x = x[:half].astype(F32) + self.swap(x[half:].astype(BF16), bit).astype(F32)
+        return x
+
+    def order(self, size):
+        block = size // self.count
+        mask = [0]
+        for bit in self.bits:
+            mask = mask + [m | bit for m in mask]
+        relative = jnp.repeat(jnp.asarray(mask, jnp.int32) ^ self.index, block) * block
+        relative = relative + jnp.tile(jnp.arange(block, dtype=jnp.int32), self.count)
+        return (jnp.arange(size, dtype=jnp.int32)[:, None] == relative[None, :]).astype(BF16)
 
 
 def on_device(
@@ -633,21 +654,41 @@
     states = ssm_decay.shape[1] * lax.axis_size(DATA)
     taps = shift_taps.shape[0] * lax.axis_size(DATA)
 
+    rows = Rows()
+    order = rows.order(model)
+    taps_order = rows.order(taps)
+    block = mixer_query.shape[0]
+    unit_rows = shift_taps.shape[0]
     own_gains = jnp.stack([gain_mixer, gain_ffn1, gain_attn, gain_ffn2], axis=0)
-    small = gather_rows(
+    small = jnp.zeros((16, model), BF16)
+    small = small.at[:unit_rows, : 3 * width].set(
         jnp.concatenate([shift_taps, ssm_decay.T, ssm_coef.T], axis=1)
-    ).astype(F32)
-    gains = lax.all_gather(own_gains, DATA, axis=1, tiled=True).astype(F32)
-    mixer_w = gather_rows(
+    )
+    small = small.at[12:16, :block].set(own_gains)
+    small = rows.gather(small).reshape(rows.count, 16, model)
+    mixer_w = rows.gather(
         jnp.concatenate([mixer_query, mixer_key, mixer_value, mixer_out.T], axis=1)
     )
-    ffn1_w = gather_rows(jnp.concatenate([ffn1_up, ffn1_down.T], axis=1))
-    attn_w = gather_rows(jnp.concatenate([attn_query, attn_key, attn_value, attn_out.T], axis=1))
-    ffn2_w = gather_rows(jnp.concatenate([ffn2_up, ffn2_down.T], axis=1))
-    hidden_units = ffn1_up.shape[1]
-
-    start = group.both_halves(tokens).astype(F32)
-    taps_w, decay_t, coef_t = (small[:, i * width : (i + 1) * width] for i in range(3))
+    up1 = rows.gather(ffn1_up)
+    down1 = rows.gather(ffn1_down.T)
+    attn_w = rows.gather(jnp.concatenate([attn_query, attn_key, attn_value, attn_out.T], axis=1))
+    up2 = rows.gather(ffn2_up)
+    down2 = rows.gather(ffn2_down.T)
+
+    def to_relative(x):
+        return jnp.dot(x, order, preferred_element_type=F32).astype(BF16)
+
+    def to_true(x):
+        return lax.dot_general(
+            x.astype(BF16), order, (((1,), (1,)), ((), ())), preferred_element_type=F32
+        ).astype(BF16)
+
+    gains = small[:, 12:16, :block].transpose(1, 0, 2).reshape(4, model).astype(F32)
+    vectors = small[:, :unit_rows, : 3 * width].reshape(states, 3 * width)
+    taps_w = jnp.dot(taps_order, vectors[:, :width], preferred_element_type=F32)
+    decay_t = vectors[:, width : 2 * width].astype(F32)
+    coef_t = vectors[:, 2 * width :].astype(F32)
+    start = group.both_halves(to_relative(tokens)).astype(F32)
     spectra = kernel_spectra(decay_t, coef_t, taps_w, fwd, length)
 
     normed1, unit1, inverse1 = norm_rows(start, gains[0])
@@ -661,7 +702,7 @@
 
     normed2, unit2, inverse2 = norm_rows(after_mixer, gains[1])
     x2 = group.all_rows(normed2)
-    out, hidden1 = ffn_forward(x2, ffn1_w[:, :hidden_units], ffn1_w[:, hidden_units:])
+    out, hidden1 = ffn_forward(x2, up1, down1)
     after_ffn1 = after_mixer + group.total(out)
 
     normed3, unit3, inverse3 = norm_rows(after_ffn1, gains[2])
@@ -671,20 +712,21 @@
 
     normed4, unit4, inverse4 = norm_rows(after_attn, gains[3])
     x4 = group.all_rows(normed4)
-    out, hidden2 = ffn_forward(x4, ffn2_w[:, :hidden_units], ffn2_w[:, hidden_units:])
+    out, hidden2 = ffn_forward(x4, up2, down2)
     final = after_attn + group.total(out)
-    output = lax.dynamic_index_in_dim(final, group.chip, 0, keepdims=False).astype(BF16)
+    output = to_true(lax.dynamic_index_in_dim(final, group.chip, 0, keepdims=False))
 
     positions = lax.axis_index(TENSOR) * quarter + jnp.arange(quarter)
     live = (positions < seq_lengths[0])[:, None]
     masked = jnp.where(live, cotangent, jnp.zeros_like(cotangent))
-    grad_low = group.both_halves(masked)
+    grad_low = group.both_halves(to_relative(masked))
     grad = grad_low.astype(F32)
 
     g4 = group.all_rows(grad_low)
-    out, ffn2_g = ffn_backward(x4, hidden2, g4, ffn2_w[:, :hidden_units], ffn2_w[:, hidden_units:])
+    out, u2, d2 = ffn_backward(x4, hidden2, g4, up2, down2)
     grad = grad + norm_back(group.total(out), unit4, inverse4, gains[3])
-    ffn2_g = scatter_rows(ffn2_g)
+    u2 = rows.scatter(u2)
+    d2 = rows.scatter(d2)
 
     g3 = group.all_rows(grad.astype(BF16))
     out, gq, gk, gv = attn_backward_kernel(seq_lengths, g3, attn_w, q2, k2, v2, log_total)
@@ -692,12 +734,13 @@
         [rows_dot(x3, gq), rows_dot(x3, gk), rows_dot(x3, gv), rows_dot(g3, attended_t.T)], axis=1
     )
     grad = grad + norm_back(group.total(out), unit3, inverse3, gains[2])
-    attn_g = scatter_rows(attn_g.astype(BF16))
+    attn_g = rows.scatter(attn_g)
 
     g2 = group.all_rows(grad.astype(BF16))
-    out, ffn1_g = ffn_backward(x2, hidden1, g2, ffn1_w[:, :hidden_units], ffn1_w[:, hidden_units:])
+    out, u1, d1 = ffn_backward(x2, hidden1, g2, up1, down1)
     grad = grad + norm_back(group.total(out), unit2, inverse2, gains[1])
-    ffn1_g = scatter_rows(ffn1_g)
+    u1 = rows.scatter(u1)
+    d1 = rows.scatter(d1)
 
     g1 = group.all_rows(grad.astype(BF16))
     gq, gk, gv, grad_taps, grad_kernel = mixer_backward_kernel(
@@ -708,14 +751,13 @@
         grad_joined, mixer_w[:, : 3 * width], (((1,), (1,)), ((), ())), preferred_element_type=F32
     ).astype(BF16)
     grad = grad + norm_back(group.total(out), unit1, inverse1, gains[0])
-    input_grad = lax.dynamic_index_in_dim(grad, group.chip, 0, keepdims=False).astype(BF16)
-    mixer_g = scatter_rows(
-        jnp.concatenate([rows_dot(x1, grad_joined), rows_dot(g1, mixed)], axis=1).astype(BF16)
+    input_grad = to_true(lax.dynamic_index_in_dim(grad, group.chip, 0, keepdims=False))
+    mixer_g = rows.scatter(
+        jnp.concatenate([rows_dot(x1, grad_joined), rows_dot(g1, mixed)], axis=1)
     )
     grad_decay, grad_coef = ssm_grad_kernel(grad_kernel, decay_t, coef_t)
-    small_g = scatter_rows(
-        jnp.concatenate([grad_taps, grad_decay, grad_coef], axis=1).astype(BF16)
-    )
+    grad_taps = rows_dot(taps_order, grad_taps.astype(BF16))
+    small_g = rows.scatter(jnp.concatenate([grad_taps, grad_decay, grad_coef], axis=1))
 
     def gain_sum(grads, weights, gain):
         products = sum(g * w.astype(F32) for g, w in zip(grads, weights))
@@ -726,8 +768,6 @@
 
     mq, mk, mv, mo = cut(mixer_g, width)
     aq, ak, av, ao = cut(attn_g, width)
-    u1, d1 = cut(ffn1_g, hidden_units)
-    u2, d2 = cut(ffn2_g, hidden_units)
     gt, gd, gc = cut(small_g, width)
     gain_grads = lax.psum(
         jnp.stack(

time: 704 us -> 516 us (0.73)
  waiting for transfers between devices: 363 us -> 204 us
  starting transfers between devices: 17.8 us -> 66 us
  blocking collectives: 57.1 us -> 9.25 us
  local copies, waits for them, and re-layouts: 70 us -> 43.6 us
  between operations: 17.2 us -> 4.03 us
    ppermute x0 -> x42, waiting for transfers between devices: none -> 186 us  [swap(): return lax.ppermute(x, DATA, [(i, i ^ bit) for i in range(self.count)])]
    unnamed x14 -> x0, waiting for transfers between devices: 184 us -> none
    ppermute x26, waiting for transfers between devices: 121 us -> 17.5 us  [swap(): return lax.ppermute(x, TENSOR, [(i, i ^ bit) for i in range(4)])]
    all_gather x4 -> x0, waiting for transfers between devices: 58 us -> none  [gather_rows(): return lax.all_gather(x, DATA, axis=0, tiled=True)]
    all_gather x2 -> x0, blocking collectives: 51.4 us -> none  [the longest x1 30.6 us: gather_rows(): return lax.all_gather(x, DATA, axis=0, tiled=True)]
    ppermute x0 -> x42, starting transfers between devices: none -> 47.8 us  [swap(): return lax.ppermute(x, DATA, [(i, i ^ bit) for i in range(self.count)])]
    unnamed x216 -> x215, local copies, waits for them, and re-layouts: 50.5 us -> 25.2 us
    dot_general x0 -> x5, matrix products: none -> 7.96 us  [the longest x2 4.12 us: to_true(): lax.dot_general(x.astype(BF16), order, (((1,), (1,)), ((), ())), preferre...]
  transfers between devices with their start and end apart: 35 -> 68, of which waited for: 24 -> 33; matrix products, arithmetic and copies ran while one was open for 16% -> 19% of each run, Pallas kernels for 6% -> 5%
where the time goes in v2:
time: 516 us; the launch traced here: 508 us
  waiting for transfers between devices  204 us (40%)
  Pallas kernels  82.2 us (16%)
  starting transfers between devices  66 us (13%)
  other arithmetic  55.9 us (11%)
  local copies, waits for them, and re-layouts  43.6 us (8%)
  matrix products  43.2 us (8%)
  blocking collectives  9.25 us (2%)
    ppermute x42, waiting for transfers between devices, swap(): return lax.ppermute(x, DATA, [(i, i ^ bit) for i in range(self.count)])  186 us
    ppermute x42, starting transfers between devices, swap(): return lax.ppermute(x, DATA, [(i, i ^ bit) for i in range(self.count)])  47.8 us
    unnamed x215, local copies, waits for them, and re-layouts  25.2 us
    ppermute x26, starting transfers between devices, swap(): return lax.ppermute(x, TENSOR, [(i, i ^ bit) for i in range(4)])  18.2 us
    ppermute x26, waiting for transfers between devices, swap(): return lax.ppermute(x, TENSOR, [(i, i ^ bit) for i in range(4)])  17.5 us
    pallas_call x1, Pallas kernels, ssm_grad_kernel(): pl.pallas_call(ssm_grad_body, out_shape=(out, out), compiler_params=pltpu...  15.8 us
    pallas_call x1, Pallas kernels, mixer_backward_kernel(): pl.pallas_call(mixer_bwd_body, out_shape=(row_b, row_b, row_b, jax.ShapeD...  15.3 us
    pallas_call x1, Pallas kernels, attn_backward_kernel(): pl.pallas_call(attn_bwd_body, in_specs=[pl.BlockSpec(memory_space=pltpu.S...  14.8 us
  transfers between devices with their start and end apart: 68, of which 33 were waited for; matrix products, arithmetic and copies ran while one was open for 19% of the time, Pallas kernels for 5%

profile of v2, /device:TPU:0, one launch (start us, length us, event | category | flops | bytes accessed | tf_op | source)
XLA Modules:
  0.0 507.7 jit_solution(9852175656449762372)
XLA Ops:
  24.3 7.8 %collective-permute-done.6 = bf16[192,768]{0,1:T(8,128)(2,1)S(1)} collective-permute-done((bf16[192,768]{0,1:T(8,128)(2,1)S(1)}, bf16[192,768]{0,1:T(8,128)(2,1)S(1)}, u32[]{:S(2)}, u32[]{:S(2)}) %collective-permute-start.6) | collective-permute-done | bytes 294944 | tf_op jit(solution)/shard_map/ppermute | solution.py:619
  36.6 11.5 %kernel_spectra.1 = (f32[8,128,192]{2,1,0:T(8,128)}, f32[8,128,192]{2,1,0:T(8,128)}, f32[128,192]{1,0:T(8,128)}, f32[128,192]{1,0:T(8,128)}) custom-call(f32[64,192]{1,0:T(8,128)} %get-tuple-element.212.decay_ref, f32[64,192]{1,0:T(8,128)} %get-tuple-element.211.coef_ref, f32[64,192]{1,0:T(8,128)} %fusion.71.taps_ref, bf16[256,384]{1,0:T(8,128)(2,1)} %constant.159.clone.fwd_ref), custom_call_target="tpu_custom_call" | custom-call | tf_op jit(solution)/shard_map/kernel_spectra/pallas_call | solution.py:130
  55.4 13.8 %mixer_forward.1 = (bf16[1024,768]{1,0:T(8,128)(2,1)}, bf16[1024,192]{1,0:T(8,128)(2,1)}, f32[1024,192]{1,0:T(8,128)}, f32[1024,192]{1,0:T(8,128)}, f32[1024,192...) custom-call(bf16[1024,768]{1,0:T(8,128)(2,1)} %bitcast.203, ...), custom_call_target="tpu_custom_call" | custom-call | tf_op jit(solution)/shard_map/mixer_forward/pallas_call | solution.py:233
  77.3 8.6 %collective-permute-done.11 = bf16[96,768]{1,0:T(8,128)(2,1)S(1)} collective-permute-done((bf16[96,768]{1,0:T(8,128)(2,1)S(1)}, bf16[96,768]{1,0:T(8,128)(2,1)S(1)}, u32[]{:S(2)}, u32[]{:S(2)}) %collective-permute-start.11) | collective-permute-done | bytes 147488 | tf_op jit(solution)/shard_map/ppermute | solution.py:619
  89.0 9.1 %collective-permute-done.12 = bf16[192,768]{1,0:T(8,128)(2,1)S(1)} collective-permute-done((bf16[192,768]{1,0:T(8,128)(2,1)S(1)}, bf16[192,768]{1,0:T(8,128)(2,1)S(1)}, u32[]{:S(2)}, u32[]{:S(2)}) %collective-permute-start.12) | collective-permute-done | bytes 294944 | tf_op jit(solution)/shard_map/ppermute | solution.py:619
  102.6 8.8 %collective-permute-done.15 = bf16[192,768]{1,0:T(8,128)(2,1)S(1)} collective-permute-done((bf16[192,768]{1,0:T(8,128)(2,1)S(1)}, bf16[192,768]{1,0:T(8,128)(2,1)S(1)}, u32[]{:S(2)}, u32[]{:S(2)}) %collective-permute-start.15) | collective-permute-done | bytes 294944 | tf_op jit(solution)/shard_map/ppermute | solution.py:619
  116.5 10.4 %collective-permute-done.16 = bf16[384,768]{1,0:T(8,128)(2,1)S(1)} collective-permute-done((bf16[384,768]{1,0:T(8,128)(2,1)S(1)}, bf16[384,768]{1,0:T(8,128)(2,1)S(1)}, u32[]{:S(2)}, u32[]{:S(2)}) %collective-permute-start.16) | collective-permute-done | bytes 589856 | tf_op jit(solution)/shard_map/ppermute | solution.py:619
  137.2 7.0 %collective-permute-done.20 = bf16[96,768]{1,0:T(8,128)(2,1)S(1)} collective-permute-done((bf16[96,768]{1,0:T(8,128)(2,1)S(1)}, bf16[96,768]{1,0:T(8,128)(2,1)S(1)}, u32[]{:S(2)}, u32[]{:S(2)}) %collective-permute-start.20) | collective-permute-done | bytes 147488 | tf_op jit(solution)/shard_map/ppermute | solution.py:619
  158.6 13.2 %collective-permute-done.22 = bf16[384,768]{1,0:T(8,128)(2,1)S(1)} collective-permute-done((bf16[384,768]{1,0:T(8,128)(2,1)S(1)}, bf16[384,768]{1,0:T(8,128)(2,1)S(1)}, u32[]{:S(2)}, u32[]{:S(2)}) %collective-permute-start.22) | collective-permute-done | bytes 589856 | tf_op jit(solution)/shard_map/ppermute | solution.py:619
  175.9 10.9 %attn_forward.1 = (bf16[1024,768]{1,0:T(8,128)(2,1)}, bf16[1024,192]{1,0:T(8,128)(2,1)}, bf16[1024,192]{1,0:T(8,128)(2,1)}, bf16[1024,192]{1,0:T(8,128)(2,1)}, b...) custom-call(s32[1]{0:T(128)} %copy.123.len_ref, bf16[1024,768]{1,0:T(8,128)(2,1)} %bitcast.195, ...), custom_call_target="tpu_custom_call" | custom-call | tf_op jit(solution)/shard_map/attn_forward/pallas_call | solution.py:463
  239.0 8.6 %collective-permute-done.31 = bf16[384,768]{1,0:T(8,128)(2,1)S(1)} collective-permute-done((bf16[384,768]{1,0:T(8,128)(2,1)S(1)}, bf16[384,768]{1,0:T(8,128)(2,1)S(1)}, u32[]{:S(2)}, u32[]{:S(2)}) %collective-permute-start.31) | collective-permute-done | bytes 589856 | tf_op jit(solution)/shard_map/ppermute | solution.py:619
  263.9 9.0 %collective-permute-done.56 = bf16[384,768]{1,0:T(8,128)(2,1)S(1)} collective-permute-done((bf16[384,768]{1,0:T(8,128)(2,1)S(1)}, bf16[384,768]{1,0:T(8,128)(2,1)S(1)}, u32[]{:S(2)}, u32[]{:S(2)}) %collective-permute-start.56) | collective-permute-done | bytes 589856 | tf_op jit(solution)/shard_map/ppermute | solution.py:619
  273.4 11.7 %collective-permute-done.65 = bf16[384,768]{1,0:T(8,128)(2,1)S(1)} collective-permute-done((bf16[384,768]{1,0:T(8,128)(2,1)S(1)}, bf16[384,768]{1,0:T(8,128)(2,1)S(1)}, u32[]{:S(2)}, u32[]{:S(2)}) %collective-permute-start.65) | collective-permute-done | bytes 589856 | tf_op jit(solution)/shard_map/ppermute | solution.py:619
  299.4 14.8 %attn_backward.1 = (bf16[1024,768]{1,0:T(8,128)(2,1)}, bf16[1024,192]{1,0:T(8,128)(2,1)}, bf16[1024,192]{1,0:T(8,128)(2,1)}, bf16[1024,192]{1,0:T(8,128)(2,1)}) custom-call(s32[1]{0:T(128)} %copy.123.len_ref, bf16[1024,768]{1,0:T(8,128)(2,1)} %bitcast.201, bf16[768,768]{1,0:T(8,128)(2,1)} %pad_maximum_fusion.13.w_ref, ...), custom_call_target="tpu_custom_call" | custom-call | tf_op jit(solution)/shard_map/attn_backward/pallas_call | solution.py:520
  326.1 8.2 %collective-permute-done.53 = bf16[384,768]{0,1:T(8,128)(2,1)S(1)} collective-permute-done((bf16[384,768]{0,1:T(8,128)(2,1)S(1)}, bf16[384,768]{0,1:T(8,128)(2,1)S(1)}, u32[]{:S(2)}, u32[]{:S(2)}) %collective-permute-start.53) | collective-permute-done | bytes 589856 | tf_op jit(solution)/shard_map/ppermute | solution.py:619
  348.4 6.9 %collective-permute-done.55 = bf16[96,768]{0,1:T(8,128)(2,1)S(1)} collective-permute-done((bf16[96,768]{0,1:T(8,128)(2,1)S(1)}, bf16[96,768]{0,1:T(8,128)(2,1)S(1)}, u32[]{:S(2)}, u32[]{:S(2)}) %collective-permute-start.55) | collective-permute-done | bytes 147488 | tf_op jit(solution)/shard_map/ppermute | solution.py:619
  375.0 9.9 %collective-permute-done.62 = bf16[384,768]{1,0:T(8,128)(2,1)S(1)} collective-permute-done((bf16[384,768]{1,0:T(8,128)(2,1)S(1)}, bf16[384,768]{1,0:T(8,128)(2,1)S(1)}, u32[]{:S(2)}, u32[]{:S(2)}) %collective-permute-start.62) | collective-permute-done | bytes 589856 | tf_op jit(solution)/shard_map/ppermute | solution.py:619
  385.1 12.0 %collective-permute-done.50 = bf16[384,768]{1,0:T(8,128)(2,1)S(1)} collective-permute-done((bf16[384,768]{1,0:T(8,128)(2,1)S(1)}, bf16[384,768]{1,0:T(8,128)(2,1)S(1)}, u32[]{:S(2)}, u32[]{:S(2)}) %collective-permute-start.50) | collective-permute-done | bytes 589856 | tf_op jit(solution)/shard_map/ppermute | solution.py:619
  401.6 7.1 %collective-permute-done.51 = bf16[192,768]{1,0:T(8,128)(2,1)S(1)} collective-permute-done((bf16[192,768]{1,0:T(8,128)(2,1)S(1)}, bf16[192,768]{1,0:T(8,128)(2,1)S(1)}, u32[]{:S(2)}, u32[]{:S(2)}) %collective-permute-start.51) | collective-permute-done | bytes 294944 | tf_op jit(solution)/shard_map/ppermute | solution.py:619
  419.7 15.3 %mixer_backward.1 = (bf16[1024,192]{1,0:T(8,128)(2,1)}, bf16[1024,192]{1,0:T(8,128)(2,1)}, bf16[1024,192]{1,0:T(8,128)(2,1)}, f32[64,192]{1,0:T(8,128)}, f32[1024,192]{1,0:T(8,128)}) custom-call(bf16[1024,768]{1,0:T(8,128)(2,1)} %bitcast.200, bf16[192,768]{1,0:T(8,128)(2,1)} %get-tuple-element.192.wo_ref, f32[1024,192]{1,0:T(8,128)} %get-tuple-element.87.q_ref, ...), custom_call_target="tpu_custom_call" | custom-call | tf_op jit(solution)/shard_map/mixer_backward/pallas_call | solution.py:334
  436.3 15.8 %ssm_grad.1 = (f32[64,192]{1,0:T(8,128)}, f32[64,192]{1,0:T(8,128)}) custom-call(f32[1024,192]{1,0:T(8,128)} %get-tuple-element.104.dk_ref, f32[64,192]{1,0:T(8,128)} %get-tuple-element.212.decay_ref, f32[64,192]{1,0:T(8,128)} %get-tuple-element.211.coef_ref), custom_call_target="tpu_custom_call" | custom-call | tf_op jit(solution)/shard_map/ssm_grad/pallas_call | solution.py:407
  464.8 7.0 %collective-permute-done.47 = bf16[384,768]{0,1:T(8,128)(2,1)S(1)} collective-permute-done((bf16[384,768]{0,1:T(8,128)(2,1)S(1)}, bf16[384,768]{0,1:T(8,128)(2,1)S(1)}, u32[]{:S(2)}, u32[]{:S(2)}) %collective-permute-start.47) | collective-permute-done | bytes 589856 | tf_op jit(solution)/shard_map/ppermute | solution.py:619
  472.9 8.5 %collective-permute-done.48 = bf16[192,768]{0,1:T(8,128)(2,1)S(1)} collective-permute-done((bf16[192,768]{0,1:T(8,128)(2,1)S(1)}, bf16[192,768]{0,1:T(8,128)(2,1)S(1)}, u32[]{:S(2)}, u32[]{:S(2)}) %collective-permute-start.48) | collective-permute-done | bytes 294944 | tf_op jit(solution)/shard_map/ppermute | solution.py:619
  493.9 9.2 %psum.7 = f32[4,96]{1,0:T(4,128)S(1)} all-reduce(f32[4,96]{1,0:T(4,128)S(1)} %pad_maximum_fusion.45), channel_id=1, replica_groups=mesh['dp'=8,'tensor'=4] {'tensor'}, use_global_device_ids=true, to_apply=%region_20.21 | all-reduce | flops 384 | bytes 3072 | tf_op jit(solution)/shard_map/psum | solution.py:772
  (532 shorter events, 258.5 us)
Async XLA Ops:
  35.2 17.1 %collective-permute-start.4 = (bf16[2,256,768]{2,1,0:T(8,128)(2,1)}, bf16[2,256,768]{2,1,0:T(8,128)(2,1)}, u32[]{:S(2)}, u32[]{:S(2)}) collective-permute-start(bf16[2,256,768]{2,1,0:T(8,128)(2,1)} %multiply_convert_fusion.5), channel_id=1, source_target_pairs={{0,1},{1,0},{2,3},{3,2},{4,5},{5,4},{6,7},{7,6},{8,9},{9,8},{10,11... | collective-permute-start | bytes 2359304 | tf_op jit(solution)/shard_map/ppermute | solution.py:541
  74.5 24.3 %collective-permute-start.9 = (bf16[2,256,768]{2,1,0:T(8,128)(2,1)S(1)}, bf16[2,256,768]{2,1,0:T(8,128)(2,1)}, u32[]{:S(2)}, u32[]{:S(2)}) collective-permute-start(bf16[2,256,768]{2,1,0:T(8,128)(2,1)S(1)} %fusion.28), channel_id=1, source_target_pairs={{0,2},{1,3},{2,0},{3,1},{4,6},{5,7},{6,4},{7,5},{8,10},{9,11},{10,... | collective-permute-start | bytes 2359304 | tf_op jit(solution)/shard_map/ppermute | solution.py:541
  132.7 19.8 %collective-permute-start.18 = (bf16[2,256,768]{2,1,0:T(8,128)(2,1)S(1)}, bf16[2,256,768]{2,1,0:T(8,128)(2,1)}, u32[]{:S(2)}, u32[]{:S(2)}) collective-permute-start(bf16[2,256,768]{2,1,0:T(8,128)(2,1)S(1)} %fusion.27), channel_id=1, source_target_pairs={{0,2},{1,3},{2,0},{3,1},{4,6},{5,7},{6,4},{7,5},{8,10},{9,11},{10,... | collective-permute-start | bytes 2359304 | tf_op jit(solution)/shard_map/ppermute | solution.py:541
  154.8 19.1 %collective-permute-start.19 = (bf16[2,256,768]{2,1,0:T(8,128)(2,1)S(1)}, bf16[2,256,768]{2,1,0:T(8,128)(2,1)S(1)}, u32[]{:S(2)}, u32[]{:S(2)}) collective-permute-start(bf16[2,256,768]{2,1,0:T(8,128)(2,1)S(1)} %multiply_convert_fusion.3), channel_id=1, source_target_pairs={{0,1},{1,0},{2,3},{3,2},{4,5},{5,4},{6,7},{7,6},{8,9},{9,8},{10,11... | collective-permute-start | bytes 2359304 | tf_op jit(solution)/shard_map/ppermute | solution.py:541
  191.4 17.8 %collective-permute-start.26 = (bf16[96,768]{1,0:T(8,128)(2,1)}, bf16[96,768]{1,0:T(8,128)(2,1)}, u32[]{:S(2)}, u32[]{:S(2)}) collective-permute-start(bf16[96,768]{1,0:T(8,128)(2,1)} %param.50), channel_id=1, source_target_pairs={{0,16},{4,20},{8,24},{12,28},{16,0},{20,4},{24,8},{28,12},{1,17},{... | collective-permute-start | bytes 442376 | tf_op jit(solution)/shard_map/ppermute | solution.py:619
  194.3 20.3 %collective-permute-start.34 = (bf16[256,768]{1,0:T(8,128)(2,1)}, bf16[256,768]{1,0:T(8,128)(2,1)}, u32[]{:S(2)}, u32[]{:S(2)}) collective-permute-start(bf16[256,768]{1,0:T(8,128)(2,1)} %fusion.31), channel_id=1, source_target_pairs={{0,2},{1,3},{2,0},{3,1},{4,6},{5,7},{6,4},{7,5},{8,10},{9,11},{10,... | collective-permute-start | bytes 1179656 | tf_op jit(solution)/shard_map/ppermute | solution.py:541
  204.8 24.4 %collective-permute-start.30 = (bf16[192,768]{1,0:T(8,128)(2,1)}, bf16[192,768]{1,0:T(8,128)(2,1)}, u32[]{:S(2)}, u32[]{:S(2)}) collective-permute-start(bf16[192,768]{1,0:T(8,128)(2,1)} %pad_maximum_fusion.30), channel_id=1, source_target_pairs={{0,8},{4,12},{8,0},{12,4},{16,24},{20,28},{24,16},{28,20},{1,9},{5... | collective-permute-start | bytes 884744 | tf_op jit(solution)/shard_map/ppermute | solution.py:619
  207.5 19.3 %collective-permute-start.24 = (bf16[2,256,768]{2,1,0:T(8,128)(2,1)}, bf16[2,256,768]{2,1,0:T(8,128)(2,1)}, u32[]{:S(2)}, u32[]{:S(2)}) collective-permute-start(bf16[2,256,768]{2,1,0:T(8,128)(2,1)} %fusion.26), channel_id=1, source_target_pairs={{0,2},{1,3},{2,0},{3,1},{4,6},{5,7},{6,4},{7,5},{8,10},{9,11},{10,... | collective-permute-start | bytes 2359304 | tf_op jit(solution)/shard_map/ppermute | solution.py:541
  215.9 20.6 %collective-permute-start.35 = (bf16[2,256,768]{2,1,0:T(8,128)(2,1)S(1)}, bf16[2,256,768]{2,1,0:T(8,128)(2,1)S(1)}, u32[]{:S(2)}, u32[]{:S(2)}) collective-permute-start(bf16[2,256,768]{2,1,0:T(8,128)(2,1)S(1)} %pad_maximum_fusion.16), channel_id=1, source_target_pairs={{0,1},{1,0},{2,3},{3,2},{4,5},{5,4},{6,7},{7,6},{8,9},{9,8},{10,11... | collective-permute-start | bytes 2359304 | tf_op jit(solution)/shard_map/ppermute | solution.py:541
  230.4 17.3 %collective-permute-start.31 = (bf16[384,768]{1,0:T(8,128)(2,1)S(1)}, bf16[384,768]{1,0:T(8,128)(2,1)S(1)}, u32[]{:S(2)}, u32[]{:S(2)}) collective-permute-start(bf16[384,768]{1,0:T(8,128)(2,1)S(1)} %pad_maximum_fusion.22), channel_id=1, source_target_pairs={{0,4},{4,0},{8,12},{12,8},{16,20},{20,16},{24,28},{28,24},{1,5},{5... | collective-permute-start | bytes 1769480 | tf_op jit(solution)/shard_map/ppermute | solution.py:619
  256.7 16.2 %collective-permute-start.56 = (bf16[384,768]{1,0:T(8,128)(2,1)S(1)}, bf16[384,768]{1,0:T(8,128)(2,1)S(1)}, u32[]{:S(2)}, u32[]{:S(2)}) collective-permute-start(bf16[384,768]{1,0:T(8,128)(2,1)S(1)} %slice.505), channel_id=1, source_target_pairs={{0,4},{4,0},{8,12},{12,8},{16,20},{20,16},{24,28},{28,24},{1,5},{5... | collective-permute-start | bytes 1769480 | tf_op jit(solution)/shard_map/ppermute | solution.py:619
  258.5 26.6 %collective-permute-start.65 = (bf16[384,768]{1,0:T(8,128)(2,1)S(1)}, bf16[384,768]{1,0:T(8,128)(2,1)S(1)}, u32[]{:S(2)}, u32[]{:S(2)}) collective-permute-start(bf16[384,768]{1,0:T(8,128)(2,1)S(1)} %slice.503), channel_id=1, source_target_pairs={{0,4},{4,0},{8,12},{12,8},{16,20},{20,16},{24,28},{28,24},{1,5},{5... | collective-permute-start | bytes 1769480 | tf_op jit(solution)/shard_map/ppermute | solution.py:619
  259.0 26.7 %collective-permute-start.37 = (bf16[2,256,768]{2,1,0:T(8,128)(2,1)S(1)}, bf16[2,256,768]{2,1,0:T(8,128)(2,1)S(1)}, u32[]{:S(2)}, u32[]{:S(2)}) collective-permute-start(bf16[2,256,768]{2,1,0:T(8,128)(2,1)S(1)} %fusion.24), channel_id=1, source_target_pairs={{0,2},{1,3},{2,0},{3,1},{4,6},{5,7},{6,4},{7,5},{8,10},{9,11},{10,... | collective-permute-start | bytes 2359304 | tf_op jit(solution)/shard_map/ppermute | solution.py:541
  263.8 23.6 %collective-permute-start.32 = (bf16[2,256,768]{2,1,0:T(8,128)(2,1)S(1)}, bf16[2,256,768]{2,1,0:T(8,128)(2,1)S(1)}, u32[]{:S(2)}, u32[]{:S(2)}) collective-permute-start(bf16[2,256,768]{2,1,0:T(8,128)(2,1)S(1)} %dynamic-slice_bitcast_fusion.4), channel_id=1, source_target_pairs={{0,1},{1,0},{2,3},{3,2},{4,5},{5,4},{6,7},{7,6},{8,9},{9,8},{10,11... | collective-permute-start | bytes 2359304 | tf_op jit(solution)/shard_map/ppermute | solution.py:541
  273.0 17.5 %collective-permute-start.57 = (bf16[192,768]{1,0:T(8,128)(2,1)S(1)}, bf16[192,768]{1,0:T(8,128)(2,1)S(1)}, u32[]{:S(2)}, u32[]{:S(2)}) collective-permute-start(bf16[192,768]{1,0:T(8,128)(2,1)S(1)} %slice.512), channel_id=1, source_target_pairs={{0,8},{4,12},{8,0},{12,4},{16,24},{20,28},{24,16},{28,20},{1,9},{5... | collective-permute-start | bytes 884744 | tf_op jit(solution)/shard_map/ppermute | solution.py:619
  288.5 57.3 %collective-permute-start.33 = (bf16[2,256,768]{2,1,0:T(8,128)(2,1)}, bf16[2,256,768]{2,1,0:T(8,128)(2,1)}, u32[]{:S(2)}, u32[]{:S(2)}) collective-permute-start(bf16[2,256,768]{2,1,0:T(8,128)(2,1)} %fusion.25), channel_id=1, source_target_pairs={{0,2},{1,3},{2,0},{3,1},{4,6},{5,7},{6,4},{7,5},{8,10},{9,11},{10,... | collective-permute-start | bytes 2359304 | tf_op jit(solution)/shard_map/ppermute | solution.py:541
  291.4 32.3 %collective-permute-start.58 = (bf16[96,768]{1,0:T(8,128)(2,1)}, bf16[96,768]{1,0:T(8,128)(2,1)}, u32[]{:S(2)}, u32[]{:S(2)}) collective-permute-start(bf16[96,768]{1,0:T(8,128)(2,1)} %slice.518), channel_id=1, source_target_pairs={{0,16},{4,20},{8,24},{12,28},{16,0},{20,4},{24,8},{28,12},{1,17},{... | collective-permute-start | bytes 442376 | tf_op jit(solution)/shard_map/ppermute | solution.py:619
  295.6 26.4 %collective-permute-start.67 = (bf16[96,768]{1,0:T(8,128)(2,1)}, bf16[96,768]{1,0:T(8,128)(2,1)}, u32[]{:S(2)}, u32[]{:S(2)}) collective-permute-start(bf16[96,768]{1,0:T(8,128)(2,1)} %slice.516), channel_id=1, source_target_pairs={{0,16},{4,20},{8,24},{12,28},{16,0},{20,4},{24,8},{28,12},{1,17},{... | collective-permute-start | bytes 442376 | tf_op jit(solution)/shard_map/ppermute | solution.py:619
  320.3 18.7 %collective-permute-start.40 = (bf16[2,256,768]{2,1,0:T(8,128)(2,1)S(1)}, bf16[2,256,768]{2,1,0:T(8,128)(2,1)S(1)}, u32[]{:S(2)}, u32[]{:S(2)}) collective-permute-start(bf16[2,256,768]{2,1,0:T(8,128)(2,1)S(1)} %fusion.23), channel_id=1, source_target_pairs={{0,2},{1,3},{2,0},{3,1},{4,6},{5,7},{6,4},{7,5},{8,10},{9,11},{10,... | collective-permute-start | bytes 2359304 | tf_op jit(solution)/shard_map/ppermute | solution.py:541
  372.1 25.1 %collective-permute-start.50 = (bf16[384,768]{1,0:T(8,128)(2,1)S(1)}, bf16[384,768]{1,0:T(8,128)(2,1)S(1)}, u32[]{:S(2)}, u32[]{:S(2)}) collective-permute-start(bf16[384,768]{1,0:T(8,128)(2,1)S(1)} %slice.507), channel_id=1, source_target_pairs={{0,4},{4,0},{8,12},{12,8},{16,20},{20,16},{24,28},{28,24},{1,5},{5... | collective-permute-start | bytes 1769480 | tf_op jit(solution)/shard_map/ppermute | solution.py:619
  372.7 24.8 %collective-permute-start.43 = (bf16[2,256,768]{2,1,0:T(8,128)(2,1)S(1)}, bf16[2,256,768]{2,1,0:T(8,128)(2,1)S(1)}, u32[]{:S(2)}, u32[]{:S(2)}) collective-permute-start(bf16[2,256,768]{2,1,0:T(8,128)(2,1)S(1)} %fusion.22), channel_id=1, source_target_pairs={{0,2},{1,3},{2,0},{3,1},{4,6},{5,7},{6,4},{7,5},{8,10},{9,11},{10,... | collective-permute-start | bytes 2359304 | tf_op jit(solution)/shard_map/ppermute | solution.py:541
  399.4 18.1 %collective-permute-start.44 = (bf16[2,256,768]{2,1,0:T(8,128)(2,1)S(1)}, bf16[2,256,768]{2,1,0:T(8,128)(2,1)S(1)}, u32[]{:S(2)}, u32[]{:S(2)}) collective-permute-start(bf16[2,256,768]{2,1,0:T(8,128)(2,1)S(1)} %get-tuple-element.166), channel_id=1, source_target_pairs={{0,1},{1,0},{2,3},{3,2},{4,5},{5,4},{6,7},{7,6},{8,9},{9,8},{10,11... | collective-permute-start | bytes 2359304 | tf_op jit(solution)/shard_map/ppermute | solution.py:541
  460.6 21.7 %collective-permute-start.45 = (bf16[2,256,768]{2,1,0:T(8,128)(2,1)S(1)}, bf16[2,256,768]{2,1,0:T(8,128)(2,1)S(1)}, u32[]{:S(2)}, u32[]{:S(2)}) collective-permute-start(bf16[2,256,768]{2,1,0:T(8,128)(2,1)S(1)} %dynamic-slice_bitcast_fusion), channel_id=1, source_target_pairs={{0,1},{1,0},{2,3},{3,2},{4,5},{5,4},{6,7},{7,6},{8,9},{9,8},{10,11... | collective-permute-start | bytes 2359304 | tf_op jit(solution)/shard_map/ppermute | solution.py:541
  482.6 21.0 %collective-permute-start.46 = (bf16[2,256,768]{2,1,0:T(8,128)(2,1)S(1)}, bf16[2,256,768]{2,1,0:T(8,128)(2,1)}, u32[]{:S(2)}, u32[]{:S(2)}) collective-permute-start(bf16[2,256,768]{2,1,0:T(8,128)(2,1)S(1)} %fusion.21), channel_id=1, source_target_pairs={{0,2},{1,3},{2,0},{3,1},{4,6},{5,7},{6,4},{7,5},{8,10},{9,11},{10,... | collective-permute-start | bytes 2359304 | tf_op jit(solution)/shard_map/ppermute | solution.py:541
  (142 other events, 1524.6 us)

commit v3 on v1

v3 whole, which is shorter than its diff:
```python
import numpy as np
import jax
import jax.numpy as jnp
from jax import lax
from jax.experimental import pallas as pl
from jax.experimental.pallas import tpu as pltpu
from jax.experimental.layout import Layout, with_layout_constraint
from jax.sharding import PartitionSpec as P

F32 = jnp.float32
BF16 = jnp.bfloat16
BLK = 128
VMEM_LIMIT = 56 * 1024 * 1024


def cost(us):
    return pl.CostEstimate(
        flops=int(us * 1.1e8), transcendentals=0, bytes_accessed=int(us * 3.5e5)
    )


def dot(a, b):
    return jnp.dot(a, b, preferred_element_type=F32)


def dot_nt(a, b):
    return lax.dot_general(a, b, (((1,), (1,)), ((), ())), preferred_element_type=F32)


def split(x):
    high = x.astype(BF16)
    return high, (x - high.astype(F32)).astype(BF16)


def spectral_tables():
    j = np.arange(BLK)
    f = np.arange(BLK)
    angle = 2.0 * np.pi * np.outer(f, j) / (2 * BLK)
    alternating = (-1.0) ** j
    real = np.cos(angle)
    imag = -np.sin(angle)
    imag[0] = alternating
    forward = np.concatenate([real, imag], axis=0)
    weight = np.full((BLK, 1), 2.0)
    weight[0] = 1.0
    back_real = weight * real / (2 * BLK)
    back_imag = 2.0 * imag / (2 * BLK)
    back_imag[0] = alternating / (2 * BLK)
    inverse = np.concatenate([back_real, back_imag], axis=0).T

    def halves(table):
        high = table.astype(jnp.bfloat16)
        low = (table - high.astype(np.float64)).astype(jnp.bfloat16)
        return high, low

    fh, fl = halves(forward)
    ih, il = halves(inverse)
    fwd = np.concatenate([fh, fh, fl], axis=1)
    inv = np.concatenate([ih, il], axis=0)
    return jnp.asarray(fwd), jnp.asarray(inv)


def to_spectrum(fwd_ref, x):
    high, low = split(x)
    return dot(fwd_ref[:, : 2 * BLK], jnp.concatenate([high, low], axis=0)) + dot(
        fwd_ref[:, 2 * BLK :], high
    )


def from_spectrum(inv_ref, z):
    high, low = split(z)
    both = dot(inv_ref[...], high)
    return both[:BLK] + both[BLK:] + dot(inv_ref[:BLK, :], low)


def sign_rows(shape):
    row = lax.broadcasted_iota(jnp.int32, shape, 0)
    return jnp.where(row % 2 == 0, 1.0, -1.0).astype(F32)


def lane_tiles(width):
    return [(s, min(128, width - s)) for s in range(0, width, 128)]


def fix_first(tile, re, im):
    row = lax.broadcasted_iota(jnp.int32, re.shape, 0)
    special = (row == 0) & (tile == 0)
    return jnp.where(special, im, re), jnp.where(special, 0.0, im)


def kgen_body(decay_ref, coef_ref, taps_ref, fwd_ref, kre_ref, kim_ref, tre_ref, tim_ref, mixp, kern):
    states, width = decay_ref.shape
    blocks = kre_ref.shape[0]
    decay = decay_ref[...]
    mixing = jnp.sqrt(2.0 * decay) * coef_ref[...]
    for m in range(blocks):
        mixp[m] = mixing * jnp.exp(decay * (-float(BLK * m)))
    for start, size in lane_tiles(width):
        lanes = slice(start, start + size)

        def per_tile(jt, _, lanes=lanes, size=size):
            steps = (lax.broadcasted_iota(jnp.int32, (8, size), 0) + jt * 8).astype(F32)

            def per_states(ng, acc):
                rows = pl.ds(pl.multiple_of(ng * 8, 8), 8)
                rates = -decay_ref[rows, lanes]
                scales = [mixp[m, rows, lanes] for m in range(blocks)]
                for i in range(8):
                    e = jnp.exp(rates[i : i + 1] * steps)
                    acc = tuple(a + e * s[i : i + 1] for a, s in zip(acc, scales))
                return acc

            acc = lax.fori_loop(
                0, states // 8, per_states, tuple(jnp.zeros((8, size), F32) for _ in range(blocks))
            )
            for m in range(blocks):
                kern[m, pl.ds(pl.multiple_of(jt * 8, 8), 8), lanes] = acc[m]
            return 0

        lax.fori_loop(0, BLK // 8, per_tile, 0)
    for m in range(blocks):
        spec = to_spectrum(fwd_ref, kern[m])
        kre_ref[m] = spec[:BLK]
        kim_ref[m] = spec[BLK:]
    taps = jnp.concatenate(
        [taps_ref[...], jnp.zeros((BLK - taps_ref.shape[0], width), F32)], axis=0
    )
    spec = to_spectrum(fwd_ref, taps)
    tre_ref[...] = spec[:BLK]
    tim_ref[...] = spec[BLK:]


def kernel_spectra(decay_t, coef_t, taps, fwd, length):
    states, width = decay_t.shape
    blocks = length // BLK
    return pl.pallas_call(
        kgen_body,
        out_shape=(
            jax.ShapeDtypeStruct((blocks, BLK, width), F32),
            jax.ShapeDtypeStruct((blocks, BLK, width), F32),
            jax.ShapeDtypeStruct((BLK, width), F32),
            jax.ShapeDtypeStruct((BLK, width), F32),
        ),
        scratch_shapes=[
            pltpu.VMEM((blocks, states, width), F32),
            pltpu.VMEM((blocks, BLK, width), F32),
        ],
        compiler_params=pltpu.CompilerParams(vmem_limit_bytes=VMEM_LIMIT),
        cost_estimate=cost(11),
        name="kernel_spectra",
    )(decay_t, coef_t, taps, fwd)


def conv_tiles(width, body):
    for start, size in lane_tiles(width):
        lanes = slice(start, start + size)

        def step(ft, _, lanes=lanes):
            body(ft, pl.ds(pl.multiple_of(ft * 8, 8), 8), lanes)
            return 0

        lax.fori_loop(0, BLK // 8, step, 0)


def piece_rows(core, quarter):
    places = []
    for half in range(2):
        for side in (core, 1 - core):
            places.append(pl.ds(pl.multiple_of((2 * half + side) * quarter, quarter), quarter))
    return places


def mixer_fwd_body(
    core_ref, a_ref, b_ref, c_ref, d_ref, w_ref, kre_ref, kim_ref, tre_ref, tim_ref, fwd_ref, inv_ref,
    keep_ref, send_ref,
    x_ref, mixed_ref, q_ref, v_ref, sh_ref, st_ref, sre_ref, sim_ref, ure_ref, uim_ref,
    zre, zim, keys,
):
    length, width = q_ref.shape
    blocks = length // BLK
    sign = sign_rows((BLK, width))
    row0 = lax.broadcasted_iota(jnp.int32, (BLK, width), 0) == 0
    places = piece_rows(core_ref[0], a_ref.shape[0])
    wq = w_ref[:, :width]
    wk = w_ref[:, width : 2 * width]
    wv = w_ref[:, 2 * width : 3 * width]
    for piece_ref, place in zip((a_ref, b_ref, c_ref, d_ref), places):
        piece = piece_ref[...]
        x_ref[place] = piece
        q_ref[place] = dot(piece, wq)
        v_ref[place] = dot(piece, wv)
        keys[place] = dot(piece, wk)
    tre = tre_ref[...]
    tim = tim_ref[...]
    tre2 = jnp.where(row0, tim, tre)
    tim0 = jnp.where(row0, 0.0, tim)
    last = None
    for p in range(blocks):
        rows = slice(p * BLK, (p + 1) * BLK)
        spec = to_spectrum(fwd_ref, keys[rows])
        re, im = spec[:BLK], spec[BLK:]
        sre_ref[p] = re
        sim_ref[p] = im
        pr = re * tre - im * tim0
        pi = re * tim0 + im * tre2
        if last is None:
            z = jnp.concatenate([pr, pi], axis=0)
        else:
            z = jnp.concatenate([pr + sign * last[0], pi + sign * last[1]], axis=0)
        last = (pr, pi)
        shifted = from_spectrum(inv_ref, z)
        sh_ref[rows] = shifted
        spec = to_spectrum(fwd_ref, shifted * v_ref[rows])
        ure_ref[p] = spec[:BLK]
        uim_ref[p] = spec[BLK:]

    def products(ft, fr, lanes):
        sgn = sign[:8, lanes]
        k = [(kre_ref[m, fr, lanes], kim_ref[m, fr, lanes]) for m in range(blocks)]
        k = [(a,) + fix_first(ft, a, b) for a, b in k]
        u = [(ure_ref[m, fr, lanes], uim_ref[m, fr, lanes]) for m in range(blocks)]
        prev = None
        for p in range(blocks):
            yr = yi = None
            for m in range(p + 1):
                ur, ui = u[m]
                kr, kr2, ki0 = k[p - m]
                a = ur * kr - ui * ki0
                b = ur * ki0 + ui * kr2
                yr = a if yr is None else yr + a
                yi = b if yi is None else yi + b
            if prev is None:
                zre[p, fr, lanes] = yr
                zim[p, fr, lanes] = yi
            else:
                zre[p, fr, lanes] = yr + sgn * prev[0]
                zim[p, fr, lanes] = yi + sgn * prev[1]
            prev = (yr, yi)

    conv_tiles(width, products)
    wo = w_ref[:, 3 * width :]
    for half in range(2):
        for p in range(half * blocks // 2, (half + 1) * blocks // 2):
            rows = slice(p * BLK, (p + 1) * BLK)
            state = from_spectrum(inv_ref, jnp.concatenate([zre[p], zim[p]], axis=0))
            st_ref[rows] = state
            mixed_ref[rows] = (q_ref[rows] * state).astype(BF16)
        for out_ref, place in zip((keep_ref, send_ref), places[2 * half : 2 * half + 2]):
            out_ref[half] = dot_nt(mixed_ref[place], wo).astype(BF16)


SCALAR = pl.BlockSpec(memory_space=pltpu.SMEM)
WHOLE = pl.BlockSpec(memory_space=pltpu.VMEM)


def mixer_forward_kernel(core, pieces, w, spectra, fwd, inv):
    quarter, model = pieces[0].shape
    length = 4 * quarter
    width = w.shape[1] // 4
    blocks = length // BLK
    row_f = jax.ShapeDtypeStruct((length, width), F32)
    spec_f = jax.ShapeDtypeStruct((blocks, BLK, width), F32)
    piece = jax.ShapeDtypeStruct((2, quarter, model), BF16)
    return pl.pallas_call(
        mixer_fwd_body,
        in_specs=[SCALAR] + [WHOLE] * 11,
        out_shape=(
            piece, piece,
            jax.ShapeDtypeStruct((length, model), BF16),
            jax.ShapeDtypeStruct((length, width), BF16),
            row_f, row_f, row_f, row_f, spec_f, spec_f, spec_f, spec_f,
        ),
        scratch_shapes=[pltpu.VMEM((blocks, BLK, width), F32)] * 2
        + [pltpu.VMEM((length, width), F32)],
        compiler_params=pltpu.CompilerParams(vmem_limit_bytes=VMEM_LIMIT),
        cost_estimate=cost(14),
        name="mixer_forward",
    )(core, *pieces, w, *spectra, fwd, inv)


def correlate_tiles(width, blocks, left, other, result):
    left_re, left_im = left
    other_re, other_im = other
    to_re, to_im = result
    sign = sign_rows((8, width))

    def products(ft, fr, lanes):
        sgn = sign[:, lanes]
        k = [(other_re[m, fr, lanes], other_im[m, fr, lanes]) for m in range(blocks)]
        k = [(a,) + fix_first(ft, a, b) for a, b in k]
        g = [(left_re[m, fr, lanes], left_im[m, fr, lanes]) for m in range(blocks)]
        after = None
        for p in reversed(range(blocks)):
            wr = wi = None
            for m in range(p, blocks):
                gr, gi = g[m]
                kr, kr2, ki0 = k[m - p]
                a = gr * kr + gi * ki0
                b = gi * kr2 - gr * ki0
                wr = a if wr is None else wr + a
                wi = b if wi is None else wi + b
            if after is None:
                to_re[p, fr, lanes] = wr
                to_im[p, fr, lanes] = wi
            else:
                to_re[p, fr, lanes] = wr + sgn * after[0]
                to_im[p, fr, lanes] = wi + sgn * after[1]
            after = (wr, wi)

    conv_tiles(width, products)


def mixer_bwd_body(
    core_ref, a_ref, b_ref, c_ref, d_ref, w_ref, q_ref, v_ref, sh_ref, st_ref, sre_ref, sim_ref,
    kre_ref, kim_ref, tre_ref, tim_ref, fwd_ref, inv_ref,
    keep_ref, send_ref, g_ref, gp_ref, taps_ref, gre, gim,
    wre, wim, grad_mixed,
):
    length, width = q_ref.shape
    blocks = length // BLK
    sign = sign_rows((BLK, width))
    row0 = lax.broadcasted_iota(jnp.int32, (BLK, width), 0) == 0
    places = piece_rows(core_ref[0], a_ref.shape[0])
    wo = w_ref[:, 3 * width :]
    for piece_ref, place in zip((a_ref, b_ref, c_ref, d_ref), places):
        piece = piece_ref[...]
        g_ref[place] = piece
        grad_mixed[place] = dot(piece, wo)
    for p in range(blocks):
        rows = slice(p * BLK, (p + 1) * BLK)
        gm = grad_mixed[rows]
        gp_ref[rows, :width] = (gm * st_ref[rows]).astype(BF16)
        spec = to_spectrum(fwd_ref, gm * q_ref[rows])
        gre[p] = spec[:BLK]
        gim[p] = spec[BLK:]
    correlate_tiles(width, blocks, (gre, gim), (kre_ref, kim_ref), (wre, wim))
    tre = tre_ref[...]
    tim = tim_ref[...]
    tre2 = jnp.where(row0, tim, tre)
    tim0 = jnp.where(row0, 0.0, tim)
    after = None
    next_gs = None
    zero = jnp.zeros((BLK, width), F32)
    corr = [zero, zero, zero, zero]
    for p in reversed(range(blocks)):
        rows = slice(p * BLK, (p + 1) * BLK)
        grad_u = from_spectrum(inv_ref, jnp.concatenate([wre[p], wim[p]], axis=0))
        gp_ref[rows, 2 * width :] = (grad_u * sh_ref[rows]).astype(BF16)
        spec = to_spectrum(fwd_ref, grad_u * v_ref[rows])
        re, im = spec[:BLK], spec[BLK:]
        pr = re * tre + im * tim0
        pi = im * tre2 - re * tim0
        if after is None:
            z = jnp.concatenate([pr, pi], axis=0)
        else:
            z = jnp.concatenate([pr + sign * after[0], pi + sign * after[1]], axis=0)
        after = (pr, pi)
        gp_ref[rows, width : 2 * width] = from_spectrum(inv_ref, z).astype(BF16)
        sr, si = sre_ref[p], sim_ref[p]
        sr2 = jnp.where(row0, si, sr)
        si0 = jnp.where(row0, 0.0, si)
        corr[0] = corr[0] + (re * sr + im * si0)
        corr[1] = corr[1] + (im * sr2 - re * si0)
        if next_gs is not None:
            nr, ni = next_gs
            corr[2] = corr[2] + (nr * sr + ni * si0)
            corr[3] = corr[3] + (ni * sr2 - nr * si0)
        next_gs = (re, im)
    z = jnp.concatenate([corr[0] + sign * corr[2], corr[1] + sign * corr[3]], axis=0)
    taps_ref[...] = from_spectrum(inv_ref, z)[: taps_ref.shape[0]]
    wp = w_ref[:, : 3 * width]
    for i, place in enumerate(places):
        (keep_ref, send_ref)[i % 2][i // 2] = dot_nt(gp_ref[place], wp).astype(BF16)


def mixer_backward_kernel(core, pieces, w, saved, spectra, fwd, inv, taps):
    quarter, model = pieces[0].shape
    length = 4 * quarter
    width = w.shape[1] // 4
    blocks = length // BLK
    piece = jax.ShapeDtypeStruct((2, quarter, model), BF16)
    spec_f = jax.ShapeDtypeStruct((blocks, BLK, width), F32)
    return pl.pallas_call(
        mixer_bwd_body,
        in_specs=[SCALAR] + [WHOLE] * 17,
        out_shape=(
            piece, piece,
            jax.ShapeDtypeStruct((length, model), BF16),
            jax.ShapeDtypeStruct((length, 3 * width), BF16),
            jax.ShapeDtypeStruct((taps, width), F32),
            spec_f, spec_f,
        ),
        scratch_shapes=[pltpu.VMEM((blocks, BLK, width), F32)] * 2
        + [pltpu.VMEM((length, width), F32)],
        compiler_params=pltpu.CompilerParams(vmem_limit_bytes=VMEM_LIMIT),
        cost_estimate=cost(15),
        name="mixer_backward",
    )(core, *pieces, w, *saved, *spectra, fwd, inv)


def ssm_grad_body(
    gre, gim, ure, uim, decay_ref, coef_ref, inv_ref, gd_ref, gc_ref, vre, vim, dk_ref
):
    states, width = decay_ref.shape
    blocks = gre.shape[0]
    correlate_tiles(width, blocks, (gre, gim), (ure, uim), (vre, vim))
    for p in range(blocks):
        dk_ref[p * BLK : (p + 1) * BLK] = from_spectrum(
            inv_ref, jnp.concatenate([vre[p], vim[p]], axis=0)
        )
    group = 4
    for start, size in lane_tiles(width):
        lanes = slice(start, start + size)
        base = lax.broadcasted_iota(jnp.int32, (8, size), 0).astype(F32)

        def per_group(ng, _, lanes=lanes, size=size, base=base):
            rows = pl.ds(pl.multiple_of(ng * 8, 8), 8)
            rates = decay_ref[rows, lanes]
            row_ids = lax.broadcasted_iota(jnp.int32, (8, size), 0)
            sums_a = jnp.zeros((8, size), F32)
            sums_b = jnp.zeros((8, size), F32)
            for half in range(8 // group):
                d = [rates[half * group + i : half * group + i + 1] for i in range(group)]
                p = [jnp.broadcast_to(jnp.exp(-float(BLK) * x), (8, size)) for x in d]
                step8 = [jnp.broadcast_to(jnp.exp(-8.0 * x), (8, size)) for x in d]
                e0 = tuple(jnp.exp(-x * base) for x in d)
                zero = jnp.zeros((8, size), F32)

                def per_tile(jt, carry, p=p, step8=step8):
                    e, a, b = carry
                    steps = base + (jt * 8).astype(F32)
                    dk = [
                        dk_ref[pl.ds(pl.multiple_of(m * BLK + jt * 8, 8), 8), lanes]
                        for m in range(blocks)
                    ]
                    ne, na, nb = [], [], []
                    for i in range(group):
                        h = dk[blocks - 1]
                        s = None
                        for m in reversed(range(blocks - 1)):
                            s = h if s is None else s * p[i] + h
                            h = h * p[i] + dk[m]
                        eh = e[i] * h
                        na.append(a[i] + eh)
                        nb.append(b[i] + steps * eh + (float(BLK) * e[i]) * (s * p[i]))
                        ne.append(e[i] * step8[i])
                    return tuple(ne), tuple(na), tuple(nb)

                _, a, b = lax.fori_loop(
                    0, BLK // 8, per_tile, (e0, (zero,) * group, (zero,) * group)
                )
                for i in range(group):
                    here = row_ids == half * group + i
                    sums_a = jnp.where(here, jnp.sum(a[i], axis=0, keepdims=True), sums_a)
                    sums_b = jnp.where(here, jnp.sum(b[i], axis=0, keepdims=True), sums_b)
            root = jnp.sqrt(2.0 * rates)
            gc_ref[rows, lanes] = root * sums_a
            gd_ref[rows, lanes] = coef_ref[rows, lanes] * (sums_a / root - root * sums_b)
            return 0

        lax.fori_loop(0, states // 8, per_group, 0)


def ssm_grad_kernel(g_spectrum, u_spectrum, decay_t, coef_t, inv):
    states, width = decay_t.shape
    blocks = g_spectrum[0].shape[0]
    out = jax.ShapeDtypeStruct((states, width), F32)
    return pl.pallas_call(
        ssm_grad_body,
        out_shape=(out, out),
        scratch_shapes=[pltpu.VMEM((blocks, BLK, width), F32)] * 2
        + [pltpu.VMEM((blocks * BLK, width), F32)],
        compiler_params=pltpu.CompilerParams(vmem_limit_bytes=VMEM_LIMIT),
        cost_estimate=cost(19),
        name="ssm_grad",
    )(*g_spectrum, *u_spectrum, decay_t, coef_t, inv)


HEAD = 64
QROWS = 256


def dot_tn(a, b):
    return lax.dot_general(a, b, (((0,), (0,)), ((), ())), preferred_element_type=F32)


def allowed_keys(keys, first_query, queries, length):
    key = lax.broadcasted_iota(jnp.int32, (keys, queries), 0)
    query = lax.broadcasted_iota(jnp.int32, (keys, queries), 1) + first_query
    return (key <= query) & (key < length)


def attn_fwd_body(
    core_ref, len_ref, a_ref, b_ref, c_ref, d_ref, w_ref,
    keep_ref, send_ref, x_ref, q_ref, k_ref, v_ref, att_ref, lse_ref,
):
    rows, width = q_ref.shape
    places = piece_rows(core_ref[0], a_ref.shape[0])
    wq = w_ref[:, :width]
    wk = w_ref[:, width : 2 * width]
    wv = w_ref[:, 2 * width : 3 * width]
    for piece_ref, place in zip((a_ref, b_ref, c_ref, d_ref), places):
        piece = piece_ref[...]
        x_ref[place] = piece
        q_ref[place] = dot(piece, wq).astype(BF16)
        k_ref[place] = dot(piece, wk).astype(BF16)
        v_ref[place] = dot(piece, wv).astype(BF16)
    length = len_ref[0]
    lse_ref[...] = jnp.zeros(lse_ref.shape, F32)
    scale = HEAD**-0.5
    for h in range(width // HEAD):
        lanes = slice(h * HEAD, (h + 1) * HEAD)
        q = q_ref[:, lanes] * jnp.asarray(scale, BF16)
        k = k_ref[:, lanes]
        vt = v_ref[:, lanes].T
        for first in range(0, rows, QROWS):
            n = first + QROWS
            s = dot_nt(k[:n], q[first:n])
            s = jnp.where(allowed_keys(n, first, QROWS, length), s, -jnp.inf)
            top = jnp.max(s, axis=0, keepdims=True)
            e = jnp.exp(s - top)
            total = jnp.sum(e, axis=0, keepdims=True)
            probs = (e * (1.0 / total)).astype(BF16)
            att_ref[lanes, first:n] = dot(vt[:, :n], probs).astype(BF16)
            lse_ref[h : h + 1, first:n] = top + jnp.log(total)
    wo = w_ref[:, 3 * width :]
    out = lax.dot_general(
        att_ref[...], wo, (((0,), (1,)), ((), ())), preferred_element_type=F32
    ).astype(BF16)
    quarter = a_ref.shape[0]
    first = core_ref[0] == 0
    for half in range(2):
        low = out[2 * half * quarter : (2 * half + 1) * quarter]
        high = out[(2 * half + 1) * quarter : (2 * half + 2) * quarter]
        keep_ref[half] = jnp.where(first, low, high)
        send_ref[half] = jnp.where(first, high, low)


def attn_forward_kernel(core, length, pieces, w):
    quarter, model = pieces[0].shape
    rows = 4 * quarter
    width = w.shape[1] // 4
    row_b = jax.ShapeDtypeStruct((rows, width), BF16)
    piece = jax.ShapeDtypeStruct((2, quarter, model), BF16)
    return pl.pallas_call(
        attn_fwd_body,
        in_specs=[SCALAR, SCALAR] + [WHOLE] * 5,
        out_shape=(
            piece, piece,
            jax.ShapeDtypeStruct((rows, model), BF16),
            row_b, row_b, row_b,
            jax.ShapeDtypeStruct((width, rows), BF16),
            jax.ShapeDtypeStruct((8, rows), F32),
        ),
        compiler_params=pltpu.CompilerParams(vmem_limit_bytes=VMEM_LIMIT),
        cost_estimate=cost(12),
        name="attn_forward",
    )(core, length, *pieces, w)


def attn_bwd_body(
    core_ref, len_ref, a_ref, b_ref, c_ref, d_ref, w_ref, q_ref, k_ref, v_ref, lse_ref,
    keep_ref, send_ref, g_ref, gp_ref, ga, gqt, acck, accv
):
    rows, width = q_ref.shape
    places = piece_rows(core_ref[0], a_ref.shape[0])
    wo = w_ref[:, 3 * width :]
    for piece_ref, place in zip((a_ref, b_ref, c_ref, d_ref), places):
        piece = piece_ref[...]
        g_ref[place] = piece
        ga[place] = dot(piece, wo).astype(BF16)
    length = len_ref[0]
    scale = HEAD**-0.5
    acck[...] = jnp.zeros(acck.shape, F32)
    accv[...] = jnp.zeros(accv.shape, F32)
    for h in range(width // HEAD):
        lanes = slice(h * HEAD, (h + 1) * HEAD)
        q = q_ref[:, lanes] * jnp.asarray(scale, BF16)
        k = k_ref[:, lanes]
        kt = k.T
        v = v_ref[:, lanes]
        g = ga[:, lanes]
        for first in range(0, rows, QROWS):
            n = first + QROWS
            s = dot_nt(k[:n], q[first:n])
            probs = jnp.where(
                allowed_keys(n, first, QROWS, length), jnp.exp(s - lse_ref[h : h + 1, first:n]), 0.0
            )
            gp = dot_nt(v[:n], g[first:n])
            inner = jnp.sum(probs * gp, axis=0, keepdims=True)
            gs = (probs * (gp - inner)).astype(BF16)
            gqt[lanes, first:n] = dot(kt[:, :n], gs) * scale
            acck[h, :n] += dot(gs, q[first:n])
            accv[h, :n] += dot(probs.astype(BF16), g[first:n])
        gp_ref[:, width + h * HEAD : width + (h + 1) * HEAD] = acck[h].astype(BF16)
        gp_ref[:, 2 * width + h * HEAD : 2 * width + (h + 1) * HEAD] = accv[h].astype(BF16)
    gp_ref[:, :width] = gqt[...].T.astype(BF16)
    wp = w_ref[:, : 3 * width]
    for i, place in enumerate(places):
        (keep_ref, send_ref)[i % 2][i // 2] = dot_nt(gp_ref[place], wp).astype(BF16)


def attn_backward_kernel(core, length, pieces, w, q, k, v, lse):
    quarter, model = pieces[0].shape
    rows, width = q.shape
    piece = jax.ShapeDtypeStruct((2, quarter, model), BF16)
    heads = width // HEAD
    return pl.pallas_call(
        attn_bwd_body,
        in_specs=[SCALAR, SCALAR] + [WHOLE] * 9,
        out_shape=(
            piece, piece,
            jax.ShapeDtypeStruct((rows, model), BF16),
            jax.ShapeDtypeStruct((rows, 3 * width), BF16),
        ),
        scratch_shapes=[
            pltpu.VMEM((rows, width), BF16),
            pltpu.VMEM((width, rows), F32),
            pltpu.VMEM((heads, rows, HEAD), F32),
            pltpu.VMEM((heads, rows, HEAD), F32),
        ],
        compiler_params=pltpu.CompilerParams(vmem_limit_bytes=VMEM_LIMIT),
        cost_estimate=cost(14),
        name="attn_backward",
    )(core, length, *pieces, w, q, k, v, lse)


EPSILON = 1e-05


def kernel_call(body, outs, name, us, scalars=0, scratch=()):
    def call(*args):
        return pl.pallas_call(
            body,
            in_specs=[SCALAR] * scalars + [WHOLE] * (len(args) - scalars),
            out_shape=outs,
            scratch_shapes=list(scratch),
            cost_estimate=cost(us),
            compiler_params=pltpu.CompilerParams(vmem_limit_bytes=VMEM_LIMIT),
            name=name,
        )(*args)

    return call


def shaped(shape, dtype):
    return jax.ShapeDtypeStruct(shape, dtype)


def statistics(h):
    average = jnp.mean(h, axis=1, keepdims=True)
    centred = h - average
    inverse = lax.rsqrt(jnp.mean(centred * centred, axis=1, keepdims=True) + EPSILON)
    return centred * inverse, inverse


def norm_gradient(grad_normed, h, gain):
    unit, inverse = statistics(h)
    scaled = grad_normed * gain
    first_mean = jnp.mean(scaled, axis=1, keepdims=True)
    second_mean = jnp.mean(scaled * unit, axis=1, keepdims=True)
    return inverse * (scaled - first_mean - unit * second_mean)


def first_norm_body(chip_ref, mine_ref, other_ref, gain_ref, h0_ref, n0_ref, h1_ref, n1_ref):
    mine = mine_ref[...].astype(F32)
    other = other_ref[...].astype(F32)
    first = chip_ref[0] == 0
    for h, h_ref, n_ref in (
        (jnp.where(first, mine, other), h0_ref, n0_ref),
        (jnp.where(first, other, mine), h1_ref, n1_ref),
    ):
        h_ref[...] = h
        unit, _ = statistics(h)
        n_ref[...] = (unit * gain_ref[...]).astype(BF16)


def first_norm(chip, mine, other, gain):
    state, normed = shaped(mine.shape, F32), shaped(mine.shape, BF16)
    outs = (state, normed, state, normed)
    return kernel_call(first_norm_body, outs, "first_norm", 2.5, 1)(chip, mine, other, gain)


def both(pair_ref, received_ref):
    return pair_ref[...].astype(F32) + received_ref[...].astype(F32)


def norm_body(h_ref, pair_ref, received_ref, gain_ref, state_ref, normed_ref):
    h = h_ref[...] + both(pair_ref, received_ref)
    state_ref[...] = h
    unit, _ = statistics(h)
    normed_ref[...] = (unit * gain_ref[...]).astype(BF16)


def norm_step(h, pair, received, gain):
    outs = (shaped(h.shape, F32), shaped(h.shape, BF16))
    return kernel_call(norm_body, outs, "norm_step", 1.5)(h, pair, received, gain)


def back_body(g_ref, pair_ref, received_ref, h_ref, gain_ref, grad_ref, low_ref):
    grad = g_ref[...].astype(F32) + norm_gradient(
        both(pair_ref, received_ref), h_ref[...], gain_ref[...]
    )
    grad_ref[...] = grad
    low_ref[...] = grad.astype(BF16)


def back_step(g, pair, received, h, gain):
    outs = (shaped(g.shape, F32), shaped(g.shape, BF16))
    return kernel_call(back_body, outs, "back_step", 2)(g, pair, received, h, gain)


def last_back_body(chip_ref, g0, p0, h0, g1, p1, h1, received_ref, gain_ref, out_ref):
    first = chip_ref[0] == 0
    grad_normed = jnp.where(first, p0[...], p1[...]).astype(F32) + received_ref[...].astype(F32)
    h = jnp.where(first, h0[...], h1[...])
    grad = jnp.where(first, g0[...], g1[...])
    out_ref[...] = (grad + norm_gradient(grad_normed, h, gain_ref[...])).astype(BF16)


def last_back(chip, grads, pairs, states, received, gain):
    outs = shaped(received.shape, BF16)
    return kernel_call(last_back_body, outs, "last_back", 2, 1)(
        chip, grads[0], pairs[0], states[0], grads[1], pairs[1], states[1], received, gain
    )


ROOT = 0.7978845608028654
CUBIC = 0.044715


def gelu(u):
    return 0.5 * u * (1.0 + jnp.tanh(ROOT * (u + CUBIC * u * u * u)))


def gelu_parts(u):
    square = u * u
    t = jnp.tanh(ROOT * (u + CUBIC * u * square))
    half = 0.5 * (1.0 + t)
    slope = half + 0.5 * u * (1.0 - t * t) * (ROOT * (1.0 + 3.0 * CUBIC * square))
    return u * half, slope


def ffn_fwd_body(
    h_ref, pair_ref, received_ref, gain_ref, own_ref, mate_ref, state_ref, n_ref, hidden_ref, out_ref
):
    units = own_ref.shape[1] // 2
    h = h_ref[...] + both(pair_ref, received_ref)
    state_ref[...] = h
    unit, _ = statistics(h)
    n = (unit * gain_ref[...]).astype(BF16)
    n_ref[...] = n
    out = None
    for side, w_ref in enumerate((own_ref, mate_ref)):
        hidden = dot(n, w_ref[:, :units])
        hidden_ref[:, side * units : (side + 1) * units] = hidden
        part = dot_nt(gelu(hidden).astype(BF16), w_ref[:, units:])
        out = part if out is None else out + part
    out_ref[...] = out.astype(BF16)


def ffn_forward(h, pair, received, gain, own, mate):
    piece = shaped(h.shape, BF16)
    outs = (shaped(h.shape, F32), piece, shaped((h.shape[0], own.shape[1]), F32), piece)
    return kernel_call(ffn_fwd_body, outs, "ffn_forward", 5)(h, pair, received, gain, own, mate)


def ffn_both_body(
    h_ref, pair_ref, received_ref, gain_ref, g_ref, own_ref, mate_ref,
    state_ref, n_ref, grad_ref, active_ref, out_ref,
):
    units = own_ref.shape[1] // 2
    h = h_ref[...] + both(pair_ref, received_ref)
    state_ref[...] = h
    unit, _ = statistics(h)
    n = (unit * gain_ref[...]).astype(BF16)
    n_ref[...] = n
    g = g_ref[...]
    out = None
    for side, w_ref in enumerate((own_ref, mate_ref)):
        lanes = slice(side * units, (side + 1) * units)
        active, slope = gelu_parts(dot(n, w_ref[:, :units]))
        active_ref[:, lanes] = active.astype(BF16)
        grad = (dot(g, w_ref[:, units:]) * slope).astype(BF16)
        grad_ref[:, lanes] = grad
        part = dot_nt(grad, w_ref[:, :units])
        out = part if out is None else out + part
    out_ref[...] = out.astype(BF16)


def ffn_both(h, pair, received, gain, g, own, mate):
    piece = shaped(h.shape, BF16)
    rows = shaped((h.shape[0], own.shape[1]), BF16)
    outs = (shaped(h.shape, F32), piece, rows, rows, piece)
    return kernel_call(ffn_both_body, outs, "ffn_both", 6)(h, pair, received, gain, g, own, mate)


def ffn_bwd_body(
    g_ref, pair_ref, received_ref, h_ref, gain_ref, hidden_ref, own_ref, mate_ref,
    total_ref, low_ref, grad_ref, active_ref, out_ref,
):
    units = own_ref.shape[1] // 2
    total = g_ref[...] + norm_gradient(both(pair_ref, received_ref), h_ref[...], gain_ref[...])
    total_ref[...] = total
    g = total.astype(BF16)
    low_ref[...] = g
    out = None
    for side, w_ref in enumerate((own_ref, mate_ref)):
        lanes = slice(side * units, (side + 1) * units)
        active, slope = gelu_parts(hidden_ref[:, lanes])
        active_ref[:, lanes] = active.astype(BF16)
        grad = (dot(g, w_ref[:, units:]) * slope).astype(BF16)
        grad_ref[:, lanes] = grad
        part = dot_nt(grad, w_ref[:, :units])
        out = part if out is None else out + part
    out_ref[...] = out.astype(BF16)


def ffn_backward(g, pair, received, h, gain, hidden, own, mate):
    piece = shaped(h.shape, BF16)
    rows = shaped(hidden.shape, BF16)
    outs = (shaped(h.shape, F32), piece, rows, rows, piece)
    return kernel_call(ffn_bwd_body, outs, "ffn_backward", 6)(
        g, pair, received, h, gain, hidden, own, mate
    )


def ffn_out_body(a0_ref, a1_ref, own_ref, mate_ref, out0_ref, out1_ref):
    units = own_ref.shape[1] // 2
    for a_ref, out_ref in ((a0_ref, out0_ref), (a1_ref, out1_ref)):
        out = dot_nt(a_ref[:, :units], own_ref[:, units:]) + dot_nt(
            a_ref[:, units:], mate_ref[:, units:]
        )
        out_ref[...] = out.astype(BF16)


def ffn_out(active0, active1, own, mate):
    piece = shaped((active0.shape[0], own.shape[0]), BF16)
    return kernel_call(ffn_out_body, (piece, piece), "ffn_out", 3)(active0, active1, own, mate)


def ffn_grads_body(n0, n1, g0, g1, gh0, gh1, a0, a1, own_ref, mate_ref):
    units = own_ref.shape[1] // 2
    for side, out_ref in ((1, mate_ref), (0, own_ref)):
        lanes = slice(side * units, (side + 1) * units)
        out_ref[:, :units] = (
            dot_tn(n0[...], gh0[:, lanes]) + dot_tn(n1[...], gh1[:, lanes])
        ).astype(BF16)
        out_ref[:, units:] = (
            dot_tn(g0[...], a0[:, lanes]) + dot_tn(g1[...], a1[:, lanes])
        ).astype(BF16)


def ffn_grads(n, g, grad_hidden, active):
    outs = shaped((n[0].shape[1], active[0].shape[1]), BF16)
    return kernel_call(ffn_grads_body, (outs, outs), "ffn_grads", 6)(
        *n, *g, *grad_hidden, *active
    )


def attn_grads_body(x_ref, gp_ref, g_ref, att_ref, own_ref, mate_ref, out_ref):
    first = own_ref.shape[1]
    joined = first + gp_ref.shape[1]
    out_ref[:, :first] = (own_ref[...].astype(F32) + mate_ref[...].astype(F32)).astype(BF16)
    out_ref[:, first:joined] = dot_tn(x_ref[...], gp_ref[...]).astype(BF16)
    out_ref[:, joined:] = lax.dot_general(
        g_ref[...], att_ref[...], (((0,), (1,)), ((), ())), preferred_element_type=F32
    ).astype(BF16)


def attn_grads(x, joined, g, attended_t, own, mate):
    columns = own.shape[1] + joined.shape[1] + attended_t.shape[0]
    outs = shaped((x.shape[1], columns), BF16)
    return kernel_call(attn_grads_body, outs, "attn_grads", 8)(
        x, joined, g, attended_t, own, mate
    )


def halved(side, count, bit, rows_of, keep_ref, send_ref):
    block = keep_ref.shape[0] * 2 // count
    place = 0
    for j in range(count):
        if j & bit:
            continue
        low, high = rows_of(j * block, block), rows_of((j | bit) * block, block)
        here = slice(place, place + block)
        keep_ref[here] = jnp.where(side == 0, low, high).astype(BF16)
        send_ref[here] = jnp.where(side == 0, high, low).astype(BF16)
        place += block


def halves_of(rows, columns):
    return (shaped((rows // 2, columns), BF16),) * 2


def ffn_cut(side, own, mate, count, bit):
    def body(side_ref, own_ref, mate_ref, keep_ref, send_ref):
        def rows_of(first, size):
            here = slice(first, first + size)
            return own_ref[here].astype(F32) + mate_ref[here].astype(F32)

        halved(side_ref[0], count, bit, rows_of, keep_ref, send_ref)

    return kernel_call(body, halves_of(*own.shape), "ffn_cut", 3, 1)(side, own, mate)


def mixer_grads(side, x, joined, g, mixed, count, bit):
    model, columns = x.shape[1], joined.shape[1] + mixed.shape[1]

    def body(side_ref, x_ref, gp_ref, g_ref, mixed_ref, keep_ref, send_ref, total):
        total[:, : gp_ref.shape[1]] = dot_tn(x_ref[...], gp_ref[...])
        total[:, gp_ref.shape[1] :] = dot_tn(g_ref[...], mixed_ref[...])
        halved(
            side_ref[0], count, bit, lambda first, size: total[first : first + size], keep_ref, send_ref
        )

    return kernel_call(
        body, halves_of(model, columns), "mixer_grads", 6, 1, [pltpu.VMEM((model, columns), F32)]
    )(side, x, joined, g, mixed)


TENSOR = "tensor"
DATA = "dp"


def swap(x, bit):
    return lax.ppermute(x, TENSOR, [(i, i ^ bit) for i in range(4)])


def from_mate(x):
    return swap(x, 1)


def from_chip(x):
    return swap(x, 2)


def tie(*values):
    return lax.optimization_barrier(values)


def after(value, *others):
    return lax.optimization_barrier((value,) + others)[0]


def row_major(x):
    return with_layout_constraint(x, Layout(major_to_minor=tuple(range(x.ndim))))


def add_cores(keep, send):
    return (keep.astype(F32) + from_mate(send).astype(F32)).astype(BF16)


class Rows:
    def __init__(self):
        self.count = lax.axis_size(DATA)
        self.index = lax.axis_index(DATA)
        self.depth = self.count.bit_length() - 1
        self.bits = [1 << i for i in reversed(range(self.depth))]

    def swap(self, x, bit):
        return lax.ppermute(x, DATA, [(i, i ^ bit) for i in range(self.count)])

    def gather_send(self, x, step):
        return self.swap(x, self.bits[step])

    def gather_merge(self, x, other, step):
        upper = (self.index & self.bits[step]) != 0
        return jnp.stack([jnp.where(upper, other, x), jnp.where(upper, x, other)], axis=step)

    def gather_step(self, x, step):
        return self.gather_merge(x, self.gather_send(x, step), step)

    def gather(self, x, first=0, last=None):
        for step in range(first, self.depth if last is None else last):
            x = self.gather_step(x, step)
        return x

    def flat(self, x):
        return x.reshape(self.count * x.shape[-2], x.shape[-1])

    def parts(self, x):
        return x.reshape((2,) * self.depth + (x.shape[0] // self.count, x.shape[1]))

    def cut(self, x, step):
        side = ((self.index & self.bits[step]) != 0).astype(jnp.int32)
        keep = lax.dynamic_slice_in_dim(x, side, 1, step)
        send = lax.dynamic_slice_in_dim(x, 1 - side, 1, step)
        return keep, send.astype(BF16)

    def side(self, step):
        return ((self.index & self.bits[step]) != 0).astype(jnp.int32).reshape(1)

    def without(self, x, step):
        shape = [2] * self.depth
        shape[step] = 1
        return x.reshape(tuple(shape) + (x.shape[0] * 2 // self.count, x.shape[1]))

    def scatter(self, x, steps):
        for step in steps:
            keep, send = self.cut(x, step)
            x = keep.astype(F32) + self.swap(send, self.bits[step]).astype(F32)
        return x.reshape(x.shape[-2:])


def on_device(
    tokens, cotangent, seq_lengths,
    gain_mixer, mixer_query, mixer_key, mixer_value, shift_taps, ssm_decay, ssm_coef, mixer_out,
    gain_ffn1, ffn1_up, ffn1_down,
    gain_attn, attn_query, attn_key, attn_value, attn_out,
    gain_ffn2, ffn2_up, ffn2_down,
):
    place = lax.axis_index(TENSOR)
    chip = place >> 1
    core = (place & 1).astype(jnp.int32).reshape(1)
    chips = chip.astype(jnp.int32).reshape(1)
    rows = Rows()
    fwd, inv = spectral_tables()
    quarter, model = tokens.shape
    length = 4 * quarter
    block, width = mixer_query.shape
    units = ffn1_up.shape[1]
    unit_rows = shift_taps.shape[0]
    states = unit_rows * rows.count

    own_gains = jnp.stack([gain_mixer, gain_ffn1, gain_attn, gain_ffn2], axis=0)
    small = jnp.zeros((16, model), BF16)
    small = small.at[:unit_rows, : 3 * width].set(
        jnp.concatenate([shift_taps, ssm_decay.T, ssm_coef.T], axis=1)
    )
    small = small.at[12:16, :block].set(own_gains)
    mixer_own = jnp.concatenate([mixer_query, mixer_key, mixer_value, mixer_out.T], axis=1)
    ffn1_own = jnp.concatenate([ffn1_up, ffn1_down.T], axis=1)
    attn_own = jnp.concatenate([attn_query, attn_key, attn_value, attn_out.T], axis=1)
    ffn2_own = jnp.concatenate([ffn2_up, ffn2_down.T], axis=1)
    top = rows.depth - 1
    positions = place * quarter + jnp.arange(quarter)
    live = (positions < seq_lengths[0])[:, None]
    masked = jnp.where(live, cotangent, jnp.zeros_like(cotangent))
    small = rows.gather(small, 0, 1)
    mixer_w = rows.gather(mixer_own, 0, 1)
    there = from_chip(tokens)
    first_w = lax.all_gather(
        jnp.concatenate([ffn1_own, attn_own], axis=1), DATA, axis=0, tiled=True
    )
    small = rows.gather(small, 1, top)
    mixer_w = rows.gather(mixer_w, 1, top)
    small = rows.gather(small, top).reshape(rows.count, 16, model)
    small, mixer_w = tie(small, mixer_w)
    mixer_other = rows.gather_send(mixer_w, top)

    gains = small[:, 12:16, :block].transpose(1, 0, 2).reshape(4, 1, model).astype(F32)
    vectors = small[:, :unit_rows, : 3 * width].reshape(states, 3 * width).astype(F32)
    taps_w, decay_t, coef_t = (vectors[:, i * width : (i + 1) * width] for i in range(3))
    h0, n0, h1, n1 = first_norm(chips, tokens, there, gains[0])
    start = [h0, h1]
    grad_other = from_chip(after(masked, n0))
    spectra = kernel_spectra(after(decay_t, n0), coef_t, taps_w, fwd, length)
    pieces = [n0, from_mate(n0), n1, from_mate(n1)]
    mixer_other, grad_other = after((mixer_other, grad_other), spectra[0])
    mixer_w = rows.flat(rows.gather_merge(mixer_w, mixer_other, top))
    keep, send, x1, mixed, *saved = mixer_forward_kernel(
        core, pieces, mixer_w, spectra, fwd, inv
    )

    def core_sums(keep, send):
        other = from_mate(send)
        return [(keep[i].astype(F32) + other[i].astype(F32)).astype(BF16) for i in range(2)]

    def exchanged(keep, send):
        sums = core_sums(keep, send)
        return sums, [from_chip(p) for p in sums]

    pairs, received = exchanged(keep, send)
    first_w = after(first_w, pairs[1])
    ffn1_w, attn_w = first_w[:, : 2 * units], first_w[:, 2 * units :]
    ffn1_mate = from_mate(ffn1_w)
    ffn2_w = lax.all_gather(after(ffn2_own, pairs[1]), DATA, axis=0, tiled=True)
    ffn1_mate = after(ffn1_mate, received[0])
    after_mixer, n2, hidden1, nexts, arrived = [], [], [], [], []
    for half in range(2):
        wait = received[0] if half == 0 else after(received[1], nexts[0])
        h, n, hidden, out = ffn_forward(
            start[half], pairs[half], wait, gains[1], ffn1_w, ffn1_mate
        )
        after_mixer.append(h)
        n2.append(n)
        hidden1.append(hidden)
        nexts.append(out)
        arrived.append(from_chip(out))
    after_ffn1, pieces = [], []
    for half in range(2):
        wait = after(arrived[half], nexts[1]) if half == 0 else after(arrived[1], pieces[0])
        h, n = norm_step(after_mixer[half], nexts[half], wait, gains[2])
        after_ffn1.append(h)
        pieces += [n, from_mate(n)]
    attn_w, pieces[2] = tie(attn_w, pieces[2])
    keep, send, x3, q2, k2, v2, attended_t, log_total = attn_forward_kernel(
        core, seq_lengths, pieces, attn_w
    )
    pairs, received = exchanged(keep, send)

    ffn2_w = after(ffn2_w, pairs[1])
    ffn2_mate = from_mate(ffn2_w)
    grad = [jnp.where(chip == 0, masked, grad_other), jnp.where(chip == 0, grad_other, masked)]
    g4 = list(grad)
    ffn2_mate = after(ffn2_mate, received[0])
    after_attn, n4, gh, act, nexts, arrived = [], [], [], [], [], []
    for half in range(2):
        wait = received[0] if half == 0 else after(received[1], nexts[0])
        h, n, grad_hidden, active, out = ffn_both(
            after_ffn1[half], pairs[half], wait, gains[3], g4[half], ffn2_w, ffn2_mate
        )
        after_attn.append(h)
        n4.append(n)
        gh.append(grad_hidden)
        act.append(active)
        nexts.append(out)
        arrived.append(from_chip(out))
    lows = []
    wait = after(arrived[0], nexts[1])
    grad[0], low = back_step(grad[0], nexts[0], wait, after_attn[0], gains[3])
    lows.append(low)
    gh, act = after((gh, act), low)
    own, mate = ffn_grads(n4, g4, gh, act)
    wait = after(arrived[1], mate)
    grad[1], low = back_step(grad[1], nexts[1], wait, after_attn[1], gains[3])
    lows.append(low)
    pieces = [lows[0], from_mate(after(lows[0], low)), lows[1], from_mate(lows[1])]
    ffn2_mate_g = from_mate(after(mate, pieces[1], pieces[3]))
    keep, send, g3, grad_joined = attn_backward_kernel(
        core, seq_lengths, pieces, attn_w, q2, k2, v2, log_total
    )
    pairs, received = exchanged(keep, send)
    own, ffn2_mate_g = after((own, ffn2_mate_g), pairs[1])
    second_p = attn_grads(x3, grad_joined, g3, attended_t, own, ffn2_mate_g)
    second_g = lax.psum_scatter(second_p, DATA, scatter_dimension=0, tiled=True)
    step = rows.depth - 1
    received[0] = after(received[0], second_p)
    final = ffn_out(*after(tuple(act), second_p), ffn2_w, ffn2_mate)
    final_sent = jnp.where(chip == 0, final[1], final[0])
    received[0], final_sent = tie(received[0], final_sent)

    g2, gh, act_b, nexts, arrived = [], [], [], [], []
    for half in range(2):
        wait = received[0] if half == 0 else after(received[1], nexts[0])
        grad[half], low, grad_hidden, active, out = ffn_backward(
            grad[half].astype(F32), pairs[half], wait, after_ffn1[half], gains[2], hidden1[half],
            ffn1_w, ffn1_mate,
        )
        g2.append(low)
        gh.append(grad_hidden)
        act_b.append(active)
        nexts.append(out)
        arrived.append(from_chip(out))
    lows = []
    wait = after(arrived[0], nexts[1])
    grad[0], low = back_step(grad[0], nexts[0], wait, after_mixer[0], gains[1])
    lows.append(low)
    gh, act_b = after((gh, act_b), low)
    own, mate = ffn_grads(n2, g2, gh, act_b)
    wait = after(arrived[1], mate)
    grad[1], low = back_step(grad[1], nexts[1], wait, after_mixer[1], gains[1])
    lows.append(low)
    final_sent = after(final_sent, low)
    mate_g = from_mate(after(mate, low))
    pieces = [lows[0], from_mate(lows[0]), lows[1], from_mate(lows[1])]
    mate_g, pieces[1], pieces[3] = tie(mate_g, pieces[1], pieces[3])
    ffn1_keep, ffn1_send = ffn_cut(rows.side(step), own, mate_g, rows.count, rows.bits[step])
    pieces[0], ffn1_send, final_sent = tie(pieces[0], ffn1_send, final_sent)
    ffn1_received = rows.swap(ffn1_send, rows.bits[step])
    final_received = from_chip(final_sent)
    keep, send, g1, grad_joined, grad_taps, *g_spectrum = mixer_backward_kernel(
        core, pieces, mixer_w, saved[:6], spectra, fwd, inv, states
    )
    final_received = after(final_received, keep)
    mixer_keep, mixer_send = mixer_grads(
        rows.side(step - 1), x1, grad_joined, g1, mixed, rows.count, rows.bits[step - 1]
    )
    mixer_received = rows.swap(mixer_send, rows.bits[step - 1])
    g_spectrum = after(tuple(g_spectrum), mixer_send, second_g)
    grad_decay, grad_coef = ssm_grad_kernel(g_spectrum, saved[6:], decay_t, coef_t, inv)
    ffn1_received, send = after((ffn1_received, send), grad_decay)
    last = core_sums(keep, send)
    last_sent = jnp.where(chip == 0, last[1], last[0])
    last_received = from_chip(last_sent)
    ffn1_g = rows.without(ffn1_keep.astype(F32) + ffn1_received.astype(F32), step)
    ffn1_keep, ffn1_send = rows.cut(ffn1_g, step - 1)
    ffn1_received = rows.swap(ffn1_send, rows.bits[step - 1])
    mixer_received = after(mixer_received, ffn1_send)
    mixer_g = rows.without(mixer_keep.astype(F32) + mixer_received.astype(F32), step - 1)
    small_g = rows.parts(jnp.concatenate([grad_taps, grad_decay, grad_coef], axis=1))
    mixer_g, small_g, last_received = tie(mixer_g, small_g, last_received)
    rest = list(reversed(range(step - 1)))
    mixer_g = rows.scatter(mixer_g, [step] + rest)
    small_g = rows.scatter(small_g, [step, step - 1] + rest)
    ffn1_g = rows.scatter(ffn1_keep.astype(F32) + ffn1_received.astype(F32), rest)
    output = jnp.where(chip == 0, after_attn[0], after_attn[1]) + (
        jnp.where(chip == 0, final[0], final[1]).astype(F32) + final_received.astype(F32)
    )
    second_g = second_g.astype(F32)
    ffn2_g, attn_g = second_g[:, : 2 * units], second_g[:, 2 * units :]
    input_grad = last_back(chips, grad, last, start, last_received, gains[0])

    def gain_sum(grads, weights, gain):
        products = sum(g * w.astype(F32) for g, w in zip(grads, weights))
        return jnp.sum(products, axis=1) / gain.astype(F32)

    def cut(grads, size):
        return [grads[:, i : i + size] for i in range(0, grads.shape[1], size)]

    mq, mk, mv, mo = cut(mixer_g, width)
    aq, ak, av, ao = cut(attn_g, width)
    u1, d1 = cut(ffn1_g, units)
    u2, d2 = cut(ffn2_g, units)
    gt, gd, gc = cut(small_g, width)
    gain_grads = jnp.stack(
        [
            gain_sum((mq, mk, mv), (mixer_query, mixer_key, mixer_value), gain_mixer),
            gain_sum((u1,), (ffn1_up,), gain_ffn1),
            gain_sum((aq, ak, av), (attn_query, attn_key, attn_value), gain_attn),
            gain_sum((u2,), (ffn2_up,), gain_ffn2),
        ]
    )
    gain_grads = gain_grads + swap(gain_grads, 1)
    gain_grads = gain_grads + swap(gain_grads, 2)
    return (
        output.astype(BF16), input_grad,
        gain_grads[0], mq, mk, mv, gt, gd.T, gc.T, mo.T,
        gain_grads[1], u1, d1.T,
        gain_grads[2], aq, ak, av, ao.T,
        gain_grads[3], u2, d2.T,
    )


def solution(mesh):
    rows = P(("dp", "tensor"), None)
    up = P("dp", "tensor")
    down = P("tensor", "dp")
    vector = P("dp")
    mixer = (vector, up, up, up, up, down, down, down)
    ffn = (vector, up, down)
    attn = (vector, up, up, up, down)
    weights = mixer + ffn + attn + ffn
    return jax.shard_map(
        on_device,
        mesh=mesh,
        in_specs=(rows, rows, vector) + weights,
        out_specs=(rows, rows) + weights,
        check_vma=False,
    )
```

time: 704 us -> 423 us (0.60)
  waiting for transfers between devices: 363 us -> 118 us
  Pallas kernels: 82 us -> 184 us
  blocking collectives: 57.1 us -> 0 us
  matrix products: 38.4 us -> 0 us
  local copies, waits for them, and re-layouts: 70 us -> 34.9 us
  other arithmetic: 50 us -> 20.1 us
  starting transfers between devices: 17.8 us -> 41.9 us
    unnamed x14 -> x3, waiting for transfers between devices: 184 us -> 0.05 us
    pallas_call x5 -> x25, Pallas kernels: 70.5 us -> 173 us  [the longest x20 98.5 us: call(): pl.pallas_call(body, in_specs=[SCALAR] * scalars + [WHOLE] * (len(args) -...]
    ppermute x26 -> x34, waiting for transfers between devices: 121 us -> 54.2 us  [swap(): return lax.ppermute(x, TENSOR, [(i, i ^ bit) for i in range(4)])]
    ppermute x0 -> x15, waiting for transfers between devices: none -> 63.6 us  [swap(): return lax.ppermute(x, DATA, [(i, i ^ bit) for i in range(self.count)])]
    all_gather x4 -> x2, waiting for transfers between devices: 58 us -> 0.05 us  [the longest x1 0.02 us: on_device(): lax.all_gather(jnp.concatenate([ffn1_own, attn_own], axis=1), DATA, axis=...]
    all_gather x2 -> x0, blocking collectives: 51.4 us -> none  [the longest x1 30.6 us: gather_rows(): return lax.all_gather(x, DATA, axis=0, tiled=True)]
    dot_general x19 -> x0, matrix products: 38.4 us -> none  [the longest x10 13.1 us: rows_dot(): lax.dot_general(left, right, (((0,), (0,)), ((), ())), preferred_element_...]
    unnamed x216 -> x133, local copies, waits for them, and re-layouts: 50.5 us -> 20.3 us
  transfers between devices with their start and end apart: 35 -> 52, of which waited for: 24 -> 26; matrix products, arithmetic and copies ran while one was open for 16% -> 9% of each run, Pallas kernels for 6% -> 42%
where the time goes in v3:
time: 423 us; the launch traced here: 415 us
  Pallas kernels  184 us (43%)
  waiting for transfers between devices  118 us (28%)
  starting transfers between devices  41.9 us (10%)
  local copies, waits for them, and re-layouts  34.9 us (8%)
  other arithmetic  20.1 us (5%)
  between operations  15.9 us (4%)
    pallas_call x20, Pallas kernels, call(): pl.pallas_call(body, in_specs=[SCALAR] * scalars + [WHOLE] * (len(args) -...  98.5 us
    ppermute x15, waiting for transfers between devices, swap(): return lax.ppermute(x, DATA, [(i, i ^ bit) for i in range(self.count)])  63.6 us
    ppermute x34, waiting for transfers between devices, swap(): return lax.ppermute(x, TENSOR, [(i, i ^ bit) for i in range(4)])  54.2 us
    ppermute x15, starting transfers between devices, swap(): return lax.ppermute(x, DATA, [(i, i ^ bit) for i in range(self.count)])  21.7 us
    unnamed x133, local copies, waits for them, and re-layouts  20.3 us
    ppermute x34, starting transfers between devices, swap(): return lax.ppermute(x, TENSOR, [(i, i ^ bit) for i in range(4)])  19.8 us
    pallas_call x1, Pallas kernels, ssm_grad_kernel(): pl.pallas_call(ssm_grad_body, out_shape=(out, out), scratch_shapes=[pltpu...  19.1 us
    pallas_call x1, Pallas kernels, mixer_backward_kernel(): pl.pallas_call(mixer_bwd_body, in_specs=[SCALAR] + [WHOLE] * 17, out_shap...  15 us
  transfers between devices with their start and end apart: 52, of which 26 were waited for; matrix products, arithmetic and copies ran while one was open for 9% of the time, Pallas kernels for 42%

profile of v3, /device:TPU:0, one launch (start us, length us, event | category | flops | bytes accessed | tf_op | source)
XLA Modules:
  0.0 415.0 jit_solution(9424110911553568357)
XLA Ops:
  32.7 14.3 %collective-permute-done.5 = bf16[2,96,768]{2,1,0:T(8,128)(2,1)S(1)} collective-permute-done((bf16[2,96,768]{2,1,0:T(8,128)(2,1)S(1)}, bf16[2,96,768]{2,1,0:T(8,128)(2,1)S(1)}, u32[]{:S(2)}, u32[]{:S(2)}) %collective-permute-start.5) | collective-permute-done | bytes 294944 | tf_op jit(solution)/shard_map/ppermute | solution.py:962
  54.4 11.5 %kernel_spectra.1 = (f32[8,128,192]{2,1,0:T(8,128)}, f32[8,128,192]{2,1,0:T(8,128)}, f32[128,192]{1,0:T(8,128)}, f32[128,192]{1,0:T(8,128)}) custom-call(f32[64,192]{1,0:T(8,128)} %get-tuple-element.198.decay_ref, f32[64,192]{1,0:T(8,128)} %get-tuple-element.440.coef_ref, f32[64,192]{1,0:T(8,128)} %get-tuple-element.439.taps_ref, ...), custom_call_target="tpu_custom_call" | custom-call | flops 1210000000 | bytes 3850000 | tf_op jit(solution)/shard_map/kernel_spectra/pallas_call | solution.py:136
  65.9 6.2 %collective-permute-done.8 = bf16[2,2,96,768]{3,2,1,0:T(8,128)(2,1)S(1)} collective-permute-done((bf16[2,2,96,768]{3,2,1,0:T(8,128)(2,1)S(1)}, bf16[2,2,96,768]{3,2,1,0:T(8,128)(2,1)S(1)}, u32[]{:S(2)}, u32[]{:S(2)}) %collective-permute-start.8) | collective-permute-done | bytes 589856 | tf_op jit(solution)/shard_map/ppermute | solution.py:962
  74.4 14.1 %mixer_forward.1 = (bf16[2,256,768]{2,1,0:T(8,128)(2,1)}, bf16[2,256,768]{2,1,0:T(8,128)(2,1)}, bf16[1024,768]{1,0:T(8,128)(2,1)}, bf16[1024,192]{1,0:T(8,128)(2...) custom-call(s32[1]{0:T(128)} %bitcast.23.core_ref, ...), custom_call_target="tpu_custom_call" | custom-call | flops 1540000000 | bytes 4900000 | tf_op jit(solution)/shard_map/mixer_forward/pallas_call | solution.py:264
  98.8 9.3 %collective-permute-done.11.received_ref = bf16[256,768]{1,0:T(8,128)(2,1)} collective-permute-done((bf16[256,768]{1,0:T(8,128)(2,1)S(1)}, bf16[256,768]{1,0:T(8,128)(2,1)}, u32[]{:S(2)}, u32[]{:S(2)}) %collective-permute-start.11) | collective-permute-done | bytes 393248 | tf_op jit(solution)/shard_map/ppermute | solution.py:927
  108.1 5.7 %ffn_forward.2 = (f32[256,768]{1,0:T(8,128)}, bf16[256,768]{1,0:T(8,128)(2,1)}, f32[256,1536]{1,0:T(8,128)}, bf16[256,768]{1,0:T(8,128)(2,1)}) custom-call(f32[256,768]{1,0:T(8,128)} %get-tuple-element.193.h_ref.h0, bf16[256,768]{1,0:T(8,128)(2,1)} %copy-done.10, bf16[256,768]{1,0:T(8,128)(2,1)} %collective-permute-done.11.received_ref, ...), custom_call_target="tpu_custom_call" | custom-call | flops 550000000 | bytes 1750000 | tf_op jit(solution)/shard_map/ffn_forward/pallas_call | solution.py:633
  116.2 5.6 %ffn_forward.3 = (f32[256,768]{1,0:T(8,128)}, bf16[256,768]{1,0:T(8,128)(2,1)}, f32[256,1536]{1,0:T(8,128)}, bf16[256,768]{1,0:T(8,128)(2,1)}) custom-call(f32[256,768]{1,0:T(8,128)} %get-tuple-element.210.h_ref.h1, bf16[256,768]{1,0:T(8,128)(2,1)} %copy-done.9, bf16[256,768]{1,0:T(8,128)(2,1)} %collective-permute-done.14.received_ref, ...), custom_call_target="tpu_custom_call" | custom-call | flops 550000000 | bytes 1750000 | tf_op jit(solution)/shard_map/ffn_forward/pallas_call | solution.py:633
  140.1 11.5 %attn_forward.1 = (bf16[2,256,768]{2,1,0:T(8,128)(2,1)}, bf16[2,256,768]{2,1,0:T(8,128)(2,1)}, bf16[1024,768]{1,0:T(8,128)(2,1)}, bf16[1024,192]{1,0:T(8,128)(2,...) custom-call(s32[1]{0:T(128)} %bitcast.23.core_ref, ...), custom_call_target="tpu_custom_call" | custom-call | flops 1320000000 | bytes 4200000 | tf_op jit(solution)/shard_map/attn_forward/pallas_call | solution.py:545
  161.1 6.9 %collective-permute-done.19.received_ref = bf16[256,768]{1,0:T(8,128)(2,1)} collective-permute-done((bf16[256,768]{1,0:T(8,128)(2,1)S(1)}, bf16[256,768]{1,0:T(8,128)(2,1)}, u32[]{:S(2)}, u32[]{:S(2)}) %collective-permute-start.19) | collective-permute-done | bytes 393248 | tf_op jit(solution)/shard_map/ppermute | solution.py:927
  169.5 6.4 %ffn_both.2 = (f32[256,768]{1,0:T(8,128)}, bf16[256,768]{1,0:T(8,128)(2,1)}, bf16[256,1536]{1,0:T(8,128)(2,1)}, bf16[256,1536]{1,0:T(8,128)(2,1)}, bf16[256,768]{1,0:T(8,128)(2,1)}) custom-call(f32[256,768]{1,0:T(8,128)} %get-tuple-element.214.h_ref, bf16[256,768]{1,0:T(8,128)(2,1)} %copy-done.15, bf16[256,768]{1,0:T(8,128)(2,1)} %collective-permute-done.19.received_ref, ...), custom_call_target="tpu_custom_call" | custom-call | flops 660000000 | bytes 2100000 | tf_op jit(solution)/shard_map/ffn_both/pallas_call | solution.py:633
  176.4 6.4 %ffn_both.3 = (f32[256,768]{1,0:T(8,128)}, bf16[256,768]{1,0:T(8,128)(2,1)}, bf16[256,1536]{1,0:T(8,128)(2,1)}, bf16[256,1536]{1,0:T(8,128)(2,1)}, bf16[256,768]{1,0:T(8,128)(2,1)}) custom-call(f32[256,768]{1,0:T(8,128)} %get-tuple-element.228.h_ref, bf16[256,768]{1,0:T(8,128)(2,1)} %copy-done.14, bf16[256,768]{1,0:T(8,128)(2,1)} %collective-permute-done.21.received_ref, ...), custom_call_target="tpu_custom_call" | custom-call | flops 660000000 | bytes 2100000 | tf_op jit(solution)/shard_map/ffn_both/pallas_call | solution.py:633
  190.7 6.3 %ffn_grads.2 = (bf16[768,1536]{1,0:T(8,128)(2,1)}, bf16[768,1536]{1,0:T(8,128)(2,1)}) custom-call(bf16[256,768]{1,0:T(8,128)(2,1)} %get-tuple-element.242.n0, bf16[256,768]{1,0:T(8,128)(2,1)} %get-tuple-element.243.n1, bf16[256,768]{1,0:T(8,128)(2,1)} %get-tuple-element.426.g_ref.g0, bf16[256,768]{1,0:T(8,128)(2,1)} %get-tuple-element.425.g_ref.g1, ...), custom_call_target="tpu_custom_call" | custom-call | flops 660000000 | bytes 2100000 | tf_op jit(solution)/shard_map/ffn_grads/pallas_call | solution.py:633
  204.1 14.4 %attn_backward.1 = (bf16[2,256,768]{2,1,0:T(8,128)(2,1)}, bf16[2,256,768]{2,1,0:T(8,128)(2,1)}, bf16[1024,768]{1,0:T(8,128)(2,1)}, bf16[1024,576]{1,0:T(8,128)(2,1)}) custom-call(s32[1]{0:T(128)} %bitcast.23.core_ref, s32[1]{0:T(128)} %copy.98.len_ref, bf16[256,768]{1,0:T(8,128)(2,1)} %get-tuple-element.249.a_ref, bf16[256,768]{1,0:T(8,128)(2,1)} %copy-done.59, ...), custom_call_target="tpu_custom_call" | custom-call | flops 1540000000 | bytes 4900000 | tf_op jit(solution)/shard_map/attn_backward/pallas_call | solution.py:608
  223.9 8.7 %attn_grads.1 = bf16[768,2304]{1,0:T(8,128)(2,1)} custom-call(bf16[1024,768]{1,0:T(8,128)(2,1)} %get-tuple-element.241.x_ref, bf16[1024,576]{1,0:T(8,128)(2,1)} %get-tuple-element.254.gp_ref, bf16[1024,768]{1,0:T(8,128)(2,1)} %get-tuple-element.255.g_ref, bf16[192,1024]{1,0:T(8,128)(2,1)} %get-tuple-element.256.att_ref, ...), custom_call_target="tpu_custom_call" | custom-call | flops 880000000 | bytes 2800000 | tf_op jit(solution)/shard_map/attn_grads/pallas_call | solution.py:633
  234.7 9.9 %collective-permute-done.28.received_ref = bf16[256,768]{1,0:T(8,128)(2,1)S(1)} collective-permute-done((bf16[256,768]{1,0:T(8,128)(2,1)S(1)}, bf16[256,768]{1,0:T(8,128)(2,1)S(1)}, u32[]{:S(2)}, u32[]{:S(2)}) %collective-permute-start.28) | collective-permute-done | bytes 393248 | tf_op jit(solution)/shard_map/ppermute | solution.py:927
  251.6 7.0 %ffn_backward.2 = (f32[256,768]{1,0:T(8,128)}, bf16[256,768]{1,0:T(8,128)(2,1)}, bf16[256,1536]{1,0:T(8,128)(2,1)}, bf16[256,1536]{1,0:T(8,128)(2,1)}, bf16[256,768]{1,0:T(8,128)(2,1)}) custom-call(f32[256,768]{1,0:T(8,128)} %get-tuple-element.267.g_ref, bf16[256,768]{1,0:T(8,128)(2,1)} %copy-done.8, bf16[256,768]{1,0:T(8,128)(2,1)} %copy-done.32, ...), custom_call_target="tpu_custom_call" | custom-call | flops 660000000 | bytes 2100000 | tf_op jit(solution)/shard_map/ffn_backward/pallas_call | solution.py:633
  259.4 6.8 %ffn_backward.3 = (f32[256,768]{1,0:T(8,128)}, bf16[256,768]{1,0:T(8,128)(2,1)}, bf16[256,1536]{1,0:T(8,128)(2,1)}, bf16[256,1536]{1,0:T(8,128)(2,1)}, bf16[256,768]{1,0:T(8,128)(2,1)}) custom-call(f32[256,768]{1,0:T(8,128)} %get-tuple-element.273.g_ref, bf16[256,768]{1,0:T(8,128)(2,1)} %copy-done.7, bf16[256,768]{1,0:T(8,128)(2,1)} %copy-done.31, ...), custom_call_target="tpu_custom_call" | custom-call | flops 660000000 | bytes 2100000 | tf_op jit(solution)/shard_map/ffn_backward/pallas_call | solution.py:633
  273.1 6.4 %ffn_grads.3 = (bf16[768,1536]{1,0:T(8,128)(2,1)}, bf16[768,1536]{1,0:T(8,128)(2,1)}) custom-call(bf16[256,768]{1,0:T(8,128)(2,1)} %get-tuple-element.279.n0, bf16[256,768]{1,0:T(8,128)(2,1)} %get-tuple-element.280.n1, bf16[256,768]{1,0:T(8,128)(2,1)} %get-tuple-element.281.g0, bf16[256,768]{1,0:T(8,128)(2,1)} %get-tuple-element.282.g1, ...), custom_call_target="tpu_custom_call" | custom-call | flops 660000000 | bytes 2100000 | tf_op jit(solution)/shard_map/ffn_grads/pallas_call | solution.py:633
  300.0 15.0 %mixer_backward.1 = (bf16[2,256,768]{2,1,0:T(8,128)(2,1)}, bf16[2,256,768]{2,1,0:T(8,128)(2,1)}, bf16[1024,768]{1,0:T(8,128)(2,1)}, bf16[1024,576]{1,0:T(8,128)(...) custom-call(s32[1]{0:T(128)} %bitcast.23.core_ref, ...), custom_call_target="tpu_custom_call" | custom-call | flops 1650000000 | bytes 5250000 | tf_op jit(solution)/shard_map/mixer_backward/pallas_call | solution.py:383
  323.0 19.1 %ssm_grad.1 = (f32[64,192]{1,0:T(8,128)}, f32[64,192]{1,0:T(8,128)}) custom-call(f32[8,128,192]{2,1,0:T(8,128)} %get-tuple-element.323.gre, f32[8,128,192]{2,1,0:T(8,128)} %get-tuple-element.324.gim, f32[8,128,192]{2,1,0:T(8,128)} %get-tuple-element.325.ure, f32[8,128,192]{2,1,0:T(8,128)} %get-tuple-element.326.uim, f32[64,192]{1,0:T(8,128)} %get-tuple-element.198.decay_ref, ...), custom_call_target="tpu_custom_call" | custom-call | flops 2090000000 | bytes 6650000 | tf_op jit(solution)/shard_map/ssm_grad/pallas_call | solution.py:468
  346.1 12.3 %collective-permute-done.42 = bf16[2,1,1,96,1536]{4,3,2,1,0:T(8,128)(2,1)S(1)} collective-permute-done((bf16[2,1,1,96,1536]{4,3,2,1,0:T(8,128)(2,1)S(1)}, bf16[2,1,1,96,1536]{4,3,2,1,0:T(8,128)(2,1)S(1)}, u32[]{:S(2)}, u32[]{:S(2)}) %collective-permute-start.42) | collective-permute-done | bytes 589856 | tf_op jit(solution)/shard_map/ppermute | solution.py:962
  367.1 8.3 %collective-permute-done.43 = bf16[1,1,1,96,1536]{4,3,2,1,0:T(8,128)(2,1)} collective-permute-done((bf16[1,1,1,96,1536]{4,3,2,1,0:T(8,128)(2,1)}, bf16[1,1,1,96,1536]{4,3,2,1,0:T(8,128)(2,1)}, u32[]{:S(2)}, u32[]{:S(2)}) %collective-permute-start.43) | collective-permute-done | bytes 294944 | tf_op jit(solution)/shard_map/ppermute | solution.py:962
  384.3 6.1 %collective-permute-done.40 = bf16[2,1,1,96,768]{3,4,2,1,0:T(8,128)(2,1)S(1)} collective-permute-done((bf16[2,1,1,96,768]{3,4,2,1,0:T(8,128)(2,1)S(1)}, bf16[2,1,1,96,768]{3,4,2,1,0:T(8,128)(2,1)S(1)}, u32[]{:S(2)}, u32[]{:S(2)}) %collective-permute-start.40) | collective-permute-done | bytes 294944 | tf_op jit(solution)/shard_map/ppermute | solution.py:962
  393.6 8.1 %collective-permute-done.41 = bf16[1,1,1,96,768]{3,4,2,1,0:T(8,128)(2,1)S(1)} collective-permute-done((bf16[1,1,1,96,768]{3,4,2,1,0:T(8,128)(2,1)S(1)}, bf16[1,1,1,96,768]{3,4,2,1,0:T(8,128)(2,1)S(1)}, u32[]{:S(2)}, u32[]{:S(2)}) %collective-permute-start.41) | collective-permute-done | bytes 147488 | tf_op jit(solution)/shard_map/ppermute | solution.py:962
  (312 shorter events, 172.4 us)
Async XLA Ops:
  7.2 85.2 %all-gather.3.cloned.1.call-start = ((), (), s32[]{:S(2)}) async-start(), calls=%async_computation.1 | async-start | bytes 3981312 | tf_op jit(solution)/shard_map/all_gather | solution.py:1043
  10.2 145.4 %all-gather.5.cloned.1.call-start = ((), (), s32[]{:S(2)}) async-start(), calls=%async_computation.2 | async-start | bytes 2654208 | tf_op jit(solution)/shard_map/all_gather | solution.py:1078
  17.1 15.2 %collective-permute-start.4 = (bf16[96,768]{1,0:T(8,128)(2,1)S(1)}, bf16[96,768]{1,0:T(8,128)(2,1)S(1)}, u32[]{:S(2)}, u32[]{:S(2)}) collective-permute-start(bf16[96,768]{1,0:T(8,128)(2,1)S(1)} %pad_maximum_fusion.6), channel_id=1, source_target_pairs={{0,16},{4,20},{8,24},{12,28},{16,0},{20,4},{24,8},{28,12},{1,17},{... | collective-permute-start | bytes 442376 | tf_op jit(solution)/shard_map/ppermute | solution.py:962
  17.2 32.1 %collective-permute-start = (bf16[256,768]{1,0:T(8,128)(2,1)}, bf16[256,768]{1,0:T(8,128)(2,1)}, u32[]{:S(2)}, u32[]{:S(2)}) collective-permute-start(bf16[256,768]{1,0:T(8,128)(2,1)} %mine_ref.1), channel_id=1, source_target_pairs={{0,2},{1,3},{2,0},{3,1},{4,6},{5,7},{6,4},{7,5},{8,10},{9,11},{10,... | collective-permute-start | bytes 1179656 | tf_op jit(solution)/shard_map/ppermute | solution.py:927
  32.5 14.4 %collective-permute-start.5 = (bf16[2,96,768]{2,1,0:T(8,128)(2,1)S(1)}, bf16[2,96,768]{2,1,0:T(8,128)(2,1)S(1)}, u32[]{:S(2)}, u32[]{:S(2)}) collective-permute-start(bf16[2,96,768]{2,1,0:T(8,128)(2,1)S(1)} %pad_maximum_fusion.2), channel_id=1, source_target_pairs={{0,8},{4,12},{8,0},{12,4},{16,24},{20,28},{24,16},{28,20},{1,9},{5... | collective-permute-start | bytes 884744 | tf_op jit(solution)/shard_map/ppermute | solution.py:962
  47.0 25.1 %collective-permute-start.8 = (bf16[2,2,96,768]{3,2,1,0:T(8,128)(2,1)S(1)}, bf16[2,2,96,768]{3,2,1,0:T(8,128)(2,1)S(1)}, u32[]{:S(2)}, u32[]{:S(2)}) collective-permute-start(bf16[2,2,96,768]{3,2,1,0:T(8,128)(2,1)S(1)} %pad_maximum_fusion.1), channel_id=1, source_target_pairs={{0,4},{4,0},{8,12},{12,8},{16,20},{20,16},{24,28},{28,24},{1,5},{5... | collective-permute-start | bytes 1769480 | tf_op jit(solution)/shard_map/ppermute | solution.py:962
  52.3 13.6 %collective-permute-start.9 = (bf16[256,768]{1,0:T(8,128)(2,1)S(1)}, bf16[256,768]{1,0:T(8,128)(2,1)S(1)}, u32[]{:S(2)}, u32[]{:S(2)}) collective-permute-start(bf16[256,768]{1,0:T(8,128)(2,1)S(1)} %broadcast_select_fusion), channel_id=1, source_target_pairs={{0,2},{1,3},{2,0},{3,1},{4,6},{5,7},{6,4},{7,5},{8,10},{9,11},{10,... | collective-permute-start | bytes 1179656 | tf_op jit(solution)/shard_map/ppermute | solution.py:927
  53.1 20.4 %collective-permute-start.6 = (bf16[256,768]{1,0:T(8,128)(2,1)}, bf16[256,768]{1,0:T(8,128)(2,1)S(1)}, u32[]{:S(2)}, u32[]{:S(2)}) collective-permute-start(bf16[256,768]{1,0:T(8,128)(2,1)} %get-tuple-element.194.a_ref), channel_id=1, source_target_pairs={{0,1},{1,0},{2,3},{3,2},{4,5},{5,4},{6,7},{7,6},{8,9},{9,8},{10,11... | collective-permute-start | bytes 1179656 | tf_op jit(solution)/shard_map/ppermute | solution.py:927
  53.9 19.6 %collective-permute-start.7 = (bf16[256,768]{1,0:T(8,128)(2,1)}, bf16[256,768]{1,0:T(8,128)(2,1)S(1)}, u32[]{:S(2)}, u32[]{:S(2)}) collective-permute-start(bf16[256,768]{1,0:T(8,128)(2,1)} %get-tuple-element.195.c_ref), channel_id=1, source_target_pairs={{0,1},{1,0},{2,3},{3,2},{4,5},{5,4},{6,7},{7,6},{8,9},{9,8},{10,11... | collective-permute-start | bytes 1179656 | tf_op jit(solution)/shard_map/ppermute | solution.py:927
  94.6 13.5 %collective-permute-start.12 = (bf16[768,1536]{1,0:T(8,128)(2,1)S(1)}, bf16[768,1536]{1,0:T(8,128)(2,1)}, u32[]{:S(2)}, u32[]{:S(2)}) collective-permute-start(bf16[768,1536]{1,0:T(8,128)(2,1)S(1)} %slice.214.own_ref), channel_id=1, source_target_pairs={{0,1},{1,0},{2,3},{3,2},{4,5},{5,4},{6,7},{7,6},{8,9},{9,8},{10,11... | collective-permute-start | bytes 7077896 | tf_op jit(solution)/shard_map/ppermute | solution.py:927
  95.8 227.2 %reduce-scatter.2.cloned.1.call-start = ((), (), s32[]{:S(2)}) async-start(), calls=%async_computation.3 | async-start | bytes 3981312 | tf_op jit(solution)/shard_map/reduce_scatter | solution.py:1137
  96.7 19.5 %collective-permute-start.14 = (bf16[256,768]{1,0:T(8,128)(2,1)S(1)}, bf16[256,768]{1,0:T(8,128)(2,1)}, u32[]{:S(2)}, u32[]{:S(2)}) collective-permute-start(bf16[256,768]{1,0:T(8,128)(2,1)S(1)} %get-tuple-element.421.pair_ref), channel_id=1, source_target_pairs={{0,2},{1,3},{2,0},{3,1},{4,6},{5,7},{6,4},{7,5},{8,10},{9,11},{10,... | collective-permute-start | bytes 1179656 | tf_op jit(solution)/shard_map/ppermute | solution.py:927
  155.6 12.5 %collective-permute-start.20 = (bf16[768,1536]{1,0:T(8,128)(2,1)}, bf16[768,1536]{1,0:T(8,128)(2,1)S(1)}, u32[]{:S(2)}, u32[]{:S(2)}) collective-permute-start(bf16[768,1536]{1,0:T(8,128)(2,1)} %all-gather.5.cloned.1.call-done.own_ref), channel_id=1, source_target_pairs={{0,1},{1,0},{2,3},{3,2},{4,5},{5,4},{6,7},{7,6},{8,9},{9,8},{10,11... | collective-permute-start | bytes 7077896 | tf_op jit(solution)/shard_map/ppermute | solution.py:927
  156.5 19.9 %collective-permute-start.21 = (bf16[256,768]{1,0:T(8,128)(2,1)S(1)}, bf16[256,768]{1,0:T(8,128)(2,1)}, u32[]{:S(2)}, u32[]{:S(2)}) collective-permute-start(bf16[256,768]{1,0:T(8,128)(2,1)S(1)} %get-tuple-element.419.pair_ref), channel_id=1, source_target_pairs={{0,2},{1,3},{2,0},{3,1},{4,6},{5,7},{6,4},{7,5},{8,10},{9,11},{10,... | collective-permute-start | bytes 1179656 | tf_op jit(solution)/shard_map/ppermute | solution.py:927
  182.8 14.3 %collective-permute-start.23 = (bf16[256,768]{1,0:T(8,128)(2,1)}, bf16[256,768]{1,0:T(8,128)(2,1)S(1)}, u32[]{:S(2)}, u32[]{:S(2)}) collective-permute-start(bf16[256,768]{1,0:T(8,128)(2,1)} %get-tuple-element.236.pair_ref), channel_id=1, source_target_pairs={{0,2},{1,3},{2,0},{3,1},{4,6},{5,7},{6,4},{7,5},{8,10},{9,11},{10,... | collective-permute-start | bytes 1179656 | tf_op jit(solution)/shard_map/ppermute | solution.py:927
  203.3 19.1 %collective-permute-start.26 = (bf16[768,1536]{1,0:T(8,128)(2,1)}, bf16[768,1536]{1,0:T(8,128)(2,1)S(1)}, u32[]{:S(2)}, u32[]{:S(2)}) collective-permute-start(bf16[768,1536]{1,0:T(8,128)(2,1)} %get-tuple-element.258), channel_id=1, source_target_pairs={{0,1},{1,0},{2,3},{3,2},{4,5},{5,4},{6,7},{7,6},{8,9},{9,8},{10,11... | collective-permute-start | bytes 7077896 | tf_op jit(solution)/shard_map/ppermute | solution.py:927
  232.7 26.0 %collective-permute-start.30 = (bf16[256,768]{1,0:T(8,128)(2,1)S(1)}, bf16[256,768]{1,0:T(8,128)(2,1)S(1)}, u32[]{:S(2)}, u32[]{:S(2)}) collective-permute-start(bf16[256,768]{1,0:T(8,128)(2,1)S(1)} %get-tuple-element.417.pair_ref), channel_id=1, source_target_pairs={{0,2},{1,3},{2,0},{3,1},{4,6},{5,7},{6,4},{7,5},{8,10},{9,11},{10,... | collective-permute-start | bytes 1179656 | tf_op jit(solution)/shard_map/ppermute | solution.py:927
  266.2 13.3 %collective-permute-start.31 = (bf16[256,768]{1,0:T(8,128)(2,1)}, bf16[256,768]{1,0:T(8,128)(2,1)S(1)}, u32[]{:S(2)}, u32[]{:S(2)}) collective-permute-start(bf16[256,768]{1,0:T(8,128)(2,1)} %get-tuple-element.276.pair_ref), channel_id=1, source_target_pairs={{0,2},{1,3},{2,0},{3,1},{4,6},{5,7},{6,4},{7,5},{8,10},{9,11},{10,... | collective-permute-start | bytes 1179656 | tf_op jit(solution)/shard_map/ppermute | solution.py:927
  295.3 46.8 %collective-permute-start.36 = (bf16[384,1536]{1,0:T(8,128)(2,1)}, bf16[384,1536]{1,0:T(8,128)(2,1)S(1)}, u32[]{:S(2)}, u32[]{:S(2)}) collective-permute-start(bf16[384,1536]{1,0:T(8,128)(2,1)} %get-tuple-element.314), channel_id=1, source_target_pairs={{0,4},{4,0},{8,12},{12,8},{16,20},{20,16},{24,28},{28,24},{1,5},{5... | collective-permute-start | bytes 3538952 | tf_op jit(solution)/shard_map/ppermute | solution.py:962
  297.8 24.2 %collective-permute-start.35 = (bf16[256,768]{1,0:T(8,128)(2,1)}, bf16[256,768]{1,0:T(8,128)(2,1)S(1)}, u32[]{:S(2)}, u32[]{:S(2)}) collective-permute-start(bf16[256,768]{1,0:T(8,128)(2,1)} %broadcast_select_fusion.1), channel_id=1, source_target_pairs={{0,2},{1,3},{2,0},{3,1},{4,6},{5,7},{6,4},{7,5},{8,10},{9,11},{10,... | collective-permute-start | bytes 1179656 | tf_op jit(solution)/shard_map/ppermute | solution.py:927
  320.5 24.7 %collective-permute-start.38 = (bf16[384,768]{1,0:T(8,128)(2,1)}, bf16[384,768]{1,0:T(8,128)(2,1)S(1)}, u32[]{:S(2)}, u32[]{:S(2)}) collective-permute-start(bf16[384,768]{1,0:T(8,128)(2,1)} %get-tuple-element.322), channel_id=1, source_target_pairs={{0,8},{4,12},{8,0},{12,4},{16,24},{20,28},{24,16},{28,20},{1,9},{5... | collective-permute-start | bytes 1769480 | tf_op jit(solution)/shard_map/ppermute | solution.py:962
  342.1 20.6 %collective-permute-start.37 = (bf16[2,256,768]{2,1,0:T(8,128)(2,1)}, bf16[2,256,768]{2,1,0:T(8,128)(2,1)}, u32[]{:S(2)}, u32[]{:S(2)}) collective-permute-start(bf16[2,256,768]{2,1,0:T(8,128)(2,1)} %get-tuple-element.328), channel_id=1, source_target_pairs={{0,1},{1,0},{2,3},{3,2},{4,5},{5,4},{6,7},{7,6},{8,9},{9,8},{10,11... | collective-permute-start | bytes 2359304 | tf_op jit(solution)/shard_map/ppermute | solution.py:927
  342.6 15.8 %collective-permute-start.42 = (bf16[2,1,1,96,1536]{4,3,2,1,0:T(8,128)(2,1)S(1)}, bf16[2,1,1,96,1536]{4,3,2,1,0:T(8,128)(2,1)S(1)}, u32[]{:S(2)}, u32[]{:S(2)}) collective-permute-start(bf16[2,1,1,96,1536]{4,3,2,1,0:T(8,128)(2,1)S(1)} %dynamic-slice_convert_fusion), channel_id=1, source_target_pairs={{0,8},{4,12},{8,0},{12,4},{16,24},{20,28},{24,16},{28,20},{1,9},{5... | collective-permute-start | bytes 1769480 | tf_op jit(solution)/shard_map/ppermute | solution.py:962
  359.3 16.1 %collective-permute-start.43 = (bf16[1,1,1,96,1536]{4,3,2,1,0:T(8,128)(2,1)}, bf16[1,1,1,96,1536]{4,3,2,1,0:T(8,128)(2,1)}, u32[]{:S(2)}, u32[]{:S(2)}) collective-permute-start(bf16[1,1,1,96,1536]{4,3,2,1,0:T(8,128)(2,1)} %dynamic-slice_convert_fusion.2), channel_id=1, source_target_pairs={{0,16},{4,20},{8,24},{12,28},{16,0},{20,4},{24,8},{28,12},{1,17},{... | collective-permute-start | bytes 884744 | tf_op jit(solution)/shard_map/ppermute | solution.py:962
  (90 other events, 630.0 us)
Sparse Core Ops, SparseCore 0:
  10.3 82.0 all-gather.2
  95.9 52.8 all-gather.4
  232.7 82.2 reduce-scatter.1

commit v4 on v3

--- a/solution.py
+++ b/solution.py
@@ -10,6 +10,8 @@
 F32 = jnp.float32
 BF16 = jnp.bfloat16
 BLK = 128
+GROUP = 8
+UNROLL = 2
 VMEM_LIMIT = 56 * 1024 * 1024
 
 
@@ -60,17 +62,19 @@
     return jnp.asarray(fwd), jnp.asarray(inv)
 
 
-def to_spectrum(fwd_ref, x):
+def to_spectrum_exact(fwd_ref, x):
     high, low = split(x)
     return dot(fwd_ref[:, : 2 * BLK], jnp.concatenate([high, low], axis=0)) + dot(
         fwd_ref[:, 2 * BLK :], high
     )
 
 
-def from_spectrum(inv_ref, z):
-    high, low = split(z)
-    both = dot(inv_ref[...], high)
-    return both[:BLK] + both[BLK:] + dot(inv_ref[:BLK, :], low)
+def to_spectrum(fwd_ref, x):
+    return dot(fwd_ref[:, :BLK], x.astype(BF16))
+
+
+def from_spectrum(inv_ref, re, im):
+    return dot(inv_ref[:BLK], jnp.concatenate([re.astype(BF16), im.astype(BF16)], axis=0))
 
 
 def sign_rows(shape):
@@ -88,44 +92,61 @@
     return jnp.where(special, im, re), jnp.where(special, 0.0, im)
 
 
-def kgen_body(decay_ref, coef_ref, taps_ref, fwd_ref, kre_ref, kim_ref, tre_ref, tim_ref, mixp, kern):
+def channel_tiles(width):
+    return [(s, min(128, width - s), 128 // min(128, width - s)) for s in range(0, width, 128)]
+
+
+def side_by_side(x, start, size, copies):
+    rows = x.shape[0] // copies
+    parts = [x[i * rows : (i + 1) * rows, start : start + size] for i in range(copies)]
+    return parts[0] if copies == 1 else jnp.concatenate(parts, axis=1)
+
+
+def kgen_body(decay_ref, coef_ref, taps_ref, fwd_ref, kre_ref, kim_ref, tre_ref, tim_ref, rate, mixp, kern):
     states, width = decay_ref.shape
     blocks = kre_ref.shape[0]
     decay = decay_ref[...]
     mixing = jnp.sqrt(2.0 * decay) * coef_ref[...]
-    for m in range(blocks):
-        mixp[m] = mixing * jnp.exp(decay * (-float(BLK * m)))
-    for start, size in lane_tiles(width):
-        lanes = slice(start, start + size)
-
-        def per_tile(jt, _, lanes=lanes, size=size):
-            steps = (lax.broadcasted_iota(jnp.int32, (8, size), 0) + jt * 8).astype(F32)
+    for start, size, copies in channel_tiles(width):
+        rows = states // copies
+        tile_decay = side_by_side(decay, start, size, copies)
+        tile_mixing = side_by_side(mixing, start, size, copies)
+        rate[:rows] = -tile_decay
+        for m in range(blocks):
+            mixp[m, :rows] = tile_mixing * jnp.exp(tile_decay * (-float(BLK * m)))
+
+        def per_tile(jt, _, start=start, size=size, copies=copies, rows=rows):
+            steps = (lax.broadcasted_iota(jnp.int32, (8, 128), 0) + jt * 8).astype(F32)
 
             def per_states(ng, acc):
-                rows = pl.ds(pl.multiple_of(ng * 8, 8), 8)
-                rates = -decay_ref[rows, lanes]
-                scales = [mixp[m, rows, lanes] for m in range(blocks)]
+                here = pl.ds(pl.multiple_of(ng * 8, 8), 8)
+                rates = rate[here]
+                scales = [mixp[m, here] for m in range(blocks)]
                 for i in range(8):
                     e = jnp.exp(rates[i : i + 1] * steps)
                     acc = tuple(a + e * s[i : i + 1] for a, s in zip(acc, scales))
                 return acc
 
             acc = lax.fori_loop(
-                0, states // 8, per_states, tuple(jnp.zeros((8, size), F32) for _ in range(blocks))
+                0, rows // 8, per_states, tuple(jnp.zeros((8, 128), F32) for _ in range(blocks))
             )
+            place = pl.ds(pl.multiple_of(jt * 8, 8), 8)
             for m in range(blocks):
-                kern[m, pl.ds(pl.multiple_of(jt * 8, 8), 8), lanes] = acc[m]
+                total = acc[m][:, :size]
+                for i in range(1, copies):
+                    total = total + acc[m][:, i * size : (i + 1) * size]
+                kern[m, place, start : start + size] = total
             return 0
 
         lax.fori_loop(0, BLK // 8, per_tile, 0)
     for m in range(blocks):
-        spec = to_spectrum(fwd_ref, kern[m])
+        spec = to_spectrum_exact(fwd_ref, kern[m])
         kre_ref[m] = spec[:BLK]
         kim_ref[m] = spec[BLK:]
     taps = jnp.concatenate(
         [taps_ref[...], jnp.zeros((BLK - taps_ref.shape[0], width), F32)], axis=0
     )
-    spec = to_spectrum(fwd_ref, taps)
+    spec = to_spectrum_exact(fwd_ref, taps)
     tre_ref[...] = spec[:BLK]
     tim_ref[...] = spec[BLK:]
 
@@ -142,7 +163,8 @@
             jax.ShapeDtypeStruct((BLK, width), F32),
         ),
         scratch_shapes=[
-            pltpu.VMEM((blocks, states, width), F32),
+            pltpu.VMEM((states, 128), F32),
+            pltpu.VMEM((blocks, states, 128), F32),
             pltpu.VMEM((blocks, BLK, width), F32),
         ],
         compiler_params=pltpu.CompilerParams(vmem_limit_bytes=VMEM_LIMIT),
@@ -174,7 +196,7 @@
     core_ref, a_ref, b_ref, c_ref, d_ref, w_ref, kre_ref, kim_ref, tre_ref, tim_ref, fwd_ref, inv_ref,
     keep_ref, send_ref,
     x_ref, mixed_ref, q_ref, v_ref, sh_ref, st_ref, sre_ref, sim_ref, ure_ref, uim_ref,
-    zre, zim, keys,
+    zre, zim, keys, queries, values, ure, uim,
 ):
     length, width = q_ref.shape
     blocks = length // BLK
@@ -187,9 +209,11 @@
     for piece_ref, place in zip((a_ref, b_ref, c_ref, d_ref), places):
         piece = piece_ref[...]
         x_ref[place] = piece
-        q_ref[place] = dot(piece, wq)
-        v_ref[place] = dot(piece, wv)
+        queries[place] = dot(piece, wq)
+        values[place] = dot(piece, wv)
         keys[place] = dot(piece, wk)
+    q_ref[...] = queries[...].astype(BF16)
+    v_ref[...] = values[...].astype(BF16)
     tre = tre_ref[...]
     tim = tim_ref[...]
     tre2 = jnp.where(row0, tim, tre)
@@ -199,26 +223,28 @@
         rows = slice(p * BLK, (p + 1) * BLK)
         spec = to_spectrum(fwd_ref, keys[rows])
         re, im = spec[:BLK], spec[BLK:]
-        sre_ref[p] = re
-        sim_ref[p] = im
+        sre_ref[p] = re.astype(BF16)
+        sim_ref[p] = im.astype(BF16)
         pr = re * tre - im * tim0
         pi = re * tim0 + im * tre2
         if last is None:
-            z = jnp.concatenate([pr, pi], axis=0)
+            z = (pr, pi)
         else:
-            z = jnp.concatenate([pr + sign * last[0], pi + sign * last[1]], axis=0)
+            z = (pr + sign * last[0], pi + sign * last[1])
         last = (pr, pi)
-        shifted = from_spectrum(inv_ref, z)
-        sh_ref[rows] = shifted
-        spec = to_spectrum(fwd_ref, shifted * v_ref[rows])
-        ure_ref[p] = spec[:BLK]
-        uim_ref[p] = spec[BLK:]
+        shifted = from_spectrum(inv_ref, *z)
+        sh_ref[rows] = shifted.astype(BF16)
+        spec = to_spectrum(fwd_ref, shifted * values[rows])
+        ure[p] = spec[:BLK]
+        uim[p] = spec[BLK:]
+        ure_ref[p] = spec[:BLK].astype(BF16)
+        uim_ref[p] = spec[BLK:].astype(BF16)
 
     def products(ft, fr, lanes):
         sgn = sign[:8, lanes]
         k = [(kre_ref[m, fr, lanes], kim_ref[m, fr, lanes]) for m in range(blocks)]
         k = [(a,) + fix_first(ft, a, b) for a, b in k]
-        u = [(ure_ref[m, fr, lanes], uim_ref[m, fr, lanes]) for m in range(blocks)]
+        u = [(ure[m, fr, lanes], uim[m, fr, lanes]) for m in range(blocks)]
         prev = None
         for p in range(blocks):
             yr = yi = None
@@ -242,9 +268,9 @@
     for half in range(2):
         for p in range(half * blocks // 2, (half + 1) * blocks // 2):
             rows = slice(p * BLK, (p + 1) * BLK)
-            state = from_spectrum(inv_ref, jnp.concatenate([zre[p], zim[p]], axis=0))
-            st_ref[rows] = state
-            mixed_ref[rows] = (q_ref[rows] * state).astype(BF16)
+            state = from_spectrum(inv_ref, zre[p], zim[p])
+            st_ref[rows] = state.astype(BF16)
+            mixed_ref[rows] = (queries[rows] * state).astype(BF16)
         for out_ref, place in zip((keep_ref, send_ref), places[2 * half : 2 * half + 2]):
             out_ref[half] = dot_nt(mixed_ref[place], wo).astype(BF16)
 
@@ -258,8 +284,8 @@
     length = 4 * quarter
     width = w.shape[1] // 4
     blocks = length // BLK
-    row_f = jax.ShapeDtypeStruct((length, width), F32)
-    spec_f = jax.ShapeDtypeStruct((blocks, BLK, width), F32)
+    row_f = jax.ShapeDtypeStruct((length, width), BF16)
+    spec_f = jax.ShapeDtypeStruct((blocks, BLK, width), BF16)
     piece = jax.ShapeDtypeStruct((2, quarter, model), BF16)
     return pl.pallas_call(
         mixer_fwd_body,
@@ -271,7 +297,8 @@
             row_f, row_f, row_f, row_f, spec_f, spec_f, spec_f, spec_f,
         ),
         scratch_shapes=[pltpu.VMEM((blocks, BLK, width), F32)] * 2
-        + [pltpu.VMEM((length, width), F32)],
+        + [pltpu.VMEM((length, width), F32)] * 3
+        + [pltpu.VMEM((blocks, BLK, width), F32)] * 2,
         compiler_params=pltpu.CompilerParams(vmem_limit_bytes=VMEM_LIMIT),
         cost_estimate=cost(14),
         name="mixer_forward",
@@ -313,8 +340,8 @@
 def mixer_bwd_body(
     core_ref, a_ref, b_ref, c_ref, d_ref, w_ref, q_ref, v_ref, sh_ref, st_ref, sre_ref, sim_ref,
     kre_ref, kim_ref, tre_ref, tim_ref, fwd_ref, inv_ref,
-    keep_ref, send_ref, g_ref, gp_ref, taps_ref, gre, gim,
-    wre, wim, grad_mixed,
+    keep_ref, send_ref, g_ref, gp_ref, taps_ref, gre_ref, gim_ref,
+    wre, wim, gre, gim, grad_mixed,
 ):
     length, width = q_ref.shape
     blocks = length // BLK
@@ -329,10 +356,12 @@
     for p in range(blocks):
         rows = slice(p * BLK, (p + 1) * BLK)
         gm = grad_mixed[rows]
-        gp_ref[rows, :width] = (gm * st_ref[rows]).astype(BF16)
-        spec = to_spectrum(fwd_ref, gm * q_ref[rows])
+        gp_ref[rows, :width] = (gm * st_ref[rows].astype(F32)).astype(BF16)
+        spec = to_spectrum(fwd_ref, gm * q_ref[rows].astype(F32))
         gre[p] = spec[:BLK]
         gim[p] = spec[BLK:]
+        gre_ref[p] = spec[:BLK].astype(BF16)
+        gim_ref[p] = spec[BLK:].astype(BF16)
     correlate_tiles(width, blocks, (gre, gim), (kre_ref, kim_ref), (wre, wim))
     tre = tre_ref[...]
     tim = tim_ref[...]
@@ -344,19 +373,19 @@
     corr = [zero, zero, zero, zero]
     for p in reversed(range(blocks)):
         rows = slice(p * BLK, (p + 1) * BLK)
-        grad_u = from_spectrum(inv_ref, jnp.concatenate([wre[p], wim[p]], axis=0))
-        gp_ref[rows, 2 * width :] = (grad_u * sh_ref[rows]).astype(BF16)
-        spec = to_spectrum(fwd_ref, grad_u * v_ref[rows])
+        grad_u = from_spectrum(inv_ref, wre[p], wim[p])
+        gp_ref[rows, 2 * width :] = (grad_u * sh_ref[rows].astype(F32)).astype(BF16)
+        spec = to_spectrum(fwd_ref, grad_u * v_ref[rows].astype(F32))
         re, im = spec[:BLK], spec[BLK:]
         pr = re * tre + im * tim0
         pi = im * tre2 - re * tim0
         if after is None:
-            z = jnp.concatenate([pr, pi], axis=0)
+            z = (pr, pi)
         else:
-            z = jnp.concatenate([pr + sign * after[0], pi + sign * after[1]], axis=0)
+            z = (pr + sign * after[0], pi + sign * after[1])
         after = (pr, pi)
-        gp_ref[rows, width : 2 * width] = from_spectrum(inv_ref, z).astype(BF16)
-        sr, si = sre_ref[p], sim_ref[p]
+        gp_ref[rows, width : 2 * width] = from_spectrum(inv_ref, *z).astype(BF16)
+        sr, si = sre_ref[p].astype(F32), sim_ref[p].astype(F32)
         sr2 = jnp.where(row0, si, sr)
         si0 = jnp.where(row0, 0.0, si)
         corr[0] = corr[0] + (re * sr + im * si0)
@@ -366,8 +395,8 @@
             corr[2] = corr[2] + (nr * sr + ni * si0)
             corr[3] = corr[3] + (ni * sr2 - nr * si0)
         next_gs = (re, im)
-    z = jnp.concatenate([corr[0] + sign * corr[2], corr[1] + sign * corr[3]], axis=0)
-    taps_ref[...] = from_spectrum(inv_ref, z)[: taps_ref.shape[0]]
+    taps = from_spectrum(inv_ref, corr[0] + sign * corr[2], corr[1] + sign * corr[3])
+    taps_ref[...] = taps[: taps_ref.shape[0]]
     wp = w_ref[:, : 3 * width]
     for i, place in enumerate(places):
         (keep_ref, send_ref)[i % 2][i // 2] = dot_nt(gp_ref[place], wp).astype(BF16)
@@ -379,7 +408,7 @@
     width = w.shape[1] // 4
     blocks = length // BLK
     piece = jax.ShapeDtypeStruct((2, quarter, model), BF16)
-    spec_f = jax.ShapeDtypeStruct((blocks, BLK, width), F32)
+    spec_f = jax.ShapeDtypeStruct((blocks, BLK, width), BF16)
     return pl.pallas_call(
         mixer_bwd_body,
         in_specs=[SCALAR] + [WHOLE] * 17,
@@ -390,7 +419,7 @@
             jax.ShapeDtypeStruct((taps, width), F32),
             spec_f, spec_f,
         ),
-        scratch_shapes=[pltpu.VMEM((blocks, BLK, width), F32)] * 2
+        scratch_shapes=[pltpu.VMEM((blocks, BLK, width), F32)] * 4
         + [pltpu.VMEM((length, width), F32)],
         compiler_params=pltpu.CompilerParams(vmem_limit_bytes=VMEM_LIMIT),
         cost_estimate=cost(15),
@@ -398,41 +427,43 @@
     )(core, *pieces, w, *saved, *spectra, fwd, inv)
 
 
-def ssm_grad_body(
-    gre, gim, ure, uim, decay_ref, coef_ref, inv_ref, gd_ref, gc_ref, vre, vim, dk_ref
-):
-    states, width = decay_ref.shape
-    blocks = gre.shape[0]
-    correlate_tiles(width, blocks, (gre, gim), (ure, uim), (vre, vim))
-    for p in range(blocks):
-        dk_ref[p * BLK : (p + 1) * BLK] = from_spectrum(
-            inv_ref, jnp.concatenate([vre[p], vim[p]], axis=0)
-        )
-    group = 4
-    for start, size in lane_tiles(width):
-        lanes = slice(start, start + size)
-        base = lax.broadcasted_iota(jnp.int32, (8, size), 0).astype(F32)
-
-        def per_group(ng, _, lanes=lanes, size=size, base=base):
-            rows = pl.ds(pl.multiple_of(ng * 8, 8), 8)
-            rates = decay_ref[rows, lanes]
-            row_ids = lax.broadcasted_iota(jnp.int32, (8, size), 0)
-            sums_a = jnp.zeros((8, size), F32)
-            sums_b = jnp.zeros((8, size), F32)
-            for half in range(8 // group):
-                d = [rates[half * group + i : half * group + i + 1] for i in range(group)]
-                p = [jnp.broadcast_to(jnp.exp(-float(BLK) * x), (8, size)) for x in d]
-                step8 = [jnp.broadcast_to(jnp.exp(-8.0 * x), (8, size)) for x in d]
+def ssm_grad_kernel(g_spectrum, u_spectrum, decay_t, coef_t, inv, tile):
+    states, width = decay_t.shape
+    blocks = g_spectrum[0].shape[0]
+    start, size, copies = channel_tiles(width)[tile]
+    lanes = slice(start, start + size)
+    rows = states // copies
+    group = GROUP
+
+    def body(g_re, g_im, u_re, u_im, decay_ref, coef_ref, inv_ref, gd_ref, gc_ref,
+             gre, gim, ure, uim, vre, vim, dk_ref, rate, sum_a, sum_b):
+        for scratch, ref in ((gre, g_re), (gim, g_im), (ure, u_re), (uim, u_im)):
+            scratch[...] = ref[:, :, lanes].astype(F32)
+        correlate_tiles(size, blocks, (gre, gim), (ure, uim), (vre, vim))
+        rate[:rows] = side_by_side(decay_ref[...], start, size, copies)
+        for p in range(blocks):
+            part = from_spectrum(inv_ref, vre[p], vim[p])
+            dk_ref[p] = part if copies == 1 else jnp.concatenate([part] * copies, axis=1)
+        base = lax.broadcasted_iota(jnp.int32, (8, 128), 0).astype(F32)
+
+        def per_group(ng, _):
+            here = pl.ds(pl.multiple_of(ng * 8, 8), 8)
+            rates = rate[here]
+            row_ids = lax.broadcasted_iota(jnp.int32, (8, 128), 0)
+            sums_a = jnp.zeros((8, 128), F32)
+            sums_b = jnp.zeros((8, 128), F32)
+            for first in range(0, 8, group):
+                d = [rates[first + i : first + i + 1] for i in range(group)]
+                p = [jnp.broadcast_to(jnp.exp(-float(BLK) * x), (8, 128)) for x in d]
+                step8 = [jnp.broadcast_to(jnp.exp(-8.0 * x), (8, 128)) for x in d]
                 e0 = tuple(jnp.exp(-x * base) for x in d)
-                zero = jnp.zeros((8, size), F32)
+                zero = jnp.zeros((8, 128), F32)
 
                 def per_tile(jt, carry, p=p, step8=step8):
                     e, a, b = carry
                     steps = base + (jt * 8).astype(F32)
-                    dk = [
-                        dk_ref[pl.ds(pl.multiple_of(m * BLK + jt * 8, 8), 8), lanes]
-                        for m in range(blocks)
-                    ]
+                    place = pl.ds(pl.multiple_of(jt * 8, 8), 8)
+                    dk = [dk_ref[m, place] for m in range(blocks)]
                     ne, na, nb = [], [], []
                     for i in range(group):
                         h = dk[blocks - 1]
@@ -440,38 +471,40 @@
                         for m in reversed(range(blocks - 1)):
                             s = h if s is None else s * p[i] + h
                             h = h * p[i] + dk[m]
-                        eh = e[i] * h
-                        na.append(a[i] + eh)
-                        nb.append(b[i] + steps * eh + (float(BLK) * e[i]) * (s * p[i]))
+                        na.append(a[i] + e[i] * h)
+                        nb.append(b[i] + e[i] * (steps * h + float(BLK) * (s * p[i])))
                         ne.append(e[i] * step8[i])
                     return tuple(ne), tuple(na), tuple(nb)
 
                 _, a, b = lax.fori_loop(
-                    0, BLK // 8, per_tile, (e0, (zero,) * group, (zero,) * group)
+                    0, BLK // 8, per_tile, (e0, (zero,) * group, (zero,) * group), unroll=UNROLL
                 )
                 for i in range(group):
-                    here = row_ids == half * group + i
-                    sums_a = jnp.where(here, jnp.sum(a[i], axis=0, keepdims=True), sums_a)
-                    sums_b = jnp.where(here, jnp.sum(b[i], axis=0, keepdims=True), sums_b)
-            root = jnp.sqrt(2.0 * rates)
-            gc_ref[rows, lanes] = root * sums_a
-            gd_ref[rows, lanes] = coef_ref[rows, lanes] * (sums_a / root - root * sums_b)
+                    mine = row_ids == first + i
+                    sums_a = jnp.where(mine, jnp.sum(a[i], axis=0, keepdims=True), sums_a)
+                    sums_b = jnp.where(mine, jnp.sum(b[i], axis=0, keepdims=True), sums_b)
+            sum_a[here] = sums_a
+            sum_b[here] = sums_b
             return 0
 
-        lax.fori_loop(0, states // 8, per_group, 0)
-
-
-def ssm_grad_kernel(g_spectrum, u_spectrum, decay_t, coef_t, inv):
-    states, width = decay_t.shape
-    blocks = g_spectrum[0].shape[0]
-    out = jax.ShapeDtypeStruct((states, width), F32)
+        lax.fori_loop(0, rows // 8, per_group, 0)
+        for i in range(copies):
+            here = slice(i * rows, (i + 1) * rows)
+            part = slice(i * size, (i + 1) * size)
+            a, b = sum_a[:rows, part], sum_b[:rows, part]
+            root = jnp.sqrt(2.0 * decay_ref[here, lanes])
+            gc_ref[here] = root * a
+            gd_ref[here] = coef_ref[here, lanes] * (a / root - root * b)
+
+    out = jax.ShapeDtypeStruct((states, size), F32)
     return pl.pallas_call(
-        ssm_grad_body,
+        body,
         out_shape=(out, out),
-        scratch_shapes=[pltpu.VMEM((blocks, BLK, width), F32)] * 2
-        + [pltpu.VMEM((blocks * BLK, width), F32)],
+        scratch_shapes=[pltpu.VMEM((blocks, BLK, size), F32)] * 6
+        + [pltpu.VMEM((blocks, BLK, 128), F32)]
+        + [pltpu.VMEM((states, 128), F32)] * 3,
+        cost_estimate=cost(10),
         compiler_params=pltpu.CompilerParams(vmem_limit_bytes=VMEM_LIMIT),
-        cost_estimate=cost(19),
         name="ssm_grad",
     )(*g_spectrum, *u_spectrum, decay_t, coef_t, inv)
 
@@ -710,19 +743,32 @@
     return kernel_call(back_body, outs, "back_step", 2)(g, pair, received, h, gain)
 
 
-def last_back_body(chip_ref, g0, p0, h0, g1, p1, h1, received_ref, gain_ref, out_ref):
+def last_back_body(chip_ref, g0, h0, g1, h1, own_ref, received_ref, gain_ref, out_ref):
     first = chip_ref[0] == 0
-    grad_normed = jnp.where(first, p0[...], p1[...]).astype(F32) + received_ref[...].astype(F32)
+    grad_normed = both(own_ref, received_ref)
     h = jnp.where(first, h0[...], h1[...])
     grad = jnp.where(first, g0[...], g1[...])
     out_ref[...] = (grad + norm_gradient(grad_normed, h, gain_ref[...])).astype(BF16)
 
 
-def last_back(chip, grads, pairs, states, received, gain):
+def last_back(chip, grads, states, own, received, gain):
     outs = shaped(received.shape, BF16)
     return kernel_call(last_back_body, outs, "last_back", 2, 1)(
-        chip, grads[0], pairs[0], states[0], grads[1], pairs[1], states[1], received, gain
-    )
+        chip, grads[0], states[0], grads[1], states[1], own, received, gain
+    )
+
+
+def own_half_body(chip_ref, keep_ref, received_ref, own_ref, send_ref):
+    first = chip_ref[0] == 0
+    low = keep_ref[0].astype(F32) + received_ref[0].astype(F32)
+    high = keep_ref[1].astype(F32) + received_ref[1].astype(F32)
+    own_ref[...] = jnp.where(first, low, high).astype(BF16)
+    send_ref[...] = jnp.where(first, high, low).astype(BF16)
+
+
+def own_half(chip, keep, received):
+    piece = shaped(keep.shape[1:], BF16)
+    return kernel_call(own_half_body, (piece, piece), "own_half", 2, 1)(chip, keep, received)
 
 
 ROOT = 0.7978845608028654
@@ -741,35 +787,44 @@
     return u * half, slope
 
 
+PIECE = 256
+
+
+def unit_pieces(units, *refs):
+    for i, ref in enumerate(refs):
+        yield slice(i * units, (i + 1) * units), ref[:, :units], ref[:, units : 2 * units]
+
+
 def ffn_fwd_body(
     h_ref, pair_ref, received_ref, gain_ref, own_ref, mate_ref, state_ref, n_ref, hidden_ref, out_ref
 ):
-    units = own_ref.shape[1] // 2
+    units = mate_ref.shape[1] // 2
     h = h_ref[...] + both(pair_ref, received_ref)
     state_ref[...] = h
     unit, _ = statistics(h)
     n = (unit * gain_ref[...]).astype(BF16)
     n_ref[...] = n
     out = None
-    for side, w_ref in enumerate((own_ref, mate_ref)):
-        hidden = dot(n, w_ref[:, :units])
-        hidden_ref[:, side * units : (side + 1) * units] = hidden
-        part = dot_nt(gelu(hidden).astype(BF16), w_ref[:, units:])
+    for lanes, up, down in unit_pieces(units, own_ref, mate_ref):
+        hidden = dot(n, up)
+        hidden_ref[:, lanes] = hidden
+        part = dot_nt(gelu(hidden).astype(BF16), down)
         out = part if out is None else out + part
     out_ref[...] = out.astype(BF16)
 
 
 def ffn_forward(h, pair, received, gain, own, mate):
     piece = shaped(h.shape, BF16)
-    outs = (shaped(h.shape, F32), piece, shaped((h.shape[0], own.shape[1]), F32), piece)
-    return kernel_call(ffn_fwd_body, outs, "ffn_forward", 5)(h, pair, received, gain, own, mate)
+    hidden = shaped((h.shape[0], mate.shape[1]), F32)
+    outs = (shaped(h.shape, F32), piece, hidden, piece)
+    return kernel_call(ffn_fwd_body, outs, "ffn_forward", 50)(h, pair, received, gain, own, mate)
 
 
 def ffn_both_body(
     h_ref, pair_ref, received_ref, gain_ref, g_ref, own_ref, mate_ref,
     state_ref, n_ref, grad_ref, active_ref, out_ref,
 ):
-    units = own_ref.shape[1] // 2
+    units = mate_ref.shape[1] // 2
     h = h_ref[...] + both(pair_ref, received_ref)
     state_ref[...] = h
     unit, _ = statistics(h)
@@ -777,41 +832,39 @@
     n_ref[...] = n
     g = g_ref[...]
     out = None
-    for side, w_ref in enumerate((own_ref, mate_ref)):
-        lanes = slice(side * units, (side + 1) * units)
-        active, slope = gelu_parts(dot(n, w_ref[:, :units]))
+    for lanes, up, down in unit_pieces(units, own_ref, mate_ref):
+        active, slope = gelu_parts(dot(n, up))
         active_ref[:, lanes] = active.astype(BF16)
-        grad = (dot(g, w_ref[:, units:]) * slope).astype(BF16)
+        grad = (dot(g, down) * slope).astype(BF16)
         grad_ref[:, lanes] = grad
-        part = dot_nt(grad, w_ref[:, :units])
+        part = dot_nt(grad, up)
         out = part if out is None else out + part
     out_ref[...] = out.astype(BF16)
 
 
 def ffn_both(h, pair, received, gain, g, own, mate):
     piece = shaped(h.shape, BF16)
-    rows = shaped((h.shape[0], own.shape[1]), BF16)
+    rows = shaped((h.shape[0], mate.shape[1]), BF16)
     outs = (shaped(h.shape, F32), piece, rows, rows, piece)
-    return kernel_call(ffn_both_body, outs, "ffn_both", 6)(h, pair, received, gain, g, own, mate)
+    return kernel_call(ffn_both_body, outs, "ffn_both", 60)(h, pair, received, gain, g, own, mate)
 
 
 def ffn_bwd_body(
     g_ref, pair_ref, received_ref, h_ref, gain_ref, hidden_ref, own_ref, mate_ref,
     total_ref, low_ref, grad_ref, active_ref, out_ref,
 ):
-    units = own_ref.shape[1] // 2
+    units = mate_ref.shape[1] // 2
     total = g_ref[...] + norm_gradient(both(pair_ref, received_ref), h_ref[...], gain_ref[...])
     total_ref[...] = total
     g = total.astype(BF16)
     low_ref[...] = g
     out = None
-    for side, w_ref in enumerate((own_ref, mate_ref)):
-        lanes = slice(side * units, (side + 1) * units)
+    for lanes, up, down in unit_pieces(units, own_ref, mate_ref):
         active, slope = gelu_parts(hidden_ref[:, lanes])
         active_ref[:, lanes] = active.astype(BF16)
-        grad = (dot(g, w_ref[:, units:]) * slope).astype(BF16)
+        grad = (dot(g, down) * slope).astype(BF16)
         grad_ref[:, lanes] = grad
-        part = dot_nt(grad, w_ref[:, :units])
+        part = dot_nt(grad, up)
         out = part if out is None else out + part
     out_ref[...] = out.astype(BF16)
 
@@ -820,48 +873,75 @@
     piece = shaped(h.shape, BF16)
     rows = shaped(hidden.shape, BF16)
     outs = (shaped(h.shape, F32), piece, rows, rows, piece)
-    return kernel_call(ffn_bwd_body, outs, "ffn_backward", 6)(
+    return kernel_call(ffn_bwd_body, outs, "ffn_backward", 60)(
         g, pair, received, h, gain, hidden, own, mate
     )
 
 
-def ffn_out_body(a0_ref, a1_ref, own_ref, mate_ref, out0_ref, out1_ref):
-    units = own_ref.shape[1] // 2
-    for a_ref, out_ref in ((a0_ref, out0_ref), (a1_ref, out1_ref)):
-        out = dot_nt(a_ref[:, :units], own_ref[:, units:]) + dot_nt(
-            a_ref[:, units:], mate_ref[:, units:]
-        )
-        out_ref[...] = out.astype(BF16)
-
-
-def ffn_out(active0, active1, own, mate):
+def ffn_out_body(chip_ref, a0_ref, a1_ref, own_ref, mate_ref, out_ref, send_ref):
+    units = mate_ref.shape[1] // 2
+    outs = []
+    for a_ref in (a0_ref, a1_ref):
+        out = None
+        for lanes, _, down in unit_pieces(units, own_ref, mate_ref):
+            part = dot_nt(a_ref[:, lanes], down)
+            out = part if out is None else out + part
+        outs.append(out)
+    first = chip_ref[0] == 0
+    out_ref[...] = jnp.where(first, outs[0], outs[1]).astype(BF16)
+    send_ref[...] = jnp.where(first, outs[1], outs[0]).astype(BF16)
+
+
+def ffn_out(chip, active0, active1, own, mate):
     piece = shaped((active0.shape[0], own.shape[0]), BF16)
-    return kernel_call(ffn_out_body, (piece, piece), "ffn_out", 3)(active0, active1, own, mate)
-
-
-def ffn_grads_body(n0, n1, g0, g1, gh0, gh1, a0, a1, own_ref, mate_ref):
-    units = own_ref.shape[1] // 2
-    for side, out_ref in ((1, mate_ref), (0, own_ref)):
-        lanes = slice(side * units, (side + 1) * units)
-        out_ref[:, :units] = (
+    return kernel_call(ffn_out_body, (piece, piece), "ffn_out", 3, 1)(
+        chip, active0, active1, own, mate
+    )
+
+
+def output_body(chip_ref, h0_ref, h1_ref, own_ref, received_ref, out_ref):
+    h = jnp.where(chip_ref[0] == 0, h0_ref[...], h1_ref[...])
+    out_ref[...] = (h + both(own_ref, received_ref)).astype(BF16)
+
+
+def output_step(chip, states, own, received):
+    outs = shaped(own.shape, BF16)
+    return kernel_call(output_body, outs, "output_step", 2, 1)(chip, *states, own, received)
+
+
+def ffn_grads_body(n0, n1, g0, g1, gh0, gh1, a0, a1, own_ref, *mate_refs):
+    count = len(mate_refs) // 2
+    units = count * PIECE
+    for i in range(count):
+        lanes = slice(units + i * PIECE, units + (i + 1) * PIECE)
+        mate_refs[i][...] = (
             dot_tn(n0[...], gh0[:, lanes]) + dot_tn(n1[...], gh1[:, lanes])
         ).astype(BF16)
-        out_ref[:, units:] = (
+        mate_refs[count + i][...] = (
             dot_tn(g0[...], a0[:, lanes]) + dot_tn(g1[...], a1[:, lanes])
         ).astype(BF16)
+    own_ref[:, :units] = (
+        dot_tn(n0[...], gh0[:, :units]) + dot_tn(n1[...], gh1[:, :units])
+    ).astype(BF16)
+    own_ref[:, units:] = (
+        dot_tn(g0[...], a0[:, :units]) + dot_tn(g1[...], a1[:, :units])
+    ).astype(BF16)
 
 
 def ffn_grads(n, g, grad_hidden, active):
-    outs = shaped((n[0].shape[1], active[0].shape[1]), BF16)
-    return kernel_call(ffn_grads_body, (outs, outs), "ffn_grads", 6)(
-        *n, *g, *grad_hidden, *active
-    )
-
-
-def attn_grads_body(x_ref, gp_ref, g_ref, att_ref, own_ref, mate_ref, out_ref):
+    model, units = n[0].shape[1], active[0].shape[1]
+    outs = (shaped((model, units), BF16),) + (shaped((model, PIECE), BF16),) * (units // PIECE)
+    own, *mate = kernel_call(ffn_grads_body, outs, "ffn_grads", 6)(*n, *g, *grad_hidden, *active)
+    return own, mate
+
+
+def attn_grads_body(x_ref, gp_ref, g_ref, att_ref, own_ref, *refs):
+    *mate_refs, out_ref = refs
     first = own_ref.shape[1]
     joined = first + gp_ref.shape[1]
-    out_ref[:, :first] = (own_ref[...].astype(F32) + mate_ref[...].astype(F32)).astype(BF16)
+    for i, mate_ref in enumerate(mate_refs):
+        lanes = slice(i * PIECE, (i + 1) * PIECE)
+        out_ref[:, lanes] = (own_ref[:, lanes].astype(F32) + mate_ref[...].astype(F32)).astype(BF16)
     out_ref[:, first:joined] = dot_tn(x_ref[...], gp_ref[...]).astype(BF16)
     out_ref[:, joined:] = lax.dot_general(
         g_ref[...], att_ref[...], (((0,), (1,)), ((), ())), preferred_element_type=F32
@@ -872,11 +952,11 @@
     columns = own.shape[1] + joined.shape[1] + attended_t.shape[0]
     outs = shaped((x.shape[1], columns), BF16)
     return kernel_call(attn_grads_body, outs, "attn_grads", 8)(
-        x, joined, g, attended_t, own, mate
-    )
-
-
-def halved(side, count, bit, rows_of, keep_ref, send_ref):
+        x, joined, g, attended_t, own, *mate
+    )
+
+
+def halved(side, count, bit, rows_of, keep_ref, send_ref, lanes=slice(None)):
     block = keep_ref.shape[0] * 2 // count
     place = 0
     for j in range(count):
@@ -884,8 +964,8 @@
             continue
         low, high = rows_of(j * block, block), rows_of((j | bit) * block, block)
         here = slice(place, place + block)
-        keep_ref[here] = jnp.where(side == 0, low, high).astype(BF16)
-        send_ref[here] = jnp.where(side == 0, high, low).astype(BF16)
+        keep_ref[here, lanes] = jnp.where(side == 0, low, high).astype(BF16)
+        send_ref[here, lanes] = jnp.where(side == 0, high, low).astype(BF16)
         place += block
 
 
@@ -894,14 +974,18 @@
 
 
 def ffn_cut(side, own, mate, count, bit):
-    def body(side_ref, own_ref, mate_ref, keep_ref, send_ref):
-        def rows_of(first, size):
-            here = slice(first, first + size)
-            return own_ref[here].astype(F32) + mate_ref[here].astype(F32)
-
-        halved(side_ref[0], count, bit, rows_of, keep_ref, send_ref)
-
-    return kernel_call(body, halves_of(*own.shape), "ffn_cut", 3, 1)(side, own, mate)
+    def body(side_ref, own_ref, *refs):
+        *mate_refs, keep_ref, send_ref = refs
+        for i, mate_ref in enumerate(mate_refs):
+            lanes = slice(i * PIECE, (i + 1) * PIECE)
+
+            def rows_of(first, size, mate_ref=mate_ref, lanes=lanes):
+                here = slice(first, first + size)
+                return own_ref[here, lanes].astype(F32) + mate_ref[here].astype(F32)
+
+            halved(side_ref[0], count, bit, rows_of, keep_ref, send_ref, lanes)
+
+    return kernel_call(body, halves_of(*own.shape), "ffn_cut", 3, 1)(side, own, *mate)
 
 
 def mixer_grads(side, x, joined, g, mixed, count, bit):
@@ -919,6 +1003,77 @@
     )(side, x, joined, g, mixed)
 
 
+def scatter_step(side, keep, received, count, bit):
+    def body(side_ref, kept_ref, received_ref, keep_ref, send_ref):
+        def rows_of(first, size):
+            here = slice(first, first + size)
+            return kept_ref[here].astype(F32) + received_ref[here].astype(F32)
+
+        halved(side_ref[0], count, bit, rows_of, keep_ref, send_ref)
+
+    return kernel_call(body, halves_of(*keep.shape), "scatter_step", 2, 1)(side, keep, received)
+
+
+def small_cut(side, taps, tiles, count, bit):
+    width = taps.shape[1]
+    starts = [0] * len(tiles)
+    for i in range(1, len(tiles)):
+        starts[i] = starts[i - 1] + tiles[i - 1][0].shape[1]
+
+    def body(side_ref, taps_ref, *refs):
+        *tile_refs, keep_ref, send_ref, total = refs
+        total[:, :width] = taps_ref[...]
+        for i, start in enumerate(starts):
+            size = tile_refs[2 * i].shape[1]
+            total[:, width + start : width + start + size] = tile_refs[2 * i][...]
+            total[:, 2 * width + start : 2 * width + start + size] = tile_refs[2 * i + 1][...]
+        halved(
+            side_ref[0], count, bit, lambda first, size: total[first : first + size], keep_ref, send_ref
+        )
+
+    shape = (taps.shape[0], 3 * width)
+    return kernel_call(
+        body, halves_of(*shape), "small_cut", 2, 1, [pltpu.VMEM(shape, F32)]
+    )(side, taps, *[x for tile in tiles for x in tile])
+
+
+def summed(parts, lanes):
+    total = parts[0][:, lanes].astype(F32)
+    for part in parts[1:]:
+        total = total + part[:, lanes].astype(F32)
+    return total
+
+
+def finish(parts, ffn_parts, first, ffn_first, weights, up, gain, ffn_gain):
+    rows, width = weights[0].shape
+    units = up.shape[1]
+    count = len(parts)
+
+    def body(wq_ref, wk_ref, wv_ref, up_ref, gain_ref, ffn_gain_ref, *refs):
+        part_refs, ffn_refs = refs[:count], refs[count : 2 * count]
+        q_ref, k_ref, v_ref, o_ref, up_grad_ref, down_ref, gain_grad_ref = refs[2 * count :]
+        weighted = None
+        for i, (w_ref, out_ref) in enumerate(((wq_ref, q_ref), (wk_ref, k_ref), (wv_ref, v_ref))):
+            grad = summed(part_refs, slice(first + i * width, first + (i + 1) * width))
+            out_ref[...] = grad
+            grad = grad * w_ref[...].astype(F32)
+            weighted = grad if weighted is None else weighted + grad
+        o_ref[...] = summed(part_refs, slice(first + 3 * width, first + 4 * width)).T
+        gain_grad_ref[:1] = jnp.sum(weighted.T, axis=0, keepdims=True) / gain_ref[...]
+        grad = summed(ffn_refs, slice(ffn_first, ffn_first + units))
+        up_grad_ref[...] = grad
+        down_ref[...] = summed(ffn_refs, slice(ffn_first + units, ffn_first + 2 * units)).T
+        weighted = grad * up_ref[...].astype(F32)
+        gain_grad_ref[1:] = jnp.sum(weighted.T, axis=0, keepdims=True) / ffn_gain_ref[...]
+
+    square = shaped((rows, width), F32)
+    outs = (
+        square, square, square, shaped((width, rows), F32),
+        shaped((rows, units), F32), shaped((units, rows), F32), shaped((2, rows), F32),
+    )
+    return kernel_call(body, outs, "finish", 5)(*weights, up, gain, ffn_gain, *parts, *ffn_parts)
+
+
 TENSOR = "tensor"
 DATA = "dp"
 
@@ -1000,7 +1155,7 @@
         for step in steps:
             keep, send = self.cut(x, step)
             x = keep.astype(F32) + self.swap(send, self.bits[step]).astype(F32)
-        return x.reshape(x.shape[-2:])
+        return x
 
 
 def on_device(
@@ -1099,8 +1254,8 @@
         core, seq_lengths, pieces, attn_w
     )
     pairs, received = exchanged(keep, send)
-
     ffn2_w = after(ffn2_w, pairs[1])
+
     ffn2_mate = from_mate(ffn2_w)
     grad = [jnp.where(chip == 0, masked, grad_other), jnp.where(chip == 0, grad_other, masked)]
     g4 = list(grad)
@@ -1123,27 +1278,24 @@
     lows.append(low)
     gh, act = after((gh, act), low)
     own, mate = ffn_grads(n4, g4, gh, act)
-    wait = after(arrived[1], mate)
+    wait = after(arrived[1], mate[-1])
     grad[1], low = back_step(grad[1], nexts[1], wait, after_attn[1], gains[3])
     lows.append(low)
     pieces = [lows[0], from_mate(after(lows[0], low)), lows[1], from_mate(lows[1])]
-    ffn2_mate_g = from_mate(after(mate, pieces[1], pieces[3]))
+    ffn2_mate_g = [from_mate(x) for x in after(tuple(mate), pieces[1], pieces[3])]
     keep, send, g3, grad_joined = attn_backward_kernel(
         core, seq_lengths, pieces, attn_w, q2, k2, v2, log_total
     )
     pairs, received = exchanged(keep, send)
     own, ffn2_mate_g = after((own, ffn2_mate_g), pairs[1])
     second_p = attn_grads(x3, grad_joined, g3, attended_t, own, ffn2_mate_g)
-    second_g = lax.psum_scatter(second_p, DATA, scatter_dimension=0, tiled=True)
     step = rows.depth - 1
-    received[0] = after(received[0], second_p)
-    final = ffn_out(*after(tuple(act), second_p), ffn2_w, ffn2_mate)
-    final_sent = jnp.where(chip == 0, final[1], final[0])
-    received[0], final_sent = tie(received[0], final_sent)
+    final_own, final_sent = ffn_out(chips, *after(tuple(act), second_p), ffn2_w, ffn2_mate)
+    received = list(after(tuple(received), second_p, final_sent))
 
     g2, gh, act_b, nexts, arrived = [], [], [], [], []
     for half in range(2):
-        wait = received[0] if half == 0 else after(received[1], nexts[0])
+        wait = received[half]
         grad[half], low, grad_hidden, active, out = ffn_backward(
             grad[half].astype(F32), pairs[half], wait, after_ffn1[half], gains[2], hidden1[half],
             ffn1_w, ffn1_mate,
@@ -1153,83 +1305,108 @@
         act_b.append(active)
         nexts.append(out)
         arrived.append(from_chip(out))
+    second_g = lax.psum_scatter(after(second_p, nexts[0]), DATA, scatter_dimension=0, tiled=True)
     lows = []
     wait = after(arrived[0], nexts[1])
     grad[0], low = back_step(grad[0], nexts[0], wait, after_mixer[0], gains[1])
     lows.append(low)
     gh, act_b = after((gh, act_b), low)
     own, mate = ffn_grads(n2, g2, gh, act_b)
-    wait = after(arrived[1], mate)
+    wait = after(arrived[1], mate[-1])
     grad[1], low = back_step(grad[1], nexts[1], wait, after_mixer[1], gains[1])
     lows.append(low)
-    final_sent = after(final_sent, low)
-    mate_g = from_mate(after(mate, low))
     pieces = [lows[0], from_mate(lows[0]), lows[1], from_mate(lows[1])]
+    mate_g = [from_mate(x) for x in after(tuple(mate), pieces[1], arrived[1])]
     mate_g, pieces[1], pieces[3] = tie(mate_g, pieces[1], pieces[3])
     ffn1_keep, ffn1_send = ffn_cut(rows.side(step), own, mate_g, rows.count, rows.bits[step])
     pieces[0], ffn1_send, final_sent = tie(pieces[0], ffn1_send, final_sent)
+    final_received = from_chip(final_sent)
     ffn1_received = rows.swap(ffn1_send, rows.bits[step])
-    final_received = from_chip(final_sent)
     keep, send, g1, grad_joined, grad_taps, *g_spectrum = mixer_backward_kernel(
         core, pieces, mixer_w, saved[:6], spectra, fwd, inv, states
     )
-    final_received = after(final_received, keep)
+    output = output_step(chips, after_attn, final_own, after(final_received, keep))
     mixer_keep, mixer_send = mixer_grads(
         rows.side(step - 1), x1, grad_joined, g1, mixed, rows.count, rows.bits[step - 1]
     )
     mixer_received = rows.swap(mixer_send, rows.bits[step - 1])
-    g_spectrum = after(tuple(g_spectrum), mixer_send, second_g)
-    grad_decay, grad_coef = ssm_grad_kernel(g_spectrum, saved[6:], decay_t, coef_t, inv)
-    ffn1_received, send = after((ffn1_received, send), grad_decay)
-    last = core_sums(keep, send)
-    last_sent = jnp.where(chip == 0, last[1], last[0])
+    own, last_sent = own_half(chips, keep, from_mate(after(send, mixer_send)))
     last_received = from_chip(last_sent)
-    ffn1_g = rows.without(ffn1_keep.astype(F32) + ffn1_received.astype(F32), step)
-    ffn1_keep, ffn1_send = rows.cut(ffn1_g, step - 1)
+    g_spectrum = after(tuple(g_spectrum), last_sent)
+    ssm = [ssm_grad_kernel(g_spectrum, saved[6:], decay_t, coef_t, inv, 0)]
+
+    half, pair = rows.count // 2, rows.count // 4
+
+    def send_on(arrays, step, *ready):
+        return [rows.swap(x, rows.bits[step]) for x in arrays]
+
+    ffn1_received = after(ffn1_received, ssm[0][0])
+    ffn1_keep, ffn1_send = scatter_step(rows.side(step - 1), ffn1_keep, ffn1_received, half, 1)
+    mixer_received = after(mixer_received, ffn1_send)
+    mixer_keep, mixer_send = scatter_step(rows.side(step), mixer_keep, mixer_received, half, 1)
     ffn1_received = rows.swap(ffn1_send, rows.bits[step - 1])
-    mixer_received = after(mixer_received, ffn1_send)
-    mixer_g = rows.without(mixer_keep.astype(F32) + mixer_received.astype(F32), step - 1)
-    small_g = rows.parts(jnp.concatenate([grad_taps, grad_decay, grad_coef], axis=1))
-    mixer_g, small_g, last_received = tie(mixer_g, small_g, last_received)
-    rest = list(reversed(range(step - 1)))
-    mixer_g = rows.scatter(mixer_g, [step] + rest)
-    small_g = rows.scatter(small_g, [step, step - 1] + rest)
-    ffn1_g = rows.scatter(ffn1_keep.astype(F32) + ffn1_received.astype(F32), rest)
-    output = jnp.where(chip == 0, after_attn[0], after_attn[1]) + (
-        jnp.where(chip == 0, final[0], final[1]).astype(F32) + final_received.astype(F32)
-    )
-    second_g = second_g.astype(F32)
-    ffn2_g, attn_g = second_g[:, : 2 * units], second_g[:, 2 * units :]
-    input_grad = last_back(chips, grad, last, start, last_received, gains[0])
-
-    def gain_sum(grads, weights, gain):
-        products = sum(g * w.astype(F32) for g, w in zip(grads, weights))
-        return jnp.sum(products, axis=1) / gain.astype(F32)
-
-    def cut(grads, size):
-        return [grads[:, i : i + size] for i in range(0, grads.shape[1], size)]
-
-    mq, mk, mv, mo = cut(mixer_g, width)
-    aq, ak, av, ao = cut(attn_g, width)
-    u1, d1 = cut(ffn1_g, units)
-    u2, d2 = cut(ffn2_g, units)
-    gt, gd, gc = cut(small_g, width)
-    gain_grads = jnp.stack(
-        [
-            gain_sum((mq, mk, mv), (mixer_query, mixer_key, mixer_value), gain_mixer),
-            gain_sum((u1,), (ffn1_up,), gain_ffn1),
-            gain_sum((aq, ak, av), (attn_query, attn_key, attn_value), gain_attn),
-            gain_sum((u2,), (ffn2_up,), gain_ffn2),
-        ]
-    )
-    gain_grads = gain_grads + swap(gain_grads, 1)
-    gain_grads = gain_grads + swap(gain_grads, 2)
+    mixer_received = rows.swap(mixer_send, rows.bits[step])
+    g_spectrum = after(g_spectrum, mixer_send)
+    ssm += [
+        ssm_grad_kernel(g_spectrum, saved[6:], decay_t, coef_t, inv, i)
+        for i in range(1, len(channel_tiles(width)))
+    ]
+    small_keep, small_send = small_cut(
+        rows.side(step), grad_taps, ssm, rows.count, rows.bits[step]
+    )
+    small_received = rows.swap(small_send, rows.bits[step])
+    ffn1_received, mixer_received, last_received, small_received = tie(
+        *after((ffn1_received, mixer_received, last_received, small_received), small_send)
+    )
+    ffn1_keep, ffn1_send = scatter_step(rows.side(step - 2), ffn1_keep, ffn1_received, pair, 1)
+    mixer_received, small_received = after((mixer_received, small_received), ffn1_send)
+    mixer_keep, mixer_send = scatter_step(rows.side(step - 2), mixer_keep, mixer_received, pair, 1)
+    small_keep, small_send = scatter_step(
+        rows.side(step - 1), small_keep, after(small_received, mixer_send), half, 1
+    )
+    ffn1_send, mixer_send, small_send = tie(ffn1_send, mixer_send, small_send)
+    ffn1_received = rows.swap(ffn1_send, rows.bits[step - 2])
+    mixer_received = rows.swap(mixer_send, rows.bits[step - 2])
+    small_received = rows.swap(small_send, rows.bits[step - 1])
+    input_grad = last_back(chips, grad, start, own, after(last_received, small_send), gains[0])
+    small_keep, small_send = scatter_step(rows.side(step - 2), small_keep, small_received, pair, 1)
+    small_received = rows.swap(small_send, rows.bits[step - 2])
+    second_g = [after(second_g, small_send)]
+
+    def column(gain):
+        return gain.astype(F32)[None, :]
+
+    aq, ak, av, ao, u2, d2, gains_second = finish(
+        second_g, second_g, 2 * units, 0, (attn_query, attn_key, attn_value), ffn2_up,
+        column(gain_attn), column(gain_ffn2),
+    )
+    ffn1_received, mixer_received, small_received = after(
+        (ffn1_received, mixer_received, small_received), gains_second
+    )
+    level, tail = pair // 2, step - 3
+    while tail >= 0:
+        ffn1_keep, ffn1_send = scatter_step(rows.side(tail), ffn1_keep, ffn1_received, level, 1)
+        mixer_keep, mixer_send = scatter_step(rows.side(tail), mixer_keep, mixer_received, level, 1)
+        small_keep, small_send = scatter_step(rows.side(tail), small_keep, small_received, level, 1)
+        ffn1_received = rows.swap(ffn1_send, rows.bits[tail])
+        mixer_received = rows.swap(mixer_send, rows.bits[tail])
+        small_received = rows.swap(small_send, rows.bits[tail])
+        level, tail = level // 2, tail - 1
+    mq, mk, mv, mo, u1, d1, gains_first = finish(
+        [mixer_keep, mixer_received], [ffn1_keep, ffn1_received], 0, 0,
+        (mixer_query, mixer_key, mixer_value), ffn1_up, column(gain_mixer), column(gain_ffn1),
+    )
+    small_g = small_keep.astype(F32) + small_received.astype(F32)
+    gt, gd, gc = (small_g[:, i * width : (i + 1) * width] for i in range(3))
+    first_gains, second_gains = (
+        g + swap(g, 1) + (swap(g, 2) + swap(g, 3)) for g in (gains_first, gains_second)
+    )
     return (
-        output.astype(BF16), input_grad,
-        gain_grads[0], mq, mk, mv, gt, gd.T, gc.T, mo.T,
-        gain_grads[1], u1, d1.T,
-        gain_grads[2], aq, ak, av, ao.T,
-        gain_grads[3], u2, d2.T,
+        output, input_grad,
+        first_gains[0], mq, mk, mv, gt, gd.T, gc.T, mo,
+        first_gains[1], u1, d1,
+        second_gains[0], aq, ak, av, ao,
+        second_gains[1], u2, d2,
     )
 
 

time: 423 us -> 410 us (0.969)
  waiting for transfers between devices: 118 us -> 87 us
  Pallas kernels: 184 us -> 200 us
  starting transfers between devices: 41.9 us -> 52.3 us
  other arithmetic: 20.1 us -> 11.2 us
    pallas_call x20 -> x31, Pallas kernels: 98.5 us -> 122 us  [call(): pl.pallas_call(body, in_specs=[SCALAR] * scalars + [WHOLE] * (len(args) -...]
    ppermute x15, waiting for transfers between devices: 63.6 us -> 40.8 us  [swap(): return lax.ppermute(x, DATA, [(i, i ^ bit) for i in range(self.count)])]
    ppermute x34 -> x48, waiting for transfers between devices: 54.2 us -> 44.1 us  [swap(): return lax.ppermute(x, TENSOR, [(i, i ^ bit) for i in range(4)])]
    ppermute x34 -> x48, starting transfers between devices: 19.8 us -> 25.1 us  [swap(): return lax.ppermute(x, TENSOR, [(i, i ^ bit) for i in range(4)])]
    ppermute x15, starting transfers between devices: 21.7 us -> 26.8 us  [swap(): return lax.ppermute(x, DATA, [(i, i ^ bit) for i in range(self.count)])]
    unnamed x133 -> x166, local copies, waits for them, and re-layouts: 20.3 us -> 24.5 us
    pallas_call x1 -> x2, Pallas kernels: 19.1 us -> 15.6 us  [ssm_grad_kernel(): pl.pallas_call(body, out_shape=(out, out), scratch_shapes=[pltpu.VMEM((bl...]
  transfers between devices with their start and end apart: 52 -> 66, of which waited for: 26 -> 29; matrix products, arithmetic and copies ran while one was open for 9% -> 6% of each run, Pallas kernels for 42% -> 43%
where the time goes in v4:
time: 410 us; the launch traced here: 403 us
  Pallas kernels  200 us (49%)
  waiting for transfers between devices  87 us (21%)
  starting transfers between devices  52.3 us (13%)
  local copies, waits for them, and re-layouts  37.2 us (9%)
  between operations  15.6 us (4%)
  other arithmetic  11.2 us (3%)
    pallas_call x31, Pallas kernels, call(): pl.pallas_call(body, in_specs=[SCALAR] * scalars + [WHOLE] * (len(args) -...  122 us
    ppermute x48, waiting for transfers between devices, swap(): return lax.ppermute(x, TENSOR, [(i, i ^ bit) for i in range(4)])  44.1 us
    ppermute x15, waiting for transfers between devices, swap(): return lax.ppermute(x, DATA, [(i, i ^ bit) for i in range(self.count)])  40.8 us
    ppermute x15, starting transfers between devices, swap(): return lax.ppermute(x, DATA, [(i, i ^ bit) for i in range(self.count)])  26.8 us
    ppermute x48, starting transfers between devices, swap(): return lax.ppermute(x, TENSOR, [(i, i ^ bit) for i in range(4)])  25.1 us
    unnamed x166, local copies, waits for them, and re-layouts  24.5 us
    pallas_call x2, Pallas kernels, ssm_grad_kernel(): pl.pallas_call(body, out_shape=(out, out), scratch_shapes=[pltpu.VMEM((bl...  15.6 us
    pallas_call x1, Pallas kernels, attn_backward_kernel(): pl.pallas_call(attn_bwd_body, in_specs=[SCALAR, SCALAR] + [WHOLE] * 9, ou...  14.7 us
  transfers between devices with their start and end apart: 66, of which 29 were waited for; matrix products, arithmetic and copies ran while one was open for 6% of the time, Pallas kernels for 43%

profile of v4, /device:TPU:0, one launch (start us, length us, event | category | flops | bytes accessed | tf_op | source)
XLA Modules:
  0.0 402.8 jit_solution(10830388575551583869)
XLA Ops:
  22.6 4.9 %collective-permute-done.2 = bf16[2,16,768]{2,1,0:T(8,128)(2,1)S(1)} collective-permute-done((bf16[2,16,768]{2,1,0:T(8,128)(2,1)S(1)}, bf16[2,16,768]{2,1,0:T(8,128)(2,1)S(1)}, u32[]{:S(2)}, u32[]{:S(2)}) %collective-permute-start.2) | collective-permute-done | bytes 49184 | tf_op jit(solution)/shard_map/ppermute | solution.py:1117
  32.6 14.3 %collective-permute-done.5 = bf16[2,96,768]{2,1,0:T(8,128)(2,1)S(1)} collective-permute-done((bf16[2,96,768]{2,1,0:T(8,128)(2,1)S(1)}, bf16[2,96,768]{2,1,0:T(8,128)(2,1)S(1)}, u32[]{:S(2)}, u32[]{:S(2)}) %collective-permute-start.5) | collective-permute-done | bytes 294944 | tf_op jit(solution)/shard_map/ppermute | solution.py:1117
  55.1 10.3 %kernel_spectra.1 = (f32[8,128,192]{2,1,0:T(8,128)}, f32[8,128,192]{2,1,0:T(8,128)}, f32[128,192]{1,0:T(8,128)}, f32[128,192]{1,0:T(8,128)}) custom-call(f32[64,192]{1,0:T(8,128)} %get-tuple-element.276.decay_ref, f32[64,192]{1,0:T(8,128)} %get-tuple-element.579.coef_ref, f32[64,192]{1,0:T(8,128)} %get-tuple-element.578.taps_ref, ...), custom_call_target="tpu_custom_call" | custom-call | flops 1210000000 | bytes 3850000 | tf_op jit(solution)/shard_map/kernel_spectra/pallas_call | solution.py:157
  65.4 8.1 %collective-permute-done.8 = bf16[2,2,96,768]{3,2,1,0:T(8,128)(2,1)S(1)} collective-permute-done((bf16[2,2,96,768]{3,2,1,0:T(8,128)(2,1)S(1)}, bf16[2,2,96,768]{3,2,1,0:T(8,128)(2,1)S(1)}, u32[]{:S(2)}, u32[]{:S(2)}) %collective-permute-start.8) | collective-permute-done | bytes 589856 | tf_op jit(solution)/shard_map/ppermute | solution.py:1117
  75.7 11.5 %mixer_forward.1 = (bf16[2,256,768]{2,1,0:T(8,128)(2,1)}, bf16[2,256,768]{2,1,0:T(8,128)(2,1)}, bf16[1024,768]{1,0:T(8,128)(2,1)}, bf16[1024,192]{1,0:T(8,128)(2...) custom-call(s32[1]{0:T(128)} %bitcast.23.core_ref, ...), custom_call_target="tpu_custom_call" | custom-call | flops 1540000000 | bytes 4900000 | tf_op jit(solution)/shard_map/mixer_forward/pallas_call | solution.py:290
  99.0 9.3 %collective-permute-done.11.received_ref = bf16[256,768]{1,0:T(8,128)(2,1)} collective-permute-done((bf16[256,768]{1,0:T(8,128)(2,1)S(1)}, bf16[256,768]{1,0:T(8,128)(2,1)}, u32[]{:S(2)}, u32[]{:S(2)}) %collective-permute-start.11) | collective-permute-done | bytes 393248 | tf_op jit(solution)/shard_map/ppermute | solution.py:1082
  108.4 5.7 %ffn_forward.2 = (f32[256,768]{1,0:T(8,128)}, bf16[256,768]{1,0:T(8,128)(2,1)}, f32[256,1536]{1,0:T(8,128)}, bf16[256,768]{1,0:T(8,128)(2,1)}) custom-call(f32[256,768]{1,0:T(8,128)} %get-tuple-element.271.h_ref.h0, bf16[256,768]{1,0:T(8,128)(2,1)} %copy-done.24, bf16[256,768]{1,0:T(8,128)(2,1)} %collective-permute-done.11.received_ref, ...), custom_call_target="tpu_custom_call" | custom-call | flops 5500000256 | bytes 17500000 | tf_op jit(solution)/shard_map/ffn_forward/pallas_call | solution.py:666
  117.1 5.7 %ffn_forward.3 = (f32[256,768]{1,0:T(8,128)}, bf16[256,768]{1,0:T(8,128)(2,1)}, f32[256,1536]{1,0:T(8,128)}, bf16[256,768]{1,0:T(8,128)(2,1)}) custom-call(f32[256,768]{1,0:T(8,128)} %get-tuple-element.288.h_ref.h1, bf16[256,768]{1,0:T(8,128)(2,1)} %copy-done.19, bf16[256,768]{1,0:T(8,128)(2,1)} %copy-done.69, f32[1,768]{1,0:T(1,128)} %squeeze.20.gain_ref, ...), custom_call_target="tpu_custom_call" | custom-call | flops 5500000256 | bytes 17500000 | tf_op jit(solution)/shard_map/ffn_forward/pallas_call | solution.py:666
  127.8 5.5 %collective-permute-done.16.received_ref = bf16[256,768]{1,0:T(8,128)(2,1)S(1)} collective-permute-done((bf16[256,768]{1,0:T(8,128)(2,1)}, bf16[256,768]{1,0:T(8,128)(2,1)S(1)}, u32[]{:S(2)}, u32[]{:S(2)}) %collective-permute-start.16) | collective-permute-done | bytes 393248 | tf_op jit(solution)/shard_map/ppermute | solution.py:1082
  141.1 11.5 %attn_forward.1 = (bf16[2,256,768]{2,1,0:T(8,128)(2,1)}, bf16[2,256,768]{2,1,0:T(8,128)(2,1)}, bf16[1024,768]{1,0:T(8,128)(2,1)}, bf16[1024,192]{1,0:T(8,128)(2,...) custom-call(s32[1]{0:T(128)} %bitcast.23.core_ref, ...), custom_call_target="tpu_custom_call" | custom-call | flops 1320000000 | bytes 4200000 | tf_op jit(solution)/shard_map/attn_forward/pallas_call | solution.py:578
  161.7 7.0 %collective-permute-done.19.received_ref = bf16[256,768]{1,0:T(8,128)(2,1)} collective-permute-done((bf16[256,768]{1,0:T(8,128)(2,1)S(1)}, bf16[256,768]{1,0:T(8,128)(2,1)}, u32[]{:S(2)}, u32[]{:S(2)}) %collective-permute-start.19) | collective-permute-done | bytes 393248 | tf_op jit(solution)/shard_map/ppermute | solution.py:1082
  170.1 6.4 %ffn_both.2 = (f32[256,768]{1,0:T(8,128)}, bf16[256,768]{1,0:T(8,128)(2,1)}, bf16[256,1536]{1,0:T(8,128)(2,1)}, bf16[256,1536]{1,0:T(8,128)(2,1)}, bf16[256,768]{1,0:T(8,128)(2,1)}) custom-call(f32[256,768]{1,0:T(8,128)} %get-tuple-element.292.h_ref, bf16[256,768]{1,0:T(8,128)(2,1)} %copy-done.26, bf16[256,768]{1,0:T(8,128)(2,1)} %collective-permute-done.19.received_ref, ...), custom_call_target="tpu_custom_call" | custom-call | flops 6600000000 | bytes 21000000 | tf_op jit(solution)/shard_map/ffn_both/pallas_call | solution.py:666
  178.3 6.4 %ffn_both.3 = (f32[256,768]{1,0:T(8,128)}, bf16[256,768]{1,0:T(8,128)(2,1)}, bf16[256,1536]{1,0:T(8,128)(2,1)}, bf16[256,1536]{1,0:T(8,128)(2,1)}, bf16[256,768]{1,0:T(8,128)(2,1)}) custom-call(f32[256,768]{1,0:T(8,128)} %get-tuple-element.306.h_ref, bf16[256,768]{1,0:T(8,128)(2,1)} %copy-done.18, bf16[256,768]{1,0:T(8,128)(2,1)} %copy-done.68, ...), custom_call_target="tpu_custom_call" | custom-call | flops 6600000000 | bytes 21000000 | tf_op jit(solution)/shard_map/ffn_both/pallas_call | solution.py:666
  190.9 6.4 %ffn_grads.2 = (bf16[768,1536]{1,0:T(8,128)(2,1)}, bf16[768,256]{1,0:T(8,128)(2,1)}, bf16[768,256]{1,0:T(8,128)(2,1)}, bf16[768,256]{1,0:T(8,128)(2,1)}, bf16[76...) custom-call(bf16[256,768]{1,0:T(8,128)(2,1)} %get-tuple-element.320.n0, ...), custom_call_target="tpu_custom_call" | custom-call | flops 660000000 | bytes 2100000 | tf_op jit(solution)/shard_map/ffn_grads/pallas_call | solution.py:666
  204.4 14.7 %attn_backward.1 = (bf16[2,256,768]{2,1,0:T(8,128)(2,1)}, bf16[2,256,768]{2,1,0:T(8,128)(2,1)}, bf16[1024,768]{1,0:T(8,128)(2,1)}, bf16[1024,576]{1,0:T(8,128)(2,1)}) custom-call(s32[1]{0:T(128)} %bitcast.23.core_ref, s32[1]{0:T(128)} %copy.71.len_ref, bf16[256,768]{1,0:T(8,128)(2,1)} %get-tuple-element.327.a_ref, bf16[256,768]{1,0:T(8,128)(2,1)} %copy-done.71, ...), custom_call_target="tpu_custom_call" | custom-call | flops 1540000000 | bytes 4900000 | tf_op jit(solution)/shard_map/attn_backward/pallas_call | solution.py:641
  227.0 8.5 %attn_grads.1 = bf16[768,2304]{1,0:T(8,128)(2,1)} custom-call(bf16[1024,768]{1,0:T(8,128)(2,1)} %get-tuple-element.319.x_ref, bf16[1024,576]{1,0:T(8,128)(2,1)} %get-tuple-element.332.gp_ref, bf16[1024,768]{1,0:T(8,128)(2,1)} %get-tuple-element.333.g_ref, bf16[192,1024]{1,0:T(8,128)(2,1)} %get-tuple-element.334.att_ref, ...), custom_call_target="tpu_custom_call" | custom-call | flops 880000000 | bytes 2800000 | tf_op jit(solution)/shard_map/attn_grads/pallas_call | solution.py:666
  235.5 5.2 %ffn_out.1 = (bf16[256,768]{1,0:T(8,128)(2,1)}, bf16[256,768]{1,0:T(8,128)(2,1)}) custom-call(s32[1]{0:T(128)} %bitcast.chip_ref, bf16[256,1536]{1,0:T(8,128)(2,1)} %get-tuple-element.356.a0.a0_ref, bf16[256,1536]{1,0:T(8,128)(2,1)} %get-tuple-element.357.a1.a1_ref, bf16[768,1536]{1,0:T(8,128)(2,1)} %all-gather.5.cloned.1.call-done.own_ref, ...), custom_call_target="tpu_custom_call" | custom-call | flops 330000000 | bytes 1050000 | tf_op jit(solution)/shard_map/ffn_out/pallas_call | solution.py:666
  243.5 7.1 %ffn_backward.2 = (f32[256,768]{1,0:T(8,128)}, bf16[256,768]{1,0:T(8,128)(2,1)}, bf16[256,1536]{1,0:T(8,128)(2,1)}, bf16[256,1536]{1,0:T(8,128)(2,1)}, bf16[256,768]{1,0:T(8,128)(2,1)}) custom-call(f32[256,768]{1,0:T(8,128)} %get-tuple-element.359.g_ref, bf16[256,768]{1,0:T(8,128)(2,1)} %copy-done.17, bf16[256,768]{1,0:T(8,128)(2,1)} %copy-done.62, ...), custom_call_target="tpu_custom_call" | custom-call | flops 6600000000 | bytes 21000000 | tf_op jit(solution)/shard_map/ffn_backward/pallas_call | solution.py:666
  252.8 6.7 %ffn_backward.3 = (f32[256,768]{1,0:T(8,128)}, bf16[256,768]{1,0:T(8,128)(2,1)}, bf16[256,1536]{1,0:T(8,128)(2,1)}, bf16[256,1536]{1,0:T(8,128)(2,1)}, bf16[256,768]{1,0:T(8,128)(2,1)}) custom-call(f32[256,768]{1,0:T(8,128)} %get-tuple-element.365.g_ref, bf16[256,768]{1,0:T(8,128)(2,1)} %copy-done.16, bf16[256,768]{1,0:T(8,128)(2,1)} %copy-done.58, ...), custom_call_target="tpu_custom_call" | custom-call | flops 6600000000 | bytes 21000000 | tf_op jit(solution)/shard_map/ffn_backward/pallas_call | solution.py:666
  266.4 6.5 %ffn_grads.3 = (bf16[768,1536]{1,0:T(8,128)(2,1)}, bf16[768,256]{1,0:T(8,128)(2,1)}, bf16[768,256]{1,0:T(8,128)(2,1)}, bf16[768,256]{1,0:T(8,128)(2,1)}, bf16[76...) custom-call(bf16[256,768]{1,0:T(8,128)(2,1)} %get-tuple-element.371.n0, ...), custom_call_target="tpu_custom_call" | custom-call | flops 660000000 | bytes 2100000 | tf_op jit(solution)/shard_map/ffn_grads/pallas_call | solution.py:666
  289.6 13.6 %mixer_backward.1 = (bf16[2,256,768]{2,1,0:T(8,128)(2,1)}, bf16[2,256,768]{2,1,0:T(8,128)(2,1)}, bf16[1024,768]{1,0:T(8,128)(2,1)}, bf16[1024,576]{1,0:T(8,128)(...) custom-call(s32[1]{0:T(128)} %bitcast.23.core_ref, ...), custom_call_target="tpu_custom_call" | custom-call | flops 1650000000 | bytes 5250000 | tf_op jit(solution)/shard_map/mixer_backward/pallas_call | solution.py:412
  303.2 5.4 %mixer_grads.1 = (bf16[384,768]{1,0:T(8,128)(2,1)}, bf16[384,768]{1,0:T(8,128)(2,1)}) custom-call(s32[1]{0:T(128)} %bitcast.40.side_ref, bf16[1024,768]{1,0:T(8,128)(2,1)} %get-tuple-element.421.x_ref, bf16[1024,576]{1,0:T(8,128)(2,1)} %get-tuple-element.422.gp_ref, bf16[1024,768]{1,0:T(8,128)(2,1)} %get-tuple-element.423.g_ref, ...), custom_call_target="tpu_custom_call" | custom-call | flops 660000000 | bytes 2100000 | tf_op jit(solution)/shard_map/mixer_grads/pallas_call | solution.py:666
  315.5 9.1 %ssm_grad.2 = (f32[64,128]{1,0:T(8,128)}, f32[64,128]{1,0:T(8,128)}) custom-call(bf16[8,128,192]{2,1,0:T(8,128)(2,1)} %get-tuple-element.445.g_re, bf16[8,128,192]{2,1,0:T(8,128)(2,1)} %get-tuple-element.446.g_im, bf16[8,128,192]{2,1,0:T(8,128)(2,1)} %get-tuple-element.435.u_re, bf16[8,128,192]{2,1,0:T(8,128)(2,1)} %get-tuple-element.436.u_im, ...), custom_call_target="tpu_custom_call" | custom-call | flops 1100000000 | bytes 3500000 | tf_op jit(solution)/shard_map/ssm_grad/pallas_call | solution.py:500
  336.6 6.5 %ssm_grad.3 = (f32[64,64]{1,0:T(8,128)}, f32[64,64]{1,0:T(8,128)}) custom-call(bf16[8,128,192]{2,1,0:T(8,128)(2,1)} %get-tuple-element.445.g_re, bf16[8,128,192]{2,1,0:T(8,128)(2,1)} %get-tuple-element.446.g_im, bf16[8,128,192]{2,1,0:T(8,128)(2,1)} %get-tuple-element.435.u_re, bf16[8,128,192]{2,1,0:T(8,128)(2,1)} %get-tuple-element.436.u_im, ...), custom_call_target="tpu_custom_call" | custom-call | flops 1100000000 | bytes 3500000 | tf_op jit(solution)/shard_map/ssm_grad/pallas_call | solution.py:500
  (358 shorter events, 190.9 us)
Async XLA Ops:
  7.2 85.8 %all-gather.3.cloned.1.call-start = ((), (), s32[]{:S(2)}) async-start(), calls=%async_computation.1 | async-start | bytes 3981312 | tf_op jit(solution)/shard_map/all_gather | solution.py:1198
  10.2 146.2 %all-gather.5.cloned.1.call-start = ((), (), s32[]{:S(2)}) async-start(), calls=%async_computation.2 | async-start | bytes 2654208 | tf_op jit(solution)/shard_map/all_gather | solution.py:1233
  17.1 15.1 %collective-permute-start.4 = (bf16[96,768]{1,0:T(8,128)(2,1)S(1)}, bf16[96,768]{1,0:T(8,128)(2,1)S(1)}, u32[]{:S(2)}, u32[]{:S(2)}) collective-permute-start(bf16[96,768]{1,0:T(8,128)(2,1)S(1)} %pad_maximum_fusion.5), channel_id=1, source_target_pairs={{0,16},{4,20},{8,24},{12,28},{16,0},{20,4},{24,8},{28,12},{1,17},{... | collective-permute-start | bytes 442376 | tf_op jit(solution)/shard_map/ppermute | solution.py:1117
  17.2 32.0 %collective-permute-start = (bf16[256,768]{1,0:T(8,128)(2,1)S(1)}, bf16[256,768]{1,0:T(8,128)(2,1)S(1)}, u32[]{:S(2)}, u32[]{:S(2)}) collective-permute-start(bf16[256,768]{1,0:T(8,128)(2,1)S(1)} %copy-done.50), channel_id=1, source_target_pairs={{0,2},{1,3},{2,0},{3,1},{4,6},{5,7},{6,4},{7,5},{8,10},{9,11},{10,... | collective-permute-start | bytes 1179656 | tf_op jit(solution)/shard_map/ppermute | solution.py:1082
  32.5 14.4 %collective-permute-start.5 = (bf16[2,96,768]{2,1,0:T(8,128)(2,1)S(1)}, bf16[2,96,768]{2,1,0:T(8,128)(2,1)S(1)}, u32[]{:S(2)}, u32[]{:S(2)}) collective-permute-start(bf16[2,96,768]{2,1,0:T(8,128)(2,1)S(1)} %pad_maximum_fusion.2), channel_id=1, source_target_pairs={{0,8},{4,12},{8,0},{12,4},{16,24},{20,28},{24,16},{28,20},{1,9},{5... | collective-permute-start | bytes 884744 | tf_op jit(solution)/shard_map/ppermute | solution.py:1117
  47.7 25.7 %collective-permute-start.8 = (bf16[2,2,96,768]{3,2,1,0:T(8,128)(2,1)S(1)}, bf16[2,2,96,768]{3,2,1,0:T(8,128)(2,1)S(1)}, u32[]{:S(2)}, u32[]{:S(2)}) collective-permute-start(bf16[2,2,96,768]{3,2,1,0:T(8,128)(2,1)S(1)} %pad_maximum_fusion.1), channel_id=1, source_target_pairs={{0,4},{4,0},{8,12},{12,8},{16,20},{20,16},{24,28},{28,24},{1,5},{5... | collective-permute-start | bytes 1769480 | tf_op jit(solution)/shard_map/ppermute | solution.py:1117
  53.8 20.9 %collective-permute-start.6 = (bf16[256,768]{1,0:T(8,128)(2,1)}, bf16[256,768]{1,0:T(8,128)(2,1)S(1)}, u32[]{:S(2)}, u32[]{:S(2)}) collective-permute-start(bf16[256,768]{1,0:T(8,128)(2,1)} %get-tuple-element.272.a_ref), channel_id=1, source_target_pairs={{0,1},{1,0},{2,3},{3,2},{4,5},{5,4},{6,7},{7,6},{8,9},{9,8},{10,11... | collective-permute-start | bytes 1179656 | tf_op jit(solution)/shard_map/ppermute | solution.py:1082
  54.6 20.1 %collective-permute-start.7 = (bf16[256,768]{1,0:T(8,128)(2,1)}, bf16[256,768]{1,0:T(8,128)(2,1)S(1)}, u32[]{:S(2)}, u32[]{:S(2)}) collective-permute-start(bf16[256,768]{1,0:T(8,128)(2,1)} %get-tuple-element.273.c_ref), channel_id=1, source_target_pairs={{0,1},{1,0},{2,3},{3,2},{4,5},{5,4},{6,7},{7,6},{8,9},{9,8},{10,11... | collective-permute-start | bytes 1179656 | tf_op jit(solution)/shard_map/ppermute | solution.py:1082
  95.0 13.4 %collective-permute-start.12 = (bf16[768,1536]{1,0:T(8,128)(2,1)S(1)}, bf16[768,1536]{1,0:T(8,128)(2,1)}, u32[]{:S(2)}, u32[]{:S(2)}) collective-permute-start(bf16[768,1536]{1,0:T(8,128)(2,1)S(1)} %slice.158.own_ref), channel_id=1, source_target_pairs={{0,1},{1,0},{2,3},{3,2},{4,5},{5,4},{6,7},{7,6},{8,9},{9,8},{10,11... | collective-permute-start | bytes 7077896 | tf_op jit(solution)/shard_map/ppermute | solution.py:1082
  96.0 280.5 %reduce-scatter.2.cloned.1.call-start = ((), (), s32[]{:S(2)}) async-start(), calls=%async_computation.3 | async-start | bytes 3981312 | tf_op jit(solution)/shard_map/reduce_scatter | solution.py:1308
  98.0 18.3 %collective-permute-start.14 = (bf16[256,768]{1,0:T(8,128)(2,1)S(1)}, bf16[256,768]{1,0:T(8,128)(2,1)S(1)}, u32[]{:S(2)}, u32[]{:S(2)}) collective-permute-start(bf16[256,768]{1,0:T(8,128)(2,1)S(1)} %get-tuple-element.566.pair_ref), channel_id=1, source_target_pairs={{0,2},{1,3},{2,0},{3,1},{4,6},{5,7},{6,4},{7,5},{8,10},{9,11},{10,... | collective-permute-start | bytes 1179656 | tf_op jit(solution)/shard_map/ppermute | solution.py:1082
  160.7 16.8 %collective-permute-start.21 = (bf16[256,768]{1,0:T(8,128)(2,1)S(1)}, bf16[256,768]{1,0:T(8,128)(2,1)S(1)}, u32[]{:S(2)}, u32[]{:S(2)}) collective-permute-start(bf16[256,768]{1,0:T(8,128)(2,1)S(1)} %get-tuple-element.564.pair_ref), channel_id=1, source_target_pairs={{0,2},{1,3},{2,0},{3,1},{4,6},{5,7},{6,4},{7,5},{8,10},{9,11},{10,... | collective-permute-start | bytes 1179656 | tf_op jit(solution)/shard_map/ppermute | solution.py:1082
  184.7 12.7 %collective-permute-start.23 = (bf16[256,768]{1,0:T(8,128)(2,1)}, bf16[256,768]{1,0:T(8,128)(2,1)S(1)}, u32[]{:S(2)}, u32[]{:S(2)}) collective-permute-start(bf16[256,768]{1,0:T(8,128)(2,1)} %get-tuple-element.314.pair_ref), channel_id=1, source_target_pairs={{0,2},{1,3},{2,0},{3,1},{4,6},{5,7},{6,4},{7,5},{8,10},{9,11},{10,... | collective-permute-start | bytes 1179656 | tf_op jit(solution)/shard_map/ppermute | solution.py:1082
  223.9 16.8 %collective-permute-start.33 = (bf16[256,768]{1,0:T(8,128)(2,1)S(1)}, bf16[256,768]{1,0:T(8,128)(2,1)S(1)}, u32[]{:S(2)}, u32[]{:S(2)}) collective-permute-start(bf16[256,768]{1,0:T(8,128)(2,1)S(1)} %get-tuple-element.562.pair_ref), channel_id=1, source_target_pairs={{0,2},{1,3},{2,0},{3,1},{4,6},{5,7},{6,4},{7,5},{8,10},{9,11},{10,... | collective-permute-start | bytes 1179656 | tf_op jit(solution)/shard_map/ppermute | solution.py:1082
  225.1 18.4 %collective-permute-start.34 = (bf16[256,768]{1,0:T(8,128)(2,1)S(1)}, bf16[256,768]{1,0:T(8,128)(2,1)S(1)}, u32[]{:S(2)}, u32[]{:S(2)}) collective-permute-start(bf16[256,768]{1,0:T(8,128)(2,1)S(1)} %get-tuple-element.563.pair_ref), channel_id=1, source_target_pairs={{0,2},{1,3},{2,0},{3,1},{4,6},{5,7},{6,4},{7,5},{8,10},{9,11},{10,... | collective-permute-start | bytes 1179656 | tf_op jit(solution)/shard_map/ppermute | solution.py:1082
  259.5 13.4 %collective-permute-start.37 = (bf16[256,768]{1,0:T(8,128)(2,1)}, bf16[256,768]{1,0:T(8,128)(2,1)S(1)}, u32[]{:S(2)}, u32[]{:S(2)}) collective-permute-start(bf16[256,768]{1,0:T(8,128)(2,1)} %get-tuple-element.368.pair_ref), channel_id=1, source_target_pairs={{0,2},{1,3},{2,0},{3,1},{4,6},{5,7},{6,4},{7,5},{8,10},{9,11},{10,... | collective-permute-start | bytes 1179656 | tf_op jit(solution)/shard_map/ppermute | solution.py:1082
  287.8 37.1 %collective-permute-start.47 = (bf16[384,1536]{1,0:T(8,128)(2,1)}, bf16[384,1536]{1,0:T(8,128)(2,1)S(1)}, u32[]{:S(2)}, u32[]{:S(2)}) collective-permute-start(bf16[384,1536]{1,0:T(8,128)(2,1)} %get-tuple-element.429), channel_id=1, source_target_pairs={{0,4},{4,0},{8,12},{12,8},{16,20},{20,16},{24,28},{28,24},{1,5},{5... | collective-permute-start | bytes 3538952 | tf_op jit(solution)/shard_map/ppermute | solution.py:1117
  308.6 24.1 %collective-permute-start.49 = (bf16[384,768]{1,0:T(8,128)(2,1)}, bf16[384,768]{1,0:T(8,128)(2,1)S(1)}, u32[]{:S(2)}, u32[]{:S(2)}) collective-permute-start(bf16[384,768]{1,0:T(8,128)(2,1)} %get-tuple-element.425), channel_id=1, source_target_pairs={{0,8},{4,12},{8,0},{12,4},{16,24},{20,28},{24,16},{28,20},{1,9},{5... | collective-permute-start | bytes 1769480 | tf_op jit(solution)/shard_map/ppermute | solution.py:1117
  328.8 24.2 %collective-permute-start.48 = (bf16[192,1536]{1,0:T(8,128)(2,1)}, bf16[192,1536]{1,0:T(8,128)(2,1)S(1)}, u32[]{:S(2)}, u32[]{:S(2)}) collective-permute-start(bf16[192,1536]{1,0:T(8,128)(2,1)} %get-tuple-element.439), channel_id=1, source_target_pairs={{0,8},{4,12},{8,0},{12,4},{16,24},{20,28},{24,16},{28,20},{1,9},{5... | collective-permute-start | bytes 1769480 | tf_op jit(solution)/shard_map/ppermute | solution.py:1117
  330.7 15.8 %collective-permute-start.51 = (bf16[256,768]{1,0:T(8,128)(2,1)S(1)}, bf16[256,768]{1,0:T(8,128)(2,1)S(1)}, u32[]{:S(2)}, u32[]{:S(2)}) collective-permute-start(bf16[256,768]{1,0:T(8,128)(2,1)S(1)} %copy-done.60), channel_id=1, source_target_pairs={{0,2},{1,3},{2,0},{3,1},{4,6},{5,7},{6,4},{7,5},{8,10},{9,11},{10,... | collective-permute-start | bytes 1179656 | tf_op jit(solution)/shard_map/ppermute | solution.py:1082
  331.3 31.6 %collective-permute-start.45 = (bf16[256,768]{1,0:T(8,128)(2,1)S(1)}, bf16[256,768]{1,0:T(8,128)(2,1)S(1)}, u32[]{:S(2)}, u32[]{:S(2)}) collective-permute-start(bf16[256,768]{1,0:T(8,128)(2,1)S(1)} %copy-done.51), channel_id=1, source_target_pairs={{0,2},{1,3},{2,0},{3,1},{4,6},{5,7},{6,4},{7,5},{8,10},{9,11},{10,... | collective-permute-start | bytes 1179656 | tf_op jit(solution)/shard_map/ppermute | solution.py:1082
  335.8 13.1 %collective-permute-start.50 = (bf16[192,768]{1,0:T(8,128)(2,1)}, bf16[192,768]{1,0:T(8,128)(2,1)S(1)}, u32[]{:S(2)}, u32[]{:S(2)}) collective-permute-start(bf16[192,768]{1,0:T(8,128)(2,1)} %get-tuple-element.442), channel_id=1, source_target_pairs={{0,4},{4,0},{8,12},{12,8},{16,20},{20,16},{24,28},{28,24},{1,5},{5... | collective-permute-start | bytes 884744 | tf_op jit(solution)/shard_map/ppermute | solution.py:1117
  359.4 23.0 %collective-permute-start.53 = (bf16[96,1536]{1,0:T(8,128)(2,1)S(1)}, bf16[96,1536]{1,0:T(8,128)(2,1)S(1)}, u32[]{:S(2)}, u32[]{:S(2)}) collective-permute-start(bf16[96,1536]{1,0:T(8,128)(2,1)S(1)} %copy-done.74), channel_id=1, source_target_pairs={{0,16},{4,20},{8,24},{12,28},{16,0},{20,4},{24,8},{28,12},{1,17},{... | collective-permute-start | bytes 884744 | tf_op jit(solution)/shard_map/ppermute | solution.py:1117
  361.5 20.8 %collective-permute-start.54 = (bf16[96,768]{1,0:T(8,128)(2,1)}, bf16[96,768]{1,0:T(8,128)(2,1)S(1)}, u32[]{:S(2)}, u32[]{:S(2)}) collective-permute-start(bf16[96,768]{1,0:T(8,128)(2,1)} %get-tuple-element.471), channel_id=1, source_target_pairs={{0,16},{4,20},{8,24},{12,28},{16,0},{20,4},{24,8},{28,12},{1,17},{... | collective-permute-start | bytes 442376 | tf_op jit(solution)/shard_map/ppermute | solution.py:1117
  (123 other events, 746.2 us)
Sparse Core Ops, SparseCore 0:
  10.3 82.7 all-gather.2
  96.1 52.8 all-gather.4
  250.8 98.1 reduce-scatter.1

commit v5 on v4

--- a/solution.py
+++ b/solution.py
@@ -1,3 +1,4 @@
+import math
 import numpy as np
 import jax
 import jax.numpy as jnp
@@ -692,7 +693,8 @@
     scaled = grad_normed * gain
     first_mean = jnp.mean(scaled, axis=1, keepdims=True)
     second_mean = jnp.mean(scaled * unit, axis=1, keepdims=True)
-    return inverse * (scaled - first_mean - unit * second_mean)
+    gain_grad = jnp.sum(grad_normed * unit, axis=0, keepdims=True)
+    return inverse * (scaled - first_mean - unit * second_mean), gain_grad
 
 
 def first_norm_body(chip_ref, mine_ref, other_ref, gain_ref, h0_ref, n0_ref, h1_ref, n1_ref):
@@ -730,16 +732,17 @@
     return kernel_call(norm_body, outs, "norm_step", 1.5)(h, pair, received, gain)
 
 
-def back_body(g_ref, pair_ref, received_ref, h_ref, gain_ref, grad_ref, low_ref):
-    grad = g_ref[...].astype(F32) + norm_gradient(
+def back_body(g_ref, pair_ref, received_ref, h_ref, gain_ref, grad_ref, low_ref, gain_grad_ref):
+    grad, gain_grad_ref[...] = norm_gradient(
         both(pair_ref, received_ref), h_ref[...], gain_ref[...]
     )
+    grad = g_ref[...].astype(F32) + grad
     grad_ref[...] = grad
     low_ref[...] = grad.astype(BF16)
 
 
 def back_step(g, pair, received, h, gain):
-    outs = (shaped(g.shape, F32), shaped(g.shape, BF16))
+    outs = (shaped(g.shape, F32), shaped(g.shape, BF16), shaped(gain.shape, F32))
     return kernel_call(back_body, outs, "back_step", 2)(g, pair, received, h, gain)
 
 
@@ -748,7 +751,7 @@
     grad_normed = both(own_ref, received_ref)
     h = jnp.where(first, h0[...], h1[...])
     grad = jnp.where(first, g0[...], g1[...])
-    out_ref[...] = (grad + norm_gradient(grad_normed, h, gain_ref[...])).astype(BF16)
+    out_ref[...] = (grad + norm_gradient(grad_normed, h, gain_ref[...])[0]).astype(BF16)
 
 
 def last_back(chip, grads, states, own, received, gain):
@@ -851,10 +854,13 @@
 
 def ffn_bwd_body(
     g_ref, pair_ref, received_ref, h_ref, gain_ref, hidden_ref, own_ref, mate_ref,
-    total_ref, low_ref, grad_ref, active_ref, out_ref,
+    total_ref, low_ref, grad_ref, active_ref, out_ref, gain_grad_ref,
 ):
     units = mate_ref.shape[1] // 2
-    total = g_ref[...] + norm_gradient(both(pair_ref, received_ref), h_ref[...], gain_ref[...])
+    total, gain_grad_ref[...] = norm_gradient(
+        both(pair_ref, received_ref), h_ref[...], gain_ref[...]
+    )
+    total = g_ref[...] + total
     total_ref[...] = total
     g = total.astype(BF16)
     low_ref[...] = g
@@ -872,7 +878,7 @@
 def ffn_backward(g, pair, received, h, gain, hidden, own, mate):
     piece = shaped(h.shape, BF16)
     rows = shaped(hidden.shape, BF16)
-    outs = (shaped(h.shape, F32), piece, rows, rows, piece)
+    outs = (shaped(h.shape, F32), piece, rows, rows, piece, shaped(gain.shape, F32))
     return kernel_call(ffn_bwd_body, outs, "ffn_backward", 60)(
         g, pair, received, h, gain, hidden, own, mate
     )
@@ -988,19 +994,25 @@
     return kernel_call(body, halves_of(*own.shape), "ffn_cut", 3, 1)(side, own, *mate)
 
 
-def mixer_grads(side, x, joined, g, mixed, count, bit):
+def mixer_grads(side, x, joined, g, mixed, w, count, bit):
     model, columns = x.shape[1], joined.shape[1] + mixed.shape[1]
-
-    def body(side_ref, x_ref, gp_ref, g_ref, mixed_ref, keep_ref, send_ref, total):
-        total[:, : gp_ref.shape[1]] = dot_tn(x_ref[...], gp_ref[...])
-        total[:, gp_ref.shape[1] :] = dot_tn(g_ref[...], mixed_ref[...])
+    inputs = joined.shape[1]
+
+    def body(side_ref, x_ref, gp_ref, g_ref, mixed_ref, w_ref, keep_ref, send_ref, gain_ref, total):
+        total[:, :inputs] = dot_tn(x_ref[...], gp_ref[...])
+        total[:, inputs:] = dot_tn(g_ref[...], mixed_ref[...])
         halved(
             side_ref[0], count, bit, lambda first, size: total[first : first + size], keep_ref, send_ref
         )
-
-    return kernel_call(
-        body, halves_of(model, columns), "mixer_grads", 6, 1, [pltpu.VMEM((model, columns), F32)]
-    )(side, x, joined, g, mixed)
+        weighted = total[:, :inputs] * w_ref[:, :inputs].astype(F32)
+        high, low = split(weighted)
+        ones = jnp.ones((8, inputs), BF16)
+        gain_ref[...] = (dot_nt(ones, high) + dot_nt(ones, low))[:1]
+
+    outs = halves_of(model, columns) + (shaped((1, model), F32),)
+    return kernel_call(body, outs, "mixer_grads", 6, 1, [pltpu.VMEM((model, columns), F32)])(
+        side, x, joined, g, mixed, w
+    )
 
 
 def scatter_step(side, keep, received, count, bit):
@@ -1014,27 +1026,68 @@
     return kernel_call(body, halves_of(*keep.shape), "scatter_step", 2, 1)(side, keep, received)
 
 
-def small_cut(side, taps, tiles, count, bit):
+def gain_places(count, rows, model, gains):
+    block = model // count
+    lanes = gains * block // rows
+    step = math.gcd(block, lanes)
+    places = []
+    for j in range(count):
+        for i in range(gains):
+            for first in range(0, block, step):
+                flat = i * block + first
+                places.append((i, j * block + first, step, j * rows + flat // lanes, flat % lanes))
+    return places, lanes
+
+
+def small_cut(side, taps, tiles, gains, count, bit):
     width = taps.shape[1]
     starts = [0] * len(tiles)
     for i in range(1, len(tiles)):
         starts[i] = starts[i - 1] + tiles[i - 1][0].shape[1]
-
-    def body(side_ref, taps_ref, *refs):
+    places, lanes = gain_places(count, taps.shape[0] // count, gains.shape[1], gains.shape[0])
+
+    def body(side_ref, taps_ref, gains_ref, *refs):
         *tile_refs, keep_ref, send_ref, total = refs
         total[:, :width] = taps_ref[...]
         for i, start in enumerate(starts):
             size = tile_refs[2 * i].shape[1]
             total[:, width + start : width + start + size] = tile_refs[2 * i][...]
             total[:, 2 * width + start : 2 * width + start + size] = tile_refs[2 * i + 1][...]
+        for i, first, size, row, lane in places:
+            here = slice(3 * width + lane, 3 * width + lane + size)
+            total[row : row + 1, here] = gains_ref[i : i + 1, first : first + size]
         halved(
             side_ref[0], count, bit, lambda first, size: total[first : first + size], keep_ref, send_ref
         )
 
-    shape = (taps.shape[0], 3 * width)
+    shape = (taps.shape[0], 3 * width + lanes)
     return kernel_call(
         body, halves_of(*shape), "small_cut", 2, 1, [pltpu.VMEM(shape, F32)]
-    )(side, taps, *[x for tile in tiles for x in tile])
+    )(side, taps, gains, *[x for tile in tiles for x in tile])
+
+
+def finish_small(keep, received, gains, width):
+    rows = keep.shape[0]
+    count, block = gains.shape
+    places, _ = gain_places(1, rows, block, count)
+
+    def body(keep_ref, received_ref, gains_ref, taps_ref, decay_ref, coef_ref, gain_grad_ref):
+        total = keep_ref[...].astype(F32) + received_ref[...].astype(F32)
+        taps_ref[...] = total[:, :width]
+        decay_ref[...] = total[:, width : 2 * width]
+        coef_ref[...] = total[:, 2 * width : 3 * width]
+        for i, first, size, row, lane in places:
+            lanes = slice(3 * width + lane, 3 * width + lane + size)
+            part = total[row : row + 1, lanes]
+            if i == 0:
+                part = part / gains_ref[:1, first : first + size]
+            gain_grad_ref[i : i + 1, first : first + size] = part
+
+    outs = (
+        shaped((rows, width), F32), shaped((rows, width), F32), shaped((rows, width), F32),
+        shaped((count, block), F32),
+    )
+    return kernel_call(body, outs, "finish_small", 2)(keep, received, gains)
 
 
 def summed(parts, lanes):
@@ -1044,34 +1097,25 @@
     return total
 
 
-def finish(parts, ffn_parts, first, ffn_first, weights, up, gain, ffn_gain):
-    rows, width = weights[0].shape
-    units = up.shape[1]
+def finish(parts, ffn_parts, first, ffn_first, width, units):
+    rows = parts[0].shape[0]
     count = len(parts)
 
-    def body(wq_ref, wk_ref, wv_ref, up_ref, gain_ref, ffn_gain_ref, *refs):
+    def body(*refs):
         part_refs, ffn_refs = refs[:count], refs[count : 2 * count]
-        q_ref, k_ref, v_ref, o_ref, up_grad_ref, down_ref, gain_grad_ref = refs[2 * count :]
-        weighted = None
-        for i, (w_ref, out_ref) in enumerate(((wq_ref, q_ref), (wk_ref, k_ref), (wv_ref, v_ref))):
-            grad = summed(part_refs, slice(first + i * width, first + (i + 1) * width))
-            out_ref[...] = grad
-            grad = grad * w_ref[...].astype(F32)
-            weighted = grad if weighted is None else weighted + grad
+        q_ref, k_ref, v_ref, o_ref, up_ref, down_ref = refs[2 * count :]
+        for i, out_ref in enumerate((q_ref, k_ref, v_ref)):
+            out_ref[...] = summed(part_refs, slice(first + i * width, first + (i + 1) * width))
         o_ref[...] = summed(part_refs, slice(first + 3 * width, first + 4 * width)).T
-        gain_grad_ref[:1] = jnp.sum(weighted.T, axis=0, keepdims=True) / gain_ref[...]
-        grad = summed(ffn_refs, slice(ffn_first, ffn_first + units))
-        up_grad_ref[...] = grad
-        down_ref[...] = summed(ffn_refs, slice(ffn_first + units, ffn_first + 2 * units)).T
-        weighted = grad * up_ref[...].astype(F32)
-        gain_grad_ref[1:] = jnp.sum(weighted.T, axis=0, keepdims=True) / ffn_gain_ref[...]
+        up_ref[...] = summed(ffn_refs, slice(ffn_first, ffn_first + units))
+        down_ref[...] = summed(ffn_refs, slice(ffn_first + units, ffn_first + 2 * units))
 
     square = shaped((rows, width), F32)
     outs = (
         square, square, square, shaped((width, rows), F32),
-        shaped((rows, units), F32), shaped((units, rows), F32), shaped((2, rows), F32),
-    )
-    return kernel_call(body, outs, "finish", 5)(*weights, up, gain, ffn_gain, *parts, *ffn_parts)
+        shaped((rows, units), F32), shaped((rows, units), F32),
+    )
+    return kernel_call(body, outs, "finish", 5)(*parts, *ffn_parts)
 
 
 TENSOR = "tensor"
@@ -1229,6 +1273,7 @@
     pairs, received = exchanged(keep, send)
     first_w = after(first_w, pairs[1])
     ffn1_w, attn_w = first_w[:, : 2 * units], first_w[:, 2 * units :]
+    received[0], attn_w = tie(received[0], attn_w)
     ffn1_mate = from_mate(ffn1_w)
     ffn2_w = lax.all_gather(after(ffn2_own, pairs[1]), DATA, axis=0, tiled=True)
     ffn1_mate = after(ffn1_mate, received[0])
@@ -1249,7 +1294,6 @@
         h, n = norm_step(after_mixer[half], nexts[half], wait, gains[2])
         after_ffn1.append(h)
         pieces += [n, from_mate(n)]
-    attn_w, pieces[2] = tie(attn_w, pieces[2])
     keep, send, x3, q2, k2, v2, attended_t, log_total = attn_forward_kernel(
         core, seq_lengths, pieces, attn_w
     )
@@ -1272,14 +1316,16 @@
         act.append(active)
         nexts.append(out)
         arrived.append(from_chip(out))
-    lows = []
+    lows, ffn2_gain = [], []
     wait = after(arrived[0], nexts[1])
-    grad[0], low = back_step(grad[0], nexts[0], wait, after_attn[0], gains[3])
+    grad[0], low, part = back_step(grad[0], nexts[0], wait, after_attn[0], gains[3])
+    ffn2_gain.append(part)
     lows.append(low)
     gh, act = after((gh, act), low)
     own, mate = ffn_grads(n4, g4, gh, act)
     wait = after(arrived[1], mate[-1])
-    grad[1], low = back_step(grad[1], nexts[1], wait, after_attn[1], gains[3])
+    grad[1], low, part = back_step(grad[1], nexts[1], wait, after_attn[1], gains[3])
+    ffn2_gain.append(part)
     lows.append(low)
     pieces = [lows[0], from_mate(after(lows[0], low)), lows[1], from_mate(lows[1])]
     ffn2_mate_g = [from_mate(x) for x in after(tuple(mate), pieces[1], pieces[3])]
@@ -1293,27 +1339,30 @@
     final_own, final_sent = ffn_out(chips, *after(tuple(act), second_p), ffn2_w, ffn2_mate)
     received = list(after(tuple(received), second_p, final_sent))
 
-    g2, gh, act_b, nexts, arrived = [], [], [], [], []
+    g2, gh, act_b, nexts, arrived, attn_gain = [], [], [], [], [], []
     for half in range(2):
         wait = received[half]
-        grad[half], low, grad_hidden, active, out = ffn_backward(
+        grad[half], low, grad_hidden, active, out, part = ffn_backward(
             grad[half].astype(F32), pairs[half], wait, after_ffn1[half], gains[2], hidden1[half],
             ffn1_w, ffn1_mate,
         )
         g2.append(low)
+        attn_gain.append(part)
         gh.append(grad_hidden)
         act_b.append(active)
         nexts.append(out)
         arrived.append(from_chip(out))
     second_g = lax.psum_scatter(after(second_p, nexts[0]), DATA, scatter_dimension=0, tiled=True)
-    lows = []
+    lows, ffn1_gain = [], []
     wait = after(arrived[0], nexts[1])
-    grad[0], low = back_step(grad[0], nexts[0], wait, after_mixer[0], gains[1])
+    grad[0], low, part = back_step(grad[0], nexts[0], wait, after_mixer[0], gains[1])
+    ffn1_gain.append(part)
     lows.append(low)
     gh, act_b = after((gh, act_b), low)
     own, mate = ffn_grads(n2, g2, gh, act_b)
     wait = after(arrived[1], mate[-1])
-    grad[1], low = back_step(grad[1], nexts[1], wait, after_mixer[1], gains[1])
+    grad[1], low, part = back_step(grad[1], nexts[1], wait, after_mixer[1], gains[1])
+    ffn1_gain.append(part)
     lows.append(low)
     pieces = [lows[0], from_mate(lows[0]), lows[1], from_mate(lows[1])]
     mate_g = [from_mate(x) for x in after(tuple(mate), pieces[1], arrived[1])]
@@ -1325,10 +1374,14 @@
     keep, send, g1, grad_joined, grad_taps, *g_spectrum = mixer_backward_kernel(
         core, pieces, mixer_w, saved[:6], spectra, fwd, inv, states
     )
-    output = output_step(chips, after_attn, final_own, after(final_received, keep))
-    mixer_keep, mixer_send = mixer_grads(
-        rows.side(step - 1), x1, grad_joined, g1, mixed, rows.count, rows.bits[step - 1]
-    )
+    mixer_keep, mixer_send, mixer_gain = mixer_grads(
+        rows.side(step - 1), x1, grad_joined, g1, mixed, mixer_w, rows.count, rows.bits[step - 1]
+    )
+    gain_rows = jnp.concatenate(
+        [mixer_gain] + [0.5 * (p[0] + p[1]) for p in (ffn1_gain, attn_gain, ffn2_gain)], axis=0
+    )
+    gain_rows = gain_rows + from_mate(gain_rows)
+    gain_rows = gain_rows + from_chip(gain_rows)
     mixer_received = rows.swap(mixer_send, rows.bits[step - 1])
     own, last_sent = own_half(chips, keep, from_mate(after(send, mixer_send)))
     last_received = from_chip(last_sent)
@@ -1352,36 +1405,32 @@
         for i in range(1, len(channel_tiles(width)))
     ]
     small_keep, small_send = small_cut(
-        rows.side(step), grad_taps, ssm, rows.count, rows.bits[step]
+        rows.side(step), grad_taps, ssm, gain_rows, rows.count, rows.bits[step]
     )
     small_received = rows.swap(small_send, rows.bits[step])
-    ffn1_received, mixer_received, last_received, small_received = tie(
-        *after((ffn1_received, mixer_received, last_received, small_received), small_send)
+    small_received = after(small_received, small_send)
+    small_keep, small_send = scatter_step(rows.side(step - 1), small_keep, small_received, half, 1)
+    small_received = rows.swap(small_send, rows.bits[step - 1])
+    ffn1_received, mixer_received, last_received = tie(
+        *after((ffn1_received, mixer_received, last_received), small_send)
     )
     ffn1_keep, ffn1_send = scatter_step(rows.side(step - 2), ffn1_keep, ffn1_received, pair, 1)
-    mixer_received, small_received = after((mixer_received, small_received), ffn1_send)
+    mixer_received = after(mixer_received, ffn1_send)
     mixer_keep, mixer_send = scatter_step(rows.side(step - 2), mixer_keep, mixer_received, pair, 1)
-    small_keep, small_send = scatter_step(
-        rows.side(step - 1), small_keep, after(small_received, mixer_send), half, 1
-    )
-    ffn1_send, mixer_send, small_send = tie(ffn1_send, mixer_send, small_send)
+    last_received, final_received = after((last_received, final_received), mixer_send)
+    input_grad = last_back(chips, grad, start, own, last_received, gains[0])
+    output = output_step(chips, after_attn, final_own, final_received)
+    small_received = after(small_received, input_grad, output)
+    small_keep, small_send = scatter_step(rows.side(step - 2), small_keep, small_received, pair, 1)
+
     ffn1_received = rows.swap(ffn1_send, rows.bits[step - 2])
     mixer_received = rows.swap(mixer_send, rows.bits[step - 2])
-    small_received = rows.swap(small_send, rows.bits[step - 1])
-    input_grad = last_back(chips, grad, start, own, after(last_received, small_send), gains[0])
-    small_keep, small_send = scatter_step(rows.side(step - 2), small_keep, small_received, pair, 1)
     small_received = rows.swap(small_send, rows.bits[step - 2])
     second_g = [after(second_g, small_send)]
 
-    def column(gain):
-        return gain.astype(F32)[None, :]
-
-    aq, ak, av, ao, u2, d2, gains_second = finish(
-        second_g, second_g, 2 * units, 0, (attn_query, attn_key, attn_value), ffn2_up,
-        column(gain_attn), column(gain_ffn2),
-    )
+    aq, ak, av, ao, u2, d2 = finish(second_g, second_g, 2 * units, 0, width, units)
     ffn1_received, mixer_received, small_received = after(
-        (ffn1_received, mixer_received, small_received), gains_second
+        (ffn1_received, mixer_received, small_received), aq, input_grad, output
     )
     level, tail = pair // 2, step - 3
     while tail >= 0:
@@ -1392,21 +1441,18 @@
         mixer_received = rows.swap(mixer_send, rows.bits[tail])
         small_received = rows.swap(small_send, rows.bits[tail])
         level, tail = level // 2, tail - 1
-    mq, mk, mv, mo, u1, d1, gains_first = finish(
-        [mixer_keep, mixer_received], [ffn1_keep, ffn1_received], 0, 0,
-        (mixer_query, mixer_key, mixer_value), ffn1_up, column(gain_mixer), column(gain_ffn1),
-    )
-    small_g = small_keep.astype(F32) + small_received.astype(F32)
-    gt, gd, gc = (small_g[:, i * width : (i + 1) * width] for i in range(3))
-    first_gains, second_gains = (
-        g + swap(g, 1) + (swap(g, 2) + swap(g, 3)) for g in (gains_first, gains_second)
+    mq, mk, mv, mo, u1, d1 = finish(
+        [mixer_keep, mixer_received], [ffn1_keep, ffn1_received], 0, 0, width, units
+    )
+    gt, gd, gc, gain_grads = finish_small(
+        small_keep, after(small_received, mq), own_gains.astype(F32), width
     )
     return (
         output, input_grad,
-        first_gains[0], mq, mk, mv, gt, gd.T, gc.T, mo,
-        first_gains[1], u1, d1,
-        second_gains[0], aq, ak, av, ao,
-        second_gains[1], u2, d2,
+        gain_grads[0], mq, mk, mv, gt, gd.T, gc.T, mo,
+        gain_grads[1], u1, d1.T,
+        gain_grads[2], aq, ak, av, ao,
+        gain_grads[3], u2, d2.T,
     )
 
 

time: 410 us -> 398 us (0.971)
  waiting for transfers between devices: 87 us -> 77.7 us
    ppermute x48 -> x44, waiting for transfers between devices: 44.1 us -> 38.9 us  [swap(): return lax.ppermute(x, TENSOR, [(i, i ^ bit) for i in range(4)])]
    unnamed x166 -> x164, local copies, waits for them, and re-layouts: 24.5 us -> 21.1 us
    ppermute x48 -> x44, starting transfers between devices: 25.1 us -> 27.4 us  [swap(): return lax.ppermute(x, TENSOR, [(i, i ^ bit) for i in range(4)])]
    pallas_call x31 -> x32, Pallas kernels: 122 us -> 124 us  [call(): pl.pallas_call(body, in_specs=[SCALAR] * scalars + [WHOLE] * (len(args) -...]
  transfers between devices with their start and end apart: 66 -> 62, of which waited for: 29 -> 27; matrix products, arithmetic and copies ran while one was open for 6% -> 5% of each run, Pallas kernels for 43% -> 44%
where the time goes in v5:
time: 398 us; the launch traced here: 391 us
  Pallas kernels  201 us (51%)
  waiting for transfers between devices  77.7 us (20%)
  starting transfers between devices  51.3 us (13%)
  local copies, waits for them, and re-layouts  33.4 us (8%)
  between operations  15.7 us (4%)
  other arithmetic  11.4 us (3%)
    pallas_call x32, Pallas kernels, call(): pl.pallas_call(body, in_specs=[SCALAR] * scalars + [WHOLE] * (len(args) -...  124 us
    ppermute x44, waiting for transfers between devices, swap(): return lax.ppermute(x, TENSOR, [(i, i ^ bit) for i in range(4)])  38.9 us
    ppermute x15, waiting for transfers between devices, swap(): return lax.ppermute(x, DATA, [(i, i ^ bit) for i in range(self.count)])  37 us
    ppermute x44, starting transfers between devices, swap(): return lax.ppermute(x, TENSOR, [(i, i ^ bit) for i in range(4)])  27.4 us
    ppermute x15, starting transfers between devices, swap(): return lax.ppermute(x, DATA, [(i, i ^ bit) for i in range(self.count)])  23.6 us
    unnamed x164, local copies, waits for them, and re-layouts  21.1 us
    pallas_call x2, Pallas kernels, ssm_grad_kernel(): pl.pallas_call(body, out_shape=(out, out), scratch_shapes=[pltpu.VMEM((bl...  15.6 us
    pallas_call x1, Pallas kernels, attn_backward_kernel(): pl.pallas_call(attn_bwd_body, in_specs=[SCALAR, SCALAR] + [WHOLE] * 9, ou...  14.7 us
  transfers between devices with their start and end apart: 62, of which 27 were waited for; matrix products, arithmetic and copies ran while one was open for 5% of the time, Pallas kernels for 44%

profile of v5, /device:TPU:0, one launch (start us, length us, event | category | flops | bytes accessed | tf_op | source)
XLA Modules:
  0.0 391.0 jit_solution(13928952155608530275)
XLA Ops:
  22.6 6.0 %collective-permute-done.2 = bf16[2,16,768]{2,1,0:T(8,128)(2,1)S(1)} collective-permute-done((bf16[2,16,768]{2,1,0:T(8,128)(2,1)S(1)}, bf16[2,16,768]{2,1,0:T(8,128)(2,1)S(1)}, u32[]{:S(2)}, u32[]{:S(2)}) %collective-permute-start.2) | collective-permute-done | bytes 49184 | tf_op jit(solution)/shard_map/ppermute | solution.py:1161
  33.4 13.7 %collective-permute-done.5 = bf16[2,96,768]{2,1,0:T(8,128)(2,1)S(1)} collective-permute-done((bf16[2,96,768]{2,1,0:T(8,128)(2,1)S(1)}, bf16[2,96,768]{2,1,0:T(8,128)(2,1)S(1)}, u32[]{:S(2)}, u32[]{:S(2)}) %collective-permute-start.5) | collective-permute-done | bytes 294944 | tf_op jit(solution)/shard_map/ppermute | solution.py:1161
  55.5 10.3 %kernel_spectra.1 = (f32[8,128,192]{2,1,0:T(8,128)}, f32[8,128,192]{2,1,0:T(8,128)}, f32[128,192]{1,0:T(8,128)}, f32[128,192]{1,0:T(8,128)}) custom-call(f32[64,192]{1,0:T(8,128)} %get-tuple-element.281.decay_ref, f32[64,192]{1,0:T(8,128)} %get-tuple-element.528.coef_ref, f32[64,192]{1,0:T(8,128)} %get-tuple-element.527.taps_ref, ...), custom_call_target="tpu_custom_call" | custom-call | flops 1210000000 | bytes 3850000 | tf_op jit(solution)/shard_map/kernel_spectra/pallas_call | solution.py:158
  65.8 7.7 %collective-permute-done.8 = bf16[2,2,96,768]{3,2,1,0:T(8,128)(2,1)S(1)} collective-permute-done((bf16[2,2,96,768]{3,2,1,0:T(8,128)(2,1)S(1)}, bf16[2,2,96,768]{3,2,1,0:T(8,128)(2,1)S(1)}, u32[]{:S(2)}, u32[]{:S(2)}) %collective-permute-start.8) | collective-permute-done | bytes 589856 | tf_op jit(solution)/shard_map/ppermute | solution.py:1161
  75.7 11.5 %mixer_forward.1 = (bf16[2,256,768]{2,1,0:T(8,128)(2,1)}, bf16[2,256,768]{2,1,0:T(8,128)(2,1)}, bf16[1024,768]{1,0:T(8,128)(2,1)}, bf16[1024,192]{1,0:T(8,128)(2...) custom-call(s32[1]{0:T(128)} %bitcast.23.core_ref, ...), custom_call_target="tpu_custom_call" | custom-call | flops 1540000000 | bytes 4900000 | tf_op jit(solution)/shard_map/mixer_forward/pallas_call | solution.py:291
  101.1 6.9 %collective-permute-done.11.received_ref = bf16[256,768]{1,0:T(8,128)(2,1)} collective-permute-done((bf16[256,768]{1,0:T(8,128)(2,1)S(1)}, bf16[256,768]{1,0:T(8,128)(2,1)}, u32[]{:S(2)}, u32[]{:S(2)}) %collective-permute-start.11) | collective-permute-done | bytes 393248 | tf_op jit(solution)/shard_map/ppermute | solution.py:1126
  108.0 5.6 %ffn_forward.2 = (f32[256,768]{1,0:T(8,128)}, bf16[256,768]{1,0:T(8,128)(2,1)}, f32[256,1536]{1,0:T(8,128)}, bf16[256,768]{1,0:T(8,128)(2,1)}) custom-call(f32[256,768]{1,0:T(8,128)} %get-tuple-element.276.h_ref.h0, bf16[256,768]{1,0:T(8,128)(2,1)} %copy-done.24, bf16[256,768]{1,0:T(8,128)(2,1)} %collective-permute-done.11.received_ref, ...), custom_call_target="tpu_custom_call" | custom-call | flops 5500000256 | bytes 17500000 | tf_op jit(solution)/shard_map/ffn_forward/pallas_call | solution.py:667
  116.8 5.6 %ffn_forward.3 = (f32[256,768]{1,0:T(8,128)}, bf16[256,768]{1,0:T(8,128)(2,1)}, f32[256,1536]{1,0:T(8,128)}, bf16[256,768]{1,0:T(8,128)(2,1)}) custom-call(f32[256,768]{1,0:T(8,128)} %get-tuple-element.294.h_ref.h1, bf16[256,768]{1,0:T(8,128)(2,1)} %copy-done.18, bf16[256,768]{1,0:T(8,128)(2,1)} %copy-done.69, f32[1,768]{1,0:T(1,128)} %squeeze.20.gain_ref, ...), custom_call_target="tpu_custom_call" | custom-call | flops 5500000256 | bytes 17500000 | tf_op jit(solution)/shard_map/ffn_forward/pallas_call | solution.py:667
  128.4 5.2 %collective-permute-done.16.received_ref = bf16[256,768]{1,0:T(8,128)(2,1)S(1)} collective-permute-done((bf16[256,768]{1,0:T(8,128)(2,1)}, bf16[256,768]{1,0:T(8,128)(2,1)S(1)}, u32[]{:S(2)}, u32[]{:S(2)}) %collective-permute-start.16) | collective-permute-done | bytes 393248 | tf_op jit(solution)/shard_map/ppermute | solution.py:1126
  139.6 11.5 %attn_forward.1 = (bf16[2,256,768]{2,1,0:T(8,128)(2,1)}, bf16[2,256,768]{2,1,0:T(8,128)(2,1)}, bf16[1024,768]{1,0:T(8,128)(2,1)}, bf16[1024,192]{1,0:T(8,128)(2,...) custom-call(s32[1]{0:T(128)} %bitcast.23.core_ref, ...), custom_call_target="tpu_custom_call" | custom-call | flops 1320000000 | bytes 4200000 | tf_op jit(solution)/shard_map/attn_forward/pallas_call | solution.py:579
  160.3 6.9 %collective-permute-done.19.received_ref = bf16[256,768]{1,0:T(8,128)(2,1)} collective-permute-done((bf16[256,768]{1,0:T(8,128)(2,1)S(1)}, bf16[256,768]{1,0:T(8,128)(2,1)}, u32[]{:S(2)}, u32[]{:S(2)}) %collective-permute-start.19) | collective-permute-done | bytes 393248 | tf_op jit(solution)/shard_map/ppermute | solution.py:1126
  168.6 6.4 %ffn_both.2 = (f32[256,768]{1,0:T(8,128)}, bf16[256,768]{1,0:T(8,128)(2,1)}, bf16[256,1536]{1,0:T(8,128)(2,1)}, bf16[256,1536]{1,0:T(8,128)(2,1)}, bf16[256,768]{1,0:T(8,128)(2,1)}) custom-call(f32[256,768]{1,0:T(8,128)} %get-tuple-element.298.h_ref, bf16[256,768]{1,0:T(8,128)(2,1)} %copy-done.26, bf16[256,768]{1,0:T(8,128)(2,1)} %collective-permute-done.19.received_ref, ...), custom_call_target="tpu_custom_call" | custom-call | flops 6600000000 | bytes 21000000 | tf_op jit(solution)/shard_map/ffn_both/pallas_call | solution.py:667
  177.2 6.4 %ffn_both.3 = (f32[256,768]{1,0:T(8,128)}, bf16[256,768]{1,0:T(8,128)(2,1)}, bf16[256,1536]{1,0:T(8,128)(2,1)}, bf16[256,1536]{1,0:T(8,128)(2,1)}, bf16[256,768]{1,0:T(8,128)(2,1)}) custom-call(f32[256,768]{1,0:T(8,128)} %get-tuple-element.311.h_ref, bf16[256,768]{1,0:T(8,128)(2,1)} %copy-done.19, bf16[256,768]{1,0:T(8,128)(2,1)} %copy-done.68, ...), custom_call_target="tpu_custom_call" | custom-call | flops 6600000000 | bytes 21000000 | tf_op jit(solution)/shard_map/ffn_both/pallas_call | solution.py:667
  189.1 6.4 %ffn_grads.2 = (bf16[768,1536]{1,0:T(8,128)(2,1)}, bf16[768,256]{1,0:T(8,128)(2,1)}, bf16[768,256]{1,0:T(8,128)(2,1)}, bf16[768,256]{1,0:T(8,128)(2,1)}, bf16[76...) custom-call(bf16[256,768]{1,0:T(8,128)(2,1)} %get-tuple-element.325.n0, ...), custom_call_target="tpu_custom_call" | custom-call | flops 660000000 | bytes 2100000 | tf_op jit(solution)/shard_map/ffn_grads/pallas_call | solution.py:667
  202.7 14.7 %attn_backward.1 = (bf16[2,256,768]{2,1,0:T(8,128)(2,1)}, bf16[2,256,768]{2,1,0:T(8,128)(2,1)}, bf16[1024,768]{1,0:T(8,128)(2,1)}, bf16[1024,576]{1,0:T(8,128)(2,1)}) custom-call(s32[1]{0:T(128)} %bitcast.23.core_ref, s32[1]{0:T(128)} %copy.65.len_ref, bf16[256,768]{1,0:T(8,128)(2,1)} %get-tuple-element.332.a_ref, bf16[256,768]{1,0:T(8,128)(2,1)} %copy-done.71, ...), custom_call_target="tpu_custom_call" | custom-call | flops 1540000000 | bytes 4900000 | tf_op jit(solution)/shard_map/attn_backward/pallas_call | solution.py:642
  225.4 8.5 %attn_grads.1 = bf16[768,2304]{1,0:T(8,128)(2,1)} custom-call(bf16[1024,768]{1,0:T(8,128)(2,1)} %get-tuple-element.324.x_ref, bf16[1024,576]{1,0:T(8,128)(2,1)} %get-tuple-element.337.gp_ref, bf16[1024,768]{1,0:T(8,128)(2,1)} %get-tuple-element.338.g_ref, bf16[192,1024]{1,0:T(8,128)(2,1)} %get-tuple-element.339.att_ref, ...), custom_call_target="tpu_custom_call" | custom-call | flops 880000000 | bytes 2800000 | tf_op jit(solution)/shard_map/attn_grads/pallas_call | solution.py:667
  233.9 5.2 %ffn_out.1 = (bf16[256,768]{1,0:T(8,128)(2,1)}, bf16[256,768]{1,0:T(8,128)(2,1)}) custom-call(s32[1]{0:T(128)} %bitcast.chip_ref, bf16[256,1536]{1,0:T(8,128)(2,1)} %get-tuple-element.361.a0.a0_ref, bf16[256,1536]{1,0:T(8,128)(2,1)} %get-tuple-element.362.a1.a1_ref, bf16[768,1536]{1,0:T(8,128)(2,1)} %all-gather.5.cloned.1.call-done.own_ref, ...), custom_call_target="tpu_custom_call" | custom-call | flops 330000000 | bytes 1050000 | tf_op jit(solution)/shard_map/ffn_out/pallas_call | solution.py:667
  242.0 7.2 %ffn_backward.2 = (f32[256,768]{1,0:T(8,128)}, bf16[256,768]{1,0:T(8,128)(2,1)}, bf16[256,1536]{1,0:T(8,128)(2,1)}, bf16[256,1536]{1,0:T(8,128)(2,1)}, bf16[256,768]{1,0:T(8,128)(2,1)}, /*index=5*/f32[1,768]{1,0:T(1,128)}) custom-call(f32[256,768]{1,0:T(8,128)} %get-tuple-element.366.g_ref, bf16[256,768]{1,0:T(8,128)(2,1)} %copy-done.17, ...), custom_call_target="tpu_custom_call" | custom-call | flops 6600000000 | bytes 21000000 | tf_op jit(solution)/shard_map/ffn_backward/pallas_call | solution.py:667
  251.9 6.8 %ffn_backward.3 = (f32[256,768]{1,0:T(8,128)}, bf16[256,768]{1,0:T(8,128)(2,1)}, bf16[256,1536]{1,0:T(8,128)(2,1)}, bf16[256,1536]{1,0:T(8,128)(2,1)}, bf16[256,768]{1,0:T(8,128)(2,1)}, /*index=5*/f32[1,768]{1,0:T(1,128)}) custom-call(f32[256,768]{1,0:T(8,128)} %get-tuple-element.371.g_ref, bf16[256,768]{1,0:T(8,128)(2,1)} %copy-done.16, ...), custom_call_target="tpu_custom_call" | custom-call | flops 6600000000 | bytes 21000000 | tf_op jit(solution)/shard_map/ffn_backward/pallas_call | solution.py:667
  264.9 6.5 %ffn_grads.3 = (bf16[768,1536]{1,0:T(8,128)(2,1)}, bf16[768,256]{1,0:T(8,128)(2,1)}, bf16[768,256]{1,0:T(8,128)(2,1)}, bf16[768,256]{1,0:T(8,128)(2,1)}, bf16[76...) custom-call(bf16[256,768]{1,0:T(8,128)(2,1)} %get-tuple-element.364.n0, ...), custom_call_target="tpu_custom_call" | custom-call | flops 660000000 | bytes 2100000 | tf_op jit(solution)/shard_map/ffn_grads/pallas_call | solution.py:667
  288.1 13.6 %mixer_backward.1 = (bf16[2,256,768]{2,1,0:T(8,128)(2,1)}, bf16[2,256,768]{2,1,0:T(8,128)(2,1)}, bf16[1024,768]{1,0:T(8,128)(2,1)}, bf16[1024,576]{1,0:T(8,128)(...) custom-call(s32[1]{0:T(128)} %bitcast.23.core_ref, ...), custom_call_target="tpu_custom_call" | custom-call | flops 1650000000 | bytes 5250000 | tf_op jit(solution)/shard_map/mixer_backward/pallas_call | solution.py:413
  301.8 6.3 %mixer_grads.1 = (bf16[384,768]{1,0:T(8,128)(2,1)}, bf16[384,768]{1,0:T(8,128)(2,1)}, f32[1,768]{1,0:T(1,128)}) custom-call(s32[1]{0:T(128)} %bitcast.38.side_ref, bf16[1024,768]{1,0:T(8,128)(2,1)} %get-tuple-element.426.x_ref, bf16[1024,576]{1,0:T(8,128)(2,1)} %get-tuple-element.427.gp_ref, bf16[1024,768]{1,0:T(8,128)(2,1)} %get-tuple-element.428.g_ref, ...), custom_call_target="tpu_custom_call" | custom-call | flops 660000000 | bytes 2100000 | tf_op jit(solution)/shard_map/mixer_grads/pallas_call | solution.py:667
  317.4 9.1 %ssm_grad.2 = (f32[64,128]{1,0:T(8,128)}, f32[64,128]{1,0:T(8,128)}) custom-call(bf16[8,128,192]{2,1,0:T(8,128)(2,1)} %get-tuple-element.452.g_re, bf16[8,128,192]{2,1,0:T(8,128)(2,1)} %get-tuple-element.453.g_im, bf16[8,128,192]{2,1,0:T(8,128)(2,1)} %get-tuple-element.435.u_re, bf16[8,128,192]{2,1,0:T(8,128)(2,1)} %get-tuple-element.436.u_im, ...), custom_call_target="tpu_custom_call" | custom-call | flops 1100000000 | bytes 3500000 | tf_op jit(solution)/shard_map/ssm_grad/pallas_call | solution.py:501
  337.2 6.5 %ssm_grad.3 = (f32[64,64]{1,0:T(8,128)}, f32[64,64]{1,0:T(8,128)}) custom-call(bf16[8,128,192]{2,1,0:T(8,128)(2,1)} %get-tuple-element.452.g_re, bf16[8,128,192]{2,1,0:T(8,128)(2,1)} %get-tuple-element.453.g_im, bf16[8,128,192]{2,1,0:T(8,128)(2,1)} %get-tuple-element.435.u_re, bf16[8,128,192]{2,1,0:T(8,128)(2,1)} %get-tuple-element.436.u_im, ...), custom_call_target="tpu_custom_call" | custom-call | flops 1100000000 | bytes 3500000 | tf_op jit(solution)/shard_map/ssm_grad/pallas_call | solution.py:501
  (348 shorter events, 180.7 us)
Async XLA Ops:
  7.3 85.5 %all-gather.3.cloned.1.call-start = ((), (), s32[]{:S(2)}) async-start(), calls=%async_computation.1 | async-start | bytes 3981312 | tf_op jit(solution)/shard_map/all_gather | solution.py:1242
  10.2 144.7 %all-gather.5.cloned.1.call-start = ((), (), s32[]{:S(2)}) async-start(), calls=%async_computation.2 | async-start | bytes 2654208 | tf_op jit(solution)/shard_map/all_gather | solution.py:1278
  17.0 14.4 %collective-permute-start.4 = (bf16[96,768]{1,0:T(8,128)(2,1)S(1)}, bf16[96,768]{1,0:T(8,128)(2,1)S(1)}, u32[]{:S(2)}, u32[]{:S(2)}) collective-permute-start(bf16[96,768]{1,0:T(8,128)(2,1)S(1)} %pad_maximum_fusion.5), channel_id=1, source_target_pairs={{0,16},{4,20},{8,24},{12,28},{16,0},{20,4},{24,8},{28,12},{1,17},{... | collective-permute-start | bytes 442376 | tf_op jit(solution)/shard_map/ppermute | solution.py:1161
  17.1 32.4 %collective-permute-start = (bf16[256,768]{1,0:T(8,128)(2,1)S(1)}, bf16[256,768]{1,0:T(8,128)(2,1)S(1)}, u32[]{:S(2)}, u32[]{:S(2)}) collective-permute-start(bf16[256,768]{1,0:T(8,128)(2,1)S(1)} %copy-done.51), channel_id=1, source_target_pairs={{0,2},{1,3},{2,0},{3,1},{4,6},{5,7},{6,4},{7,5},{8,10},{9,11},{10,... | collective-permute-start | bytes 1179656 | tf_op jit(solution)/shard_map/ppermute | solution.py:1126
  31.6 15.6 %collective-permute-start.5 = (bf16[2,96,768]{2,1,0:T(8,128)(2,1)S(1)}, bf16[2,96,768]{2,1,0:T(8,128)(2,1)S(1)}, u32[]{:S(2)}, u32[]{:S(2)}) collective-permute-start(bf16[2,96,768]{2,1,0:T(8,128)(2,1)S(1)} %pad_maximum_fusion.2), channel_id=1, source_target_pairs={{0,8},{4,12},{8,0},{12,4},{16,24},{20,28},{24,16},{28,20},{1,9},{5... | collective-permute-start | bytes 884744 | tf_op jit(solution)/shard_map/ppermute | solution.py:1161
  48.0 25.5 %collective-permute-start.8 = (bf16[2,2,96,768]{3,2,1,0:T(8,128)(2,1)S(1)}, bf16[2,2,96,768]{3,2,1,0:T(8,128)(2,1)S(1)}, u32[]{:S(2)}, u32[]{:S(2)}) collective-permute-start(bf16[2,2,96,768]{3,2,1,0:T(8,128)(2,1)S(1)} %pad_maximum_fusion.1), channel_id=1, source_target_pairs={{0,4},{4,0},{8,12},{12,8},{16,20},{20,16},{24,28},{28,24},{1,5},{5... | collective-permute-start | bytes 1769480 | tf_op jit(solution)/shard_map/ppermute | solution.py:1161
  54.2 20.6 %collective-permute-start.6 = (bf16[256,768]{1,0:T(8,128)(2,1)}, bf16[256,768]{1,0:T(8,128)(2,1)S(1)}, u32[]{:S(2)}, u32[]{:S(2)}) collective-permute-start(bf16[256,768]{1,0:T(8,128)(2,1)} %get-tuple-element.277.a_ref), channel_id=1, source_target_pairs={{0,1},{1,0},{2,3},{3,2},{4,5},{5,4},{6,7},{7,6},{8,9},{9,8},{10,11... | collective-permute-start | bytes 1179656 | tf_op jit(solution)/shard_map/ppermute | solution.py:1126
  55.0 19.8 %collective-permute-start.7 = (bf16[256,768]{1,0:T(8,128)(2,1)}, bf16[256,768]{1,0:T(8,128)(2,1)S(1)}, u32[]{:S(2)}, u32[]{:S(2)}) collective-permute-start(bf16[256,768]{1,0:T(8,128)(2,1)} %get-tuple-element.278.c_ref), channel_id=1, source_target_pairs={{0,1},{1,0},{2,3},{3,2},{4,5},{5,4},{6,7},{7,6},{8,9},{9,8},{10,11... | collective-permute-start | bytes 1179656 | tf_op jit(solution)/shard_map/ppermute | solution.py:1126
  94.6 13.4 %collective-permute-start.12 = (bf16[768,1536]{1,0:T(8,128)(2,1)S(1)}, bf16[768,1536]{1,0:T(8,128)(2,1)}, u32[]{:S(2)}, u32[]{:S(2)}) collective-permute-start(bf16[768,1536]{1,0:T(8,128)(2,1)S(1)} %slice.150.own_ref), channel_id=1, source_target_pairs={{0,1},{1,0},{2,3},{3,2},{4,5},{5,4},{6,7},{7,6},{8,9},{9,8},{10,11... | collective-permute-start | bytes 7077896 | tf_op jit(solution)/shard_map/ppermute | solution.py:1126
  95.6 276.5 %reduce-scatter.2.cloned.1.call-start = ((), (), s32[]{:S(2)}) async-start(), calls=%async_computation.3 | async-start | bytes 3981312 | tf_op jit(solution)/shard_map/reduce_scatter | solution.py:1355
  98.7 17.4 %collective-permute-start.14 = (bf16[256,768]{1,0:T(8,128)(2,1)S(1)}, bf16[256,768]{1,0:T(8,128)(2,1)S(1)}, u32[]{:S(2)}, u32[]{:S(2)}) collective-permute-start(bf16[256,768]{1,0:T(8,128)(2,1)S(1)} %get-tuple-element.515.pair_ref), channel_id=1, source_target_pairs={{0,2},{1,3},{2,0},{3,1},{4,6},{5,7},{6,4},{7,5},{8,10},{9,11},{10,... | collective-permute-start | bytes 1179656 | tf_op jit(solution)/shard_map/ppermute | solution.py:1126
  159.7 16.8 %collective-permute-start.21 = (bf16[256,768]{1,0:T(8,128)(2,1)S(1)}, bf16[256,768]{1,0:T(8,128)(2,1)S(1)}, u32[]{:S(2)}, u32[]{:S(2)}) collective-permute-start(bf16[256,768]{1,0:T(8,128)(2,1)S(1)} %get-tuple-element.513.pair_ref), channel_id=1, source_target_pairs={{0,2},{1,3},{2,0},{3,1},{4,6},{5,7},{6,4},{7,5},{8,10},{9,11},{10,... | collective-permute-start | bytes 1179656 | tf_op jit(solution)/shard_map/ppermute | solution.py:1126
  222.1 16.9 %collective-permute-start.33 = (bf16[256,768]{1,0:T(8,128)(2,1)S(1)}, bf16[256,768]{1,0:T(8,128)(2,1)S(1)}, u32[]{:S(2)}, u32[]{:S(2)}) collective-permute-start(bf16[256,768]{1,0:T(8,128)(2,1)S(1)} %get-tuple-element.511.pair_ref), channel_id=1, source_target_pairs={{0,2},{1,3},{2,0},{3,1},{4,6},{5,7},{6,4},{7,5},{8,10},{9,11},{10,... | collective-permute-start | bytes 1179656 | tf_op jit(solution)/shard_map/ppermute | solution.py:1126
  224.2 17.8 %collective-permute-start.34 = (bf16[256,768]{1,0:T(8,128)(2,1)S(1)}, bf16[256,768]{1,0:T(8,128)(2,1)S(1)}, u32[]{:S(2)}, u32[]{:S(2)}) collective-permute-start(bf16[256,768]{1,0:T(8,128)(2,1)S(1)} %get-tuple-element.512.pair_ref), channel_id=1, source_target_pairs={{0,2},{1,3},{2,0},{3,1},{4,6},{5,7},{6,4},{7,5},{8,10},{9,11},{10,... | collective-permute-start | bytes 1179656 | tf_op jit(solution)/shard_map/ppermute | solution.py:1126
  258.7 12.7 %collective-permute-start.37 = (bf16[256,768]{1,0:T(8,128)(2,1)}, bf16[256,768]{1,0:T(8,128)(2,1)S(1)}, u32[]{:S(2)}, u32[]{:S(2)}) collective-permute-start(bf16[256,768]{1,0:T(8,128)(2,1)} %get-tuple-element.381.pair_ref), channel_id=1, source_target_pairs={{0,2},{1,3},{2,0},{3,1},{4,6},{5,7},{6,4},{7,5},{8,10},{9,11},{10,... | collective-permute-start | bytes 1179656 | tf_op jit(solution)/shard_map/ppermute | solution.py:1126
  286.3 40.1 %collective-permute-start.45 = (bf16[384,1536]{1,0:T(8,128)(2,1)}, bf16[384,1536]{1,0:T(8,128)(2,1)S(1)}, u32[]{:S(2)}, u32[]{:S(2)}) collective-permute-start(bf16[384,1536]{1,0:T(8,128)(2,1)} %get-tuple-element.412), channel_id=1, source_target_pairs={{0,4},{4,0},{8,12},{12,8},{16,20},{20,16},{24,28},{28,24},{1,5},{5... | collective-permute-start | bytes 3538952 | tf_op jit(solution)/shard_map/ppermute | solution.py:1161
  308.2 24.7 %collective-permute-start.48 = (bf16[384,768]{1,0:T(8,128)(2,1)}, bf16[384,768]{1,0:T(8,128)(2,1)S(1)}, u32[]{:S(2)}, u32[]{:S(2)}) collective-permute-start(bf16[384,768]{1,0:T(8,128)(2,1)} %get-tuple-element.430), channel_id=1, source_target_pairs={{0,8},{4,12},{8,0},{12,4},{16,24},{20,28},{24,16},{28,20},{1,9},{5... | collective-permute-start | bytes 1769480 | tf_op jit(solution)/shard_map/ppermute | solution.py:1161
  311.5 19.2 %collective-permute-start.51 = (f32[4,768]{1,0:T(4,128)S(1)}, f32[4,768]{1,0:T(4,128)S(1)}, u32[]{:S(2)}, u32[]{:S(2)}) collective-permute-start(f32[4,768]{1,0:T(4,128)S(1)} %pad_maximum_fusion.8), channel_id=1, source_target_pairs={{0,1},{1,0},{2,3},{3,2},{4,5},{5,4},{6,7},{7,6},{8,9},{9,8},{10,11... | collective-permute-start | bytes 36872 | tf_op jit(solution)/shard_map/ppermute | solution.py:1126
  311.8 49.7 %collective-permute-start.54 = (bf16[256,768]{1,0:T(8,128)(2,1)S(1)}, bf16[256,768]{1,0:T(8,128)(2,1)S(1)}, u32[]{:S(2)}, u32[]{:S(2)}) collective-permute-start(bf16[256,768]{1,0:T(8,128)(2,1)S(1)} %copy-done.52), channel_id=1, source_target_pairs={{0,2},{1,3},{2,0},{3,1},{4,6},{5,7},{6,4},{7,5},{8,10},{9,11},{10,... | collective-permute-start | bytes 1179656 | tf_op jit(solution)/shard_map/ppermute | solution.py:1126
  330.5 21.4 %collective-permute-start.47 = (bf16[192,1536]{1,0:T(8,128)(2,1)}, bf16[192,1536]{1,0:T(8,128)(2,1)S(1)}, u32[]{:S(2)}, u32[]{:S(2)}) collective-permute-start(bf16[192,1536]{1,0:T(8,128)(2,1)} %get-tuple-element.439), channel_id=1, source_target_pairs={{0,8},{4,12},{8,0},{12,4},{16,24},{20,28},{24,16},{28,20},{1,9},{5... | collective-permute-start | bytes 1769480 | tf_op jit(solution)/shard_map/ppermute | solution.py:1161
  331.7 20.0 %collective-permute-start.50 = (bf16[256,768]{1,0:T(8,128)(2,1)S(1)}, bf16[256,768]{1,0:T(8,128)(2,1)S(1)}, u32[]{:S(2)}, u32[]{:S(2)}) collective-permute-start(bf16[256,768]{1,0:T(8,128)(2,1)S(1)} %copy-done.58), channel_id=1, source_target_pairs={{0,2},{1,3},{2,0},{3,1},{4,6},{5,7},{6,4},{7,5},{8,10},{9,11},{10,... | collective-permute-start | bytes 1179656 | tf_op jit(solution)/shard_map/ppermute | solution.py:1126
  336.0 15.7 %collective-permute-start.49 = (bf16[192,768]{1,0:T(8,128)(2,1)}, bf16[192,768]{1,0:T(8,128)(2,1)S(1)}, u32[]{:S(2)}, u32[]{:S(2)}) collective-permute-start(bf16[192,768]{1,0:T(8,128)(2,1)} %get-tuple-element.442), channel_id=1, source_target_pairs={{0,4},{4,0},{8,12},{12,8},{16,20},{20,16},{24,28},{28,24},{1,5},{5... | collective-permute-start | bytes 884744 | tf_op jit(solution)/shard_map/ppermute | solution.py:1161
  355.0 23.2 %collective-permute-start.56 = (bf16[96,1536]{1,0:T(8,128)(2,1)}, bf16[96,1536]{1,0:T(8,128)(2,1)S(1)}, u32[]{:S(2)}, u32[]{:S(2)}) collective-permute-start(bf16[96,1536]{1,0:T(8,128)(2,1)} %get-tuple-element.469), channel_id=1, source_target_pairs={{0,16},{4,20},{8,24},{12,28},{16,0},{20,4},{24,8},{28,12},{1,17},{... | collective-permute-start | bytes 884744 | tf_op jit(solution)/shard_map/ppermute | solution.py:1161
  359.1 19.0 %collective-permute-start.57 = (bf16[96,768]{1,0:T(8,128)(2,1)}, bf16[96,768]{1,0:T(8,128)(2,1)S(1)}, u32[]{:S(2)}, u32[]{:S(2)}) collective-permute-start(bf16[96,768]{1,0:T(8,128)(2,1)} %get-tuple-element.471), channel_id=1, source_target_pairs={{0,16},{4,20},{8,24},{12,28},{16,0},{20,4},{24,8},{28,12},{1,17},{... | collective-permute-start | bytes 442376 | tf_op jit(solution)/shard_map/ppermute | solution.py:1161
  (119 other events, 669.0 us)
Sparse Core Ops, SparseCore 0:
  10.3 82.3 all-gather.2
  95.7 53.9 all-gather.4
  249.3 97.0 reduce-scatter.1

commit v6 on v5

--- a/solution.py
+++ b/solution.py
@@ -790,7 +790,7 @@
     return u * half, slope
 
 
-PIECE = 256
+PIECE = 768
 
 
 def unit_pieces(units, *refs):
@@ -1273,7 +1273,8 @@
     pairs, received = exchanged(keep, send)
     first_w = after(first_w, pairs[1])
     ffn1_w, attn_w = first_w[:, : 2 * units], first_w[:, 2 * units :]
-    received[0], attn_w = tie(received[0], attn_w)
+    grad = [jnp.where(chip == 0, masked, grad_other), jnp.where(chip == 0, grad_other, masked)]
+    received[0], attn_w, *grad = tie(received[0], attn_w, *grad)
     ffn1_mate = from_mate(ffn1_w)
     ffn2_w = lax.all_gather(after(ffn2_own, pairs[1]), DATA, axis=0, tiled=True)
     ffn1_mate = after(ffn1_mate, received[0])
@@ -1301,7 +1302,6 @@
     ffn2_w = after(ffn2_w, pairs[1])
 
     ffn2_mate = from_mate(ffn2_w)
-    grad = [jnp.where(chip == 0, masked, grad_other), jnp.where(chip == 0, grad_other, masked)]
     g4 = list(grad)
     ffn2_mate = after(ffn2_mate, received[0])
     after_attn, n4, gh, act, nexts, arrived = [], [], [], [], [], []

time: 398 us -> 396 us (level)
  starting transfers between devices: 51.3 us -> 47.2 us
    ppermute x44 -> x36, starting transfers between devices: 27.4 us -> 24.6 us  [swap(): return lax.ppermute(x, TENSOR, [(i, i ^ bit) for i in range(4)])]
    ppermute x44 -> x36, waiting for transfers between devices: 38.9 us -> 38.2 us  [swap(): return lax.ppermute(x, TENSOR, [(i, i ^ bit) for i in range(4)])]
    unnamed x164 -> x152, local copies, waits for them, and re-layouts: 21.1 us -> 21.5 us
  transfers between devices with their start and end apart: 62 -> 54, of which waited for: 27 -> 23; matrix products, arithmetic and copies ran while one was open for 5% -> 4% of each run, Pallas kernels for 44% -> 45%
where the time goes in v6:
time: 396 us; the launch traced here: 388 us
  Pallas kernels  201 us (51%)
  waiting for transfers between devices  80.3 us (20%)
  starting transfers between devices  47.2 us (12%)
  local copies, waits for them, and re-layouts  33.8 us (9%)
  between operations  15.7 us (4%)
  other arithmetic  9.6 us (2%)
    pallas_call x32, Pallas kernels, call(): pl.pallas_call(body, in_specs=[SCALAR] * scalars + [WHOLE] * (len(args) -...  124 us
    ppermute x15, waiting for transfers between devices, swap(): return lax.ppermute(x, DATA, [(i, i ^ bit) for i in range(self.count)])  38.8 us
    ppermute x36, waiting for transfers between devices, swap(): return lax.ppermute(x, TENSOR, [(i, i ^ bit) for i in range(4)])  38.2 us
    ppermute x36, starting transfers between devices, swap(): return lax.ppermute(x, TENSOR, [(i, i ^ bit) for i in range(4)])  24.6 us
    ppermute x15, starting transfers between devices, swap(): return lax.ppermute(x, DATA, [(i, i ^ bit) for i in range(self.count)])  22.3 us
    unnamed x152, local copies, waits for them, and re-layouts  21.5 us
    pallas_call x2, Pallas kernels, ssm_grad_kernel(): pl.pallas_call(body, out_shape=(out, out), scratch_shapes=[pltpu.VMEM((bl...  15.6 us
    pallas_call x1, Pallas kernels, attn_backward_kernel(): pl.pallas_call(attn_bwd_body, in_specs=[SCALAR, SCALAR] + [WHOLE] * 9, ou...  14.7 us
  transfers between devices with their start and end apart: 54, of which 23 were waited for; matrix products, arithmetic and copies ran while one was open for 4% of the time, Pallas kernels for 45%

profile of v6, /device:TPU:0, one launch (start us, length us, event | category | flops | bytes accessed | tf_op | source)
XLA Modules:
  0.0 388.0 jit_solution(6775271819153850193)
XLA Ops:
  21.3 4.9 %collective-permute-done.2 = bf16[2,16,768]{2,1,0:T(8,128)(2,1)S(1)} collective-permute-done((bf16[2,16,768]{2,1,0:T(8,128)(2,1)S(1)}, bf16[2,16,768]{2,1,0:T(8,128)(2,1)S(1)}, u32[]{:S(2)}, u32[]{:S(2)}) %collective-permute-start.2) | collective-permute-done | bytes 49184 | tf_op jit(solution)/shard_map/ppermute | solution.py:1161
  31.0 14.8 %collective-permute-done.5 = bf16[2,96,768]{2,1,0:T(8,128)(2,1)S(1)} collective-permute-done((bf16[2,96,768]{2,1,0:T(8,128)(2,1)S(1)}, bf16[2,96,768]{2,1,0:T(8,128)(2,1)S(1)}, u32[]{:S(2)}, u32[]{:S(2)}) %collective-permute-start.5) | collective-permute-done | bytes 294944 | tf_op jit(solution)/shard_map/ppermute | solution.py:1161
  54.7 10.3 %kernel_spectra.1 = (f32[8,128,192]{2,1,0:T(8,128)}, f32[8,128,192]{2,1,0:T(8,128)}, f32[128,192]{1,0:T(8,128)}, f32[128,192]{1,0:T(8,128)}) custom-call(f32[64,192]{1,0:T(8,128)} %get-tuple-element.259.decay_ref, f32[64,192]{1,0:T(8,128)} %get-tuple-element.484.coef_ref, f32[64,192]{1,0:T(8,128)} %get-tuple-element.483.taps_ref, ...), custom_call_target="tpu_custom_call" | custom-call | flops 1210000000 | bytes 3850000 | tf_op jit(solution)/shard_map/kernel_spectra/pallas_call | solution.py:158
  65.0 6.3 %collective-permute-done.8 = bf16[2,2,96,768]{3,2,1,0:T(8,128)(2,1)S(1)} collective-permute-done((bf16[2,2,96,768]{3,2,1,0:T(8,128)(2,1)S(1)}, bf16[2,2,96,768]{3,2,1,0:T(8,128)(2,1)S(1)}, u32[]{:S(2)}, u32[]{:S(2)}) %collective-permute-start.8) | collective-permute-done | bytes 589856 | tf_op jit(solution)/shard_map/ppermute | solution.py:1161
  73.5 11.5 %mixer_forward.1 = (bf16[2,256,768]{2,1,0:T(8,128)(2,1)}, bf16[2,256,768]{2,1,0:T(8,128)(2,1)}, bf16[1024,768]{1,0:T(8,128)(2,1)}, bf16[1024,192]{1,0:T(8,128)(2...) custom-call(s32[1]{0:T(128)} %bitcast.23.core_ref, ...), custom_call_target="tpu_custom_call" | custom-call | flops 1540000000 | bytes 4900000 | tf_op jit(solution)/shard_map/mixer_forward/pallas_call | solution.py:291
  102.4 4.9 %collective-permute-done.11.received_ref = bf16[256,768]{1,0:T(8,128)(2,1)} collective-permute-done((bf16[256,768]{1,0:T(8,128)(2,1)S(1)}, bf16[256,768]{1,0:T(8,128)(2,1)}, u32[]{:S(2)}, u32[]{:S(2)}) %collective-permute-start.11) | collective-permute-done | bytes 393248 | tf_op jit(solution)/shard_map/ppermute | solution.py:1126
  107.4 5.7 %ffn_forward.2 = (f32[256,768]{1,0:T(8,128)}, bf16[256,768]{1,0:T(8,128)(2,1)}, f32[256,1536]{1,0:T(8,128)}, bf16[256,768]{1,0:T(8,128)(2,1)}) custom-call(f32[256,768]{1,0:T(8,128)} %get-tuple-element.254.h_ref.h0, bf16[256,768]{1,0:T(8,128)(2,1)} %copy-done.16, bf16[256,768]{1,0:T(8,128)(2,1)} %collective-permute-done.11.received_ref, ...), custom_call_target="tpu_custom_call" | custom-call | flops 5500000256 | bytes 17500000 | tf_op jit(solution)/shard_map/ffn_forward/pallas_call | solution.py:667
  116.1 5.6 %ffn_forward.3 = (f32[256,768]{1,0:T(8,128)}, bf16[256,768]{1,0:T(8,128)(2,1)}, f32[256,1536]{1,0:T(8,128)}, bf16[256,768]{1,0:T(8,128)(2,1)}) custom-call(f32[256,768]{1,0:T(8,128)} %get-tuple-element.273.h_ref.h1, bf16[256,768]{1,0:T(8,128)(2,1)} %copy-done.15, bf16[256,768]{1,0:T(8,128)(2,1)} %copy-done.61, f32[1,768]{1,0:T(1,128)} %squeeze.20.gain_ref, ...), custom_call_target="tpu_custom_call" | custom-call | flops 5500000256 | bytes 17500000 | tf_op jit(solution)/shard_map/ffn_forward/pallas_call | solution.py:667
  126.9 5.5 %collective-permute-done.16.received_ref = bf16[256,768]{1,0:T(8,128)(2,1)S(1)} collective-permute-done((bf16[256,768]{1,0:T(8,128)(2,1)}, bf16[256,768]{1,0:T(8,128)(2,1)S(1)}, u32[]{:S(2)}, u32[]{:S(2)}) %collective-permute-start.16) | collective-permute-done | bytes 393248 | tf_op jit(solution)/shard_map/ppermute | solution.py:1126
  138.3 11.5 %attn_forward.1 = (bf16[2,256,768]{2,1,0:T(8,128)(2,1)}, bf16[2,256,768]{2,1,0:T(8,128)(2,1)}, bf16[1024,768]{1,0:T(8,128)(2,1)}, bf16[1024,192]{1,0:T(8,128)(2,...) custom-call(s32[1]{0:T(128)} %bitcast.23.core_ref, ...), custom_call_target="tpu_custom_call" | custom-call | flops 1320000000 | bytes 4200000 | tf_op jit(solution)/shard_map/attn_forward/pallas_call | solution.py:579
  157.1 9.2 %collective-permute-done.19.received_ref = bf16[256,768]{1,0:T(8,128)(2,1)S(1)} collective-permute-done((bf16[256,768]{1,0:T(8,128)(2,1)S(1)}, bf16[256,768]{1,0:T(8,128)(2,1)S(1)}, u32[]{:S(2)}, u32[]{:S(2)}) %collective-permute-start.19) | collective-permute-done | bytes 393248 | tf_op jit(solution)/shard_map/ppermute | solution.py:1126
  167.8 6.5 %ffn_both.2 = (f32[256,768]{1,0:T(8,128)}, bf16[256,768]{1,0:T(8,128)(2,1)}, bf16[256,1536]{1,0:T(8,128)(2,1)}, bf16[256,1536]{1,0:T(8,128)(2,1)}, bf16[256,768]{1,0:T(8,128)(2,1)}) custom-call(f32[256,768]{1,0:T(8,128)} %get-tuple-element.277.h_ref, bf16[256,768]{1,0:T(8,128)(2,1)} %copy-done.21, bf16[256,768]{1,0:T(8,128)(2,1)} %copy-done.65, ...), custom_call_target="tpu_custom_call" | custom-call | flops 6600000000 | bytes 21000000 | tf_op jit(solution)/shard_map/ffn_both/pallas_call | solution.py:667
  176.3 6.4 %ffn_both.3 = (f32[256,768]{1,0:T(8,128)}, bf16[256,768]{1,0:T(8,128)(2,1)}, bf16[256,1536]{1,0:T(8,128)(2,1)}, bf16[256,1536]{1,0:T(8,128)(2,1)}, bf16[256,768]{1,0:T(8,128)(2,1)}) custom-call(f32[256,768]{1,0:T(8,128)} %get-tuple-element.290.h_ref, bf16[256,768]{1,0:T(8,128)(2,1)} %copy-done.18, bf16[256,768]{1,0:T(8,128)(2,1)} %copy-done.62, ...), custom_call_target="tpu_custom_call" | custom-call | flops 6600000000 | bytes 21000000 | tf_op jit(solution)/shard_map/ffn_both/pallas_call | solution.py:667
  188.7 6.4 %ffn_grads.2 = (bf16[768,1536]{1,0:T(8,128)(2,1)}, bf16[768,768]{1,0:T(8,128)(2,1)}, bf16[768,768]{1,0:T(8,128)(2,1)}) custom-call(bf16[256,768]{1,0:T(8,128)(2,1)} %get-tuple-element.305.n0, bf16[256,768]{1,0:T(8,128)(2,1)} %get-tuple-element.306.n1, bf16[256,768]{1,0:T(8,128)(2,1)} %get-tuple-element.285.g_ref.g0, ...), custom_call_target="tpu_custom_call" | custom-call | flops 660000000 | bytes 2100000 | tf_op jit(solution)/shard_map/ffn_grads/pallas_call | solution.py:667
  202.1 14.7 %attn_backward.1 = (bf16[2,256,768]{2,1,0:T(8,128)(2,1)}, bf16[2,256,768]{2,1,0:T(8,128)(2,1)}, bf16[1024,768]{1,0:T(8,128)(2,1)}, bf16[1024,576]{1,0:T(8,128)(2,1)}) custom-call(s32[1]{0:T(128)} %bitcast.23.core_ref, s32[1]{0:T(128)} %copy.65.len_ref, bf16[256,768]{1,0:T(8,128)(2,1)} %get-tuple-element.312.a_ref, bf16[256,768]{1,0:T(8,128)(2,1)} %copy-done.64, ...), custom_call_target="tpu_custom_call" | custom-call | flops 1540000000 | bytes 4900000 | tf_op jit(solution)/shard_map/attn_backward/pallas_call | solution.py:642
  224.2 8.6 %attn_grads.1 = bf16[768,2304]{1,0:T(8,128)(2,1)} custom-call(bf16[1024,768]{1,0:T(8,128)(2,1)} %get-tuple-element.304.x_ref, bf16[1024,576]{1,0:T(8,128)(2,1)} %get-tuple-element.317.gp_ref, bf16[1024,768]{1,0:T(8,128)(2,1)} %get-tuple-element.318.g_ref, bf16[192,1024]{1,0:T(8,128)(2,1)} %get-tuple-element.319.att_ref, ...), custom_call_target="tpu_custom_call" | custom-call | flops 880000000 | bytes 2800000 | tf_op jit(solution)/shard_map/attn_grads/pallas_call | solution.py:667
  232.9 5.2 %ffn_out.1 = (bf16[256,768]{1,0:T(8,128)(2,1)}, bf16[256,768]{1,0:T(8,128)(2,1)}) custom-call(s32[1]{0:T(128)} %bitcast.chip_ref, bf16[256,1536]{1,0:T(8,128)(2,1)} %get-tuple-element.329.a0.a0_ref, bf16[256,1536]{1,0:T(8,128)(2,1)} %get-tuple-element.330.a1.a1_ref, bf16[768,1536]{1,0:T(8,128)(2,1)} %all-gather.5.cloned.1.call-done.own_ref, ...), custom_call_target="tpu_custom_call" | custom-call | flops 330000000 | bytes 1050000 | tf_op jit(solution)/shard_map/ffn_out/pallas_call | solution.py:667
  240.3 7.1 %ffn_backward.2 = (f32[256,768]{1,0:T(8,128)}, bf16[256,768]{1,0:T(8,128)(2,1)}, bf16[256,1536]{1,0:T(8,128)(2,1)}, bf16[256,1536]{1,0:T(8,128)(2,1)}, bf16[256,768]{1,0:T(8,128)(2,1)}, /*index=5*/f32[1,768]{1,0:T(1,128)}) custom-call(f32[256,768]{1,0:T(8,128)} %get-tuple-element.334.g_ref, bf16[256,768]{1,0:T(8,128)(2,1)} %copy-done.17, ...), custom_call_target="tpu_custom_call" | custom-call | flops 6600000000 | bytes 21000000 | tf_op jit(solution)/shard_map/ffn_backward/pallas_call | solution.py:667
  249.9 6.8 %ffn_backward.3 = (f32[256,768]{1,0:T(8,128)}, bf16[256,768]{1,0:T(8,128)(2,1)}, bf16[256,1536]{1,0:T(8,128)(2,1)}, bf16[256,1536]{1,0:T(8,128)(2,1)}, bf16[256,768]{1,0:T(8,128)(2,1)}, /*index=5*/f32[1,768]{1,0:T(1,128)}) custom-call(f32[256,768]{1,0:T(8,128)} %get-tuple-element.339.g_ref, bf16[256,768]{1,0:T(8,128)(2,1)} %copy-done.14, ...), custom_call_target="tpu_custom_call" | custom-call | flops 6600000000 | bytes 21000000 | tf_op jit(solution)/shard_map/ffn_backward/pallas_call | solution.py:667
  262.9 6.4 %ffn_grads.3 = (bf16[768,1536]{1,0:T(8,128)(2,1)}, bf16[768,768]{1,0:T(8,128)(2,1)}, bf16[768,768]{1,0:T(8,128)(2,1)}) custom-call(bf16[256,768]{1,0:T(8,128)(2,1)} %get-tuple-element.332.n0, bf16[256,768]{1,0:T(8,128)(2,1)} %get-tuple-element.333.n1, bf16[256,768]{1,0:T(8,128)(2,1)} %get-tuple-element.338.g0, bf16[256,768]{1,0:T(8,128)(2,1)} %get-tuple-element.342.g1, ...), custom_call_target="tpu_custom_call" | custom-call | flops 660000000 | bytes 2100000 | tf_op jit(solution)/shard_map/ffn_grads/pallas_call | solution.py:667
  283.1 13.5 %mixer_backward.1 = (bf16[2,256,768]{2,1,0:T(8,128)(2,1)}, bf16[2,256,768]{2,1,0:T(8,128)(2,1)}, bf16[1024,768]{1,0:T(8,128)(2,1)}, bf16[1024,576]{1,0:T(8,128)(...) custom-call(s32[1]{0:T(128)} %bitcast.23.core_ref, ...), custom_call_target="tpu_custom_call" | custom-call | flops 1650000000 | bytes 5250000 | tf_op jit(solution)/shard_map/mixer_backward/pallas_call | solution.py:413
  296.7 6.3 %mixer_grads.1 = (bf16[384,768]{1,0:T(8,128)(2,1)}, bf16[384,768]{1,0:T(8,128)(2,1)}, f32[1,768]{1,0:T(1,128)}) custom-call(s32[1]{0:T(128)} %bitcast.38.side_ref, bf16[1024,768]{1,0:T(8,128)(2,1)} %get-tuple-element.382.x_ref, bf16[1024,576]{1,0:T(8,128)(2,1)} %get-tuple-element.383.gp_ref, bf16[1024,768]{1,0:T(8,128)(2,1)} %get-tuple-element.384.g_ref, ...), custom_call_target="tpu_custom_call" | custom-call | flops 660000000 | bytes 2100000 | tf_op jit(solution)/shard_map/mixer_grads/pallas_call | solution.py:667
  312.7 9.1 %ssm_grad.2 = (f32[64,128]{1,0:T(8,128)}, f32[64,128]{1,0:T(8,128)}) custom-call(bf16[8,128,192]{2,1,0:T(8,128)(2,1)} %get-tuple-element.408.g_re, bf16[8,128,192]{2,1,0:T(8,128)(2,1)} %get-tuple-element.409.g_im, bf16[8,128,192]{2,1,0:T(8,128)(2,1)} %get-tuple-element.391.u_re, bf16[8,128,192]{2,1,0:T(8,128)(2,1)} %get-tuple-element.392.u_im, ...), custom_call_target="tpu_custom_call" | custom-call | flops 1100000000 | bytes 3500000 | tf_op jit(solution)/shard_map/ssm_grad/pallas_call | solution.py:501
  333.1 6.6 %ssm_grad.3 = (f32[64,64]{1,0:T(8,128)}, f32[64,64]{1,0:T(8,128)}) custom-call(bf16[8,128,192]{2,1,0:T(8,128)(2,1)} %get-tuple-element.408.g_re, bf16[8,128,192]{2,1,0:T(8,128)(2,1)} %get-tuple-element.409.g_im, bf16[8,128,192]{2,1,0:T(8,128)(2,1)} %get-tuple-element.391.u_re, bf16[8,128,192]{2,1,0:T(8,128)(2,1)} %get-tuple-element.392.u_im, ...), custom_call_target="tpu_custom_call" | custom-call | flops 1100000000 | bytes 3500000 | tf_op jit(solution)/shard_map/ssm_grad/pallas_call | solution.py:501
  (320 shorter events, 178.5 us)
Async XLA Ops:
  7.3 84.8 %all-gather.3.cloned.1.call-start = ((), (), s32[]{:S(2)}) async-start(), calls=%async_computation.1 | async-start | bytes 3981312 | tf_op jit(solution)/shard_map/all_gather | solution.py:1242
  10.3 143.4 %all-gather.5.cloned.1.call-start = ((), (), s32[]{:S(2)}) async-start(), calls=%async_computation.2 | async-start | bytes 2654208 | tf_op jit(solution)/shard_map/all_gather | solution.py:1279
  15.8 32.4 %collective-permute-start = (bf16[256,768]{1,0:T(8,128)(2,1)S(1)}, bf16[256,768]{1,0:T(8,128)(2,1)S(1)}, u32[]{:S(2)}, u32[]{:S(2)}) collective-permute-start(bf16[256,768]{1,0:T(8,128)(2,1)S(1)} %copy-done.52), channel_id=1, source_target_pairs={{0,2},{1,3},{2,0},{3,1},{4,6},{5,7},{6,4},{7,5},{8,10},{9,11},{10,... | collective-permute-start | bytes 1179656 | tf_op jit(solution)/shard_map/ppermute | solution.py:1126
  28.0 17.8 %collective-permute-start.5 = (bf16[2,96,768]{2,1,0:T(8,128)(2,1)S(1)}, bf16[2,96,768]{2,1,0:T(8,128)(2,1)S(1)}, u32[]{:S(2)}, u32[]{:S(2)}) collective-permute-start(bf16[2,96,768]{2,1,0:T(8,128)(2,1)S(1)} %pad_maximum_fusion.2), channel_id=1, source_target_pairs={{0,8},{4,12},{8,0},{12,4},{16,24},{20,28},{24,16},{28,20},{1,9},{5... | collective-permute-start | bytes 884744 | tf_op jit(solution)/shard_map/ppermute | solution.py:1161
  46.7 24.6 %collective-permute-start.8 = (bf16[2,2,96,768]{3,2,1,0:T(8,128)(2,1)S(1)}, bf16[2,2,96,768]{3,2,1,0:T(8,128)(2,1)S(1)}, u32[]{:S(2)}, u32[]{:S(2)}) collective-permute-start(bf16[2,2,96,768]{3,2,1,0:T(8,128)(2,1)S(1)} %pad_maximum_fusion.1), channel_id=1, source_target_pairs={{0,4},{4,0},{8,12},{12,8},{16,20},{20,16},{24,28},{28,24},{1,5},{5... | collective-permute-start | bytes 1769480 | tf_op jit(solution)/shard_map/ppermute | solution.py:1161
  52.0 12.9 %collective-permute-start.9 = (bf16[256,768]{1,0:T(8,128)(2,1)S(1)}, bf16[256,768]{1,0:T(8,128)(2,1)S(1)}, u32[]{:S(2)}, u32[]{:S(2)}) collective-permute-start(bf16[256,768]{1,0:T(8,128)(2,1)S(1)} %broadcast_select_fusion), channel_id=1, source_target_pairs={{0,2},{1,3},{2,0},{3,1},{4,6},{5,7},{6,4},{7,5},{8,10},{9,11},{10,... | collective-permute-start | bytes 1179656 | tf_op jit(solution)/shard_map/ppermute | solution.py:1126
  53.4 19.2 %collective-permute-start.6 = (bf16[256,768]{1,0:T(8,128)(2,1)}, bf16[256,768]{1,0:T(8,128)(2,1)S(1)}, u32[]{:S(2)}, u32[]{:S(2)}) collective-permute-start(bf16[256,768]{1,0:T(8,128)(2,1)} %get-tuple-element.255.a_ref), channel_id=1, source_target_pairs={{0,1},{1,0},{2,3},{3,2},{4,5},{5,4},{6,7},{7,6},{8,9},{9,8},{10,11... | collective-permute-start | bytes 1179656 | tf_op jit(solution)/shard_map/ppermute | solution.py:1126
  54.2 18.4 %collective-permute-start.7 = (bf16[256,768]{1,0:T(8,128)(2,1)}, bf16[256,768]{1,0:T(8,128)(2,1)S(1)}, u32[]{:S(2)}, u32[]{:S(2)}) collective-permute-start(bf16[256,768]{1,0:T(8,128)(2,1)} %get-tuple-element.256.c_ref), channel_id=1, source_target_pairs={{0,1},{1,0},{2,3},{3,2},{4,5},{5,4},{6,7},{7,6},{8,9},{9,8},{10,11... | collective-permute-start | bytes 1179656 | tf_op jit(solution)/shard_map/ppermute | solution.py:1126
  94.0 13.4 %collective-permute-start.12 = (bf16[768,1536]{1,0:T(8,128)(2,1)S(1)}, bf16[768,1536]{1,0:T(8,128)(2,1)}, u32[]{:S(2)}, u32[]{:S(2)}) collective-permute-start(bf16[768,1536]{1,0:T(8,128)(2,1)S(1)} %slice.150.own_ref), channel_id=1, source_target_pairs={{0,1},{1,0},{2,3},{3,2},{4,5},{5,4},{6,7},{7,6},{8,9},{9,8},{10,11... | collective-permute-start | bytes 7077896 | tf_op jit(solution)/shard_map/ppermute | solution.py:1126
  95.0 273.7 %reduce-scatter.2.cloned.1.call-start = ((), (), s32[]{:S(2)}) async-start(), calls=%async_computation.3 | async-start | bytes 3981312 | tf_op jit(solution)/shard_map/reduce_scatter | solution.py:1355
  99.2 16.1 %collective-permute-start.14 = (bf16[256,768]{1,0:T(8,128)(2,1)S(1)}, bf16[256,768]{1,0:T(8,128)(2,1)S(1)}, u32[]{:S(2)}, u32[]{:S(2)}) collective-permute-start(bf16[256,768]{1,0:T(8,128)(2,1)S(1)} %get-tuple-element.471.pair_ref), channel_id=1, source_target_pairs={{0,2},{1,3},{2,0},{3,1},{4,6},{5,7},{6,4},{7,5},{8,10},{9,11},{10,... | collective-permute-start | bytes 1179656 | tf_op jit(solution)/shard_map/ppermute | solution.py:1126
  156.3 19.3 %collective-permute-start.21 = (bf16[256,768]{1,0:T(8,128)(2,1)S(1)}, bf16[256,768]{1,0:T(8,128)(2,1)S(1)}, u32[]{:S(2)}, u32[]{:S(2)}) collective-permute-start(bf16[256,768]{1,0:T(8,128)(2,1)S(1)} %get-tuple-element.469.pair_ref), channel_id=1, source_target_pairs={{0,2},{1,3},{2,0},{3,1},{4,6},{5,7},{6,4},{7,5},{8,10},{9,11},{10,... | collective-permute-start | bytes 1179656 | tf_op jit(solution)/shard_map/ppermute | solution.py:1126
  220.6 17.4 %collective-permute-start.29 = (bf16[256,768]{1,0:T(8,128)(2,1)S(1)}, bf16[256,768]{1,0:T(8,128)(2,1)S(1)}, u32[]{:S(2)}, u32[]{:S(2)}) collective-permute-start(bf16[256,768]{1,0:T(8,128)(2,1)S(1)} %get-tuple-element.467.pair_ref), channel_id=1, source_target_pairs={{0,2},{1,3},{2,0},{3,1},{4,6},{5,7},{6,4},{7,5},{8,10},{9,11},{10,... | collective-permute-start | bytes 1179656 | tf_op jit(solution)/shard_map/ppermute | solution.py:1126
  222.2 18.0 %collective-permute-start.30 = (bf16[256,768]{1,0:T(8,128)(2,1)S(1)}, bf16[256,768]{1,0:T(8,128)(2,1)S(1)}, u32[]{:S(2)}, u32[]{:S(2)}) collective-permute-start(bf16[256,768]{1,0:T(8,128)(2,1)S(1)} %get-tuple-element.468.pair_ref), channel_id=1, source_target_pairs={{0,2},{1,3},{2,0},{3,1},{4,6},{5,7},{6,4},{7,5},{8,10},{9,11},{10,... | collective-permute-start | bytes 1179656 | tf_op jit(solution)/shard_map/ppermute | solution.py:1126
  256.7 12.6 %collective-permute-start.33 = (bf16[256,768]{1,0:T(8,128)(2,1)}, bf16[256,768]{1,0:T(8,128)(2,1)S(1)}, u32[]{:S(2)}, u32[]{:S(2)}) collective-permute-start(bf16[256,768]{1,0:T(8,128)(2,1)} %get-tuple-element.349.pair_ref), channel_id=1, source_target_pairs={{0,2},{1,3},{2,0},{3,1},{4,6},{5,7},{6,4},{7,5},{8,10},{9,11},{10,... | collective-permute-start | bytes 1179656 | tf_op jit(solution)/shard_map/ppermute | solution.py:1126
  281.5 40.3 %collective-permute-start.37 = (bf16[384,1536]{1,0:T(8,128)(2,1)}, bf16[384,1536]{1,0:T(8,128)(2,1)S(1)}, u32[]{:S(2)}, u32[]{:S(2)}) collective-permute-start(bf16[384,1536]{1,0:T(8,128)(2,1)} %get-tuple-element.368), channel_id=1, source_target_pairs={{0,4},{4,0},{8,12},{12,8},{16,20},{20,16},{24,28},{28,24},{1,5},{5... | collective-permute-start | bytes 3538952 | tf_op jit(solution)/shard_map/ppermute | solution.py:1161
  303.2 25.3 %collective-permute-start.40 = (bf16[384,768]{1,0:T(8,128)(2,1)}, bf16[384,768]{1,0:T(8,128)(2,1)S(1)}, u32[]{:S(2)}, u32[]{:S(2)}) collective-permute-start(bf16[384,768]{1,0:T(8,128)(2,1)} %get-tuple-element.386), channel_id=1, source_target_pairs={{0,8},{4,12},{8,0},{12,4},{16,24},{20,28},{24,16},{28,20},{1,9},{5... | collective-permute-start | bytes 1769480 | tf_op jit(solution)/shard_map/ppermute | solution.py:1161
  306.8 19.6 %collective-permute-start.43 = (f32[4,768]{1,0:T(4,128)S(1)}, f32[4,768]{1,0:T(4,128)S(1)}, u32[]{:S(2)}, u32[]{:S(2)}) collective-permute-start(f32[4,768]{1,0:T(4,128)S(1)} %pad_maximum_fusion.8), channel_id=1, source_target_pairs={{0,1},{1,0},{2,3},{3,2},{4,5},{5,4},{6,7},{7,6},{8,9},{9,8},{10,11... | collective-permute-start | bytes 36872 | tf_op jit(solution)/shard_map/ppermute | solution.py:1126
  307.1 50.3 %collective-permute-start.46 = (bf16[256,768]{1,0:T(8,128)(2,1)S(1)}, bf16[256,768]{1,0:T(8,128)(2,1)S(1)}, u32[]{:S(2)}, u32[]{:S(2)}) collective-permute-start(bf16[256,768]{1,0:T(8,128)(2,1)S(1)} %copy-done.53), channel_id=1, source_target_pairs={{0,2},{1,3},{2,0},{3,1},{4,6},{5,7},{6,4},{7,5},{8,10},{9,11},{10,... | collective-permute-start | bytes 1179656 | tf_op jit(solution)/shard_map/ppermute | solution.py:1126
  325.9 23.5 %collective-permute-start.39 = (bf16[192,1536]{1,0:T(8,128)(2,1)}, bf16[192,1536]{1,0:T(8,128)(2,1)S(1)}, u32[]{:S(2)}, u32[]{:S(2)}) collective-permute-start(bf16[192,1536]{1,0:T(8,128)(2,1)} %get-tuple-element.395), channel_id=1, source_target_pairs={{0,8},{4,12},{8,0},{12,4},{16,24},{20,28},{24,16},{28,20},{1,9},{5... | collective-permute-start | bytes 1769480 | tf_op jit(solution)/shard_map/ppermute | solution.py:1161
  328.2 19.4 %collective-permute-start.42 = (bf16[256,768]{1,0:T(8,128)(2,1)S(1)}, bf16[256,768]{1,0:T(8,128)(2,1)S(1)}, u32[]{:S(2)}, u32[]{:S(2)}) collective-permute-start(bf16[256,768]{1,0:T(8,128)(2,1)S(1)} %copy-done.55), channel_id=1, source_target_pairs={{0,2},{1,3},{2,0},{3,1},{4,6},{5,7},{6,4},{7,5},{8,10},{9,11},{10,... | collective-permute-start | bytes 1179656 | tf_op jit(solution)/shard_map/ppermute | solution.py:1126
  331.6 16.0 %collective-permute-start.41 = (bf16[192,768]{1,0:T(8,128)(2,1)}, bf16[192,768]{1,0:T(8,128)(2,1)S(1)}, u32[]{:S(2)}, u32[]{:S(2)}) collective-permute-start(bf16[192,768]{1,0:T(8,128)(2,1)} %get-tuple-element.398), channel_id=1, source_target_pairs={{0,4},{4,0},{8,12},{12,8},{16,20},{20,16},{24,28},{28,24},{1,5},{5... | collective-permute-start | bytes 884744 | tf_op jit(solution)/shard_map/ppermute | solution.py:1161
  352.4 22.7 %collective-permute-start.48 = (bf16[96,1536]{1,0:T(8,128)(2,1)}, bf16[96,1536]{1,0:T(8,128)(2,1)S(1)}, u32[]{:S(2)}, u32[]{:S(2)}) collective-permute-start(bf16[96,1536]{1,0:T(8,128)(2,1)} %get-tuple-element.425), channel_id=1, source_target_pairs={{0,16},{4,20},{8,24},{12,28},{16,0},{20,4},{24,8},{28,12},{1,17},{... | collective-permute-start | bytes 884744 | tf_op jit(solution)/shard_map/ppermute | solution.py:1161
  356.6 18.6 %collective-permute-start.49 = (bf16[96,768]{1,0:T(8,128)(2,1)}, bf16[96,768]{1,0:T(8,128)(2,1)S(1)}, u32[]{:S(2)}, u32[]{:S(2)}) collective-permute-start(bf16[96,768]{1,0:T(8,128)(2,1)} %get-tuple-element.427), channel_id=1, source_target_pairs={{0,16},{4,20},{8,24},{12,28},{16,0},{20,4},{24,8},{28,12},{1,17},{... | collective-permute-start | bytes 442376 | tf_op jit(solution)/shard_map/ppermute | solution.py:1161
  (105 other events, 565.6 us)
Sparse Core Ops, SparseCore 0:
  10.4 81.6 all-gather.2
  95.1 53.0 all-gather.4
  247.5 96.0 reduce-scatter.1

commit v7 on v6

--- a/solution.py
+++ b/solution.py
@@ -512,16 +512,27 @@
 
 HEAD = 64
 QROWS = 256
+LIVE = 512
 
 
 def dot_tn(a, b):
     return lax.dot_general(a, b, (((0,), (0,)), ((), ())), preferred_element_type=F32)
 
 
-def allowed_keys(keys, first_query, queries, length):
-    key = lax.broadcasted_iota(jnp.int32, (keys, queries), 0)
-    query = lax.broadcasted_iota(jnp.int32, (keys, queries), 1) + first_query
-    return (key <= query) & (key < length)
+def masked(s, first, length):
+    key = lax.broadcasted_iota(jnp.int32, (QROWS, QROWS), 0)
+    query = lax.broadcasted_iota(jnp.int32, (QROWS, QROWS), 1)
+    parts = []
+    for start in range(0, first + QROWS, QROWS):
+        part = s[start : start + QROWS]
+        allowed = None
+        if start == first:
+            allowed = key <= query
+        if start >= LIVE:
+            short = key < length - start
+            allowed = short if allowed is None else allowed & short
+        parts.append(part if allowed is None else jnp.where(allowed, part, -jnp.inf))
+    return parts[0] if len(parts) == 1 else jnp.concatenate(parts, axis=0)
 
 
 def attn_fwd_body(
@@ -550,7 +561,7 @@
         for first in range(0, rows, QROWS):
             n = first + QROWS
             s = dot_nt(k[:n], q[first:n])
-            s = jnp.where(allowed_keys(n, first, QROWS, length), s, -jnp.inf)
+            s = masked(s, first, length)
             top = jnp.max(s, axis=0, keepdims=True)
             e = jnp.exp(s - top)
             total = jnp.sum(e, axis=0, keepdims=True)
@@ -617,9 +628,7 @@
         for first in range(0, rows, QROWS):
             n = first + QROWS
             s = dot_nt(k[:n], q[first:n])
-            probs = jnp.where(
-                allowed_keys(n, first, QROWS, length), jnp.exp(s - lse_ref[h : h + 1, first:n]), 0.0
-            )
+            probs = jnp.exp(masked(s, first, length) - lse_ref[h : h + 1, first:n])
             gp = dot_nt(v[:n], g[first:n])
             inner = jnp.sum(probs * gp, axis=0, keepdims=True)
             gs = (probs * (gp - inner)).astype(BF16)

time: 396 us -> 396 us (level)
  no operation moved by 1% of the time
where the time goes in v7:
time: 396 us; the launch traced here: 388 us
  Pallas kernels  202 us (51%)
  waiting for transfers between devices  80.4 us (20%)
  starting transfers between devices  46.8 us (12%)
  local copies, waits for them, and re-layouts  33.8 us (9%)
  between operations  15.7 us (4%)
  other arithmetic  9.6 us (2%)
    pallas_call x32, Pallas kernels, call(): pl.pallas_call(body, in_specs=[SCALAR] * scalars + [WHOLE] * (len(args) -...  125 us
    ppermute x15, waiting for transfers between devices, swap(): return lax.ppermute(x, DATA, [(i, i ^ bit) for i in range(self.count)])  38.8 us
    ppermute x36, waiting for transfers between devices, swap(): return lax.ppermute(x, TENSOR, [(i, i ^ bit) for i in range(4)])  38.3 us
    ppermute x36, starting transfers between devices, swap(): return lax.ppermute(x, TENSOR, [(i, i ^ bit) for i in range(4)])  24.2 us
    ppermute x15, starting transfers between devices, swap(): return lax.ppermute(x, DATA, [(i, i ^ bit) for i in range(self.count)])  22.3 us
    unnamed x152, local copies, waits for them, and re-layouts  21.5 us
    pallas_call x2, Pallas kernels, ssm_grad_kernel(): pl.pallas_call(body, out_shape=(out, out), scratch_shapes=[pltpu.VMEM((bl...  15.6 us
    pallas_call x1, Pallas kernels, attn_backward_kernel(): pl.pallas_call(attn_bwd_body, in_specs=[SCALAR, SCALAR] + [WHOLE] * 9, ou...  14.7 us
  transfers between devices with their start and end apart: 54, of which 23 were waited for; matrix products, arithmetic and copies ran while one was open for 4% of the time, Pallas kernels for 45%

profile of v7, /device:TPU:0, one launch (start us, length us, event | category | flops | bytes accessed | tf_op | source)
XLA Modules:
  0.0 388.0 jit_solution(3174661175420120357)
XLA Ops:
  21.3 4.9 %collective-permute-done.2 = bf16[2,16,768]{2,1,0:T(8,128)(2,1)S(1)} collective-permute-done((bf16[2,16,768]{2,1,0:T(8,128)(2,1)S(1)}, bf16[2,16,768]{2,1,0:T(8,128)(2,1)S(1)}, u32[]{:S(2)}, u32[]{:S(2)}) %collective-permute-start.2) | collective-permute-done | bytes 49184 | tf_op jit(solution)/shard_map/ppermute | solution.py:1170
  31.0 14.8 %collective-permute-done.5 = bf16[2,96,768]{2,1,0:T(8,128)(2,1)S(1)} collective-permute-done((bf16[2,96,768]{2,1,0:T(8,128)(2,1)S(1)}, bf16[2,96,768]{2,1,0:T(8,128)(2,1)S(1)}, u32[]{:S(2)}, u32[]{:S(2)}) %collective-permute-start.5) | collective-permute-done | bytes 294944 | tf_op jit(solution)/shard_map/ppermute | solution.py:1170
  54.7 10.3 %kernel_spectra.1 = (f32[8,128,192]{2,1,0:T(8,128)}, f32[8,128,192]{2,1,0:T(8,128)}, f32[128,192]{1,0:T(8,128)}, f32[128,192]{1,0:T(8,128)}) custom-call(f32[64,192]{1,0:T(8,128)} %get-tuple-element.259.decay_ref, f32[64,192]{1,0:T(8,128)} %get-tuple-element.484.coef_ref, f32[64,192]{1,0:T(8,128)} %get-tuple-element.483.taps_ref, ...), custom_call_target="tpu_custom_call" | custom-call | flops 1210000000 | bytes 3850000 | tf_op jit(solution)/shard_map/kernel_spectra/pallas_call | solution.py:158
  65.0 6.3 %collective-permute-done.8 = bf16[2,2,96,768]{3,2,1,0:T(8,128)(2,1)S(1)} collective-permute-done((bf16[2,2,96,768]{3,2,1,0:T(8,128)(2,1)S(1)}, bf16[2,2,96,768]{3,2,1,0:T(8,128)(2,1)S(1)}, u32[]{:S(2)}, u32[]{:S(2)}) %collective-permute-start.8) | collective-permute-done | bytes 589856 | tf_op jit(solution)/shard_map/ppermute | solution.py:1170
  73.5 11.5 %mixer_forward.1 = (bf16[2,256,768]{2,1,0:T(8,128)(2,1)}, bf16[2,256,768]{2,1,0:T(8,128)(2,1)}, bf16[1024,768]{1,0:T(8,128)(2,1)}, bf16[1024,192]{1,0:T(8,128)(2...) custom-call(s32[1]{0:T(128)} %bitcast.23.core_ref, ...), custom_call_target="tpu_custom_call" | custom-call | flops 1540000000 | bytes 4900000 | tf_op jit(solution)/shard_map/mixer_forward/pallas_call | solution.py:291
  102.4 4.9 %collective-permute-done.11.received_ref = bf16[256,768]{1,0:T(8,128)(2,1)} collective-permute-done((bf16[256,768]{1,0:T(8,128)(2,1)S(1)}, bf16[256,768]{1,0:T(8,128)(2,1)}, u32[]{:S(2)}, u32[]{:S(2)}) %collective-permute-start.11) | collective-permute-done | bytes 393248 | tf_op jit(solution)/shard_map/ppermute | solution.py:1135
  107.4 5.7 %ffn_forward.2 = (f32[256,768]{1,0:T(8,128)}, bf16[256,768]{1,0:T(8,128)(2,1)}, f32[256,1536]{1,0:T(8,128)}, bf16[256,768]{1,0:T(8,128)(2,1)}) custom-call(f32[256,768]{1,0:T(8,128)} %get-tuple-element.254.h_ref.h0, bf16[256,768]{1,0:T(8,128)(2,1)} %copy-done.16, bf16[256,768]{1,0:T(8,128)(2,1)} %collective-permute-done.11.received_ref, ...), custom_call_target="tpu_custom_call" | custom-call | flops 5500000256 | bytes 17500000 | tf_op jit(solution)/shard_map/ffn_forward/pallas_call | solution.py:676
  116.1 5.6 %ffn_forward.3 = (f32[256,768]{1,0:T(8,128)}, bf16[256,768]{1,0:T(8,128)(2,1)}, f32[256,1536]{1,0:T(8,128)}, bf16[256,768]{1,0:T(8,128)(2,1)}) custom-call(f32[256,768]{1,0:T(8,128)} %get-tuple-element.273.h_ref.h1, bf16[256,768]{1,0:T(8,128)(2,1)} %copy-done.15, bf16[256,768]{1,0:T(8,128)(2,1)} %copy-done.61, f32[1,768]{1,0:T(1,128)} %squeeze.20.gain_ref, ...), custom_call_target="tpu_custom_call" | custom-call | flops 5500000256 | bytes 17500000 | tf_op jit(solution)/shard_map/ffn_forward/pallas_call | solution.py:676
  126.9 5.5 %collective-permute-done.16.received_ref = bf16[256,768]{1,0:T(8,128)(2,1)S(1)} collective-permute-done((bf16[256,768]{1,0:T(8,128)(2,1)}, bf16[256,768]{1,0:T(8,128)(2,1)S(1)}, u32[]{:S(2)}, u32[]{:S(2)}) %collective-permute-start.16) | collective-permute-done | bytes 393248 | tf_op jit(solution)/shard_map/ppermute | solution.py:1135
  138.3 11.4 %attn_forward.1 = (bf16[2,256,768]{2,1,0:T(8,128)(2,1)}, bf16[2,256,768]{2,1,0:T(8,128)(2,1)}, bf16[1024,768]{1,0:T(8,128)(2,1)}, bf16[1024,192]{1,0:T(8,128)(2,...) custom-call(s32[1]{0:T(128)} %bitcast.23.core_ref, ...), custom_call_target="tpu_custom_call" | custom-call | flops 1320000000 | bytes 4200000 | tf_op jit(solution)/shard_map/attn_forward/pallas_call | solution.py:590
  156.5 9.2 %collective-permute-done.19.received_ref = bf16[256,768]{1,0:T(8,128)(2,1)S(1)} collective-permute-done((bf16[256,768]{1,0:T(8,128)(2,1)S(1)}, bf16[256,768]{1,0:T(8,128)(2,1)S(1)}, u32[]{:S(2)}, u32[]{:S(2)}) %collective-permute-start.19) | collective-permute-done | bytes 393248 | tf_op jit(solution)/shard_map/ppermute | solution.py:1135
  167.3 6.9 %ffn_both.2 = (f32[256,768]{1,0:T(8,128)}, bf16[256,768]{1,0:T(8,128)(2,1)}, bf16[256,1536]{1,0:T(8,128)(2,1)}, bf16[256,1536]{1,0:T(8,128)(2,1)}, bf16[256,768]{1,0:T(8,128)(2,1)}) custom-call(f32[256,768]{1,0:T(8,128)} %get-tuple-element.277.h_ref, bf16[256,768]{1,0:T(8,128)(2,1)} %copy-done.21, bf16[256,768]{1,0:T(8,128)(2,1)} %copy-done.65, ...), custom_call_target="tpu_custom_call" | custom-call | flops 6600000000 | bytes 21000000 | tf_op jit(solution)/shard_map/ffn_both/pallas_call | solution.py:676
  176.1 6.4 %ffn_both.3 = (f32[256,768]{1,0:T(8,128)}, bf16[256,768]{1,0:T(8,128)(2,1)}, bf16[256,1536]{1,0:T(8,128)(2,1)}, bf16[256,1536]{1,0:T(8,128)(2,1)}, bf16[256,768]{1,0:T(8,128)(2,1)}) custom-call(f32[256,768]{1,0:T(8,128)} %get-tuple-element.290.h_ref, bf16[256,768]{1,0:T(8,128)(2,1)} %copy-done.18, bf16[256,768]{1,0:T(8,128)(2,1)} %copy-done.62, ...), custom_call_target="tpu_custom_call" | custom-call | flops 6600000000 | bytes 21000000 | tf_op jit(solution)/shard_map/ffn_both/pallas_call | solution.py:676
  188.5 6.4 %ffn_grads.2 = (bf16[768,1536]{1,0:T(8,128)(2,1)}, bf16[768,768]{1,0:T(8,128)(2,1)}, bf16[768,768]{1,0:T(8,128)(2,1)}) custom-call(bf16[256,768]{1,0:T(8,128)(2,1)} %get-tuple-element.305.n0, bf16[256,768]{1,0:T(8,128)(2,1)} %get-tuple-element.306.n1, bf16[256,768]{1,0:T(8,128)(2,1)} %get-tuple-element.285.g_ref.g0, ...), custom_call_target="tpu_custom_call" | custom-call | flops 660000000 | bytes 2100000 | tf_op jit(solution)/shard_map/ffn_grads/pallas_call | solution.py:676
  201.9 14.7 %attn_backward.1 = (bf16[2,256,768]{2,1,0:T(8,128)(2,1)}, bf16[2,256,768]{2,1,0:T(8,128)(2,1)}, bf16[1024,768]{1,0:T(8,128)(2,1)}, bf16[1024,576]{1,0:T(8,128)(2,1)}) custom-call(s32[1]{0:T(128)} %bitcast.23.core_ref, s32[1]{0:T(128)} %copy.65.len_ref, bf16[256,768]{1,0:T(8,128)(2,1)} %get-tuple-element.312.a_ref, bf16[256,768]{1,0:T(8,128)(2,1)} %copy-done.64, ...), custom_call_target="tpu_custom_call" | custom-call | flops 1540000000 | bytes 4900000 | tf_op jit(solution)/shard_map/attn_backward/pallas_call | solution.py:651
  224.1 8.6 %attn_grads.1 = bf16[768,2304]{1,0:T(8,128)(2,1)} custom-call(bf16[1024,768]{1,0:T(8,128)(2,1)} %get-tuple-element.304.x_ref, bf16[1024,576]{1,0:T(8,128)(2,1)} %get-tuple-element.317.gp_ref, bf16[1024,768]{1,0:T(8,128)(2,1)} %get-tuple-element.318.g_ref, bf16[192,1024]{1,0:T(8,128)(2,1)} %get-tuple-element.319.att_ref, ...), custom_call_target="tpu_custom_call" | custom-call | flops 880000000 | bytes 2800000 | tf_op jit(solution)/shard_map/attn_grads/pallas_call | solution.py:676
  232.7 5.2 %ffn_out.1 = (bf16[256,768]{1,0:T(8,128)(2,1)}, bf16[256,768]{1,0:T(8,128)(2,1)}) custom-call(s32[1]{0:T(128)} %bitcast.chip_ref, bf16[256,1536]{1,0:T(8,128)(2,1)} %get-tuple-element.329.a0.a0_ref, bf16[256,1536]{1,0:T(8,128)(2,1)} %get-tuple-element.330.a1.a1_ref, bf16[768,1536]{1,0:T(8,128)(2,1)} %all-gather.5.cloned.1.call-done.own_ref, ...), custom_call_target="tpu_custom_call" | custom-call | flops 330000000 | bytes 1050000 | tf_op jit(solution)/shard_map/ffn_out/pallas_call | solution.py:676
  240.1 7.1 %ffn_backward.2 = (f32[256,768]{1,0:T(8,128)}, bf16[256,768]{1,0:T(8,128)(2,1)}, bf16[256,1536]{1,0:T(8,128)(2,1)}, bf16[256,1536]{1,0:T(8,128)(2,1)}, bf16[256,768]{1,0:T(8,128)(2,1)}, /*index=5*/f32[1,768]{1,0:T(1,128)}) custom-call(f32[256,768]{1,0:T(8,128)} %get-tuple-element.334.g_ref, bf16[256,768]{1,0:T(8,128)(2,1)} %copy-done.17, ...), custom_call_target="tpu_custom_call" | custom-call | flops 6600000000 | bytes 21000000 | tf_op jit(solution)/shard_map/ffn_backward/pallas_call | solution.py:676
  249.8 6.8 %ffn_backward.3 = (f32[256,768]{1,0:T(8,128)}, bf16[256,768]{1,0:T(8,128)(2,1)}, bf16[256,1536]{1,0:T(8,128)(2,1)}, bf16[256,1536]{1,0:T(8,128)(2,1)}, bf16[256,768]{1,0:T(8,128)(2,1)}, /*index=5*/f32[1,768]{1,0:T(1,128)}) custom-call(f32[256,768]{1,0:T(8,128)} %get-tuple-element.339.g_ref, bf16[256,768]{1,0:T(8,128)(2,1)} %copy-done.14, ...), custom_call_target="tpu_custom_call" | custom-call | flops 6600000000 | bytes 21000000 | tf_op jit(solution)/shard_map/ffn_backward/pallas_call | solution.py:676
  262.8 6.4 %ffn_grads.3 = (bf16[768,1536]{1,0:T(8,128)(2,1)}, bf16[768,768]{1,0:T(8,128)(2,1)}, bf16[768,768]{1,0:T(8,128)(2,1)}) custom-call(bf16[256,768]{1,0:T(8,128)(2,1)} %get-tuple-element.332.n0, bf16[256,768]{1,0:T(8,128)(2,1)} %get-tuple-element.333.n1, bf16[256,768]{1,0:T(8,128)(2,1)} %get-tuple-element.338.g0, bf16[256,768]{1,0:T(8,128)(2,1)} %get-tuple-element.342.g1, ...), custom_call_target="tpu_custom_call" | custom-call | flops 660000000 | bytes 2100000 | tf_op jit(solution)/shard_map/ffn_grads/pallas_call | solution.py:676
  283.1 13.5 %mixer_backward.1 = (bf16[2,256,768]{2,1,0:T(8,128)(2,1)}, bf16[2,256,768]{2,1,0:T(8,128)(2,1)}, bf16[1024,768]{1,0:T(8,128)(2,1)}, bf16[1024,576]{1,0:T(8,128)(...) custom-call(s32[1]{0:T(128)} %bitcast.23.core_ref, ...), custom_call_target="tpu_custom_call" | custom-call | flops 1650000000 | bytes 5250000 | tf_op jit(solution)/shard_map/mixer_backward/pallas_call | solution.py:413
  296.7 6.3 %mixer_grads.1 = (bf16[384,768]{1,0:T(8,128)(2,1)}, bf16[384,768]{1,0:T(8,128)(2,1)}, f32[1,768]{1,0:T(1,128)}) custom-call(s32[1]{0:T(128)} %bitcast.38.side_ref, bf16[1024,768]{1,0:T(8,128)(2,1)} %get-tuple-element.382.x_ref, bf16[1024,576]{1,0:T(8,128)(2,1)} %get-tuple-element.383.gp_ref, bf16[1024,768]{1,0:T(8,128)(2,1)} %get-tuple-element.384.g_ref, ...), custom_call_target="tpu_custom_call" | custom-call | flops 660000000 | bytes 2100000 | tf_op jit(solution)/shard_map/mixer_grads/pallas_call | solution.py:676
  312.7 9.1 %ssm_grad.2 = (f32[64,128]{1,0:T(8,128)}, f32[64,128]{1,0:T(8,128)}) custom-call(bf16[8,128,192]{2,1,0:T(8,128)(2,1)} %get-tuple-element.408.g_re, bf16[8,128,192]{2,1,0:T(8,128)(2,1)} %get-tuple-element.409.g_im, bf16[8,128,192]{2,1,0:T(8,128)(2,1)} %get-tuple-element.391.u_re, bf16[8,128,192]{2,1,0:T(8,128)(2,1)} %get-tuple-element.392.u_im, ...), custom_call_target="tpu_custom_call" | custom-call | flops 1100000000 | bytes 3500000 | tf_op jit(solution)/shard_map/ssm_grad/pallas_call | solution.py:501
  333.1 6.5 %ssm_grad.3 = (f32[64,64]{1,0:T(8,128)}, f32[64,64]{1,0:T(8,128)}) custom-call(bf16[8,128,192]{2,1,0:T(8,128)(2,1)} %get-tuple-element.408.g_re, bf16[8,128,192]{2,1,0:T(8,128)(2,1)} %get-tuple-element.409.g_im, bf16[8,128,192]{2,1,0:T(8,128)(2,1)} %get-tuple-element.391.u_re, bf16[8,128,192]{2,1,0:T(8,128)(2,1)} %get-tuple-element.392.u_im, ...), custom_call_target="tpu_custom_call" | custom-call | flops 1100000000 | bytes 3500000 | tf_op jit(solution)/shard_map/ssm_grad/pallas_call | solution.py:501
  (320 shorter events, 178.2 us)
Async XLA Ops:
  7.3 84.8 %all-gather.3.cloned.1.call-start = ((), (), s32[]{:S(2)}) async-start(), calls=%async_computation.1 | async-start | bytes 3981312 | tf_op jit(solution)/shard_map/all_gather | solution.py:1251
  10.3 143.3 %all-gather.5.cloned.1.call-start = ((), (), s32[]{:S(2)}) async-start(), calls=%async_computation.2 | async-start | bytes 2654208 | tf_op jit(solution)/shard_map/all_gather | solution.py:1288
  15.8 32.4 %collective-permute-start = (bf16[256,768]{1,0:T(8,128)(2,1)S(1)}, bf16[256,768]{1,0:T(8,128)(2,1)S(1)}, u32[]{:S(2)}, u32[]{:S(2)}) collective-permute-start(bf16[256,768]{1,0:T(8,128)(2,1)S(1)} %copy-done.52), channel_id=1, source_target_pairs={{0,2},{1,3},{2,0},{3,1},{4,6},{5,7},{6,4},{7,5},{8,10},{9,11},{10,... | collective-permute-start | bytes 1179656 | tf_op jit(solution)/shard_map/ppermute | solution.py:1135
  28.0 17.8 %collective-permute-start.5 = (bf16[2,96,768]{2,1,0:T(8,128)(2,1)S(1)}, bf16[2,96,768]{2,1,0:T(8,128)(2,1)S(1)}, u32[]{:S(2)}, u32[]{:S(2)}) collective-permute-start(bf16[2,96,768]{2,1,0:T(8,128)(2,1)S(1)} %pad_maximum_fusion.2), channel_id=1, source_target_pairs={{0,8},{4,12},{8,0},{12,4},{16,24},{20,28},{24,16},{28,20},{1,9},{5... | collective-permute-start | bytes 884744 | tf_op jit(solution)/shard_map/ppermute | solution.py:1170
  46.7 24.6 %collective-permute-start.8 = (bf16[2,2,96,768]{3,2,1,0:T(8,128)(2,1)S(1)}, bf16[2,2,96,768]{3,2,1,0:T(8,128)(2,1)S(1)}, u32[]{:S(2)}, u32[]{:S(2)}) collective-permute-start(bf16[2,2,96,768]{3,2,1,0:T(8,128)(2,1)S(1)} %pad_maximum_fusion.1), channel_id=1, source_target_pairs={{0,4},{4,0},{8,12},{12,8},{16,20},{20,16},{24,28},{28,24},{1,5},{5... | collective-permute-start | bytes 1769480 | tf_op jit(solution)/shard_map/ppermute | solution.py:1170
  52.0 12.9 %collective-permute-start.9 = (bf16[256,768]{1,0:T(8,128)(2,1)S(1)}, bf16[256,768]{1,0:T(8,128)(2,1)S(1)}, u32[]{:S(2)}, u32[]{:S(2)}) collective-permute-start(bf16[256,768]{1,0:T(8,128)(2,1)S(1)} %broadcast_select_fusion), channel_id=1, source_target_pairs={{0,2},{1,3},{2,0},{3,1},{4,6},{5,7},{6,4},{7,5},{8,10},{9,11},{10,... | collective-permute-start | bytes 1179656 | tf_op jit(solution)/shard_map/ppermute | solution.py:1135
  53.4 19.2 %collective-permute-start.6 = (bf16[256,768]{1,0:T(8,128)(2,1)}, bf16[256,768]{1,0:T(8,128)(2,1)S(1)}, u32[]{:S(2)}, u32[]{:S(2)}) collective-permute-start(bf16[256,768]{1,0:T(8,128)(2,1)} %get-tuple-element.255.a_ref), channel_id=1, source_target_pairs={{0,1},{1,0},{2,3},{3,2},{4,5},{5,4},{6,7},{7,6},{8,9},{9,8},{10,11... | collective-permute-start | bytes 1179656 | tf_op jit(solution)/shard_map/ppermute | solution.py:1135
  54.2 18.4 %collective-permute-start.7 = (bf16[256,768]{1,0:T(8,128)(2,1)}, bf16[256,768]{1,0:T(8,128)(2,1)S(1)}, u32[]{:S(2)}, u32[]{:S(2)}) collective-permute-start(bf16[256,768]{1,0:T(8,128)(2,1)} %get-tuple-element.256.c_ref), channel_id=1, source_target_pairs={{0,1},{1,0},{2,3},{3,2},{4,5},{5,4},{6,7},{7,6},{8,9},{9,8},{10,11... | collective-permute-start | bytes 1179656 | tf_op jit(solution)/shard_map/ppermute | solution.py:1135
  94.0 13.4 %collective-permute-start.12 = (bf16[768,1536]{1,0:T(8,128)(2,1)S(1)}, bf16[768,1536]{1,0:T(8,128)(2,1)}, u32[]{:S(2)}, u32[]{:S(2)}) collective-permute-start(bf16[768,1536]{1,0:T(8,128)(2,1)S(1)} %slice.150.own_ref), channel_id=1, source_target_pairs={{0,1},{1,0},{2,3},{3,2},{4,5},{5,4},{6,7},{7,6},{8,9},{9,8},{10,11... | collective-permute-start | bytes 7077896 | tf_op jit(solution)/shard_map/ppermute | solution.py:1135
  95.0 273.7 %reduce-scatter.2.cloned.1.call-start = ((), (), s32[]{:S(2)}) async-start(), calls=%async_computation.3 | async-start | bytes 3981312 | tf_op jit(solution)/shard_map/reduce_scatter | solution.py:1364
  99.2 16.1 %collective-permute-start.14 = (bf16[256,768]{1,0:T(8,128)(2,1)S(1)}, bf16[256,768]{1,0:T(8,128)(2,1)S(1)}, u32[]{:S(2)}, u32[]{:S(2)}) collective-permute-start(bf16[256,768]{1,0:T(8,128)(2,1)S(1)} %get-tuple-element.471.pair_ref), channel_id=1, source_target_pairs={{0,2},{1,3},{2,0},{3,1},{4,6},{5,7},{6,4},{7,5},{8,10},{9,11},{10,... | collective-permute-start | bytes 1179656 | tf_op jit(solution)/shard_map/ppermute | solution.py:1135
  155.7 19.7 %collective-permute-start.21 = (bf16[256,768]{1,0:T(8,128)(2,1)S(1)}, bf16[256,768]{1,0:T(8,128)(2,1)S(1)}, u32[]{:S(2)}, u32[]{:S(2)}) collective-permute-start(bf16[256,768]{1,0:T(8,128)(2,1)S(1)} %get-tuple-element.469.pair_ref), channel_id=1, source_target_pairs={{0,2},{1,3},{2,0},{3,1},{4,6},{5,7},{6,4},{7,5},{8,10},{9,11},{10,... | collective-permute-start | bytes 1179656 | tf_op jit(solution)/shard_map/ppermute | solution.py:1135
  220.5 17.4 %collective-permute-start.29 = (bf16[256,768]{1,0:T(8,128)(2,1)S(1)}, bf16[256,768]{1,0:T(8,128)(2,1)S(1)}, u32[]{:S(2)}, u32[]{:S(2)}) collective-permute-start(bf16[256,768]{1,0:T(8,128)(2,1)S(1)} %get-tuple-element.467.pair_ref), channel_id=1, source_target_pairs={{0,2},{1,3},{2,0},{3,1},{4,6},{5,7},{6,4},{7,5},{8,10},{9,11},{10,... | collective-permute-start | bytes 1179656 | tf_op jit(solution)/shard_map/ppermute | solution.py:1135
  222.1 18.0 %collective-permute-start.30 = (bf16[256,768]{1,0:T(8,128)(2,1)S(1)}, bf16[256,768]{1,0:T(8,128)(2,1)S(1)}, u32[]{:S(2)}, u32[]{:S(2)}) collective-permute-start(bf16[256,768]{1,0:T(8,128)(2,1)S(1)} %get-tuple-element.468.pair_ref), channel_id=1, source_target_pairs={{0,2},{1,3},{2,0},{3,1},{4,6},{5,7},{6,4},{7,5},{8,10},{9,11},{10,... | collective-permute-start | bytes 1179656 | tf_op jit(solution)/shard_map/ppermute | solution.py:1135
  256.6 12.6 %collective-permute-start.33 = (bf16[256,768]{1,0:T(8,128)(2,1)}, bf16[256,768]{1,0:T(8,128)(2,1)S(1)}, u32[]{:S(2)}, u32[]{:S(2)}) collective-permute-start(bf16[256,768]{1,0:T(8,128)(2,1)} %get-tuple-element.349.pair_ref), channel_id=1, source_target_pairs={{0,2},{1,3},{2,0},{3,1},{4,6},{5,7},{6,4},{7,5},{8,10},{9,11},{10,... | collective-permute-start | bytes 1179656 | tf_op jit(solution)/shard_map/ppermute | solution.py:1135
  281.4 40.4 %collective-permute-start.37 = (bf16[384,1536]{1,0:T(8,128)(2,1)}, bf16[384,1536]{1,0:T(8,128)(2,1)S(1)}, u32[]{:S(2)}, u32[]{:S(2)}) collective-permute-start(bf16[384,1536]{1,0:T(8,128)(2,1)} %get-tuple-element.368), channel_id=1, source_target_pairs={{0,4},{4,0},{8,12},{12,8},{16,20},{20,16},{24,28},{28,24},{1,5},{5... | collective-permute-start | bytes 3538952 | tf_op jit(solution)/shard_map/ppermute | solution.py:1170
  303.2 25.3 %collective-permute-start.40 = (bf16[384,768]{1,0:T(8,128)(2,1)}, bf16[384,768]{1,0:T(8,128)(2,1)S(1)}, u32[]{:S(2)}, u32[]{:S(2)}) collective-permute-start(bf16[384,768]{1,0:T(8,128)(2,1)} %get-tuple-element.386), channel_id=1, source_target_pairs={{0,8},{4,12},{8,0},{12,4},{16,24},{20,28},{24,16},{28,20},{1,9},{5... | collective-permute-start | bytes 1769480 | tf_op jit(solution)/shard_map/ppermute | solution.py:1170
  306.8 19.6 %collective-permute-start.43 = (f32[4,768]{1,0:T(4,128)S(1)}, f32[4,768]{1,0:T(4,128)S(1)}, u32[]{:S(2)}, u32[]{:S(2)}) collective-permute-start(f32[4,768]{1,0:T(4,128)S(1)} %pad_maximum_fusion.8), channel_id=1, source_target_pairs={{0,1},{1,0},{2,3},{3,2},{4,5},{5,4},{6,7},{7,6},{8,9},{9,8},{10,11... | collective-permute-start | bytes 36872 | tf_op jit(solution)/shard_map/ppermute | solution.py:1135
  307.0 50.4 %collective-permute-start.46 = (bf16[256,768]{1,0:T(8,128)(2,1)S(1)}, bf16[256,768]{1,0:T(8,128)(2,1)S(1)}, u32[]{:S(2)}, u32[]{:S(2)}) collective-permute-start(bf16[256,768]{1,0:T(8,128)(2,1)S(1)} %copy-done.53), channel_id=1, source_target_pairs={{0,2},{1,3},{2,0},{3,1},{4,6},{5,7},{6,4},{7,5},{8,10},{9,11},{10,... | collective-permute-start | bytes 1179656 | tf_op jit(solution)/shard_map/ppermute | solution.py:1135
  325.9 23.5 %collective-permute-start.39 = (bf16[192,1536]{1,0:T(8,128)(2,1)}, bf16[192,1536]{1,0:T(8,128)(2,1)S(1)}, u32[]{:S(2)}, u32[]{:S(2)}) collective-permute-start(bf16[192,1536]{1,0:T(8,128)(2,1)} %get-tuple-element.395), channel_id=1, source_target_pairs={{0,8},{4,12},{8,0},{12,4},{16,24},{20,28},{24,16},{28,20},{1,9},{5... | collective-permute-start | bytes 1769480 | tf_op jit(solution)/shard_map/ppermute | solution.py:1170
  328.2 19.4 %collective-permute-start.42 = (bf16[256,768]{1,0:T(8,128)(2,1)S(1)}, bf16[256,768]{1,0:T(8,128)(2,1)S(1)}, u32[]{:S(2)}, u32[]{:S(2)}) collective-permute-start(bf16[256,768]{1,0:T(8,128)(2,1)S(1)} %copy-done.55), channel_id=1, source_target_pairs={{0,2},{1,3},{2,0},{3,1},{4,6},{5,7},{6,4},{7,5},{8,10},{9,11},{10,... | collective-permute-start | bytes 1179656 | tf_op jit(solution)/shard_map/ppermute | solution.py:1135
  331.6 16.0 %collective-permute-start.41 = (bf16[192,768]{1,0:T(8,128)(2,1)}, bf16[192,768]{1,0:T(8,128)(2,1)S(1)}, u32[]{:S(2)}, u32[]{:S(2)}) collective-permute-start(bf16[192,768]{1,0:T(8,128)(2,1)} %get-tuple-element.398), channel_id=1, source_target_pairs={{0,4},{4,0},{8,12},{12,8},{16,20},{20,16},{24,28},{28,24},{1,5},{5... | collective-permute-start | bytes 884744 | tf_op jit(solution)/shard_map/ppermute | solution.py:1170
  352.4 22.8 %collective-permute-start.48 = (bf16[96,1536]{1,0:T(8,128)(2,1)}, bf16[96,1536]{1,0:T(8,128)(2,1)S(1)}, u32[]{:S(2)}, u32[]{:S(2)}) collective-permute-start(bf16[96,1536]{1,0:T(8,128)(2,1)} %get-tuple-element.425), channel_id=1, source_target_pairs={{0,16},{4,20},{8,24},{12,28},{16,0},{20,4},{24,8},{28,12},{1,17},{... | collective-permute-start | bytes 884744 | tf_op jit(solution)/shard_map/ppermute | solution.py:1170
  356.6 18.6 %collective-permute-start.49 = (bf16[96,768]{1,0:T(8,128)(2,1)}, bf16[96,768]{1,0:T(8,128)(2,1)S(1)}, u32[]{:S(2)}, u32[]{:S(2)}) collective-permute-start(bf16[96,768]{1,0:T(8,128)(2,1)} %get-tuple-element.427), channel_id=1, source_target_pairs={{0,16},{4,20},{8,24},{12,28},{16,0},{20,4},{24,8},{28,12},{1,17},{... | collective-permute-start | bytes 442376 | tf_op jit(solution)/shard_map/ppermute | solution.py:1170
  (105 other events, 564.3 us)
Sparse Core Ops, SparseCore 0:
  10.4 81.6 all-gather.2
  95.1 53.0 all-gather.4
  247.4 96.3 reduce-scatter.1
